TPU v7x, 32 devices: a whole 2x2x4 slice. The times are simulated.
32 devices in a mesh: fsdp: 8 (over z, y), seq: 4 (over x, core).
Axes of the slice: x: 2, y: 2, z: 4, core: 2. Of those that a mesh axis runs over, the one named last changes fastest.
Arguments:
- tokens: bfloat16 [2, 8, 1024, 1024], P(None, 'fsdp', 'seq'), may hold values from -6 to 6
- doc_lengths: int32 [2, 8, 16], P(None, 'fsdp'), may hold values from 1 to 256, 1024 in all within a row
- cotangent: bfloat16 [2, 8, 1024, 1024], P(None, 'fsdp', 'seq'), may hold values from -6 to 6
- query_weight: bfloat16 [2, 1024, 1024], P(None, ('fsdp', 'seq')), may hold values from -0.1875 to 0.1875
- key_weight: bfloat16 [2, 1024, 1024], P(None, ('fsdp', 'seq')), may hold values from -0.1875 to 0.1875
- value_weight: bfloat16 [2, 1024, 1024], P(None, ('fsdp', 'seq')), may hold values from -0.1875 to 0.1875
- mix_weight: bfloat16 [2, 1024, 1024], P(None, ('fsdp', 'seq')), may hold values from -0.75 to 0.75
- query_bias: bfloat16 [2, 1024], P(None, ('fsdp', 'seq')), may hold values from -3 to 3
- value_bias: bfloat16 [2, 1024], P(None, ('fsdp', 'seq')), may hold values from -1.1953125 to 1.1953125
- mix_bias: bfloat16 [2, 1024], P(None, ('fsdp', 'seq')), may hold values from -1.796875 to 1.796875
- first_gain: bfloat16 [2, 1024], P(None, ('fsdp', 'seq')), may hold values from 0.5 to 1.5
- first_shift: bfloat16 [2, 1024], P(None, ('fsdp', 'seq')), may hold values from -1.796875 to 1.796875
- inner_weight: bfloat16 [2, 1024, 4096], P(None, ('fsdp', 'seq')), may hold values from -0.1875 to 0.1875
- inner_bias: bfloat16 [2, 4096], P(None, ('fsdp', 'seq')), may hold values from -1.796875 to 1.796875
- outer_weight: bfloat16 [2, 4096, 1024], P(None, ('fsdp', 'seq')), may hold values from -0.125 to 0.125
- outer_bias: bfloat16 [2, 1024], P(None, ('fsdp', 'seq')), may hold values from -1.796875 to 1.796875
- second_gain: bfloat16 [2, 1024], P(None, ('fsdp', 'seq')), may hold values from 0.5 to 1.5
- second_shift: bfloat16 [2, 1024], P(None, ('fsdp', 'seq')), may hold values from -1.796875 to 1.796875
Outputs:
- activations: float32 [2, 8, 1024, 1024], P(None, 'fsdp', 'seq')
- token_grad: float32 [2, 8, 1024, 1024], P(None, 'fsdp', 'seq')
- weight_query: float32 [2, 1024, 1024], P(None, ('fsdp', 'seq'))
- weight_key: float32 [2, 1024, 1024], P(None, ('fsdp', 'seq'))
- weight_value: float32 [2, 1024, 1024], P(None, ('fsdp', 'seq'))
- weight_mix: float32 [2, 1024, 1024], P(None, ('fsdp', 'seq'))
- bias_query: float32 [2, 1024], P(None, ('fsdp', 'seq'))
- bias_value: float32 [2, 1024], P(None, ('fsdp', 'seq'))
- bias_mix: float32 [2, 1024], P(None, ('fsdp', 'seq'))
- gain_first: float32 [2, 1024], P(None, ('fsdp', 'seq'))
- shift_first: float32 [2, 1024], P(None, ('fsdp', 'seq'))
- weight_inner: float32 [2, 1024, 4096], P(None, ('fsdp', 'seq'))
- bias_inner: float32 [2, 4096], P(None, ('fsdp', 'seq'))
- weight_outer: float32 [2, 4096, 1024], P(None, ('fsdp', 'seq'))
- bias_outer: float32 [2, 1024], P(None, ('fsdp', 'seq'))
- gain_second: float32 [2, 1024], P(None, ('fsdp', 'seq'))
- shift_second: float32 [2, 1024], P(None, ('fsdp', 'seq'))
Inputs may be any that keep to these rules, and one draw needn't show every extreme that they name: `doc_lengths`: in each packed row the first 15 entries are the documents in order and the last is padding at the row's end; the entries sum to 1024 and the largest is 256.
All inputs are finite; a program needn't handle non-finite values.
Results may differ from a plain program's by a relative error of at most 0.024.
Values may be sent and summed in bfloat16 or wider, within the bound.
No kernel may reach another device: no remote copies, remote signals or barrier semaphores. Data moves between devices by JAX's collectives and lax.ppermute only.
A program may use at most 384 MiB of HBM per device.

v0:
```python
from functools import partial

import jax
import jax.numpy as jnp
from jax import lax
from jax.sharding import PartitionSpec as P

D = 1024
HEAD_DIM = 64
SEQ_LEN = 1024
NDOC = 16
QBLOCK = 512


epsilon = 1e-05


def as_sent(array):
    return jax.tree.map(lambda a: a.astype(jnp.bfloat16) if a.dtype == jnp.float32 else a, array)


def layer_norm(total, gain, shift):
    center = jnp.mean(total, axis=-1, keepdims=True)
    centered = total - center
    spread = jnp.mean(centered * centered, axis=-1, keepdims=True)
    return centered * lax.rsqrt(spread + epsilon) * gain + shift


def forward_dot(left, right):
    return jnp.dot(left, right, preferred_element_type=jnp.float32)


def contract_rows(left, right):
    return lax.dot_general(
        left, right, (((0,), (0,)), ((), ())), preferred_element_type=jnp.float32
    )


def contract_cols(left, right):
    return lax.dot_general(
        left, right, (((1,), (1,)), ((), ())), preferred_element_type=jnp.float32
    )


def column_sum(values_low):
    return jnp.sum(values_low.astype(jnp.float32), axis=0)


def segments_of(lengths):
    bounds = jnp.cumsum(lengths, axis=1)
    places = lax.broadcasted_iota(jnp.int32, (1, SEQ_LEN, 1), 1)
    return jnp.sum((places >= bounds[:, None, :]).astype(jnp.int32), axis=2)


def allowed_block(segment, block_start):
    query_segment = lax.dynamic_slice_in_dim(segment, block_start, QBLOCK, 0)
    query_places = block_start + lax.broadcasted_iota(jnp.int32, (QBLOCK, 1), 0)
    key_places = lax.broadcasted_iota(jnp.int32, (1, SEQ_LEN), 1)
    same = (query_segment[:, None] == segment[None, :]) & (segment[None, :] != NDOC - 1)
    return same | (query_places == key_places)


def block_scores(query_block, key_heads, segment, block_start):
    scores = jnp.einsum("qhd,khd->hqk", query_block, key_heads, preferred_element_type=jnp.float32)
    scores = scores * HEAD_DIM ** (-0.5)
    return jnp.where(allowed_block(segment, block_start)[None], scores, -1e30)


def attend_forward(head_queries, head_keys, head_values, segment):
    head_count = head_queries.shape[1] // HEAD_DIM
    query_heads = head_queries.reshape(SEQ_LEN, head_count, HEAD_DIM)
    key_heads = head_keys.reshape(SEQ_LEN, head_count, HEAD_DIM)
    value_heads = head_values.reshape(SEQ_LEN, head_count, HEAD_DIM)

    def one_block(block_start):
        query_block = lax.dynamic_slice_in_dim(query_heads, block_start, QBLOCK, 0)
        scores = block_scores(query_block, key_heads, segment, block_start)
        top_score = jnp.max(scores, axis=2, keepdims=True)
        raised = jnp.exp(scores - top_score)
        totals = jnp.sum(raised, axis=2, keepdims=True)
        shares = (raised / totals).astype(jnp.bfloat16)
        mixed = jnp.einsum("hqk,khd->qhd", shares, value_heads, preferred_element_type=jnp.float32)
        mixed = mixed.astype(jnp.bfloat16).reshape(QBLOCK, head_count * HEAD_DIM)
        return (mixed, (top_score + jnp.log(totals))[:, :, 0])

    starts = jnp.arange(SEQ_LEN // QBLOCK, dtype=jnp.int32) * QBLOCK
    mixed, log_total = lax.map(one_block, starts)
    return (mixed.reshape(SEQ_LEN, head_count * HEAD_DIM), log_total)


def attend_backward(head_queries, head_keys, head_values, segment, log_total, head_grads):
    head_count = head_queries.shape[1] // HEAD_DIM
    width = head_count * HEAD_DIM
    query_heads = head_queries.reshape(SEQ_LEN, head_count, HEAD_DIM)
    key_heads = head_keys.reshape(SEQ_LEN, head_count, HEAD_DIM)
    value_heads = head_values.reshape(SEQ_LEN, head_count, HEAD_DIM)
    grad_heads = head_grads.reshape(SEQ_LEN, head_count, HEAD_DIM)
    scale = HEAD_DIM ** (-0.5)

    def one_block(carry, item):
        key_sum, value_sum = carry
        block_start, block_total = item
        query_block = lax.dynamic_slice_in_dim(query_heads, block_start, QBLOCK, 0)
        grad_block = lax.dynamic_slice_in_dim(grad_heads, block_start, QBLOCK, 0)
        scores = block_scores(query_block, key_heads, segment, block_start)
        shares = jnp.exp(scores - block_total[:, :, None])
        share_grads = jnp.einsum(
            "qhd,khd->hqk", grad_block, value_heads, preferred_element_type=jnp.float32
        )
        inner_sums = jnp.sum(shares * share_grads, axis=2, keepdims=True)
        score_grads = (shares * (share_grads - inner_sums)).astype(jnp.bfloat16)
        query_grad = (
            jnp.einsum("hqk,khd->qhd", score_grads, key_heads, preferred_element_type=jnp.float32)
            * scale
        )
        key_sum = (
            key_sum
            + jnp.einsum(
                "hqk,qhd->khd", score_grads, query_block, preferred_element_type=jnp.float32
            )
            * scale
        )
        value_sum = value_sum + jnp.einsum(
            "hqk,qhd->khd",
            shares.astype(jnp.bfloat16),
            grad_block,
            preferred_element_type=jnp.float32,
        )
        return ((key_sum, value_sum), query_grad.astype(jnp.bfloat16))

    starts = jnp.arange(SEQ_LEN // QBLOCK, dtype=jnp.int32) * QBLOCK
    zeros = jnp.zeros((SEQ_LEN, head_count, HEAD_DIM), jnp.float32)
    (key_sum, value_sum), query_grads = lax.scan(one_block, (zeros, zeros), (starts, log_total))
    return (
        query_grads.reshape(SEQ_LEN, width),
        key_sum.astype(jnp.bfloat16).reshape(SEQ_LEN, width),
        value_sum.astype(jnp.bfloat16).reshape(SEQ_LEN, width),
    )


def forward_layer(stream, layer_params, segment, row_count):
    (
        query_weight,
        key_weight,
        value_weight,
        mix_weight,
        query_bias,
        value_bias,
        mix_bias,
        first_gain,
        first_shift,
        inner_weight,
        inner_bias,
        outer_weight,
        outer_bias,
        second_gain,
        second_shift,
    ) = layer_params
    token_count = stream.shape[0] // row_count
    stream_low = stream.astype(jnp.bfloat16)
    queries = (forward_dot(stream_low, query_weight) + query_bias.astype(jnp.float32)).astype(
        jnp.bfloat16
    )
    key_rows = forward_dot(stream_low, key_weight).astype(jnp.bfloat16)
    values = (forward_dot(stream_low, value_weight) + value_bias.astype(jnp.float32)).astype(
        jnp.bfloat16
    )
    head_queries, head_keys, head_values = (
        lax.all_to_all(
            queries.reshape(row_count, token_count, D),
            "seq",
            split_axis=2,
            concat_axis=1,
            tiled=True,
        ),
        lax.all_to_all(
            key_rows.reshape(row_count, token_count, D),
            "seq",
            split_axis=2,
            concat_axis=1,
            tiled=True,
        ),
        lax.all_to_all(
            values.reshape(row_count, token_count, D),
            "seq",
            split_axis=2,
            concat_axis=1,
            tiled=True,
        ),
    )
    mixed, log_total = jax.vmap(attend_forward)(head_queries, head_keys, head_values, segment)
    mixed_tokens = lax.all_to_all(mixed, "seq", split_axis=1, concat_axis=2, tiled=True).reshape(
        -1, D
    )
    first_sum = stream + (forward_dot(mixed_tokens, mix_weight) + mix_bias.astype(jnp.float32))
    first = layer_norm(first_sum, first_gain.astype(jnp.float32), first_shift.astype(jnp.float32))
    first_low = first.astype(jnp.bfloat16)
    inner = forward_dot(first_low, inner_weight) + inner_bias.astype(jnp.float32)
    active = jax.nn.gelu(inner, approximate=False).astype(jnp.bfloat16)
    second_sum = first + (forward_dot(active, outer_weight) + outer_bias.astype(jnp.float32))
    output = layer_norm(
        second_sum, second_gain.astype(jnp.float32), second_shift.astype(jnp.float32)
    )
    kept_state = (
        stream_low,
        head_queries,
        head_keys,
        head_values,
        log_total,
        mixed_tokens,
        first_sum,
        first_low,
        inner,
        active,
        second_sum,
    )
    return (output, kept_state)


def backward_layer(upstream, layer_params, segment, kept_state, row_count):
    (
        query_weight,
        key_weight,
        value_weight,
        mix_weight,
        query_bias,
        value_bias,
        mix_bias,
        first_gain,
        first_shift,
        inner_weight,
        inner_bias,
        outer_weight,
        outer_bias,
        second_gain,
        second_shift,
    ) = layer_params
    (
        stream_low,
        head_queries,
        head_keys,
        head_values,
        log_total,
        mixed_tokens,
        first_sum,
        first_low,
        inner,
        active,
        second_sum,
    ) = kept_state
    second_pull = jax.vjp(
        layer_norm, second_sum, second_gain.astype(jnp.float32), second_shift.astype(jnp.float32)
    )[1]
    second_sum_grad, gain_second, shift_second = second_pull(upstream)
    second_low = second_sum_grad.astype(jnp.bfloat16)
    weight_outer = contract_rows(active, second_low)
    bias_outer = column_sum(second_low)
    active_grad = contract_cols(second_low, outer_weight)
    gelu_pull = jax.vjp(partial(jax.nn.gelu, approximate=False), inner)[1]
    inner_grad = gelu_pull(active_grad)[0].astype(jnp.bfloat16)
    weight_inner = contract_rows(first_low, inner_grad)
    bias_inner = column_sum(inner_grad)
    first_grad = second_sum_grad + contract_cols(inner_grad, inner_weight)
    first_pull = jax.vjp(
        layer_norm, first_sum, first_gain.astype(jnp.float32), first_shift.astype(jnp.float32)
    )[1]
    first_sum_grad, gain_first, shift_first = first_pull(first_grad)
    branch_low = first_sum_grad.astype(jnp.bfloat16)
    weight_mix = contract_rows(mixed_tokens, branch_low)
    bias_mix = column_sum(branch_low)
    mixed_grad = (
        contract_cols(branch_low, mix_weight).astype(jnp.bfloat16).reshape(row_count, -1, D)
    )
    head_grads = lax.all_to_all(mixed_grad, "seq", split_axis=2, concat_axis=1, tiled=True)
    query_grads, key_grads, value_grads = jax.vmap(attend_backward)(
        head_queries, head_keys, head_values, segment, log_total, head_grads
    )
    query_tokens, key_tokens, value_tokens = (
        lax.all_to_all(query_grads, "seq", split_axis=1, concat_axis=2, tiled=True),
        lax.all_to_all(key_grads, "seq", split_axis=1, concat_axis=2, tiled=True),
        lax.all_to_all(value_grads, "seq", split_axis=1, concat_axis=2, tiled=True),
    )
    query_tokens = query_tokens.reshape(-1, D)
    key_tokens = key_tokens.reshape(-1, D)
    value_tokens = value_tokens.reshape(-1, D)
    weight_query = contract_rows(stream_low, query_tokens)
    weight_key = contract_rows(stream_low, key_tokens)
    weight_value = contract_rows(stream_low, value_tokens)
    bias_query = column_sum(query_tokens)
    bias_value = column_sum(value_tokens)
    stream_grad = (
        first_sum_grad
        + contract_cols(query_tokens, query_weight)
        + contract_cols(key_tokens, key_weight)
        + contract_cols(value_tokens, value_weight)
    )
    layer_grads = (
        lax.psum_scatter(weight_query, ("fsdp", "seq"), scatter_dimension=0, tiled=True),
        lax.psum_scatter(weight_key, ("fsdp", "seq"), scatter_dimension=0, tiled=True),
        lax.psum_scatter(weight_value, ("fsdp", "seq"), scatter_dimension=0, tiled=True),
        lax.psum_scatter(weight_mix, ("fsdp", "seq"), scatter_dimension=0, tiled=True),
        lax.psum_scatter(bias_query, ("fsdp", "seq"), scatter_dimension=0, tiled=True),
        lax.psum_scatter(bias_value, ("fsdp", "seq"), scatter_dimension=0, tiled=True),
        lax.psum_scatter(bias_mix, ("fsdp", "seq"), scatter_dimension=0, tiled=True),
        lax.psum_scatter(gain_first, ("fsdp", "seq"), scatter_dimension=0, tiled=True),
        lax.psum_scatter(shift_first, ("fsdp", "seq"), scatter_dimension=0, tiled=True),
        lax.psum_scatter(weight_inner, ("fsdp", "seq"), scatter_dimension=0, tiled=True),
        lax.psum_scatter(bias_inner, ("fsdp", "seq"), scatter_dimension=0, tiled=True),
        lax.psum_scatter(weight_outer, ("fsdp", "seq"), scatter_dimension=0, tiled=True),
        lax.psum_scatter(bias_outer, ("fsdp", "seq"), scatter_dimension=0, tiled=True),
        lax.psum_scatter(gain_second, ("fsdp", "seq"), scatter_dimension=0, tiled=True),
        lax.psum_scatter(shift_second, ("fsdp", "seq"), scatter_dimension=0, tiled=True),
    )
    return (stream_grad, layer_grads)


def fetch_layer(shards, layer_index):
    return lax.all_gather(
        as_sent(tuple((tensor[layer_index] for tensor in shards))),
        ("fsdp", "seq"),
        axis=0,
        tiled=True,
    )


def body(
    tokens,
    doc_lengths,
    cotangent,
    query_weight,
    key_weight,
    value_weight,
    mix_weight,
    query_bias,
    value_bias,
    mix_bias,
    first_gain,
    first_shift,
    inner_weight,
    inner_bias,
    outer_weight,
    outer_bias,
    second_gain,
    second_shift,
):
    shards = (
        query_weight,
        key_weight,
        value_weight,
        mix_weight,
        query_bias,
        value_bias,
        mix_bias,
        first_gain,
        first_shift,
        inner_weight,
        inner_bias,
        outer_weight,
        outer_bias,
        second_gain,
        second_shift,
    )
    layer_count = query_weight.shape[0]
    micro_count = tokens.shape[0]
    batch_rows = micro_count * tokens.shape[1]
    segment = segments_of(doc_lengths.reshape(batch_rows, -1))
    stream = tokens.reshape(-1, D).astype(jnp.float32)
    stored = []
    states = []
    for layer_index in range(layer_count):
        layer_params = fetch_layer(shards, layer_index)
        stored.append(layer_params)
        stream, kept_state = forward_layer(stream, layer_params, segment, batch_rows)
        states.append(kept_state)
    upstream = cotangent.reshape(-1, D).astype(jnp.float32)
    totals = [None] * layer_count
    for layer_index in reversed(range(layer_count)):
        layer_params = fetch_layer(shards, layer_index)
        upstream, totals[layer_index] = backward_layer(
            upstream, layer_params, segment, states[layer_index], batch_rows
        )
    stacked = tuple(
        (
            jnp.stack([totals[layer_index][member] for layer_index in range(layer_count)])
            for member in range(15)
        )
    )
    return (stream.reshape(tokens.shape), upstream.reshape(tokens.shape)) + stacked


def solution(mesh):
    in_specs = (
        P(None, "fsdp", "seq", None),
        P(None, "fsdp", None),
        P(None, "fsdp", "seq", None),
        P(None, ("fsdp", "seq"), None),
        P(None, ("fsdp", "seq"), None),
        P(None, ("fsdp", "seq"), None),
        P(None, ("fsdp", "seq"), None),
        P(None, ("fsdp", "seq")),
        P(None, ("fsdp", "seq")),
        P(None, ("fsdp", "seq")),
        P(None, ("fsdp", "seq")),
        P(None, ("fsdp", "seq")),
        P(None, ("fsdp", "seq"), None),
        P(None, ("fsdp", "seq")),
        P(None, ("fsdp", "seq"), None),
        P(None, ("fsdp", "seq")),
        P(None, ("fsdp", "seq")),
        P(None, ("fsdp", "seq")),
    )
    out_specs = (
        P(None, "fsdp", "seq", None),
        P(None, "fsdp", "seq", None),
        P(None, ("fsdp", "seq"), None),
        P(None, ("fsdp", "seq"), None),
        P(None, ("fsdp", "seq"), None),
        P(None, ("fsdp", "seq"), None),
        P(None, ("fsdp", "seq")),
        P(None, ("fsdp", "seq")),
        P(None, ("fsdp", "seq")),
        P(None, ("fsdp", "seq")),
        P(None, ("fsdp", "seq")),
        P(None, ("fsdp", "seq"), None),
        P(None, ("fsdp", "seq")),
        P(None, ("fsdp", "seq"), None),
        P(None, ("fsdp", "seq")),
        P(None, ("fsdp", "seq")),
        P(None, ("fsdp", "seq")),
    )
    return jax.shard_map(body, mesh=mesh, in_specs=in_specs, out_specs=out_specs, check_vma=False)
```

profile of v0, /device:TPU:0, one launch (start us, length us, event | category | flops | bytes accessed | tf_op | source)
XLA Modules:
  0.0 3311.7 jit_solution(3563874103770204375)
XLA Ops:
  37.7 43.5 %all-reduce.39 = (bf16[1024]{0:T(1024)(128)(2,1)S(1)}, bf16[1024]{0:T(1024)(128)(2,1)S(1)}, bf16[1024]{0:T(1024)(128)(2,1)}, bf16[1024]{0:T(1024)(128)(2,1)}, bf...) all-reduce(bf16[1024]{0:T(1024)(128)(2,1)} %dynamic-update-slice.10, ...), channel_id=3, replica_groups=mesh['fsdp'=8,'seq'=4] {'fsdp','seq'}, use_global_device_ids=true, to_apply=%add.4 | all-reduce | flops 16384 | bytes 65536
  89.7 41.1 %all-gather.47.cloned.1.call-done = bf16[1,1024,1024]{2,1,0:T(8,128)(2,1)} async-done(((bf16[1,32,1024]{2,1,0:T(8,128)(2,1)}), bf16[1,1024,1024]{2,1,0:T(8,128)(2,1)}) %all-gather.47.cloned.1.call-update) | async-done | bytes 2097168 | tf_op jit(solution)/shard_map/all_gather | solution.py:318
  139.2 50.4 %all-gather.45.cloned.1.call-done = bf16[1,1024,1024]{2,1,0:T(8,128)(2,1)} async-done(((bf16[1,32,1024]{2,1,0:T(8,128)(2,1)}), bf16[1,1024,1024]{2,1,0:T(8,128)(2,1)}) %all-gather.45.cloned.1.call-update) | async-done | bytes 2097168 | tf_op jit(solution)/shard_map/all_gather | solution.py:318
  217.7 42.5 %while.64 = (s32[]{:T(128)}, bf16[2,2,512,256]{3,2,0,1:T(8,128)(2,1)}, f32[2,2,4,512]{3,2,1,0:T(4,128)S(1)}, s32[2]{0:T(128)S(1)}, s32[2,1024]{1,0:T(2,128)S(1)}...) while((s32[]{:T(128)}, ...), condition=%wide.region_5.6_spmd, body=%wide.region_2.5_spmd.sunk | while | flops 1128004096 | bytes 60986548 | solution.py:87
  269.2 49.4 %all-gather.10 = bf16[1,4096]{1,0:T(2,128)(2,1)S(1)} all-gather(bf16[1,128]{1,0:T(2,128)(2,1)S(1)} %get-tuple-element.678), channel_id=12, replica_groups=mesh['fsdp'=8,'seq'=4] {'fsdp','seq'}, dimensions={1}, use_global_device_ids=true | all-gather | bytes 8448 | tf_op jit(solution)/shard_map/all_gather | solution.py:318
  331.2 27.5 multiply_convert_fusion.3
  358.7 51.9 %all-gather.53.cloned.1.call-done = bf16[1,4096,1024]{2,1,0:T(8,128)(2,1)} async-done(((bf16[1,128,1024]{2,1,0:T(8,128)(2,1)}), bf16[1,4096,1024]{2,1,0:T(8,128)(2,1)}) %all-gather.53.cloned.1.call-update) | async-done | bytes 8388624 | tf_op jit(solution)/shard_map/all_gather | solution.py:318
  420.9 47.6 %all-gather.59.cloned.1.call-done = bf16[1,1024,1024]{2,1,0:T(8,128)(2,1)} async-done(((bf16[1,32,1024]{2,1,0:T(8,128)(2,1)}), bf16[1,1024,1024]{2,1,0:T(8,128)(2,1)}) %all-gather.59.cloned.1.call-update) | async-done | bytes 2097168 | tf_op jit(solution)/shard_map/all_gather | solution.py:318
  477.1 49.6 %all-gather.57.cloned.1.call-done = bf16[1,1024,1024]{2,1,0:T(8,128)(2,1)} async-done(((bf16[1,32,1024]{2,1,0:T(8,128)(2,1)}), bf16[1,1024,1024]{2,1,0:T(8,128)(2,1)}) %all-gather.57.cloned.1.call-update) | async-done | bytes 2097168 | tf_op jit(solution)/shard_map/all_gather | solution.py:318
  535.2 50.3 %all-gather.55.cloned.1.call-done = bf16[1,1024,1024]{2,1,0:T(8,128)(2,1)} async-done(((bf16[1,32,1024]{2,1,0:T(8,128)(2,1)}), bf16[1,1024,1024]{2,1,0:T(8,128)(2,1)}) %all-gather.55.cloned.1.call-update) | async-done | bytes 2097168 | tf_op jit(solution)/shard_map/all_gather | solution.py:318
  615.5 41.3 %while.65 = (s32[]{:T(128)}, bf16[2,2,512,256]{3,2,0,1:T(8,128)(2,1)S(1)}, f32[2,2,4,512]{3,2,1,0:T(4,128)S(1)}, s32[2]{0:T(128)S(1)}, s32[2,1024]{1,0:T(2,128)S...) while((s32[]{:T(128)}, ...), condition=%wide.region_13.14_spmd, body=%wide.region_10.13_spmd.sunk | while | flops 1128004096 | bytes 60985536 | solution.py:87
  662.5 47.2 %all-gather.25 = bf16[1,4096]{1,0:T(2,128)(2,1)S(1)} all-gather(bf16[1,128]{1,0:T(2,128)(2,1)S(1)} %copy-done.124), channel_id=27, replica_groups=mesh['fsdp'=8,'seq'=4] {'fsdp','seq'}, dimensions={1}, use_global_device_ids=true | all-gather | bytes 8448 | tf_op jit(solution)/shard_map/all_gather | solution.py:318
  724.7 27.5 multiply_convert_fusion.2
  752.2 52.0 %all-gather.65.cloned.1.call-done = bf16[1,4096,1024]{2,1,0:T(8,128)(2,1)} async-done(((bf16[1,128,1024]{2,1,0:T(8,128)(2,1)}), bf16[1,4096,1024]{2,1,0:T(8,128)(2,1)}) %all-gather.65.cloned.1.call-update) | async-done | bytes 8388624 | tf_op jit(solution)/shard_map/all_gather | solution.py:318
  817.5 14.3 convert_reduce_fusion
  850.4 14.4 all-to-all-done.8
  870.3 126.6 %while.66 = (s32[]{:T(128)}, f32[2,1024,4,64]{1,3,2,0:T(8,128)S(1)}, f32[2,1024,4,64]{1,3,2,0:T(8,128)}, bf16[2,2,512,4,64]{2,4,3,1,0:T(8,128)(2,1)}, s32[2]{0:T...) while((s32[]{:T(128)}, ...), condition=%wide.region_24.25_spmd.clone, body=%wide.region_22.24_spmd.clone.sunk | while | flops 2754083328 | bytes 199906720 | solution.py:133
  885.0 12.5 multiply_reduce_fusion.14
  897.5 14.9 multiply_convert_fusion.6
  947.8 12.5 multiply_reduce_fusion.14
  960.3 14.9 multiply_convert_fusion.6
  1006.5 10.5 all-to-all-done.10
  1024.9 11.0 all-to-all-done.11
  1065.8 14.9 convert_reduce_fusion.1
  1099.3 14.4 all-to-all-done.12
  1119.2 125.9 %while.67 = (s32[]{:T(128)}, f32[2,1024,4,64]{1,3,2,0:T(8,128)S(1)}, f32[2,1024,4,64]{1,3,2,0:T(8,128)}, bf16[2,2,512,4,64]{2,4,3,1,0:T(8,128)(2,1)}, s32[2]{0:T...) while((s32[]{:T(128)}, ...), condition=%wide.region_31.32_spmd.clone, body=%wide.region_29.31_spmd.clone.sunk | while | flops 2754083328 | bytes 199906720 | solution.py:133
  1133.8 13.1 multiply_reduce_fusion.15
  1147.0 14.9 multiply_convert_fusion.7
  1196.2 13.2 multiply_reduce_fusion.15
  1209.4 14.9 multiply_convert_fusion.7
  1345.4 17.0 all_to_all.240
  1374.5 10.4 fusion.200
  1386.1 10.4 fusion.199
  1398.1 10.8 fusion.171
  1410.5 10.5 fusion.174
  1430.3 14.0 all-reduce.42.cloned.1.call-done
  1456.3 132.7 %reduce-scatter.47.cloned.1.call-done = f32[32,1024]{1,0:T(8,128)} async-done(((f32[1024,1024]{1,0:T(8,128)}), f32[32,1024]{1,0:T(8,128)}) %reduce-scatter.47.cloned.1.call-update) | async-done | bytes 131088
  1590.3 137.7 %reduce-scatter.39.cloned.1.call-done = f32[32,1024]{1,0:T(8,128)} async-done(((f32[1024,1024]{1,0:T(8,128)}), f32[32,1024]{1,0:T(8,128)}) %reduce-scatter.39.cloned.1.call-update) | async-done | bytes 131088
  1729.2 137.4 %reduce-scatter.43.cloned.1.call-done = f32[32,1024]{1,0:T(8,128)} async-done(((f32[1024,1024]{1,0:T(8,128)}), f32[32,1024]{1,0:T(8,128)}) %reduce-scatter.43.cloned.1.call-update) | async-done | bytes 131088
  1868.0 137.5 %reduce-scatter.27.cloned.1.call-done = f32[32,1024]{1,0:T(8,128)} async-done(((f32[1024,1024]{1,0:T(8,128)}), f32[32,1024]{1,0:T(8,128)}) %reduce-scatter.27.cloned.1.call-update) | async-done | bytes 131088 | tf_op jit(solution)/shard_map/reduce_scatter | solution.py:301
  2005.5 138.8 %reduce-scatter.25.cloned.1.call-done = f32[32,1024]{1,0:T(8,128)} async-done(((f32[1024,1024]{1,0:T(8,128)}), f32[32,1024]{1,0:T(8,128)}) %reduce-scatter.25.cloned.1.call-update) | async-done | bytes 131088 | tf_op jit(solution)/shard_map/reduce_scatter | solution.py:301
  2146.0 137.4 %reduce-scatter.45.cloned.1.call-done = f32[32,1024]{1,0:T(8,128)} async-done(((f32[1024,1024]{1,0:T(8,128)}), f32[32,1024]{1,0:T(8,128)}) %reduce-scatter.45.cloned.1.call-update) | async-done | bytes 131088
  2284.7 137.7 %reduce-scatter.37.cloned.1.call-done = f32[32,1024]{1,0:T(8,128)} async-done(((f32[1024,1024]{1,0:T(8,128)}), f32[32,1024]{1,0:T(8,128)}) %reduce-scatter.37.cloned.1.call-update) | async-done | bytes 131088
  2423.6 137.8 %reduce-scatter.41.cloned.1.call-done = f32[32,1024]{1,0:T(8,128)} async-done(((f32[1024,1024]{1,0:T(8,128)}), f32[32,1024]{1,0:T(8,128)}) %reduce-scatter.41.cloned.1.call-update) | async-done | bytes 131088
  2564.3 178.1 %reduce-scatter.35.cloned.1.call-done = f32[128,1024]{1,0:T(8,128)} async-done(((f32[4096,1024]{1,0:T(8,128)}), f32[128,1024]{1,0:T(8,128)}) %reduce-scatter.35.cloned.1.call-update) | async-done | bytes 524304 | tf_op jit(solution)/shard_map/reduce_scatter | solution.py:309
  2742.4 186.9 %reduce-scatter.33.cloned.1.call-done = f32[128,1024]{1,0:T(8,128)} async-done(((f32[4096,1024]{1,0:T(8,128)}), f32[128,1024]{1,0:T(8,128)}) %reduce-scatter.33.cloned.1.call-update) | async-done | bytes 524304 | tf_op jit(solution)/shard_map/reduce_scatter | solution.py:309
  2931.6 184.2 %reduce-scatter.31.cloned.1.call-done = f32[32,4096]{1,0:T(8,128)} async-done(((f32[1024,4096]{1,0:T(8,128)}), f32[32,4096]{1,0:T(8,128)}) %reduce-scatter.31.cloned.1.call-update) | async-done | bytes 524304 | tf_op jit(solution)/shard_map/reduce_scatter | solution.py:307
  3115.8 186.8 %reduce-scatter.29.cloned.1.call-done = f32[32,4096]{1,0:T(8,128)} async-done(((f32[1024,4096]{1,0:T(8,128)}), f32[32,4096]{1,0:T(8,128)}) %reduce-scatter.29.cloned.1.call-update) | async-done | bytes 524304 | tf_op jit(solution)/shard_map/reduce_scatter | solution.py:307
  (712 shorter events, 643.5 us)
Async XLA Ops:
  7.3 73.9 %all-gather.43.cloned.1.call-start = ((), (), s32[]{:S(2)}) async-start(), calls=%async_computation.34 | async-start | bytes 2162688 | tf_op jit(solution)/shard_map/all_gather | solution.py:318
  9.0 121.8 %all-gather.47.cloned.1.call-start = ((), (), s32[]{:S(2)}) async-start(), calls=%async_computation.36 | async-start | bytes 2162688 | tf_op jit(solution)/shard_map/all_gather | solution.py:318
  10.6 179.0 %all-gather.45.cloned.1.call-start = ((), (), s32[]{:S(2)}) async-start(), calls=%async_computation.35 | async-start | bytes 2162688 | tf_op jit(solution)/shard_map/all_gather | solution.py:318
  12.2 309.9 %all-gather.49.cloned.1.call-start = ((), (), s32[]{:S(2)}) async-start(), calls=%async_computation.37 | async-start | bytes 2162688 | tf_op jit(solution)/shard_map/all_gather | solution.py:318
  13.8 317.5 %all-gather.51.cloned.1.call-start = ((), (), s32[]{:S(2)}) async-start(), calls=%async_computation.38 | async-start | bytes 8650752 | tf_op jit(solution)/shard_map/all_gather | solution.py:318
  15.7 395.0 %all-gather.53.cloned.1.call-start = ((), (), s32[]{:S(2)}) async-start(), calls=%async_computation.39 | async-start | bytes 8650752 | tf_op jit(solution)/shard_map/all_gather | solution.py:318
  17.6 450.9 %all-gather.59.cloned.1.call-start = ((), (), s32[]{:S(2)}) async-start(), calls=%async_computation.42 | async-start | bytes 2162688 | tf_op jit(solution)/shard_map/all_gather | solution.py:318
  18.4 508.3 %all-gather.57.cloned.1.call-start = ((), (), s32[]{:S(2)}) async-start(), calls=%async_computation.41 | async-start | bytes 2162688 | tf_op jit(solution)/shard_map/all_gather | solution.py:318
  19.1 566.4 %all-gather.55.cloned.1.call-start = ((), (), s32[]{:S(2)}) async-start(), calls=%async_computation.40 | async-start | bytes 2162688 | tf_op jit(solution)/shard_map/all_gather | solution.py:318
  19.9 691.0 %all-gather.61.cloned.1.call-start = ((), (), s32[]{:S(2)}) async-start(), calls=%async_computation.43 | async-start | bytes 2162688 | tf_op jit(solution)/shard_map/all_gather | solution.py:318
  86.1 49.6 %all-to-all-start = ((bf16[2,256,1024]{1,0,2:T(2,128)(2,1)}), bf16[2,256,1024]{1,0,2:T(2,128)(2,1)S(1)}, u32[]{:S(2)}, u32[]{:S(2)}) async-start(bf16[2,256,1024]{1,0,2:T(2,128)(2,1)} %copy.190), calls=%async_computation | async-start | bytes 2097152 | tf_op jit(solution)/shard_map/all_to_all | solution.py:169
  135.7 61.4 %all-to-all-start.2 = ((bf16[2,256,1024]{1,0,2:T(2,128)(2,1)}), bf16[2,256,1024]{1,0,2:T(2,128)(2,1)S(1)}, u32[]{:S(2)}, u32[]{:S(2)}) async-start(bf16[2,256,1024]{1,0,2:T(2,128)(2,1)} %copy.194), calls=%async_computation.2 | async-start | bytes 2097152 | tf_op jit(solution)/shard_map/all_to_all | solution.py:183
  197.1 18.0 all-to-all-start.1
  200.6 524.1 %all-gather.63.cloned.1.call-start = ((), (), s32[]{:S(2)}) async-start(), calls=%async_computation.44 | async-start | bytes 8650752 | tf_op jit(solution)/shard_map/all_gather | solution.py:318
  264.3 54.4 %all-to-all-start.3 = ((bf16[2,1024,256]{2,0,1:T(2,128)(2,1)}), bf16[2,1024,256]{2,0,1:T(2,128)(2,1)}, u32[]{:S(2)}, u32[]{:S(2)}) async-start(bf16[2,1024,256]{2,0,1:T(2,128)(2,1)} %copy.197), calls=%async_computation.3 | async-start | bytes 2097152 | tf_op jit(solution)/shard_map/all_to_all | solution.py:192
  268.6 142.0 %copy-start.87 = (f32[1024]{0:T(1024)}, f32[1024]{0:T(1024)S(1)}, u32[]{:S(2)}) copy-start(f32[1024]{0:T(1024)S(1)} %convert_element_type.297) | copy-start | bytes 12292
  268.7 142.0 %copy-start.97 = (f32[1024]{0:T(1024)}, f32[1024]{0:T(1024)S(1)}, u32[]{:S(2)}) copy-start(f32[1024]{0:T(1024)S(1)} %convert_element_type.298) | copy-start | bytes 12292
  420.9 164.7 %copy-start.9 = (bf16[512,1024]{1,0:T(8,128)(2,1)}, bf16[512,1024]{1,0:T(8,128)(2,1)S(1)}, u32[]{:S(2)}) copy-start(bf16[512,1024]{1,0:T(8,128)(2,1)S(1)} %fusion.129) | copy-start | bytes 3145732
  473.4 58.2 %all-to-all-start.6 = ((bf16[2,256,1024]{1,0,2:T(2,128)(2,1)}), bf16[2,256,1024]{1,0,2:T(2,128)(2,1)S(1)}, u32[]{:S(2)}, u32[]{:S(2)}) async-start(bf16[2,256,1024]{1,0,2:T(2,128)(2,1)} %copy.203), calls=%async_computation.6 | async-start | bytes 2097152 | tf_op jit(solution)/shard_map/all_to_all | solution.py:183
  531.6 61.4 %all-to-all-start.5 = ((bf16[2,256,1024]{1,0,2:T(2,128)(2,1)}), bf16[2,256,1024]{1,0,2:T(2,128)(2,1)S(1)}, u32[]{:S(2)}, u32[]{:S(2)}) async-start(bf16[2,256,1024]{1,0,2:T(2,128)(2,1)} %copy.201), calls=%async_computation.5 | async-start | bytes 2097152 | tf_op jit(solution)/shard_map/all_to_all | solution.py:176
  593.0 18.8 all-to-all-start.4
  597.3 206.9 %all-gather.65.cloned.1.call-start = ((), (), s32[]{:S(2)}) async-start(), calls=%async_computation.45 | async-start | bytes 8650752 | tf_op jit(solution)/shard_map/all_gather | solution.py:318
  658.9 50.9 %all-to-all-start.7 = ((bf16[2,1024,256]{2,0,1:T(2,128)(2,1)}), bf16[2,1024,256]{2,0,1:T(2,128)(2,1)S(1)}, u32[]{:S(2)}, u32[]{:S(2)}) async-start(bf16[2,1024,256]{2,0,1:T(2,128)(2,1)} %copy.206), calls=%async_computation.7 | async-start | bytes 2097152 | tf_op jit(solution)/shard_map/all_to_all | solution.py:192
  662.5 179.1 %copy-start.90 = (f32[1024]{0:T(1024)}, f32[1024]{0:T(1024)S(1)}, u32[]{:S(2)}) copy-start(f32[1024]{0:T(1024)S(1)} %convert_element_type.305) | copy-start | bytes 12292
  662.5 141.7 %copy-start.99 = (f32[1024]{0:T(1024)}, f32[1024]{0:T(1024)S(1)}, u32[]{:S(2)}) copy-start(f32[1024]{0:T(1024)S(1)} %convert_element_type.306) | copy-start | bytes 12292
  715.0 126.5 %copy-start.35 = (f32[512,1024]{1,0:T(8,128)}, f32[512,1024]{1,0:T(8,128)S(1)}, u32[]{:S(2)}) copy-start(f32[512,1024]{1,0:T(8,128)S(1)} %get-tuple-element.701) | copy-start | bytes 6291460
  715.0 126.5 %copy-start.73 = (f32[512]{0:T(512)}, f32[512]{0:T(512)S(1)}, u32[]{:S(2)}) copy-start(f32[512]{0:T(512)S(1)} %broadcast_multiply_fusion.1) | copy-start | bytes 6148
  715.4 126.2 %copy-start.95 = (f32[512]{0:T(512)}, f32[512]{0:T(512)S(1)}, u32[]{:S(2)}) copy-start(f32[512]{0:T(512)S(1)} %fusion.169) | copy-start | bytes 6148
  846.8 18.0 all-to-all-start.8
  999.1 18.0 all-to-all-start.10
  1017.1 18.8 all-to-all-start.11
  1035.9 18.0 all-to-all-start.9
  1095.6 18.1 all-to-all-start.12
  1254.1 18.0 all-to-all-start.13
  1273.0 18.8 all-to-all-start.15
  1277.3 167.0 %all-reduce.42.cloned.1.call-start = ((), (), s32[]{:S(2)}) async-start(), calls=%async_computation.52 | async-start | bytes 196608
  1295.0 294.0 %reduce-scatter.47.cloned.1.call-start = ((), (), s32[]{:S(2)}) async-start(), calls=%async_computation.51 | async-start | bytes 4325376
  1299.6 428.4 %reduce-scatter.39.cloned.1.call-start = ((), (), s32[]{:S(2)}) async-start(), calls=%async_computation.47 | async-start | bytes 4325376
  1304.1 562.5 %reduce-scatter.43.cloned.1.call-start = ((), (), s32[]{:S(2)}) async-start(), calls=%async_computation.49 | async-start | bytes 4325376
  1308.9 696.6 %reduce-scatter.27.cloned.1.call-start = ((), (), s32[]{:S(2)}) async-start(), calls=%async_computation.29 | async-start | bytes 4325376 | tf_op jit(solution)/shard_map/reduce_scatter | solution.py:301
  1314.6 829.7 %reduce-scatter.25.cloned.1.call-start = ((), (), s32[]{:S(2)}) async-start(), calls=%async_computation.28 | async-start | bytes 4325376 | tf_op jit(solution)/shard_map/reduce_scatter | solution.py:301
  1319.5 963.9 %reduce-scatter.45.cloned.1.call-start = ((), (), s32[]{:S(2)}) async-start(), calls=%async_computation.50 | async-start | bytes 4325376
  1330.5 1091.8 %reduce-scatter.37.cloned.1.call-start = ((), (), s32[]{:S(2)}) async-start(), calls=%async_computation.46 | async-start | bytes 4325376
  1341.7 1219.7 %reduce-scatter.41.cloned.1.call-start = ((), (), s32[]{:S(2)}) async-start(), calls=%async_computation.48 | async-start | bytes 4325376
  1373.3 1369.1 %reduce-scatter.35.cloned.1.call-start = ((), (), s32[]{:S(2)}) async-start(), calls=%async_computation.33 | async-start | bytes 17301504 | tf_op jit(solution)/shard_map/reduce_scatter | solution.py:309
  1384.9 1544.4 %reduce-scatter.33.cloned.1.call-start = ((), (), s32[]{:S(2)}) async-start(), calls=%async_computation.32 | async-start | bytes 17301504 | tf_op jit(solution)/shard_map/reduce_scatter | solution.py:309
  1396.6 1719.3 %reduce-scatter.31.cloned.1.call-start = ((), (), s32[]{:S(2)}) async-start(), calls=%async_computation.31 | async-start | bytes 17301504 | tf_op jit(solution)/shard_map/reduce_scatter | solution.py:307
  1409.0 1893.7 %reduce-scatter.29.cloned.1.call-start = ((), (), s32[]{:S(2)}) async-start(), calls=%async_computation.30 | async-start | bytes 17301504 | tf_op jit(solution)/shard_map/reduce_scatter | solution.py:307
  (137 other events, 2465.9 us)
Sparse Core Ops, SparseCore 0:
  11.5 59.1 all-gather.42
  74.2 56.5 all-gather.46
  134.3 55.3 all-gather.44
  192.3 55.2 all-gather.48
  250.9 80.2 all-gather.50
  334.5 76.0 all-gather.52
  413.5 54.9 all-gather.58
  471.4 55.3 all-gather.56
  530.2 55.3 all-gather.54
  588.2 55.3 all-gather.60
  647.0 77.6 all-gather.62
  728.0 76.1 all-gather.64
  1295.1 149.1 all-reduce.41
  1446.4 142.4 reduce-scatter.46
  1591.1 136.8 reduce-scatter.38
  1730.1 136.5 reduce-scatter.42
  1868.8 136.6 reduce-scatter.26
  2007.6 136.6 reduce-scatter.24
  2146.6 136.7 reduce-scatter.44
  2285.6 136.7 reduce-scatter.36
  2424.6 136.7 reduce-scatter.40
  2563.7 178.5 reduce-scatter.34
  2744.7 184.5 reduce-scatter.32
  2931.5 184.3 reduce-scatter.30
  3118.1 184.4 reduce-scatter.28
where the time goes:
time: 3320 us; the launch traced here: 3310 us
  waiting for transfers between devices  2290 us (69%)
  matrix products  448 us (13%)
  local copies, waits for them, and re-layouts  190 us (6%)
  blocking collectives  157 us (5%)
  other arithmetic  133 us (4%)
  starting transfers between devices  57.1 us (2%)
    unnamed x32, waiting for transfers between devices  839 us
    reduce_scatter x2, waiting for transfers between devices, backward_layer(): lax.psum_scatter(weight_inner, ('fsdp', 'seq'), scatter_dimension=0, tile...  371 us
    reduce_scatter x2, waiting for transfers between devices, backward_layer(): lax.psum_scatter(weight_outer, ('fsdp', 'seq'), scatter_dimension=0, tile...  365 us
    all_gather x12, waiting for transfers between devices, fetch_layer(): lax.all_gather(as_sent(tuple((tensor[layer_index] for tensor in shards)))...  358 us
    reduce_scatter x2, waiting for transfers between devices, backward_layer(): lax.psum_scatter(weight_mix, ('fsdp', 'seq'), scatter_dimension=0, tiled=...  276 us
    dot_general x12, matrix products, forward_dot(): return jnp.dot(left, right, preferred_element_type=jnp.float32)  98.3 us
    all_gather x2, blocking collectives, fetch_layer(): lax.all_gather(as_sent(tuple((tensor[layer_index] for tensor in shards)))...  96.6 us
  transfers between devices with their start and end apart: 40, of which 31 were waited for; matrix products, arithmetic and copies ran while one was open for 12% of the time, Pallas kernels for 0%

commit v1 on v0

v1 whole, which is shorter than its diff:
```python
import math

import jax
import jax.numpy as jnp
from jax import lax
from jax.experimental import pallas as pl
from jax.experimental.pallas import tpu as pltpu
from jax.sharding import PartitionSpec as P

D = 1024
FF = 4096
HEAD_DIM = 64
HEADS = D // HEAD_DIM
SEQ_LEN = 1024
NDOC = 16
epsilon = 1e-05
AXES = ("fsdp", "seq")
f32 = jnp.float32
bf16 = jnp.bfloat16


def dot(left, right):
    return jnp.dot(left, right, preferred_element_type=f32)


def contract_rows(left, right):
    return lax.dot_general(left, right, (((0,), (0,)), ((), ())), preferred_element_type=f32)


def contract_cols(left, right):
    return lax.dot_general(left, right, (((1,), (1,)), ((), ())), preferred_element_type=f32)


def tie(value, *others):
    return lax.optimization_barrier((value, others))[0]


def pairs(move):
    out = []
    for i in range(32):
        z, y, x, c = i // 8, i // 4 % 2, i // 2 % 2, i % 2
        z, y, x, c = move(z, y, x, c)
        out.append((i, z * 8 + y * 4 + x * 2 + c))
    return out


TO_CORE = pairs(lambda z, y, x, c: (z, y, x, 1 - c))
TO_X = pairs(lambda z, y, x, c: (z, y, 1 - x, c))
TO_Y = pairs(lambda z, y, x, c: (z, 1 - y, x, c))
TO_Z = [pairs(lambda z, y, x, c, k=k: ((z + k) % 4, y, x, c)) for k in range(4)]


def send(value, to):
    return lax.ppermute(value, AXES, to)


def coordinates():
    fsdp, seq = lax.axis_index("fsdp"), lax.axis_index("seq")
    return jnp.stack([fsdp // 2, fsdp % 2, seq // 2, seq % 2]).astype(jnp.int32)


def place(coords, pieces, shapes, moves):
    count = len(moves(0, 0, 0, 0, None, None))

    total = len(pieces)

    def kernel(coords_ref, *refs):
        sources, targets = refs[:total], refs[total : total + len(shapes)]
        buffers, in_sems, out_sems = refs[total + len(shapes) : -2], refs[-2], refs[-1]
        loads = [
            pltpu.make_async_copy(source, buffer, in_sems.at[n])
            for n, (source, buffer) in enumerate(zip(sources, buffers))
        ]
        for load in loads:
            load.start()
        todo = moves(coords_ref[0], coords_ref[1], coords_ref[2], coords_ref[3], buffers, targets)
        stores = [
            (n, pltpu.make_async_copy(view, target, out_sems.at[k]))
            for k, (n, view, target) in enumerate(todo)
        ]
        for piece, load in enumerate(loads):
            load.wait()
            for n, store in stores:
                if n == piece:
                    store.start()
        for _, store in stores:
            store.wait()

    size = sum(math.prod(shape) for shape in shapes) * 4
    return pl.pallas_call(
        kernel,
        in_specs=[pl.BlockSpec(memory_space=pltpu.SMEM)]
        + [pl.BlockSpec(memory_space=pl.ANY)] * len(pieces),
        out_specs=[pl.BlockSpec(memory_space=pl.ANY)] * len(shapes),
        out_shape=[jax.ShapeDtypeStruct(shape, bf16) for shape in shapes],
        scratch_shapes=[pltpu.VMEM(p.shape, bf16) for p in pieces]
        + [pltpu.SemaphoreType.DMA((total,)), pltpu.SemaphoreType.DMA((count,))],
        compiler_params=pltpu.CompilerParams(vmem_limit_bytes=40 << 20),
        cost_estimate=pl.CostEstimate(flops=0, bytes_accessed=size, transcendentals=0),
    )(coords, *pieces)


class Gather:
    def __init__(self, coords):
        self.coords = coords
        self.last_z = ()
        self.last_xy = ()

    def __call__(self, pack, split, shapes, routed):
        rows, width = pack.shape
        if self.last_z:
            pack = tie(pack, *self.last_z)
        from_z = [pack] + [send(pack, TO_Z[4 - k]) for k in (1, 2, 3)]
        self.last_z = from_z[1:]
        sizes = (split, rows - split)

        def by_z(z, y, x, c, src, dst):
            return [
                (k, src and src[k].at[lo : lo + n], dst and dst[r].at[(z + k) % 4])
                for k in range(4)
                for r, (lo, n) in enumerate(zip((0, split), sizes))
            ]

        first, second = place(self.coords, from_z, [(4, n, width) for n in sizes], by_z)
        if self.last_xy:
            first, second = tie((first, second), *self.last_xy)
        first_y, second_x = send(first, TO_Y), send(second, TO_X)

        def by_two(z, y, x, c, src, dst):
            return [
                (0, src and src[0], dst and dst[0].at[:, y]),
                (1, src and src[1], dst and dst[0].at[:, 1 - y]),
                (2, src and src[2], dst and dst[1].at[:, x]),
                (3, src and src[3], dst and dst[1].at[:, 1 - x]),
            ]

        first, second = place(
            self.coords,
            [first, first_y, second, second_x],
            [(4, 2, n, width) for n in sizes],
            by_two,
        )
        first_x, second_y = send(first, TO_X), send(second, TO_Y)
        self.last_xy = (first_x, second_y)
        first_c, second_c = send(first, TO_CORE), send(second, TO_CORE)
        first_xc, second_yc = send(first_x, TO_CORE), send(second_y, TO_CORE)

        def by_block(z, y, x, c, src, dst):
            out = []
            for n, (x2, c2) in enumerate(((x, c), (1 - x, c), (x, 1 - c), (1 - x, 1 - c))):
                for lo, hi, target, column in routed[0]:
                    for z2 in range(4):
                        out.append(
                            (
                                n,
                                src and src[n].at[z2, :, lo:hi],
                                dst
                                and dst[target].at[
                                    z2, :, x2, c2, :, column * width : (column + 1) * width
                                ],
                            )
                        )
            for n, (y2, c2) in enumerate(((y, c), (1 - y, c), (y, 1 - c), (1 - y, 1 - c))):
                for lo, hi, target, column in routed[1]:
                    for z2 in range(4):
                        out.append(
                            (
                                4 + n,
                                src and src[4 + n].at[z2, :, lo:hi],
                                dst
                                and dst[target].at[
                                    z2, y2, :, c2, :, column * width : (column + 1) * width
                                ],
                            )
                        )
            return out

        return place(
            self.coords,
            [first, first_x, first_c, first_xc, second, second_y, second_c, second_yc],
            [(4, 2, 2, 2) + shape for shape in shapes],
            by_block,
        )


def pick(value, index, axis):
    return lax.dynamic_index_in_dim(value, index, axis, keepdims=False)


def summed_shards(coords, grads, x_first):
    z, y, x, c = coords[0], coords[1], coords[2], coords[3]
    blocks = [g.reshape(16, 2, g.shape[0] // 32, g.shape[1]) for g in grads]

    def joined(index):
        return jnp.concatenate([pick(b, index, 1) for b in blocks], axis=1)

    other = send(joined(1 - c).astype(bf16), TO_CORE)
    own = joined(c)
    rows, width = own.shape[1:]
    own = own.reshape(4, 2, 2, rows, width)
    other = other.reshape(4, 2, 2, rows, width)
    axis, index, to = (2, x, TO_X) if x_first else (1, y, TO_Y)

    def total(where):
        return pick(own, where, axis).astype(f32) + pick(other, where, axis).astype(f32)

    own, other = total(index), send(total(1 - index).astype(bf16), to)
    index, to = (y, TO_Y) if x_first else (x, TO_X)

    def total_two(where):
        return pick(own, where, 1).astype(f32) + pick(other, where, 1).astype(f32)

    other2 = send(total_two(1 - index).astype(bf16), to)
    quarter = total_two(index) + other2.astype(f32)
    result = pick(quarter, z, 0)
    for k in (1, 2, 3):
        result = result + send(pick(quarter, (z + k) % 4, 0).astype(bf16), TO_Z[k]).astype(f32)
    parts, start = [], 0
    for g in grads:
        size = g.shape[0] // 32
        parts.append(result[start : start + size])
        start += size
    return parts


def norm_forward(total):
    center = jnp.mean(total, axis=-1, keepdims=True)
    centered = total - center
    spread = jnp.mean(centered * centered, axis=-1, keepdims=True)
    scale = lax.rsqrt(spread + epsilon)
    return centered * scale, scale


def norm_backward(total, gain, upstream):
    unit, scale = norm_forward(total)
    lifted = upstream * gain
    grad = scale * (
        lifted
        - jnp.mean(lifted, axis=-1, keepdims=True)
        - unit * jnp.mean(lifted * unit, axis=-1, keepdims=True)
    )
    return grad, jnp.sum(upstream * unit, axis=0), jnp.sum(upstream, axis=0)


def column_sum(values):
    return jnp.sum(values.astype(f32), axis=0)


def heads_of(rows):
    return rows.reshape(rows.shape[0], HEADS, HEAD_DIM)


def masked_scores(queries, keys, allowed):
    scores = jnp.einsum("qhd,khd->hqk", queries, keys, preferred_element_type=f32)
    return jnp.where(allowed[None], scores * HEAD_DIM ** (-0.5), -1e30)


def attend_forward(queries, keys, values, allowed):
    scores = masked_scores(heads_of(queries), heads_of(keys), allowed)
    top_score = jnp.max(scores, axis=2, keepdims=True)
    raised = jnp.exp(scores - top_score)
    totals = jnp.sum(raised, axis=2, keepdims=True)
    shares = (raised / totals).astype(bf16)
    mixed = jnp.einsum("hqk,khd->qhd", shares, heads_of(values), preferred_element_type=f32)
    return mixed.astype(bf16).reshape(queries.shape), top_score + jnp.log(totals)


def attend_backward(queries, keys, values, allowed, log_total, grads):
    queries, keys, values, grads = map(heads_of, (queries, keys, values, grads))
    scale = HEAD_DIM ** (-0.5)
    shares = jnp.exp(masked_scores(queries, keys, allowed) - log_total)
    share_grads = jnp.einsum("qhd,khd->hqk", grads, values, preferred_element_type=f32)
    inner_sums = jnp.sum(shares * share_grads, axis=2, keepdims=True)
    score_grads = (shares * (share_grads - inner_sums)).astype(bf16)
    query_grad = jnp.einsum("hqk,khd->qhd", score_grads, keys, preferred_element_type=f32) * scale
    key_grad = jnp.einsum("hqk,qhd->khd", score_grads, queries, preferred_element_type=f32) * scale
    value_grad = jnp.einsum(
        "hqk,qhd->khd", shares.astype(bf16), grads, preferred_element_type=f32
    )
    flat = lambda a: a.reshape(a.shape[0], D)
    return flat(query_grad).astype(bf16), flat(key_grad), flat(value_grad)


def make_body(fsdp_size, seq_size):
    half = seq_size // 2
    staged = (fsdp_size, seq_size) == (8, 4)
    device_count = fsdp_size * seq_size
    across = [(i, (i + half) % seq_size) for i in range(seq_size)]
    groups = [[m * half + j for j in range(half)] for m in range(2)]
    length = SEQ_LEN // seq_size

    def gather_siblings(rows):
        if staged:
            return jnp.stack([rows, send(rows, TO_CORE)])
        return lax.all_gather(rows, "seq", axis_index_groups=groups)

    def scatter_siblings(own_order):
        if staged:
            return own_order[0] + send(own_order[1].astype(bf16), TO_CORE).astype(f32)
        return lax.psum_scatter(own_order, "seq", axis_index_groups=groups)

    def body(tokens, doc_lengths, cotangent, *shards):
        (
            query_weight,
            key_weight,
            value_weight,
            mix_weight,
            query_bias,
            value_bias,
            mix_bias,
            first_gain,
            first_shift,
            inner_weight,
            inner_bias,
            outer_weight,
            outer_bias,
            second_gain,
            second_shift,
        ) = shards
        layer_count = query_weight.shape[0]
        seq = lax.axis_index("seq")
        row = seq // half
        coords = coordinates()
        rows_held = D // device_count
        inner_held = FF // device_count

        def vector_rows(small, wide):
            return jnp.concatenate(
                [jnp.concatenate([v[layer] for v in small]) for layer in range(layer_count)]
                + [wide.reshape(-1)]
            )

        small_vectors = (
            query_bias,
            value_bias,
            mix_bias,
            first_gain,
            first_shift,
            outer_bias,
            second_gain,
            second_shift,
        )
        vector_count = len(small_vectors) * layer_count
        mine = vector_rows(small_vectors, inner_bias)
        held = mine.shape[0]
        if staged:
            padded = jnp.pad(mine, (0, 1024 - held)).reshape(8, 128)
            parts = jnp.stack([padded] + [send(padded, TO_Z[4 - k]) for k in (1, 2, 3)])
            z, y, x, c = coords[0], coords[1], coords[2], coords[3]
            parts = jnp.roll(parts, z, axis=0)

            def both(own, other, place_of, axis):
                return jnp.where(
                    place_of == 0,
                    jnp.stack([own, other], axis),
                    jnp.stack([other, own], axis),
                )

            parts = both(parts, send(parts, TO_Y), y, 1)
            parts = both(parts, send(parts, TO_X), x, 2)
            parts = both(parts, send(parts, TO_CORE), c, 3)
            every = parts.reshape(device_count, 1024)[:, :held]
        else:
            every = lax.all_gather(mine, AXES)
        every = every.astype(f32)
        small_held = vector_count * rows_held
        small_all = (
            every[:, :small_held]
            .reshape(device_count, vector_count, rows_held)
            .transpose(1, 0, 2)
            .reshape(layer_count, len(small_vectors), D)
        )
        wide_all = (
            every[:, small_held:]
            .reshape(device_count, layer_count, inner_held)
            .transpose(1, 0, 2)
            .reshape(layer_count, FF)
        )

        gather = Gather(coords)

        def attention_weights(layer):
            parts = [w[layer] for w in (query_weight, key_weight, value_weight, mix_weight)]
            if not staged:
                return [lax.all_gather(p, AXES, axis=0, tiled=True) for p in parts]
            r = rows_held
            got = gather(
                jnp.concatenate(parts),
                2 * r,
                [(r, D)] * 4,
                (((0, r, 0, 0), (r, 2 * r, 1, 0)), ((0, r, 2, 0), (r, 2 * r, 3, 0))),
            )
            return [g.reshape(D, D) for g in got]

        def forward_weights(layer):
            inner, outer = inner_weight[layer], outer_weight[layer]
            if not staged:
                return [lax.all_gather(p, AXES, axis=0, tiled=True) for p in (inner, outer)]
            r = rows_held
            blocks = FF // D
            got = gather(
                jnp.concatenate([inner[:, D * n : D * (n + 1)] for n in range(blocks)] + [outer]),
                blocks * r,
                [(r, FF), (inner_held, D)],
                (
                    tuple((r * n, r * (n + 1), 0, n) for n in range(blocks)),
                    ((0, inner_held, 1, 0),),
                ),
            )
            return [got[0].reshape(D, FF), got[1].reshape(FF, D)]

        def own_row(both_rows):
            kept = pick(both_rows, row, 0)
            return jnp.concatenate(
                [kept, lax.ppermute(pick(both_rows, 1 - row, 0), "seq", across)]
            )

        def both_rows(values):
            kept = values[:length]
            other = lax.ppermute(values[length:].astype(bf16), "seq", across).astype(f32)
            return jnp.where(row == 0, jnp.stack([kept, other]), jnp.stack([other, kept]))

        stream_start = own_row(tokens.reshape(2, length, D))
        upstream_start = own_row(cotangent.reshape(2, length, D))

        lengths = pick(doc_lengths.reshape(2, NDOC), row, 0)
        bounds = jnp.cumsum(lengths)
        within = lax.iota(jnp.int32, length)

        def positions(s):
            return jnp.concatenate([s * length + within, (s + half) % seq_size * length + within])

        def segments(places):
            return jnp.sum((places[:, None] >= bounds[None, :]).astype(jnp.int32), axis=1)

        query_places = positions(seq)
        if staged:
            key_places = jnp.concatenate([positions(seq), positions(seq ^ 1)])
        else:
            key_places = jnp.concatenate([positions(row * half + j) for j in range(half)])
        query_segment, key_segment = segments(query_places), segments(key_places)
        allowed = (
            (query_segment[:, None] == key_segment[None, :]) & (key_segment[None, :] != NDOC - 1)
        ) | (query_places[:, None] == key_places[None, :])

        stream = stream_start.astype(f32)
        saved = []
        for layer in range(layer_count):
            q_bias, v_bias, m_bias, gain1, shift1, o_bias, gain2, shift2 = [
                small_all[layer, n] for n in range(len(small_vectors))
            ]
            w_query, w_key, w_value, w_mix = attention_weights(layer)
            w_inner, w_outer = forward_weights(layer)
            stream_low = stream.astype(bf16)
            queries = (dot(stream_low, w_query) + q_bias).astype(bf16)
            key_rows = dot(stream_low, w_key).astype(bf16)
            values = (dot(stream_low, w_value) + v_bias).astype(bf16)
            all_keys = gather_siblings(key_rows).reshape(SEQ_LEN, D)
            all_values = gather_siblings(values).reshape(SEQ_LEN, D)
            mixed, log_total = attend_forward(queries, all_keys, all_values, allowed)
            first_sum = stream + (dot(mixed, w_mix) + m_bias)
            first = norm_forward(first_sum)[0] * gain1 + shift1
            first_low = first.astype(bf16)
            inner = dot(first_low, w_inner) + wide_all[layer]
            below = 0.5 * (1.0 + lax.erf(inner * (0.5**0.5)))
            active = (inner * below).astype(bf16)
            slope = (below + inner * jnp.exp(-0.5 * inner * inner) * (2 * math.pi) ** -0.5).astype(
                bf16
            )
            second_sum = first + (dot(active, w_outer) + o_bias)
            stream = norm_forward(second_sum)[0] * gain2 + shift2
            saved.append(
                (
                    (w_query, w_key, w_value, w_mix, w_inner, w_outer, gain1, gain2),
                    (stream_low, queries, all_keys, all_values, log_total, mixed),
                    (first_sum, first_low, slope, active, second_sum),
                )
            )
        activations = both_rows(stream)

        upstream = upstream_start.astype(f32)
        small_grads = [None] * layer_count
        wide_grads = [None] * layer_count
        results = [None] * layer_count

        def reduced(grads, x_first):
            if staged:
                return summed_shards(coords, [g.astype(bf16) for g in grads], x_first)
            return [lax.psum_scatter(g, AXES, scatter_dimension=0, tiled=True) for g in grads]

        for layer in reversed(range(layer_count)):
            (w_query, w_key, w_value, w_mix, w_inner, w_outer, gain1, gain2), kept, rest = saved[layer]
            stream_low, queries, all_keys, all_values, log_total, mixed = kept
            first_sum, first_low, slope, active, second_sum = rest
            second_grad, gain2_grad, shift2_grad = norm_backward(second_sum, gain2, upstream)
            second_low = second_grad.astype(bf16)
            (outer_grad,) = reduced([contract_rows(active, second_low)], False)
            inner_low = (contract_cols(second_low, w_outer) * slope).astype(bf16)
            (inner_grad,) = reduced([contract_rows(first_low, inner_low)], True)
            first_grad = second_grad + contract_cols(inner_low, w_inner)
            first_sum_grad, gain1_grad, shift1_grad = norm_backward(first_sum, gain1, first_grad)
            branch_low = first_sum_grad.astype(bf16)
            mix_terms = contract_rows(mixed, branch_low)
            mixed_grad = contract_cols(branch_low, w_mix).astype(bf16)
            query_low, key_terms, value_terms = attend_backward(
                queries, all_keys, all_values, allowed, log_total, mixed_grad
            )
            n = 2 * length
            key_low = scatter_siblings(key_terms.reshape(half, n, D)).astype(bf16)
            value_low = scatter_siblings(value_terms.reshape(half, n, D)).astype(bf16)
            value_grad, mix_grad = reduced([contract_rows(stream_low, value_low), mix_terms], False)
            query_grad, key_grad = reduced(
                [contract_rows(stream_low, query_low), contract_rows(stream_low, key_low)], True
            )
            upstream = (
                first_sum_grad
                + contract_cols(query_low, w_query)
                + contract_cols(key_low, w_key)
                + contract_cols(value_low, w_value)
            )
            small_grads[layer] = jnp.stack(
                [
                    column_sum(query_low),
                    column_sum(value_low),
                    column_sum(branch_low),
                    gain1_grad,
                    shift1_grad,
                    column_sum(second_low),
                    gain2_grad,
                    shift2_grad,
                ]
            )
            wide_grads[layer] = column_sum(inner_low)
            results[layer] = (query_grad, key_grad, value_grad, mix_grad, inner_grad, outer_grad)
        token_grad = both_rows(upstream)

        small_terms = (
            jnp.stack(small_grads)
            .reshape(vector_count, device_count, rows_held)
            .transpose(1, 0, 2)
            .reshape(device_count, small_held)
        )
        wide_terms = (
            jnp.stack(wide_grads)
            .reshape(layer_count, device_count, inner_held)
            .transpose(1, 0, 2)
            .reshape(device_count, layer_count * inner_held)
        )
        terms = jnp.concatenate([small_terms, wide_terms], axis=1)
        if staged:
            terms = jnp.pad(terms, ((0, 0), (0, 1024 - held))).reshape(device_count * 8, 128)
            (own_terms,) = summed_shards(coords, [terms], True)
            own_terms = own_terms.reshape(-1)[:held]
        else:
            own_terms = lax.psum_scatter(terms, AXES, scatter_dimension=0, tiled=False)
        small_own = own_terms[:small_held].reshape(layer_count, len(small_vectors), rows_held)
        wide_own = own_terms[small_held:].reshape(layer_count, inner_held)
        query_g, key_g, value_g, mix_g, inner_g, outer_g = [
            jnp.stack([results[layer][n] for layer in range(layer_count)]) for n in range(6)
        ]
        return (
            activations.reshape(tokens.shape),
            token_grad.reshape(tokens.shape),
            query_g,
            key_g,
            value_g,
            mix_g,
            small_own[:, 0],
            small_own[:, 1],
            small_own[:, 2],
            small_own[:, 3],
            small_own[:, 4],
            inner_g,
            wide_own,
            outer_g,
            small_own[:, 5],
            small_own[:, 6],
            small_own[:, 7],
        )

    return body


def solution(mesh):
    tokens = P(None, "fsdp", "seq", None)
    matrix, vector = P(None, AXES, None), P(None, AXES)
    in_specs = (tokens, P(None, "fsdp", None), tokens) + (matrix,) * 4 + (vector,) * 5
    in_specs += (matrix, vector, matrix, vector, vector, vector)
    out_specs = (tokens, tokens) + (matrix,) * 4 + (vector,) * 5
    out_specs += (matrix, vector, matrix, vector, vector, vector)
    body = make_body(mesh.shape["fsdp"], mesh.shape["seq"])
    return jax.shard_map(body, mesh=mesh, in_specs=in_specs, out_specs=out_specs, check_vma=False)
```

time: 3320 us -> 1210 us (0.36)
  waiting for transfers between devices: 2290 us -> 322 us
  blocking collectives: 157 us -> 0 us
  matrix products: 448 us -> 336 us
  starting transfers between devices: 57.1 us -> 162 us
  Pallas kernels: 0 us -> 57.9 us
  other arithmetic: 133 us -> 178 us
  local copies, waits for them, and re-layouts: 190 us -> 148 us
    reduce_scatter x6 -> x0, waiting for transfers between devices: 1010 us -> none  [the longest x2 371 us: backward_layer(): lax.psum_scatter(weight_inner, ('fsdp', 'seq'), scatter_dimension=0, tile...]
    unnamed x32 -> x0, waiting for transfers between devices: 839 us -> none
    all_gather x12 -> x0, waiting for transfers between devices: 358 us -> none  [fetch_layer(): lax.all_gather(as_sent(tuple((tensor[layer_index] for tensor in shards)))...]
    ppermute x0 -> x116, waiting for transfers between devices: none -> 322 us  [the longest x112 318 us: send(): return lax.ppermute(value, AXES, to)]
    ppermute x0 -> x116, starting transfers between devices: none -> 162 us  [the longest x112 158 us: send(): return lax.ppermute(value, AXES, to)]
    all_gather x2 -> x0, blocking collectives: 96.6 us -> none  [fetch_layer(): lax.all_gather(as_sent(tuple((tensor[layer_index] for tensor in shards)))...]
    all_to_all x15 -> x0, waiting for transfers between devices: 83.8 us -> none  [the longest x2 28.8 us: backward_layer(): lax.all_to_all(mixed_grad, 'seq', split_axis=2, concat_axis=1, tiled=True)]
    dot_general x40 -> x24, matrix products: 308 us -> 228 us  [the longest x12 53.6 us: dot(): return jnp.dot(left, right, preferred_element_type=f32)]
  transfers between devices with their start and end apart: 40 -> 116, of which waited for: 31 -> 42; matrix products, arithmetic and copies ran while one was open for 12% -> 40% of each run, Pallas kernels for 0% -> 5%
where the time goes in v1:
time: 1210 us
  matrix products  336 us (28%)
  waiting for transfers between devices  322 us (27%)
  other arithmetic  178 us (15%)
  starting transfers between devices  162 us (13%)
  local copies, waits for them, and re-layouts  148 us (12%)
  Pallas kernels  57.9 us (5%)
    ppermute x112, waiting for transfers between devices, send(): return lax.ppermute(value, AXES, to)  318 us
    ppermute x112, starting transfers between devices, send(): return lax.ppermute(value, AXES, to)  158 us
    pallas_call x12, Pallas kernels, place(): pl.pallas_call(kernel, in_specs=[pl.BlockSpec(memory_space=pltpu.SMEM)] +...  57.9 us
    dot_general x12, matrix products, contract_cols(): lax.dot_general(left, right, (((1,), (1,)), ((), ())), preferred_element_...  56.9 us
    convert_element_type x2, other arithmetic, attend_backward(): score_grads = (shares * (share_grads - inner_sums)).astype(bf16)  56.4 us
    dot_general x12, matrix products, dot(): return jnp.dot(left, right, preferred_element_type=f32)  53.6 us
    dot_general x12, matrix products, contract_rows(): lax.dot_general(left, right, (((0,), (0,)), ((), ())), preferred_element_...  50.8 us
    dot_general x2, matrix products, attend_backward(): jnp.einsum('qhd,khd->hqk', grads, values, preferred_element_type=f32)  44.6 us
  transfers between devices with their start and end apart: 116, of which 42 were waited for; matrix products, arithmetic and copies ran while one was open for 40% of the time, Pallas kernels for 5%

profile of v1, /device:TPU:0, one launch (start us, length us, event | category | flops | bytes accessed | tf_op | source)
XLA Modules:
  0.0 1206.9 jit_solution(15054299529255529718)
XLA Ops:
  24.6 9.3 collective-permute-done.2.refs_2_
  58.7 18.0 %collective-permute-done.21.refs_2_ = bf16[256,1024]{1,0:T(8,128)(2,1)S(1)} collective-permute-done((bf16[256,1024]{1,0:T(8,128)(2,1)}, bf16[256,1024]{1,0:T(8,128)(2,1)S(1)}, u32[]{:S(2)}, u32[]{:S(2)}) %collective-permute-start.21) | collective-permute-done | bytes 524320 | tf_op jit(solution)/shard_map/ppermute | solution.py:54
  79.1 11.6 collective-permute-start.33
  98.3 11.1 collective-permute-done.32.refs_2_
  147.5 11.9 collective-permute-done.24.refs_3_
  195.7 15.7 %fusion.166 = (f32[16,512]{1,0:T(8,128)S(1)}, f32[16,512,1024]{2,1,0:T(8,128)}) fusion(bf16[512,16,64]{0,2,1:T(8,128)(2,1)} %bitcast.736, bf16[1024,16,64]{0,2,1:T(8,128)(2,1)} %reshape_reshape.11, pred[512,1024]{1,0:T(8,128)(4,1)} %compare_or_fusion), kind=kOutput, calls=%fused_computation.514 | convolution fusion | flops 1098899456 | bytes 37257216 | tf_op jit(solution)/shard_map/qhd,khd->hqk/dot_general | solution.py:254
  213.5 14.3 %fusion = f32[16,512]{1,0:T(8,128)S(1)} fusion(f32[16,512,1024]{2,1,0:T(8,128)} %get-tuple-element.260, f32[16,512]{1,0:T(8,128)S(1)} %get-tuple-element.259), kind=kLoop, calls=%fused_computation.12 | loop fusion | flops 16769024 | bytes 33619968 | tf_op jit(solution)/shard_map/reduce_sum | solution.py:262
  245.7 13.0 %fusion.51 = bf16[16,64,512]{2,1,0:T(8,128)(2,1)S(1)} fusion(bf16[1024,16,64]{0,2,1:T(8,128)(2,1)S(1)} %copy-done.39, f32[16,512,1024]{2,1,0:T(8,128)} %get-tuple-element.260, f32[16,512]{1,0:T(8,128)S(1)} %fusion, f32[16,512]{1,0:T(8,128)S(1)} %get-tuple-element.259), kind=kOutput, calls=%fused_computation.201 | convolution fusion | flops 1099431936 | bytes 36765696 | tf_op jit(solution)/shard_map/hqk,khd->qhd/dot_general | solution.py:264
  258.8 10.6 collective-permute-done.36.refs_1_
  274.2 19.5 %collective-permute-done.39.refs_5_ = bf16[4,2,64,1024]{3,2,1,0:T(8,128)(2,1)S(1)} collective-permute-done((bf16[4,2,64,1024]{3,2,1,0:T(8,128)(2,1)S(1)}, bf16[4,2,64,1024]{3,2,1,0:T(8,128)(2,1)S(1)}, u32[]{:S(2)}, u32[]{:S(2)}) %collective-permute-start.39) | collective-permute-done | bytes 1048608 | tf_op jit(solution)/shard_map/ppermute | solution.py:54
  295.8 11.9 shard_map.310
  307.7 10.6 multiply_convert_fusion.5
  336.6 13.4 %collective-permute-done.48.refs_3_ = bf16[4,128,1024]{2,1,0:T(8,128)(2,1)} collective-permute-done((bf16[4,128,1024]{2,1,0:T(8,128)(2,1)}, bf16[4,128,1024]{2,1,0:T(8,128)(2,1)}, u32[]{:S(2)}, u32[]{:S(2)}) %collective-permute-start.48) | collective-permute-done | bytes 1048608 | tf_op jit(solution)/shard_map/ppermute | solution.py:54
  373.8 15.0 %fusion.169 = (f32[16,512]{1,0:T(8,128)S(1)}, f32[16,512,1024]{2,1,0:T(8,128)}) fusion(bf16[512,16,64]{0,2,1:T(8,128)(2,1)S(1)} %bitcast.738, bf16[1024,16,64]{0,2,1:T(8,128)(2,1)S(1)} %reshape_reshape.26, pred[512,1024]{1,0:T(8,128)(4,1)} %compare_or_fusion), kind=kOutput, calls=%fused_computation.517 | convolution fusion | flops 1098899456 | bytes 37257216 | tf_op jit(solution)/shard_map/qhd,khd->hqk/dot_general | solution.py:254
  398.4 14.3 %fusion.1 = f32[16,512]{1,0:T(8,128)S(1)} fusion(f32[16,512,1024]{2,1,0:T(8,128)} %get-tuple-element.268, f32[16,512]{1,0:T(8,128)S(1)} %get-tuple-element.267), kind=kLoop, calls=%fused_computation.13 | loop fusion | flops 16769024 | bytes 33619968 | tf_op jit(solution)/shard_map/reduce_sum | solution.py:262
  413.3 13.2 %fusion.50 = bf16[16,64,512]{2,1,0:T(8,128)(2,1)S(1)} fusion(bf16[1024,16,64]{0,2,1:T(8,128)(2,1)S(1)} %reshape_reshape.12, f32[16,512,1024]{2,1,0:T(8,128)} %get-tuple-element.268, f32[16,512]{1,0:T(8,128)S(1)} %fusion.1, f32[16,512]{1,0:T(8,128)S(1)} %get-tuple-element.267), kind=kOutput, calls=%fused_computation.200 | convolution fusion | flops 1099431936 | bytes 36765696 | tf_op jit(solution)/shard_map/hqk,khd->qhd/dot_general | solution.py:264
  429.9 12.4 %shard_map.316 = (bf16[4,2,2,2,32,4096]{5,4,3,2,1,0:T(8,128)(2,1)}, bf16[4,2,2,2,128,1024]{5,4,3,2,1,0:T(8,128)(2,1)}) custom-call(s32[4]{0:T(128)S(1)} %pad_add_fusion.2.coords_ref, bf16[4,2,128,1024]{3,2,1,0:T(8,128)(2,1)} %get-tuple-element.87.refs_0_, bf16[4,2,128,1024]{3,2,1,0:T(8,128)(2,1)} %collective-permute-done.49.refs_1_, ...), custom_call_target="tpu_custom_call" | custom-call | bytes 33554432 | tf_op jit(solution)/shard_map/pallas_call | solution.py:90
  442.3 9.9 multiply_convert_fusion.4
  464.5 12.6 %convert_reduce_fusion = (f32[4096]{0:T(1024)}, bf16[512,4096]{1,0:T(8,128)(2,1)}) fusion(f32[512,4096]{1,0:T(8,128)} %get-tuple-element.272, f32[4096]{0:T(1024)S(1)} %bitcast.834, bf16[4096,1024]{1,0:T(8,128)(2,1)} %bitcast.871, f32[512,1024]{1,0:T(8,128)S(1)} %get-tuple-element.114), kind=kOutput, calls=%fused_computation.34 | convolution fusion | flops 4326944768 | bytes 23101440 | tf_op jit(solution)/shard_map/dot_general | solution.py:31
  477.0 9.6 multiply_reduce_fusion.2
  493.1 9.2 convolution_convert_fusion.2
  510.9 15.2 %fusion.25 = f32[1024,16,64]{0,2,1:T(8,128)} fusion(bf16[512,16,64]{0,2,1:T(8,128)(2,1)S(1)} %bitcast.746, f32[16,512,1024]{2,1,0:T(8,128)} %get-tuple-element.268, f32[16,512]{1,0:T(8,128)S(1)} %log_add_fusion.1), kind=kOutput, calls=%fused_computation.82 | convolution fusion | flops 1090519040 | bytes 38830080 | tf_op jit(solution)/shard_map/hqk,qhd->khd/dot_general | solution.py:277
  526.1 22.3 %multiply_reduce_fusion.1 = (f32[16,512]{1,0:T(8,128)S(1)}, f32[16,512,1024]{2,1,0:T(8,128)}) fusion(f32[16,512,1024]{2,1,0:T(8,128)} %get-tuple-element.268, f32[16,512]{1,0:T(8,128)S(1)} %log_add_fusion.1, bf16[512,16,64]{0,2,1:T(8,128)(2,1)S(1)} %bitcast.747, bf16[1024,16,64]{0,2,1:T(8,128)(2,1)S(1)} %reshape_reshape.12), kind=kOutput, calls=%fused_computation.4 | convolution fusion | flops 1098899456 | bytes 70320128 | tf_op jit(solution)/shard_map/qhd,khd->hqk/dot_general | solution.py:272
  548.4 28.4 %multiply_convert_fusion.1 = bf16[16,512,1024]{2,1,0:T(8,128)(2,1)} fusion(f32[16,512,1024]{2,1,0:T(8,128)} %get-tuple-element.277, f32[16,512,1024]{2,1,0:T(8,128)} %get-tuple-element.268, f32[16,512]{1,0:T(8,128)S(1)} %get-tuple-element.276, f32[16,512]{1,0:T(8,128)S(1)} %log_add_fusion.1), kind=kLoop, calls=%fused_computation.3 | loop fusion | flops 33554432 | bytes 83951616 | tf_op jit(solution)/shard_map/convert_element_type | solution.py:274
  576.8 12.1 %convert_reduce_fusion.6 = (f32[16,64]{1,0:T(8,128)S(1)}, bf16[16,64,512]{2,1,0:T(8,128)(2,1)}) fusion(bf16[1024,16,64]{0,2,1:T(8,128)(2,1)S(1)} %copy-done.26, bf16[16,512,1024]{2,1,0:T(8,128)(2,1)} %multiply_convert_fusion.1), kind=kOutput, calls=%fused_computation.134 | convolution fusion | flops 1075837952 | bytes 19927040 | tf_op jit(solution)/shard_map/hqk,khd->qhd/dot_general | solution.py:275
  588.9 9.0 multiply_bitcast_fusion.1
  600.6 7.8 constant_dynamic-slice_fusion.3
  608.5 8.4 constant_dynamic-slice_fusion.30
  645.6 12.2 %convert_reduce_fusion.1 = (f32[4096]{0:T(1024)S(1)}, bf16[512,4096]{1,0:T(8,128)(2,1)}) fusion(f32[512,4096]{1,0:T(8,128)} %get-tuple-element.264, f32[4096]{0:T(1024)S(1)} %bitcast.832, bf16[4096,1024]{1,0:T(8,128)(2,1)} %bitcast.867, f32[512,1024]{1,0:T(8,128)S(1)} %get-tuple-element.108), kind=kOutput, calls=%fused_computation.35 | convolution fusion | flops 4326944768 | bytes 23101440 | tf_op jit(solution)/shard_map/dot_general | solution.py:31
  657.9 7.5 multiply_reduce_fusion.4
  688.6 15.4 %fusion.28 = f32[1024,16,64]{0,2,1:T(8,128)} fusion(bf16[512,16,64]{0,2,1:T(8,128)(2,1)S(1)} %bitcast.748, f32[16,512,1024]{2,1,0:T(8,128)} %get-tuple-element.260, f32[16,512]{1,0:T(8,128)S(1)} %copy-done.82), kind=kOutput, calls=%fused_computation.83 | convolution fusion | flops 1090519040 | bytes 38830080 | tf_op jit(solution)/shard_map/hqk,qhd->khd/dot_general | solution.py:277
  704.0 22.3 %multiply_reduce_fusion = (f32[16,512]{1,0:T(8,128)S(1)}, f32[16,512,1024]{2,1,0:T(8,128)}) fusion(f32[16,512,1024]{2,1,0:T(8,128)} %get-tuple-element.260, f32[16,512]{1,0:T(8,128)S(1)} %copy-done.82, bf16[512,16,64]{0,2,1:T(8,128)(2,1)S(1)} %bitcast.749, bf16[1024,16,64]{0,2,1:T(8,128)(2,1)S(1)} %copy-done.40), kind=kOutput, calls=%fused_computation.1 | convolution fusion | flops 1098899456 | bytes 70320128 | tf_op jit(solution)/shard_map/qhd,khd->hqk/dot_general | solution.py:272
  726.3 28.1 %multiply_convert_fusion = bf16[16,512,1024]{2,1,0:T(8,128)(2,1)} fusion(f32[16,512,1024]{2,1,0:T(8,128)} %get-tuple-element.281, f32[16,512,1024]{2,1,0:T(8,128)} %get-tuple-element.260, f32[16,512]{1,0:T(8,128)S(1)} %get-tuple-element.280, f32[16,512]{1,0:T(8,128)S(1)} %copy-done.82), kind=kLoop, calls=%fused_computation | loop fusion | flops 33554432 | bytes 83951616 | tf_op jit(solution)/shard_map/convert_element_type | solution.py:274
  754.4 12.1 %convert_reduce_fusion.10 = (f32[16,64]{1,0:T(8,128)S(1)}, bf16[16,64,512]{2,1,0:T(8,128)(2,1)}) fusion(bf16[1024,16,64]{0,2,1:T(8,128)(2,1)S(1)} %copy-done.24, bf16[16,512,1024]{2,1,0:T(8,128)(2,1)} %multiply_convert_fusion), kind=kOutput, calls=%fused_computation.140 | convolution fusion | flops 1075837952 | bytes 19927040 | tf_op jit(solution)/shard_map/hqk,khd->qhd/dot_general | solution.py:275
  766.5 9.0 multiply_bitcast_fusion
  795.6 8.3 constant_dynamic-slice_fusion
  803.9 8.0 constant_dynamic-slice_fusion.4
  838.4 10.9 collective-permute-start.89
  876.8 13.9 %collective-permute-done.81 = bf16[4,2,64,1024]{3,2,0,1:T(8,128)(2,1)S(1)} collective-permute-done((bf16[4,2,64,1024]{3,2,0,1:T(8,128)(2,1)S(1)}, bf16[4,2,64,1024]{3,2,0,1:T(8,128)(2,1)S(1)}, u32[]{:S(2)}, u32[]{:S(2)}) %collective-permute-start.81) | collective-permute-done | bytes 1048608 | tf_op jit(solution)/shard_map/ppermute | solution.py:54
  901.1 17.8 %collective-permute-done.69 = bf16[4,2,64,1024]{3,2,0,1:T(8,128)(2,1)S(1)} collective-permute-done((bf16[4,2,64,1024]{3,2,0,1:T(8,128)(2,1)S(1)}, bf16[4,2,64,1024]{3,2,0,1:T(8,128)(2,1)S(1)}, u32[]{:S(2)}, u32[]{:S(2)}) %collective-permute-start.69) | collective-permute-done | bytes 1048608 | tf_op jit(solution)/shard_map/ppermute | solution.py:54
  967.8 10.3 collective-permute-done.63
  993.1 36.6 %collective-permute-done.76 = bf16[4,64,1024]{2,1,0:T(8,128)(2,1)} collective-permute-done((bf16[4,64,1024]{2,1,0:T(8,128)(2,1)}, bf16[4,64,1024]{2,1,0:T(8,128)(2,1)}, u32[]{:S(2)}, u32[]{:S(2)}) %collective-permute-start.76) | collective-permute-done | bytes 524320 | tf_op jit(solution)/shard_map/ppermute | solution.py:54
  1059.5 52.4 %collective-permute-done.112 = bf16[4,128,1024]{2,1,0:T(8,128)(2,1)S(1)} collective-permute-done((bf16[4,128,1024]{2,1,0:T(8,128)(2,1)S(1)}, bf16[4,128,1024]{2,1,0:T(8,128)(2,1)S(1)}, u32[]{:S(2)}, u32[]{:S(2)}) %collective-permute-start.112) | collective-permute-done | bytes 1048608 | tf_op jit(solution)/shard_map/ppermute | solution.py:54
  1125.9 14.8 %collective-permute-start.102 = (bf16[32,4096]{1,0:T(8,128)(2,1)S(1)}, bf16[32,4096]{1,0:T(8,128)(2,1)S(1)}, u32[]{:S(2)}, u32[]{:S(2)}) collective-permute-start(bf16[32,4096]{1,0:T(8,128)(2,1)S(1)} %get-tuple-element.147), channel_id=1, source_target_pairs={{0,16},{1,17},{2,18},{3,19},{4,20},{5,21},{6,22},{7,23},{8,24},{9,... | collective-permute-start | bytes 786440 | tf_op jit(solution)/shard_map/ppermute | solution.py:54
  1141.5 8.7 collective-permute-done.114
  1150.8 8.1 collective-permute-done.102
  1173.5 11.4 collective-permute-start.96
  1184.9 13.6 %collective-permute-done.108 = bf16[128,1024]{1,0:T(8,128)(2,1)S(1)} collective-permute-done((bf16[128,1024]{1,0:T(8,128)(2,1)S(1)}, bf16[128,1024]{1,0:T(8,128)(2,1)S(1)}, u32[]{:S(2)}, u32[]{:S(2)}) %collective-permute-start.108) | collective-permute-done | bytes 262176 | tf_op jit(solution)/shard_map/ppermute | solution.py:54
  (778 shorter events, 511.8 us)
Async XLA Ops:
  45.2 31.6 %collective-permute-start.21 = (bf16[256,1024]{1,0:T(8,128)(2,1)}, bf16[256,1024]{1,0:T(8,128)(2,1)S(1)}, u32[]{:S(2)}, u32[]{:S(2)}) collective-permute-start(bf16[256,1024]{1,0:T(8,128)(2,1)} %get-tuple-element.62.refs_0_), channel_id=1, source_target_pairs={{0,16},{1,17},{2,18},{3,19},{4,20},{5,21},{6,22},{7,23},{8,24},{9,... | collective-permute-start | bytes 1572872 | tf_op jit(solution)/shard_map/ppermute | solution.py:54
  54.4 58.2 %collective-permute-start.6 = (bf16[4,2,64,1024]{3,2,1,0:T(8,128)(2,1)S(1)}, bf16[4,2,64,1024]{3,2,1,0:T(8,128)(2,1)S(1)}, u32[]{:S(2)}, u32[]{:S(2)}) collective-permute-start(bf16[4,2,64,1024]{3,2,1,0:T(8,128)(2,1)S(1)} %get-tuple-element.56.refs_0_), channel_id=1, source_target_pairs={{0,2},{1,3},{2,0},{3,1},{4,6},{5,7},{6,4},{7,5},{8,10},{9,11},{10,... | collective-permute-start | bytes 3145736 | tf_op jit(solution)/shard_map/ppermute | solution.py:54
  55.9 56.8 %collective-permute-start.9 = (bf16[4,2,64,1024]{3,2,1,0:T(8,128)(2,1)S(1)}, bf16[4,2,64,1024]{3,2,1,0:T(8,128)(2,1)}, u32[]{:S(2)}, u32[]{:S(2)}) collective-permute-start(bf16[4,2,64,1024]{3,2,1,0:T(8,128)(2,1)S(1)} %get-tuple-element.57.refs_4_), channel_id=1, source_target_pairs={{0,4},{1,5},{2,6},{3,7},{4,0},{5,1},{6,2},{7,3},{8,12},{9,13},{10,... | collective-permute-start | bytes 3145736 | tf_op jit(solution)/shard_map/ppermute | solution.py:54
  58.2 32.6 %collective-permute-start.16 = (bf16[4,2,8,128]{3,2,1,0:T(8,128)(2,1)S(1)}, bf16[4,2,8,128]{3,2,1,0:T(8,128)(2,1)S(1)}, u32[]{:S(2)}, u32[]{:S(2)}) collective-permute-start(bf16[4,2,8,128]{3,2,1,0:T(8,128)(2,1)S(1)} %maximum_select_fusion.4), channel_id=1, source_target_pairs={{0,2},{1,3},{2,0},{3,1},{4,6},{5,7},{6,4},{7,5},{8,10},{9,11},{10,... | collective-permute-start | bytes 49160 | tf_op jit(solution)/shard_map/ppermute | solution.py:54
  91.1 31.8 %collective-permute-start.7 = (bf16[4,2,64,1024]{3,2,1,0:T(8,128)(2,1)S(1)}, bf16[4,2,64,1024]{3,2,1,0:T(8,128)(2,1)}, u32[]{:S(2)}, u32[]{:S(2)}) collective-permute-start(bf16[4,2,64,1024]{3,2,1,0:T(8,128)(2,1)S(1)} %get-tuple-element.56.refs_0_), channel_id=1, source_target_pairs={{0,1},{1,0},{2,3},{3,2},{4,5},{5,4},{6,7},{7,6},{8,9},{9,8},{10,11... | collective-permute-start | bytes 3145736 | tf_op jit(solution)/shard_map/ppermute | solution.py:54
  92.1 31.4 %collective-permute-start.10 = (bf16[4,2,64,1024]{3,2,1,0:T(8,128)(2,1)S(1)}, bf16[4,2,64,1024]{3,2,1,0:T(8,128)(2,1)}, u32[]{:S(2)}, u32[]{:S(2)}) collective-permute-start(bf16[4,2,64,1024]{3,2,1,0:T(8,128)(2,1)S(1)} %get-tuple-element.57.refs_4_), channel_id=1, source_target_pairs={{0,1},{1,0},{2,3},{3,2},{4,5},{5,4},{6,7},{7,6},{8,9},{9,8},{10,11... | collective-permute-start | bytes 3145736 | tf_op jit(solution)/shard_map/ppermute | solution.py:54
  123.5 35.9 %collective-permute-start.24 = (bf16[4,128,1024]{2,1,0:T(8,128)(2,1)}, bf16[4,128,1024]{2,1,0:T(8,128)(2,1)}, u32[]{:S(2)}, u32[]{:S(2)}) collective-permute-start(bf16[4,128,1024]{2,1,0:T(8,128)(2,1)} %copy-done.7), channel_id=1, source_target_pairs={{0,2},{1,3},{2,0},{3,1},{4,6},{5,7},{6,4},{7,5},{8,10},{9,11},{10,... | collective-permute-start | bytes 3145736 | tf_op jit(solution)/shard_map/ppermute | solution.py:54
  130.8 32.7 %collective-permute-start.46 = (bf16[256,1024]{1,0:T(8,128)(2,1)}, bf16[256,1024]{1,0:T(8,128)(2,1)}, u32[]{:S(2)}, u32[]{:S(2)}) collective-permute-start(bf16[256,1024]{1,0:T(8,128)(2,1)} %get-tuple-element.82.refs_0_), channel_id=1, source_target_pairs={{0,8},{1,9},{2,10},{3,11},{4,12},{5,13},{6,14},{7,15},{8,16},{9,17... | collective-permute-start | bytes 1572872 | tf_op jit(solution)/shard_map/ppermute | solution.py:54
  130.8 37.9 %collective-permute-start.45 = (bf16[256,1024]{1,0:T(8,128)(2,1)}, bf16[256,1024]{1,0:T(8,128)(2,1)}, u32[]{:S(2)}, u32[]{:S(2)}) collective-permute-start(bf16[256,1024]{1,0:T(8,128)(2,1)} %get-tuple-element.82.refs_0_), channel_id=1, source_target_pairs={{0,16},{1,17},{2,18},{3,19},{4,20},{5,21},{6,22},{7,23},{8,24},{9,... | collective-permute-start | bytes 1572872 | tf_op jit(solution)/shard_map/ppermute | solution.py:54
  146.8 35.2 %collective-permute-start.19 = (bf16[512,1024]{1,0:T(8,128)(2,1)}, bf16[512,1024]{1,0:T(8,128)(2,1)}, u32[]{:S(2)}, u32[]{:S(2)}) collective-permute-start(bf16[512,1024]{1,0:T(8,128)(2,1)} %convolution_convert_fusion.15), channel_id=1, source_target_pairs={{0,1},{1,0},{2,3},{3,2},{4,5},{5,4},{6,7},{7,6},{8,9},{9,8},{10,11... | collective-permute-start | bytes 3145736 | tf_op jit(solution)/shard_map/ppermute | solution.py:54
  163.0 48.5 %collective-permute-start.25 = (bf16[4,2,128,1024]{3,2,1,0:T(8,128)(2,1)S(1)}, bf16[4,2,128,1024]{3,2,1,0:T(8,128)(2,1)}, u32[]{:S(2)}, u32[]{:S(2)}) collective-permute-start(bf16[4,2,128,1024]{3,2,1,0:T(8,128)(2,1)S(1)} %get-tuple-element.67.refs_0_), channel_id=1, source_target_pairs={{0,2},{1,3},{2,0},{3,1},{4,6},{5,7},{6,4},{7,5},{8,10},{9,11},{10,... | collective-permute-start | bytes 6291464 | tf_op jit(solution)/shard_map/ppermute | solution.py:54
  163.6 47.9 %collective-permute-start.28 = (bf16[4,2,128,1024]{3,2,1,0:T(8,128)(2,1)}, bf16[4,2,128,1024]{3,2,1,0:T(8,128)(2,1)}, u32[]{:S(2)}, u32[]{:S(2)}) collective-permute-start(bf16[4,2,128,1024]{3,2,1,0:T(8,128)(2,1)} %get-tuple-element.68.refs_4_), channel_id=1, source_target_pairs={{0,4},{1,5},{2,6},{3,7},{4,0},{5,1},{6,2},{7,3},{8,12},{9,13},{10,... | collective-permute-start | bytes 6291464 | tf_op jit(solution)/shard_map/ppermute | solution.py:54
  171.7 122.0 %collective-permute-start.26 = (bf16[4,2,128,1024]{3,2,1,0:T(8,128)(2,1)S(1)}, bf16[4,2,128,1024]{3,2,1,0:T(8,128)(2,1)}, u32[]{:S(2)}, u32[]{:S(2)}) collective-permute-start(bf16[4,2,128,1024]{3,2,1,0:T(8,128)(2,1)S(1)} %get-tuple-element.67.refs_0_), channel_id=1, source_target_pairs={{0,1},{1,0},{2,3},{3,2},{4,5},{5,4},{6,7},{7,6},{8,9},{9,8},{10,11... | collective-permute-start | bytes 6291464 | tf_op jit(solution)/shard_map/ppermute | solution.py:54
  171.7 122.5 %collective-permute-start.29 = (bf16[4,2,128,1024]{3,2,1,0:T(8,128)(2,1)}, bf16[4,2,128,1024]{3,2,1,0:T(8,128)(2,1)}, u32[]{:S(2)}, u32[]{:S(2)}) collective-permute-start(bf16[4,2,128,1024]{3,2,1,0:T(8,128)(2,1)} %get-tuple-element.68.refs_4_), channel_id=1, source_target_pairs={{0,1},{1,0},{2,3},{3,2},{4,5},{5,4},{6,7},{7,6},{8,9},{9,8},{10,11... | collective-permute-start | bytes 6291464 | tf_op jit(solution)/shard_map/ppermute | solution.py:54
  182.0 45.9 %collective-permute-start.18 = (bf16[512,1024]{1,0:T(8,128)(2,1)}, bf16[512,1024]{1,0:T(8,128)(2,1)}, u32[]{:S(2)}, u32[]{:S(2)}) collective-permute-start(bf16[512,1024]{1,0:T(8,128)(2,1)} %add_convert_fusion.11), channel_id=1, source_target_pairs={{0,1},{1,0},{2,3},{3,2},{4,5},{5,4},{6,7},{7,6},{8,9},{9,8},{10,11... | collective-permute-start | bytes 3145736 | tf_op jit(solution)/shard_map/ppermute | solution.py:54
  241.5 53.8 %collective-permute-start.27 = (bf16[4,2,128,1024]{3,2,1,0:T(8,128)(2,1)}, bf16[4,2,128,1024]{3,2,1,0:T(8,128)(2,1)S(1)}, u32[]{:S(2)}, u32[]{:S(2)}) collective-permute-start(bf16[4,2,128,1024]{3,2,1,0:T(8,128)(2,1)} %collective-permute-done.25.refs_1_), channel_id=1, source_target_pairs={{0,1},{1,0},{2,3},{3,2},{4,5},{5,4},{6,7},{7,6},{8,9},{9,8},{10,11... | collective-permute-start | bytes 6291464 | tf_op jit(solution)/shard_map/ppermute | solution.py:54
  241.5 53.8 %collective-permute-start.30 = (bf16[4,2,128,1024]{3,2,1,0:T(8,128)(2,1)}, bf16[4,2,128,1024]{3,2,1,0:T(8,128)(2,1)}, u32[]{:S(2)}, u32[]{:S(2)}) collective-permute-start(bf16[4,2,128,1024]{3,2,1,0:T(8,128)(2,1)} %collective-permute-done.28.refs_5_), channel_id=1, source_target_pairs={{0,1},{1,0},{2,3},{3,2},{4,5},{5,4},{6,7},{7,6},{8,9},{9,8},{10,11... | collective-permute-start | bytes 6291464 | tf_op jit(solution)/shard_map/ppermute | solution.py:54
  293.7 31.4 %collective-permute-start.40 = (bf16[4,2,64,1024]{3,2,1,0:T(8,128)(2,1)S(1)}, bf16[4,2,64,1024]{3,2,1,0:T(8,128)(2,1)S(1)}, u32[]{:S(2)}, u32[]{:S(2)}) collective-permute-start(bf16[4,2,64,1024]{3,2,1,0:T(8,128)(2,1)S(1)} %get-tuple-element.77.refs_4_), channel_id=1, source_target_pairs={{0,1},{1,0},{2,3},{3,2},{4,5},{5,4},{6,7},{7,6},{8,9},{9,8},{10,11... | collective-permute-start | bytes 3145736 | tf_op jit(solution)/shard_map/ppermute | solution.py:54
  294.2 42.4 %collective-permute-start.47 = (bf16[4,128,1024]{2,1,0:T(8,128)(2,1)S(1)}, bf16[4,128,1024]{2,1,0:T(8,128)(2,1)}, u32[]{:S(2)}, u32[]{:S(2)}) collective-permute-start(bf16[4,128,1024]{2,1,0:T(8,128)(2,1)S(1)} %get-tuple-element.85.refs_0_), channel_id=1, source_target_pairs={{0,4},{1,5},{2,6},{3,7},{4,0},{5,1},{6,2},{7,3},{8,12},{9,13},{10,... | collective-permute-start | bytes 3145736 | tf_op jit(solution)/shard_map/ppermute | solution.py:54
  333.8 31.0 %collective-permute-start.43 = (bf16[512,1024]{1,0:T(8,128)(2,1)}, bf16[512,1024]{1,0:T(8,128)(2,1)}, u32[]{:S(2)}, u32[]{:S(2)}) collective-permute-start(bf16[512,1024]{1,0:T(8,128)(2,1)} %convolution_convert_fusion.14), channel_id=1, source_target_pairs={{0,1},{1,0},{2,3},{3,2},{4,5},{5,4},{6,7},{7,6},{8,9},{9,8},{10,11... | collective-permute-start | bytes 3145736 | tf_op jit(solution)/shard_map/ppermute | solution.py:54
  334.9 122.6 %collective-permute-start.56 = (bf16[256,1024]{1,0:T(8,128)(2,1)}, bf16[256,1024]{1,0:T(8,128)(2,1)}, u32[]{:S(2)}, u32[]{:S(2)}) collective-permute-start(bf16[256,1024]{1,0:T(8,128)(2,1)} %get-tuple-element.185), channel_id=1, source_target_pairs={{0,2},{1,3},{2,0},{3,1},{4,6},{5,7},{6,4},{7,5},{8,10},{9,11},{10,... | collective-permute-start | bytes 1572872 | tf_op jit(solution)/shard_map/ppermute | solution.py:415
  354.2 74.3 %collective-permute-start.50 = (bf16[4,2,128,1024]{3,2,1,0:T(8,128)(2,1)}, bf16[4,2,128,1024]{3,2,1,0:T(8,128)(2,1)}, u32[]{:S(2)}, u32[]{:S(2)}) collective-permute-start(bf16[4,2,128,1024]{3,2,1,0:T(8,128)(2,1)} %get-tuple-element.87.refs_0_), channel_id=1, source_target_pairs={{0,1},{1,0},{2,3},{3,2},{4,5},{5,4},{6,7},{7,6},{8,9},{9,8},{10,11... | collective-permute-start | bytes 6291464 | tf_op jit(solution)/shard_map/ppermute | solution.py:54
  354.3 58.4 %collective-permute-start.49 = (bf16[4,2,128,1024]{3,2,1,0:T(8,128)(2,1)}, bf16[4,2,128,1024]{3,2,1,0:T(8,128)(2,1)}, u32[]{:S(2)}, u32[]{:S(2)}) collective-permute-start(bf16[4,2,128,1024]{3,2,1,0:T(8,128)(2,1)} %get-tuple-element.87.refs_0_), channel_id=1, source_target_pairs={{0,2},{1,3},{2,0},{3,1},{4,6},{5,7},{6,4},{7,5},{8,10},{9,11},{10,... | collective-permute-start | bytes 6291464 | tf_op jit(solution)/shard_map/ppermute | solution.py:54
  355.2 57.6 %collective-permute-start.52 = (bf16[4,2,128,1024]{3,2,1,0:T(8,128)(2,1)}, bf16[4,2,128,1024]{3,2,1,0:T(8,128)(2,1)}, u32[]{:S(2)}, u32[]{:S(2)}) collective-permute-start(bf16[4,2,128,1024]{3,2,1,0:T(8,128)(2,1)} %get-tuple-element.88.refs_4_), channel_id=1, source_target_pairs={{0,4},{1,5},{2,6},{3,7},{4,0},{5,1},{6,2},{7,3},{8,12},{9,13},{10,... | collective-permute-start | bytes 6291464 | tf_op jit(solution)/shard_map/ppermute | solution.py:54
  388.8 39.7 %collective-permute-start.53 = (bf16[4,2,128,1024]{3,2,1,0:T(8,128)(2,1)}, bf16[4,2,128,1024]{3,2,1,0:T(8,128)(2,1)}, u32[]{:S(2)}, u32[]{:S(2)}) collective-permute-start(bf16[4,2,128,1024]{3,2,1,0:T(8,128)(2,1)} %get-tuple-element.88.refs_4_), channel_id=1, source_target_pairs={{0,1},{1,0},{2,3},{3,2},{4,5},{5,4},{6,7},{7,6},{8,9},{9,8},{10,11... | collective-permute-start | bytes 6291464 | tf_op jit(solution)/shard_map/ppermute | solution.py:54
  616.9 303.6 %collective-permute-start.110 = (bf16[16,128,1024]{2,1,0:T(8,128)(2,1)}, bf16[16,128,1024]{2,1,0:T(8,128)(2,1)}, u32[]{:S(2)}, u32[]{:S(2)}) collective-permute-start(bf16[16,128,1024]{2,1,0:T(8,128)(2,1)} %get-tuple-element.124), channel_id=1, source_target_pairs={{0,1},{1,0},{2,3},{3,2},{4,5},{5,4},{6,7},{7,6},{8,9},{9,8},{10,11... | collective-permute-start | bytes 12582920 | tf_op jit(solution)/shard_map/ppermute | solution.py:54
  617.4 276.4 %collective-permute-start.98 = (bf16[16,32,4096]{2,1,0:T(8,128)(2,1)}, bf16[16,32,4096]{2,1,0:T(8,128)(2,1)}, u32[]{:S(2)}, u32[]{:S(2)}) collective-permute-start(bf16[16,32,4096]{2,1,0:T(8,128)(2,1)} %get-tuple-element.130), channel_id=1, source_target_pairs={{0,1},{1,0},{2,3},{3,2},{4,5},{5,4},{6,7},{7,6},{8,9},{9,8},{10,11... | collective-permute-start | bytes 12582920 | tf_op jit(solution)/shard_map/ppermute | solution.py:54
  779.2 82.8 %collective-permute-start.80 = (bf16[16,64,1024]{2,1,0:T(8,128)(2,1)}, bf16[16,64,1024]{2,1,0:T(8,128)(2,1)}, u32[]{:S(2)}, u32[]{:S(2)}) collective-permute-start(bf16[16,64,1024]{2,1,0:T(8,128)(2,1)} %pad_maximum_fusion.7), channel_id=1, source_target_pairs={{0,1},{1,0},{2,3},{3,2},{4,5},{5,4},{6,7},{7,6},{8,9},{9,8},{10,11... | collective-permute-start | bytes 6291464 | tf_op jit(solution)/shard_map/ppermute | solution.py:54
  786.8 33.5 %collective-permute-start.59 = (bf16[512,1024]{0,1:T(8,128)(2,1)}, bf16[512,1024]{0,1:T(8,128)(2,1)}, u32[]{:S(2)}, u32[]{:S(2)}) collective-permute-start(bf16[512,1024]{0,1:T(8,128)(2,1)} %bitcast.114), channel_id=1, source_target_pairs={{0,1},{1,0},{2,3},{3,2},{4,5},{5,4},{6,7},{7,6},{8,9},{9,8},{10,11... | collective-permute-start | bytes 3145736 | tf_op jit(solution)/shard_map/ppermute | solution.py:54
  812.8 59.7 %collective-permute-start.68 = (bf16[16,64,1024]{2,1,0:T(8,128)(2,1)}, bf16[16,64,1024]{2,1,0:T(8,128)(2,1)}, u32[]{:S(2)}, u32[]{:S(2)}) collective-permute-start(bf16[16,64,1024]{2,1,0:T(8,128)(2,1)} %pad_maximum_fusion.5), channel_id=1, source_target_pairs={{0,1},{1,0},{2,3},{3,2},{4,5},{5,4},{6,7},{7,6},{8,9},{9,8},{10,11... | collective-permute-start | bytes 6291464 | tf_op jit(solution)/shard_map/ppermute | solution.py:54
  873.3 50.3 %collective-permute-start.62 = (bf16[16,64,1024]{2,1,0:T(8,128)(2,1)S(1)}, bf16[16,64,1024]{2,1,0:T(8,128)(2,1)S(1)}, u32[]{:S(2)}, u32[]{:S(2)}) collective-permute-start(bf16[16,64,1024]{2,1,0:T(8,128)(2,1)S(1)} %copy-done.74), channel_id=1, source_target_pairs={{0,1},{1,0},{2,3},{3,2},{4,5},{5,4},{6,7},{7,6},{8,9},{9,8},{10,11... | collective-permute-start | bytes 6291464 | tf_op jit(solution)/shard_map/ppermute | solution.py:54
  890.7 89.6 %collective-permute-start.92 = (bf16[16,32,4096]{2,1,0:T(8,128)(2,1)S(1)}, bf16[16,32,4096]{2,1,0:T(8,128)(2,1)S(1)}, u32[]{:S(2)}, u32[]{:S(2)}) collective-permute-start(bf16[16,32,4096]{2,1,0:T(8,128)(2,1)S(1)} %copy-done.63), channel_id=1, source_target_pairs={{0,1},{1,0},{2,3},{3,2},{4,5},{5,4},{6,7},{7,6},{8,9},{9,8},{10,11... | collective-permute-start | bytes 12582920 | tf_op jit(solution)/shard_map/ppermute | solution.py:54
  892.1 95.4 %collective-permute-start.104 = (bf16[16,128,1024]{2,1,0:T(8,128)(2,1)}, bf16[16,128,1024]{2,1,0:T(8,128)(2,1)}, u32[]{:S(2)}, u32[]{:S(2)}) collective-permute-start(bf16[16,128,1024]{2,1,0:T(8,128)(2,1)} %get-tuple-element.122), channel_id=1, source_target_pairs={{0,1},{1,0},{2,3},{3,2},{4,5},{5,4},{6,7},{7,6},{8,9},{9,8},{10,11... | collective-permute-start | bytes 12582920 | tf_op jit(solution)/shard_map/ppermute | solution.py:54
  923.6 43.2 %collective-permute-start.75 = (bf16[4,2,64,1024]{3,2,1,0:T(8,128)(2,1)S(1)}, bf16[4,2,64,1024]{3,2,1,0:T(8,128)(2,1)S(1)}, u32[]{:S(2)}, u32[]{:S(2)}) collective-permute-start(bf16[4,2,64,1024]{3,2,1,0:T(8,128)(2,1)S(1)} %get-tuple-element.131), channel_id=1, source_target_pairs={{0,4},{1,5},{2,6},{3,7},{4,0},{5,1},{6,2},{7,3},{8,12},{9,13},{10,... | collective-permute-start | bytes 3145736 | tf_op jit(solution)/shard_map/ppermute | solution.py:54
  966.1 87.8 %collective-permute-start.111 = (bf16[4,2,128,1024]{3,2,0,1:T(8,128)(2,1)}, bf16[4,2,128,1024]{3,2,0,1:T(8,128)(2,1)}, u32[]{:S(2)}, u32[]{:S(2)}) collective-permute-start(bf16[4,2,128,1024]{3,2,0,1:T(8,128)(2,1)} %fusion.38), channel_id=1, source_target_pairs={{0,4},{1,5},{2,6},{3,7},{4,0},{5,1},{6,2},{7,3},{8,12},{9,13},{10,... | collective-permute-start | bytes 6291464 | tf_op jit(solution)/shard_map/ppermute | solution.py:54
  966.8 88.8 %collective-permute-start.99 = (bf16[4,2,32,4096]{3,2,0,1:T(8,128)(2,1)}, bf16[4,2,32,4096]{3,2,0,1:T(8,128)(2,1)S(1)}, u32[]{:S(2)}, u32[]{:S(2)}) collective-permute-start(bf16[4,2,32,4096]{3,2,0,1:T(8,128)(2,1)} %fusion.36), channel_id=1, source_target_pairs={{0,2},{1,3},{2,0},{3,1},{4,6},{5,7},{6,4},{7,5},{8,10},{9,11},{10,... | collective-permute-start | bytes 6291464 | tf_op jit(solution)/shard_map/ppermute | solution.py:54
  978.1 51.5 %collective-permute-start.76 = (bf16[4,64,1024]{2,1,0:T(8,128)(2,1)}, bf16[4,64,1024]{2,1,0:T(8,128)(2,1)}, u32[]{:S(2)}, u32[]{:S(2)}) collective-permute-start(bf16[4,64,1024]{2,1,0:T(8,128)(2,1)} %fusion.74), channel_id=1, source_target_pairs={{0,2},{1,3},{2,0},{3,1},{4,6},{5,7},{6,4},{7,5},{8,10},{9,11},{10,... | collective-permute-start | bytes 1572872 | tf_op jit(solution)/shard_map/ppermute | solution.py:54
  980.3 54.7 %collective-permute-start.64 = (bf16[4,64,1024]{2,1,0:T(8,128)(2,1)}, bf16[4,64,1024]{2,1,0:T(8,128)(2,1)}, u32[]{:S(2)}, u32[]{:S(2)}) collective-permute-start(bf16[4,64,1024]{2,1,0:T(8,128)(2,1)} %fusion.72), channel_id=1, source_target_pairs={{0,4},{1,5},{2,6},{3,7},{4,0},{5,1},{6,2},{7,3},{8,12},{9,13},{10,... | collective-permute-start | bytes 1572872 | tf_op jit(solution)/shard_map/ppermute | solution.py:54
  1048.1 73.8 %collective-permute-start.105 = (bf16[4,2,128,1024]{3,2,1,0:T(8,128)(2,1)S(1)}, bf16[4,2,128,1024]{3,2,1,0:T(8,128)(2,1)S(1)}, u32[]{:S(2)}, u32[]{:S(2)}) collective-permute-start(bf16[4,2,128,1024]{3,2,1,0:T(8,128)(2,1)S(1)} %copy-done.80), channel_id=1, source_target_pairs={{0,4},{1,5},{2,6},{3,7},{4,0},{5,1},{6,2},{7,3},{8,12},{9,13},{10,... | collective-permute-start | bytes 6291464 | tf_op jit(solution)/shard_map/ppermute | solution.py:54
  1049.9 71.2 %collective-permute-start.93 = (bf16[4,2,32,4096]{3,2,1,0:T(8,128)(2,1)S(1)}, bf16[4,2,32,4096]{3,2,1,0:T(8,128)(2,1)S(1)}, u32[]{:S(2)}, u32[]{:S(2)}) collective-permute-start(bf16[4,2,32,4096]{3,2,1,0:T(8,128)(2,1)S(1)} %copy-done.81), channel_id=1, source_target_pairs={{0,2},{1,3},{2,0},{3,1},{4,6},{5,7},{6,4},{7,5},{8,10},{9,11},{10,... | collective-permute-start | bytes 6291464 | tf_op jit(solution)/shard_map/ppermute | solution.py:54
  1055.6 56.3 %collective-permute-start.112 = (bf16[4,128,1024]{2,1,0:T(8,128)(2,1)S(1)}, bf16[4,128,1024]{2,1,0:T(8,128)(2,1)S(1)}, u32[]{:S(2)}, u32[]{:S(2)}) collective-permute-start(bf16[4,128,1024]{2,1,0:T(8,128)(2,1)S(1)} %fusion.59), channel_id=1, source_target_pairs={{0,2},{1,3},{2,0},{3,1},{4,6},{5,7},{6,4},{7,5},{8,10},{9,11},{10,... | collective-permute-start | bytes 3145736 | tf_op jit(solution)/shard_map/ppermute | solution.py:54
  1055.9 63.3 %collective-permute-start.100 = (bf16[4,32,4096]{2,1,0:T(8,128)(2,1)S(1)}, bf16[4,32,4096]{2,1,0:T(8,128)(2,1)S(1)}, u32[]{:S(2)}, u32[]{:S(2)}) collective-permute-start(bf16[4,32,4096]{2,1,0:T(8,128)(2,1)S(1)} %fusion.57), channel_id=1, source_target_pairs={{0,4},{1,5},{2,6},{3,7},{4,0},{5,1},{6,2},{7,3},{8,12},{9,13},{10,... | collective-permute-start | bytes 3145736 | tf_op jit(solution)/shard_map/ppermute | solution.py:54
  1119.1 31.0 %collective-permute-start.114 = (bf16[128,1024]{1,0:T(8,128)(2,1)S(1)}, bf16[128,1024]{1,0:T(8,128)(2,1)S(1)}, u32[]{:S(2)}, u32[]{:S(2)}) collective-permute-start(bf16[128,1024]{1,0:T(8,128)(2,1)S(1)} %get-tuple-element.141), channel_id=1, source_target_pairs={{0,16},{1,17},{2,18},{3,19},{4,20},{5,21},{6,22},{7,23},{8,24},{9,... | collective-permute-start | bytes 786440 | tf_op jit(solution)/shard_map/ppermute | solution.py:54
  1125.9 33.0 %collective-permute-start.102 = (bf16[32,4096]{1,0:T(8,128)(2,1)S(1)}, bf16[32,4096]{1,0:T(8,128)(2,1)S(1)}, u32[]{:S(2)}, u32[]{:S(2)}) collective-permute-start(bf16[32,4096]{1,0:T(8,128)(2,1)S(1)} %get-tuple-element.147), channel_id=1, source_target_pairs={{0,16},{1,17},{2,18},{3,19},{4,20},{5,21},{6,22},{7,23},{8,24},{9,... | collective-permute-start | bytes 786440 | tf_op jit(solution)/shard_map/ppermute | solution.py:54
  1166.2 32.3 %collective-permute-start.108 = (bf16[128,1024]{1,0:T(8,128)(2,1)S(1)}, bf16[128,1024]{1,0:T(8,128)(2,1)S(1)}, u32[]{:S(2)}, u32[]{:S(2)}) collective-permute-start(bf16[128,1024]{1,0:T(8,128)(2,1)S(1)} %get-tuple-element.138), channel_id=1, source_target_pairs={{0,16},{1,17},{2,18},{3,19},{4,20},{5,21},{6,22},{7,23},{8,24},{9,... | collective-permute-start | bytes 786440 | tf_op jit(solution)/shard_map/ppermute | solution.py:54
  1168.0 31.7 %collective-permute-start.95 = (bf16[32,4096]{1,0:T(8,128)(2,1)S(1)}, bf16[32,4096]{1,0:T(8,128)(2,1)S(1)}, u32[]{:S(2)}, u32[]{:S(2)}) collective-permute-start(bf16[32,4096]{1,0:T(8,128)(2,1)S(1)} %get-tuple-element.142), channel_id=1, source_target_pairs={{0,8},{1,9},{2,10},{3,11},{4,12},{5,13},{6,14},{7,15},{8,16},{9,17... | collective-permute-start | bytes 786440 | tf_op jit(solution)/shard_map/ppermute | solution.py:54
  1169.2 30.6 %collective-permute-start.97 = (bf16[32,4096]{1,0:T(8,128)(2,1)S(1)}, bf16[32,4096]{1,0:T(8,128)(2,1)S(1)}, u32[]{:S(2)}, u32[]{:S(2)}) collective-permute-start(bf16[32,4096]{1,0:T(8,128)(2,1)S(1)} %get-tuple-element.143), channel_id=1, source_target_pairs={{0,24},{1,25},{2,26},{3,27},{4,28},{5,29},{6,30},{7,31},{8,0},{9,1... | collective-permute-start | bytes 786440 | tf_op jit(solution)/shard_map/ppermute | solution.py:54
  1173.5 32.1 %collective-permute-start.96 = (bf16[32,4096]{1,0:T(8,128)(2,1)S(1)}, bf16[32,4096]{1,0:T(8,128)(2,1)S(1)}, u32[]{:S(2)}, u32[]{:S(2)}) collective-permute-start(bf16[32,4096]{1,0:T(8,128)(2,1)S(1)} %get-tuple-element.144), channel_id=1, source_target_pairs={{0,16},{1,17},{2,18},{3,19},{4,20},{5,21},{6,22},{7,23},{8,24},{9,... | collective-permute-start | bytes 786440 | tf_op jit(solution)/shard_map/ppermute | solution.py:54
  (223 other events, 3319.0 us)

commit v2 on v1

--- a/solution.py
+++ b/solution.py
@@ -47,6 +47,8 @@
 TO_CORE = pairs(lambda z, y, x, c: (z, y, x, 1 - c))
 TO_X = pairs(lambda z, y, x, c: (z, y, 1 - x, c))
 TO_Y = pairs(lambda z, y, x, c: (z, 1 - y, x, c))
+TO_FAR = pairs(lambda z, y, x, c: (z, y if c == 0 else 1 - y, 1 - x if c == 0 else x, c))
+TO_NEAR = pairs(lambda z, y, x, c: (z, 1 - y if c == 0 else y, x if c == 0 else 1 - x, c))
 TO_Z = [pairs(lambda z, y, x, c, k=k: ((z + k) % 4, y, x, c)) for k in range(4)]
 
 
@@ -100,127 +102,359 @@
     )(coords, *pieces)
 
 
-class Gather:
-    def __init__(self, coords):
-        self.coords = coords
-        self.last_z = ()
-        self.last_xy = ()
-
-    def __call__(self, pack, split, shapes, routed):
-        rows, width = pack.shape
-        if self.last_z:
-            pack = tie(pack, *self.last_z)
-        from_z = [pack] + [send(pack, TO_Z[4 - k]) for k in (1, 2, 3)]
-        self.last_z = from_z[1:]
-        sizes = (split, rows - split)
-
-        def by_z(z, y, x, c, src, dst):
-            return [
-                (k, src and src[k].at[lo : lo + n], dst and dst[r].at[(z + k) % 4])
-                for k in range(4)
-                for r, (lo, n) in enumerate(zip((0, split), sizes))
-            ]
-
-        first, second = place(self.coords, from_z, [(4, n, width) for n in sizes], by_z)
-        if self.last_xy:
-            first, second = tie((first, second), *self.last_xy)
-        first_y, second_x = send(first, TO_Y), send(second, TO_X)
-
-        def by_two(z, y, x, c, src, dst):
-            return [
-                (0, src and src[0], dst and dst[0].at[:, y]),
-                (1, src and src[1], dst and dst[0].at[:, 1 - y]),
-                (2, src and src[2], dst and dst[1].at[:, x]),
-                (3, src and src[3], dst and dst[1].at[:, 1 - x]),
-            ]
-
-        first, second = place(
-            self.coords,
-            [first, first_y, second, second_x],
-            [(4, 2, n, width) for n in sizes],
-            by_two,
-        )
-        first_x, second_y = send(first, TO_X), send(second, TO_Y)
-        self.last_xy = (first_x, second_y)
-        first_c, second_c = send(first, TO_CORE), send(second, TO_CORE)
-        first_xc, second_yc = send(first_x, TO_CORE), send(second_y, TO_CORE)
+def pick(value, index, axis):
+    return lax.dynamic_index_in_dim(value, index, axis, keepdims=False)
+
+
+def by_place(own, other, at, axis):
+    return jnp.where(at == 0, jnp.stack([own, other], axis), jnp.stack([other, own], axis))
+
+
+def phase(values, *units):
+    values, flights = lax.optimization_barrier((values, [u.flight for u in units]))
+    nexts = [u.local(flight) for u, flight in zip(units, flights)]
+    values, sends = lax.optimization_barrier((values, [[v for v, _ in n] for n in nexts]))
+    for unit, arrays, targets in zip(units, sends, nexts):
+        unit.flight = [send(array, to) for array, (_, to) in zip(arrays, targets)]
+    return values
+
+
+class GatherUnit:
+    def __init__(self, coords, pack, shapes, parts):
+        self.coords, self.pack, self.shapes, self.parts = coords, pack, shapes, parts
+        self.flight, self.step = [], 0
+
+    def local(self, got):
+        rows, width = self.pack.shape
+        self.step += 1
+        if self.step == 1:
+            return [(self.pack, TO_Z[4 - k]) for k in (1, 2, 3)]
+        if self.step == 2:
+            self.kept = jnp.concatenate([self.pack] + got).reshape(4, rows, width)
+            return [(self.kept, TO_NEAR)]
+        if self.step == 3:
+            self.kept = jnp.stack([self.kept, got[0]])
+            return [(self.kept, TO_FAR), (self.kept, TO_CORE)]
+        self.kept = [self.kept, got[0], got[1]]
+        return [(got[0], TO_CORE)]
+
+    def result(self):
+        width = self.pack.shape[1]
 
         def by_block(z, y, x, c, src, dst):
             out = []
-            for n, (x2, c2) in enumerate(((x, c), (1 - x, c), (x, 1 - c), (1 - x, 1 - c))):
-                for lo, hi, target, column in routed[0]:
-                    for z2 in range(4):
-                        out.append(
-                            (
-                                n,
-                                src and src[n].at[z2, :, lo:hi],
-                                dst
-                                and dst[target].at[
-                                    z2, :, x2, c2, :, column * width : (column + 1) * width
-                                ],
-                            )
-                        )
-            for n, (y2, c2) in enumerate(((y, c), (1 - y, c), (y, 1 - c), (1 - y, 1 - c))):
-                for lo, hi, target, column in routed[1]:
-                    for z2 in range(4):
-                        out.append(
-                            (
-                                4 + n,
-                                src and src[4 + n].at[z2, :, lo:hi],
-                                dst
-                                and dst[target].at[
-                                    z2, y2, :, c2, :, column * width : (column + 1) * width
-                                ],
-                            )
-                        )
+            for n in range(4):
+                core = c if n < 2 else 1 - c
+                for near in range(2):
+                    far = n % 2
+                    y2 = y ^ jnp.where(core == 0, near, far)
+                    x2 = x ^ jnp.where(core == 0, far, near)
+                    for k in range(4):
+                        for lo, hi, target, column in self.parts:
+                            view = None
+                            if dst:
+                                spans = (slice(0, hi - lo), slice(column * width, (column + 1) * width))
+                                view = dst[target].at[((z + k) % 4, y2, x2, core) + spans]
+                            out.append((n, src and src[n].at[near, k, lo:hi], view))
             return out
 
         return place(
-            self.coords,
-            [first, first_x, first_c, first_xc, second, second_y, second_c, second_yc],
-            [(4, 2, 2, 2) + shape for shape in shapes],
-            by_block,
-        )
-
-
-def pick(value, index, axis):
-    return lax.dynamic_index_in_dim(value, index, axis, keepdims=False)
-
-
-def summed_shards(coords, grads, x_first):
+            self.coords, self.kept + self.flight, [(4, 2, 2, 2) + shape for shape in self.shapes], by_block
+        )
+
+
+class SumUnit:
+    def __init__(self, parts):
+        self.parts = parts
+        self.flight, self.step = [], 0
+
+    def local(self, got):
+        self.step += 1
+        if self.step == 1:
+            leaving, self.kept = self.parts
+            return [(leaving, TO_FAR)]
+        if self.step == 2:
+            half = self.kept.shape[0] // 2
+            add = lambda a, b: (a.astype(f32) + b.astype(f32)).astype(bf16)
+            leaving = add(self.kept[:half], got[0][:half])
+            self.kept = add(self.kept[half:], got[0][half:])
+            return [(leaving, TO_NEAR)]
+        if self.step == 3:
+            kept, rows = self.kept, self.kept.shape[0] // 4
+            cut = lambda array, k: array[k * rows : (k + 1) * rows].astype(f32)
+            add = lambda k: cut(kept, k) + cut(got[0], k)
+            self.kept = add(3)
+            return [(add(k - 1).astype(bf16), TO_Z[k]) for k in (1, 2, 3)]
+        self.kept = self.kept + (got[0].astype(f32) + got[1].astype(f32) + got[2].astype(f32))
+        return []
+
+
+def block_order(coords):
     z, y, x, c = coords[0], coords[1], coords[2], coords[3]
-    blocks = [g.reshape(16, 2, g.shape[0] // 32, g.shape[1]) for g in grads]
-
-    def joined(index):
-        return jnp.concatenate([pick(b, index, 1) for b in blocks], axis=1)
-
-    other = send(joined(1 - c).astype(bf16), TO_CORE)
-    own = joined(c)
-    rows, width = own.shape[1:]
-    own = own.reshape(4, 2, 2, rows, width)
-    other = other.reshape(4, 2, 2, rows, width)
-    axis, index, to = (2, x, TO_X) if x_first else (1, y, TO_Y)
-
-    def total(where):
-        return pick(own, where, axis).astype(f32) + pick(other, where, axis).astype(f32)
-
-    own, other = total(index), send(total(1 - index).astype(bf16), to)
-    index, to = (y, TO_Y) if x_first else (x, TO_X)
-
-    def total_two(where):
-        return pick(own, where, 1).astype(f32) + pick(other, where, 1).astype(f32)
-
-    other2 = send(total_two(1 - index).astype(bf16), to)
-    quarter = total_two(index) + other2.astype(f32)
-    result = pick(quarter, z, 0)
-    for k in (1, 2, 3):
-        result = result + send(pick(quarter, (z + k) % 4, 0).astype(bf16), TO_Z[k]).astype(f32)
-    parts, start = [], 0
-    for g in grads:
-        size = g.shape[0] // 32
-        parts.append(result[start : start + size])
-        start += size
-    return parts
+    order = []
+    for core in (c, 1 - c):
+        for far in (1, 0):
+            for near in (1, 0):
+                for k in (1, 2, 3, 0):
+                    y2 = y ^ jnp.where(core == 0, near, far)
+                    x2 = x ^ jnp.where(core == 0, far, near)
+                    order.append((z + k) % 4 * 8 + y2 * 4 + x2 * 2 + core)
+    return jnp.stack(order).astype(jnp.int32)
+
+
+def order_matrices(order):
+    block = D // 32
+    wanted = (order[:, None] * block + lax.iota(jnp.int32, block)[None, :]).reshape(2, 1, D // 2)
+    rows = lax.broadcasted_iota(jnp.int32, (2, D, D // 2), 1)
+    chosen = (rows == wanted).astype(bf16)
+    return chosen[0], chosen[1]
+
+
+def selected(matrices, rows):
+    return [
+        lax.dot_general(m, rows, (((0,), (1,)), ((), ())), preferred_element_type=f32).astype(bf16)
+        for m in matrices
+    ]
+
+
+def weight_terms(*pairs_of):
+    rows, tokens = pairs_of[0][0][0].shape
+    tile = (1 << 19) // rows
+    counts = [pair[1][0].shape[1] // tile for pair in pairs_of]
+    starts = [sum(counts[:n]) for n in range(len(counts))]
+    columns, half = sum(counts) * tile, rows // 2
+
+    def kernel(*refs):
+        leaving, kept = refs[-2:]
+        j = pl.program_id(0)
+        for n, (start, count) in enumerate(zip(starts, counts)):
+
+            @pl.when((j >= start) & (j < start + count))
+            def _(a1=refs[4 * n], a2=refs[4 * n + 1], b1=refs[4 * n + 2], b2=refs[4 * n + 3]):
+                total = jnp.dot(a1[...], b1[...], preferred_element_type=f32)
+                total = total + jnp.dot(a2[...], b2[...], preferred_element_type=f32)
+                leaving[...] = total[:half].astype(bf16)
+                kept[...] = total[half:].astype(bf16)
+
+    in_specs, args = [], []
+    for (left, right), start, count in zip(pairs_of, starts, counts):
+        whole = pl.BlockSpec((rows, tokens), lambda j: (0, 0))
+        cut = pl.BlockSpec((tokens, tile), lambda j, s=start, n=count: (0, jnp.clip(j - s, 0, n - 1)))
+        in_specs += [whole, whole, cut, cut]
+        args += [*left, *right]
+    out = jax.ShapeDtypeStruct((half, columns), bf16)
+    return pl.pallas_call(
+        kernel,
+        grid=(columns // tile,),
+        in_specs=in_specs,
+        out_specs=[pl.BlockSpec((half, tile), lambda j: (0, j))] * 2,
+        out_shape=[out, out],
+        compiler_params=pltpu.CompilerParams(vmem_limit_bytes=48 << 20),
+        cost_estimate=pl.CostEstimate(
+            flops=4 * rows * tokens * columns,
+            bytes_accessed=4 * rows * tokens + 4 * tokens * columns + 2 * rows * columns,
+            transcendentals=0,
+        ),
+    )(*args)
+
+
+def wide_terms_of(order, left, right):
+    tokens, width = left[0].shape
+    block = width // 32
+
+    def kernel(order_ref, a1, a2, b1, b2, leaving, kept):
+        rows_dot = lambda a, b: lax.dot_general(
+            a[...], b[...], (((0,), (0,)), ((), ())), preferred_element_type=f32
+        )
+        total = (rows_dot(a1, b1) + rows_dot(a2, b2)).astype(bf16)
+
+        @pl.when(pl.program_id(0) < 8)
+        def _():
+            leaving[...] = total
+
+        @pl.when(pl.program_id(0) >= 8)
+        def _():
+            kept[...] = total
+
+    columns = right[0].shape[1]
+    cut = pl.BlockSpec((tokens, block), lambda j, order: (0, order[j]))
+    whole = pl.BlockSpec((tokens, columns), lambda j, order: (0, 0))
+    out = jax.ShapeDtypeStruct((width // 4, columns), bf16)
+    return pl.pallas_call(
+        kernel,
+        grid_spec=pltpu.PrefetchScalarGridSpec(
+            num_scalar_prefetch=1,
+            grid=(16,),
+            in_specs=[cut, cut, whole, whole],
+            out_specs=[
+                pl.BlockSpec((block, columns), lambda j, order: (jnp.minimum(j, 7), 0)),
+                pl.BlockSpec((block, columns), lambda j, order: (jnp.maximum(j - 8, 0), 0)),
+            ],
+        ),
+        out_shape=[out, out],
+        compiler_params=pltpu.CompilerParams(vmem_limit_bytes=48 << 20),
+        cost_estimate=pl.CostEstimate(
+            flops=2 * tokens * width * columns, bytes_accessed=3 * tokens * width, transcendentals=0
+        ),
+    )(order, *left, *right)
+
+
+BLOCK = 256
+WINDOW = 3 * BLOCK
+PAIR = 2 * HEAD_DIM
+
+
+def window_start(s, slot):
+    block = s ^ (2 * slot)
+    return jnp.clip(block - 1, 0, 1) * BLOCK
+
+
+def nt_dot(left, right):
+    return lax.dot_general(left, right, (((1,), (1,)), ((), ())), preferred_element_type=f32)
+
+
+def only_head(value, head, axis):
+    lane = lax.broadcasted_iota(jnp.int32, value.shape, axis)
+    return jnp.where((lane < HEAD_DIM) if head == 0 else (lane >= HEAD_DIM), value, jnp.zeros_like(value))
+
+
+def in_order(s, mine, other, scratch):
+    for n, ref in ((0, mine), (1, other)):
+        for slot in range(2):
+            scratch[pl.ds((s ^ (n + 2 * slot)) * BLOCK, BLOCK), :] = ref[slot * BLOCK : (slot + 1) * BLOCK, :]
+
+
+def attend_forward_kernel(
+    s_ref, q_ref, km_ref, ko_ref, vm_ref, vo_ref, bias_ref, mixed_ref, total_ref, keys, values
+):
+    s = s_ref[0]
+    in_order(s, km_ref, ko_ref, keys)
+    in_order(s, vm_ref, vo_ref, values)
+    for slot in range(2):
+        start = pl.multiple_of(window_start(s, slot), BLOCK)
+        k = keys[pl.ds(start, WINDOW), :]
+        v_t = values[pl.ds(start, WINDOW), :].T
+        q = q_ref[slot * BLOCK : (slot + 1) * BLOCK, :] * jnp.asarray(HEAD_DIM**-0.5, bf16)
+        bias = bias_ref[slot]
+        halves = []
+        for head in range(2):
+            scores = nt_dot(k, only_head(q, head, 1)) + bias
+            top = jnp.max(scores, axis=0, keepdims=True)
+            raised = jnp.exp(scores - top)
+            total = jnp.sum(raised, axis=0, keepdims=True)
+            mixed = jnp.dot(
+                v_t[head * HEAD_DIM : (head + 1) * HEAD_DIM],
+                raised.astype(bf16),
+                preferred_element_type=f32,
+            )
+            halves.append(mixed / total)
+            total_ref[0, head : head + 1, slot * BLOCK : (slot + 1) * BLOCK] = top + jnp.log(total)
+        mixed_ref[slot * BLOCK : (slot + 1) * BLOCK, :] = jnp.concatenate(halves, axis=0).T.astype(bf16)
+
+
+def attend_backward_kernel(
+    s_ref, q_ref, km_ref, ko_ref, vm_ref, vo_ref, bias_ref, mixed_ref, total_ref, grad_ref,
+    dq_ref, mine_ref, sent_ref, keys, values, key_sum, value_sum,
+):
+    s = s_ref[0]
+    in_order(s, km_ref, ko_ref, keys)
+    in_order(s, vm_ref, vo_ref, values)
+    key_sum[...] = jnp.zeros_like(key_sum)
+    value_sum[...] = jnp.zeros_like(value_sum)
+    for slot in range(2):
+        rows = slice(slot * BLOCK, (slot + 1) * BLOCK)
+        start = pl.multiple_of(window_start(s, slot), BLOCK)
+        window = pl.ds(start, WINDOW)
+        k, v = keys[window, :], values[window, :]
+        k_t = k.T
+        q = q_ref[rows, :] * jnp.asarray(HEAD_DIM**-0.5, bf16)
+        g = grad_ref[rows, :]
+        bias = bias_ref[slot]
+        along = (g.astype(f32) * mixed_ref[rows, :].astype(f32)).T
+        shares_low, grads_low, queries, grads, query_grads = [], [], [], [], []
+        for head in range(2):
+            span = slice(head * HEAD_DIM, (head + 1) * HEAD_DIM)
+            queries.append(only_head(q, head, 1))
+            grads.append(only_head(g, head, 1))
+            scores = nt_dot(k, queries[head]) + bias
+            shares = jnp.exp(scores - total_ref[0, head : head + 1, rows])
+            inner = jnp.sum(along[span], axis=0, keepdims=True)
+            score_grads = (shares * (nt_dot(v, grads[head]) - inner)).astype(bf16)
+            shares_low.append(shares.astype(bf16))
+            grads_low.append(score_grads)
+            query_grads.append(jnp.dot(k_t[span], score_grads, preferred_element_type=f32))
+        dq_ref[rows, :] = (jnp.concatenate(query_grads, axis=0).T * HEAD_DIM**-0.5).astype(bf16)
+        key_sum[window, :] += jnp.dot(
+            jnp.concatenate(grads_low, axis=1), jnp.concatenate(queries, axis=0), preferred_element_type=f32
+        )
+        value_sum[window, :] += jnp.dot(
+            jnp.concatenate(shares_low, axis=1), jnp.concatenate(grads, axis=0), preferred_element_type=f32
+        )
+    for slot in range(2):
+        rows = slice(slot * BLOCK, (slot + 1) * BLOCK)
+        mine, other = pl.ds((s ^ (2 * slot)) * BLOCK, BLOCK), pl.ds((s ^ (1 + 2 * slot)) * BLOCK, BLOCK)
+        mine_ref[0, rows, :] = key_sum[mine, :]
+        mine_ref[1, rows, :] = value_sum[mine, :]
+        sent_ref[0, rows, :] = key_sum[other, :].astype(bf16)
+        sent_ref[1, rows, :] = value_sum[other, :].astype(bf16)
+
+
+def call_attention(kernel, s, own, other, bias, kept, outs, scratch):
+    pairs_count = D // PAIR
+    third = lambda n: pl.BlockSpec((2 * BLOCK, PAIR), lambda h: (0, h + n * pairs_count))
+    cut = third(0)
+    double = pl.BlockSpec((2, 2 * BLOCK, PAIR), lambda h: (0, 0, h))
+    per_pair = pl.BlockSpec((1, 2, 2 * BLOCK), lambda h: (h, 0, 0))
+    whole = pl.BlockSpec(bias.shape, lambda h: (0, 0, 0))
+    in_specs = [pl.BlockSpec(memory_space=pltpu.SMEM), third(0), third(1), third(1), third(2), third(2), whole]
+    args = [s, own, own, other, own, other, bias]
+    if kept:
+        in_specs += [cut, per_pair, cut]
+        args += kept
+    shapes, specs = [], []
+    for kind, spec in outs:
+        shapes.append(
+            {
+                0: jax.ShapeDtypeStruct((2 * BLOCK, D), kind),
+                1: jax.ShapeDtypeStruct((pairs_count, 2, 2 * BLOCK), kind),
+                2: jax.ShapeDtypeStruct((2, 2 * BLOCK, D), kind),
+            }[spec]
+        )
+        specs.append((cut, per_pair, double)[spec])
+    flops = 2 * (5 if kept else 2) * HEADS * 2 * BLOCK * WINDOW * HEAD_DIM
+    return pl.pallas_call(
+        kernel,
+        grid=(pairs_count,),
+        in_specs=in_specs,
+        out_specs=specs,
+        out_shape=shapes,
+        scratch_shapes=scratch,
+        compiler_params=pltpu.CompilerParams(vmem_limit_bytes=48 << 20),
+        cost_estimate=pl.CostEstimate(
+            flops=flops * 8, bytes_accessed=16 << 20, transcendentals=HEADS * 2 * BLOCK * WINDOW
+        ),
+    )(*args)
+
+
+def attend_forward_blocks(s, own, other, bias):
+    scratch = [pltpu.VMEM((SEQ_LEN, PAIR), bf16)] * 2
+    return call_attention(attend_forward_kernel, s, own, other, bias, (), ((bf16, 0), (f32, 1)), scratch)
+
+
+def attend_backward_blocks(s, own, other, bias, mixed, totals, grads):
+    scratch = [pltpu.VMEM((SEQ_LEN, PAIR), bf16)] * 2 + [pltpu.VMEM((SEQ_LEN, PAIR), f32)] * 2
+    outs = ((bf16, 0), (f32, 2), (bf16, 2))
+    kept = (mixed, totals, grads)
+    return call_attention(attend_backward_kernel, s, own, other, bias, kept, outs, scratch)
+
+
+def window_bias(s, ids):
+    out = []
+    for slot in range(2):
+        keys = lax.dynamic_slice_in_dim(ids, window_start(s, slot), WINDOW)
+        queries = lax.dynamic_slice_in_dim(ids, (s ^ (2 * slot)) * BLOCK, BLOCK)
+        out.append(jnp.where(keys[:, None] == queries[None, :], 0.0, -1e30))
+    return jnp.stack(out).astype(f32)
 
 
 def norm_forward(total):
@@ -281,22 +515,321 @@
     return flat(query_grad).astype(bf16), flat(key_grad), flat(value_grad)
 
 
-def make_body(fsdp_size, seq_size):
+SMALL = 8
+
+
+def staged_body(tokens, doc_lengths, cotangent, *shards):
+    (
+        query_weight,
+        key_weight,
+        value_weight,
+        mix_weight,
+        query_bias,
+        value_bias,
+        mix_bias,
+        first_gain,
+        first_shift,
+        inner_weight,
+        inner_bias,
+        outer_weight,
+        outer_bias,
+        second_gain,
+        second_shift,
+    ) = shards
+    layer_count = query_weight.shape[0]
+    devices = 32
+    length = SEQ_LEN // 4
+    rows_held, inner_held = D // devices, FF // devices
+    seq = lax.axis_index("seq")
+    row = seq // 2
+    coords = coordinates()
+    z, y, x, c = coords[0], coords[1], coords[2], coords[3]
+    place_of = seq.reshape(1).astype(jnp.int32)
+
+    def split_rows(both):
+        both = both.reshape(2, length, D)
+        return pick(both, row, 0), pick(both, 1 - row, 0)
+
+    token_kept, token_left = split_rows(tokens)
+    upstream_kept, upstream_left = split_rows(cotangent)
+    token_got = send(token_left, TO_X)
+
+    def unit_a(layer):
+        r = rows_held
+        parts = [w[layer] for w in (query_weight, key_weight, value_weight, mix_weight)]
+        outs = (((0, 0), (0, 1), (0, 2), (1, 0)))
+        return GatherUnit(
+            coords,
+            jnp.concatenate(parts),
+            [(r, 3 * D), (r, D)],
+            [(r * n, r * (n + 1), target, column) for n, (target, column) in enumerate(outs)],
+        )
+
+    def unit_i(layer):
+        r, inner = rows_held, inner_weight[layer]
+        return GatherUnit(
+            coords,
+            jnp.concatenate([inner[:, D * n : D * (n + 1)] for n in range(4)]),
+            [(r, FF)],
+            [(r * n, r * (n + 1), 0, n) for n in range(4)],
+        )
+
+    def unit_o(layer):
+        return GatherUnit(coords, outer_weight[layer], [(inner_held, D)], [(0, inner_held, 0, 0)])
+
+    units = [[make(layer) for make in (unit_a, unit_i, unit_o)] for layer in range(layer_count)]
+
+    small_vectors = (
+        query_bias,
+        value_bias,
+        mix_bias,
+        first_gain,
+        first_shift,
+        outer_bias,
+        second_gain,
+        second_shift,
+    )
+    vector_count = SMALL * layer_count
+    small_held = vector_count * rows_held
+    mine = jnp.concatenate(
+        [jnp.concatenate([v[layer] for v in small_vectors]) for layer in range(layer_count)]
+        + [inner_bias.reshape(-1)]
+    )
+    held = mine.shape[0]
+    padded = jnp.pad(mine, (0, 1024 - held)).reshape(8, 128)
+
+    tok = phase(token_got, units[0][0])
+    every = jnp.stack([padded] + [send(padded, TO_Z[4 - k]) for k in (1, 2, 3)])
+    every = jnp.roll(every, z, axis=0)
+    tok = phase(tok, units[0][0])
+    tok, every = phase((tok, every), units[0][1])
+    every = by_place(every, send(every, TO_Y), y, 1)
+    tok, every = phase((tok, every), units[0][0])
+    every = by_place(every, send(every, TO_X), x, 2)
+    every = by_place(every, send(every, TO_CORE), c, 3)
+
+    lengths = pick(doc_lengths.reshape(2, NDOC), row, 0)
+    places = lax.iota(jnp.int32, SEQ_LEN)
+    segment = jnp.sum((places[:, None] >= jnp.cumsum(lengths)[None, :]).astype(jnp.int32), axis=1)
+    bias = window_bias(seq, jnp.where(segment == NDOC - 1, NDOC + places, segment))
+    order = block_order(coords)
+    matrices = order_matrices(order)
+
+    every = every.reshape(devices, 1024)[:, :held].astype(f32)
+    small_all = (
+        every[:, :small_held]
+        .reshape(devices, vector_count, rows_held)
+        .transpose(1, 0, 2)
+        .reshape(layer_count, SMALL, D)
+    )
+    wide_all = (
+        every[:, small_held:]
+        .reshape(devices, layer_count, inner_held)
+        .transpose(1, 0, 2)
+        .reshape(layer_count, FF)
+    )
+    tok, bias, matrices, small_all, wide_all = phase((tok, bias, matrices, small_all, wide_all), units[0][1])
+    tok = phase(tok, units[0][2])
+    tok = phase(tok, units[0][0])
+
+    stream = jnp.concatenate([token_kept, tok]).astype(f32)
+    saved = []
+    for layer in range(layer_count):
+        a_unit, i_unit, o_unit = units[layer]
+        later = units[layer + 1] if layer + 1 < layer_count else None
+        q_bias, v_bias, m_bias, gain1, shift1, o_bias, gain2, shift2 = [small_all[layer, n] for n in range(SMALL)]
+        w_three, w_mix = a_unit.result()
+        w_three, w_mix = w_three.reshape(D, 3 * D), w_mix.reshape(D, D)
+        stream_low = stream.astype(bf16)
+        three = (dot(stream_low, w_three) + jnp.concatenate([q_bias, jnp.zeros_like(q_bias), v_bias])).astype(bf16)
+        three_got = send(three, TO_CORE)
+        stream, stream_low, three = phase((stream, stream_low, three), i_unit)
+        if later:
+            stream_low = phase(stream_low, later[0])
+        left_stream = selected(matrices, stream_low)
+        left_stream, three, three_got = phase((left_stream, three, three_got), o_unit)
+        left_stream = (left_stream[0], send(left_stream[1], TO_CORE))
+        mixed, totals = attend_forward_blocks(place_of, three, three_got, bias)
+        mixed, totals = phase((mixed, totals), i_unit, o_unit)
+        left_mix = selected(matrices, mixed)
+        first_sum = stream + (dot(mixed, w_mix) + m_bias)
+        first = norm_forward(first_sum)[0] * gain1 + shift1
+        first_low = first.astype(bf16)
+        left_first = selected(matrices, first_low)
+        (w_inner,) = i_unit.result()
+        w_inner = w_inner.reshape(D, FF)
+        first, first_low, left_mix, left_first = lax.optimization_barrier(
+            (first, first_low, left_mix, left_first)
+        )
+        left_mix, left_first = [(m, send(t, TO_CORE)) for m, t in (left_mix, left_first)]
+        if later:
+            first, first_low = phase((first, first_low), later[0])
+            first, first_low = phase((first, first_low), later[1])
+        else:
+            (upstream_left,) = (tie(upstream_left, first_low),)
+            upstream_got = send(upstream_left, TO_X)
+        inner = dot(first_low, w_inner) + wide_all[layer]
+        below = 0.5 * (1.0 + lax.erf(inner * (0.5**0.5)))
+        active = (inner * below).astype(bf16)
+        slope = (below + inner * jnp.exp(-0.5 * inner * inner) * (2 * math.pi) ** -0.5).astype(bf16)
+        active, slope = phase((active, slope), o_unit)
+        if later:
+            active = phase(active, later[0])
+        (w_outer,) = o_unit.result()
+        w_outer = w_outer.reshape(FF, D)
+        second_sum = first + (dot(active, w_outer) + o_bias)
+        left_active = (active, send(active, TO_CORE))
+        stream = norm_forward(second_sum)[0] * gain2 + shift2
+        if later:
+            stream = phase(stream, later[1])
+            stream = phase(stream, later[2])
+            stream = phase(stream, later[0])
+        saved.append(
+            (
+                (w_three, w_mix, w_inner, w_outer, gain1, gain2),
+                (three, three_got, totals, mixed),
+                (first_sum, slope, second_sum),
+                (left_stream, left_mix, left_first, left_active),
+            )
+        )
+
+    def both_rows(kept, got):
+        got = got.astype(f32)
+        return jnp.where(row == 0, jnp.stack([kept, got]), jnp.stack([got, kept])).reshape(tokens.shape)
+
+    output = stream
+    output_got = send(output[length:].astype(bf16), TO_X)
+
+    upstream = jnp.concatenate([upstream_kept, upstream_got]).astype(f32)
+    small_grads, wide_grads = [None] * layer_count, [None] * layer_count
+    sums = [None] * layer_count
+    before = None
+    for layer in reversed(range(layer_count)):
+        weights, kept, rest, lefts = saved[layer]
+        w_three, w_mix, w_inner, w_outer, gain1, gain2 = weights
+        three, three_got, totals, mixed = kept
+        first_sum, slope, second_sum = rest
+        left_stream, left_mix, left_first, left_active = lefts
+        second_grad, gain2_grad, shift2_grad = norm_backward(second_sum, gain2, upstream)
+        second_low = second_grad.astype(bf16)
+        second_got = send(second_low, TO_CORE)
+        inner_low = (contract_cols(second_low, w_outer) * slope).astype(bf16)
+        inner_got = send(inner_low, TO_CORE)
+        o_sum = SumUnit(wide_terms_of(order, left_active, (second_low, second_got)))
+        second_grad, inner_low = phase((second_grad, inner_low), o_sum)
+        if before:
+            second_grad, inner_low = phase((second_grad, inner_low), before[0], before[2])
+        first_grad = second_grad + contract_cols(inner_low, w_inner)
+        first_sum_grad, gain1_grad, shift1_grad = norm_backward(first_sum, gain1, first_grad)
+        branch_low = first_sum_grad.astype(bf16)
+        branch_got = send(branch_low, TO_CORE)
+        i_sum = SumUnit(weight_terms((left_first, (inner_low, inner_got))))
+        first_sum_grad, branch_low = phase((first_sum_grad, branch_low), i_sum)
+        mixed_grad = contract_cols(branch_low, w_mix).astype(bf16)
+        if before:
+            mixed_grad = phase(mixed_grad, before[1], before[0])
+        else:
+            mixed_grad, output_got = lax.optimization_barrier((mixed_grad, output_got))
+        query_low, own_grads, sent_grads = attend_backward_blocks(
+            place_of, three, three_got, bias, mixed, totals, mixed_grad
+        )
+        grads_back = send(sent_grads, TO_CORE)
+        own_grads = phase(own_grads, o_sum)
+        if before:
+            own_grads = phase(own_grads, before[1])
+        sums_low = (own_grads + grads_back.astype(f32)).astype(bf16)
+        low = jnp.concatenate([query_low, sums_low[0], sums_low[1]], axis=1)
+        low_got = send(low, TO_CORE)
+        first_sum_grad, low = phase((first_sum_grad, low), i_sum)
+        upstream = first_sum_grad + contract_cols(low, w_three)
+        a_sum = SumUnit(weight_terms((left_stream, (low, low_got)), (left_mix, (branch_low, branch_got))))
+        upstream = phase(upstream, a_sum)
+        if before:
+            upstream = phase(upstream, before[1])
+        upstream = phase(upstream, o_sum)
+        small_grads[layer] = jnp.stack(
+            [
+                column_sum(low[:, :D]),
+                column_sum(low[:, 2 * D :]),
+                column_sum(branch_low),
+                gain1_grad,
+                shift1_grad,
+                column_sum(second_low),
+                gain2_grad,
+                shift2_grad,
+            ]
+        )
+        wide_grads[layer] = column_sum(inner_low)
+        before = sums[layer] = (i_sum, a_sum, o_sum)
+
+    token_back = send(upstream[length:].astype(bf16), TO_X)
+    small_terms = (
+        jnp.stack(small_grads)
+        .reshape(vector_count, devices, rows_held)
+        .transpose(1, 0, 2)
+        .reshape(devices, small_held)
+    )
+    wide_terms = (
+        jnp.stack(wide_grads)
+        .reshape(layer_count, devices, inner_held)
+        .transpose(1, 0, 2)
+        .reshape(devices, layer_count * inner_held)
+    )
+    terms = jnp.pad(jnp.concatenate([small_terms, wide_terms], axis=1), ((0, 0), (0, 1024 - held)))
+    chosen = (order[:, None] == lax.iota(jnp.int32, devices)[None, :]).astype(f32)
+    terms = jnp.dot(chosen, terms, precision=lax.Precision.HIGHEST).reshape(2, 128, 128)
+    terms = (terms[0] + send(terms[1].astype(bf16), TO_CORE).astype(f32)).astype(bf16)
+    small_sum = SumUnit((terms[:64], terms[64:]))
+
+    i_sum, a_sum, o_sum = sums[0]
+    phase((), small_sum)
+    phase((), i_sum, o_sum)
+    phase((), a_sum, small_sum)
+    phase((), i_sum)
+    phase((), a_sum, small_sum)
+    phase((), a_sum, small_sum)
+    own_terms = small_sum.kept.reshape(-1)[:held]
+    small_own = own_terms[:small_held].reshape(layer_count, SMALL, rows_held)
+    wide_own = own_terms[small_held:].reshape(layer_count, inner_held)
+    for layer in range(1, layer_count):
+        for unit in sums[layer]:
+            while unit.step < 4:
+                phase((), unit)
+    i_all, a_all, o_all = [
+        jnp.stack([sums[layer][n].kept for layer in range(layer_count)]) for n in range(3)
+    ]
+    return (
+        both_rows(output[:length], output_got),
+        both_rows(upstream[:length], token_back),
+        a_all[:, :, :D],
+        a_all[:, :, D : 2 * D],
+        a_all[:, :, 2 * D : 3 * D],
+        a_all[:, :, 3 * D :],
+        small_own[:, 0],
+        small_own[:, 1],
+        small_own[:, 2],
+        small_own[:, 3],
+        small_own[:, 4],
+        i_all,
+        wide_own,
+        o_all,
+        small_own[:, 5],
+        small_own[:, 6],
+        small_own[:, 7],
+    )
+
+
+def plain_body(fsdp_size, seq_size):
     half = seq_size // 2
-    staged = (fsdp_size, seq_size) == (8, 4)
     device_count = fsdp_size * seq_size
     across = [(i, (i + half) % seq_size) for i in range(seq_size)]
     groups = [[m * half + j for j in range(half)] for m in range(2)]
     length = SEQ_LEN // seq_size
 
     def gather_siblings(rows):
-        if staged:
-            return jnp.stack([rows, send(rows, TO_CORE)])
         return lax.all_gather(rows, "seq", axis_index_groups=groups)
 
     def scatter_siblings(own_order):
-        if staged:
-            return own_order[0] + send(own_order[1].astype(bf16), TO_CORE).astype(f32)
         return lax.psum_scatter(own_order, "seq", axis_index_groups=groups)
 
     def body(tokens, doc_lengths, cotangent, *shards):
@@ -320,7 +853,6 @@
         layer_count = query_weight.shape[0]
         seq = lax.axis_index("seq")
         row = seq // half
-        coords = coordinates()
         rows_held = D // device_count
         inner_held = FF // device_count
 
@@ -343,25 +875,7 @@
         vector_count = len(small_vectors) * layer_count
         mine = vector_rows(small_vectors, inner_bias)
         held = mine.shape[0]
-        if staged:
-            padded = jnp.pad(mine, (0, 1024 - held)).reshape(8, 128)
-            parts = jnp.stack([padded] + [send(padded, TO_Z[4 - k]) for k in (1, 2, 3)])
-            z, y, x, c = coords[0], coords[1], coords[2], coords[3]
-            parts = jnp.roll(parts, z, axis=0)
-
-            def both(own, other, place_of, axis):
-                return jnp.where(
-                    place_of == 0,
-                    jnp.stack([own, other], axis),
-                    jnp.stack([other, own], axis),
-                )
-
-            parts = both(parts, send(parts, TO_Y), y, 1)
-            parts = both(parts, send(parts, TO_X), x, 2)
-            parts = both(parts, send(parts, TO_CORE), c, 3)
-            every = parts.reshape(device_count, 1024)[:, :held]
-        else:
-            every = lax.all_gather(mine, AXES)
+        every = lax.all_gather(mine, AXES)
         every = every.astype(f32)
         small_held = vector_count * rows_held
         small_all = (
@@ -377,37 +891,9 @@
             .reshape(layer_count, FF)
         )
 
-        gather = Gather(coords)
-
-        def attention_weights(layer):
-            parts = [w[layer] for w in (query_weight, key_weight, value_weight, mix_weight)]
-            if not staged:
-                return [lax.all_gather(p, AXES, axis=0, tiled=True) for p in parts]
-            r = rows_held
-            got = gather(
-                jnp.concatenate(parts),
-                2 * r,
-                [(r, D)] * 4,
-                (((0, r, 0, 0), (r, 2 * r, 1, 0)), ((0, r, 2, 0), (r, 2 * r, 3, 0))),
-            )
-            return [g.reshape(D, D) for g in got]
-
-        def forward_weights(layer):
-            inner, outer = inner_weight[layer], outer_weight[layer]
-            if not staged:
-                return [lax.all_gather(p, AXES, axis=0, tiled=True) for p in (inner, outer)]
-            r = rows_held
-            blocks = FF // D
-            got = gather(
-                jnp.concatenate([inner[:, D * n : D * (n + 1)] for n in range(blocks)] + [outer]),
-                blocks * r,
-                [(r, FF), (inner_held, D)],
-                (
-                    tuple((r * n, r * (n + 1), 0, n) for n in range(blocks)),
-                    ((0, inner_held, 1, 0),),
-                ),
-            )
-            return [got[0].reshape(D, FF), got[1].reshape(FF, D)]
+        def whole_weights(layer):
+            weights = (query_weight, key_weight, value_weight, mix_weight, inner_weight, outer_weight)
+            return [lax.all_gather(w[layer], AXES, axis=0, tiled=True) for w in weights]
 
         def own_row(both_rows):
             kept = pick(both_rows, row, 0)
@@ -434,10 +920,7 @@
             return jnp.sum((places[:, None] >= bounds[None, :]).astype(jnp.int32), axis=1)
 
         query_places = positions(seq)
-        if staged:
-            key_places = jnp.concatenate([positions(seq), positions(seq ^ 1)])
-        else:
-            key_places = jnp.concatenate([positions(row * half + j) for j in range(half)])
+        key_places = jnp.concatenate([positions(row * half + j) for j in range(half)])
         query_segment, key_segment = segments(query_places), segments(key_places)
         allowed = (
             (query_segment[:, None] == key_segment[None, :]) & (key_segment[None, :] != NDOC - 1)
@@ -449,8 +932,7 @@
             q_bias, v_bias, m_bias, gain1, shift1, o_bias, gain2, shift2 = [
                 small_all[layer, n] for n in range(len(small_vectors))
             ]
-            w_query, w_key, w_value, w_mix = attention_weights(layer)
-            w_inner, w_outer = forward_weights(layer)
+            w_query, w_key, w_value, w_mix, w_inner, w_outer = whole_weights(layer)
             stream_low = stream.astype(bf16)
             queries = (dot(stream_low, w_query) + q_bias).astype(bf16)
             key_rows = dot(stream_low, w_key).astype(bf16)
@@ -483,9 +965,7 @@
         wide_grads = [None] * layer_count
         results = [None] * layer_count
 
-        def reduced(grads, x_first):
-            if staged:
-                return summed_shards(coords, [g.astype(bf16) for g in grads], x_first)
+        def reduced(grads):
             return [lax.psum_scatter(g, AXES, scatter_dimension=0, tiled=True) for g in grads]
 
         for layer in reversed(range(layer_count)):
@@ -494,9 +974,9 @@
             first_sum, first_low, slope, active, second_sum = rest
             second_grad, gain2_grad, shift2_grad = norm_backward(second_sum, gain2, upstream)
             second_low = second_grad.astype(bf16)
-            (outer_grad,) = reduced([contract_rows(active, second_low)], False)
+            (outer_grad,) = reduced([contract_rows(active, second_low)])
             inner_low = (contract_cols(second_low, w_outer) * slope).astype(bf16)
-            (inner_grad,) = reduced([contract_rows(first_low, inner_low)], True)
+            (inner_grad,) = reduced([contract_rows(first_low, inner_low)])
             first_grad = second_grad + contract_cols(inner_low, w_inner)
             first_sum_grad, gain1_grad, shift1_grad = norm_backward(first_sum, gain1, first_grad)
             branch_low = first_sum_grad.astype(bf16)
@@ -508,9 +988,9 @@
             n = 2 * length
             key_low = scatter_siblings(key_terms.reshape(half, n, D)).astype(bf16)
             value_low = scatter_siblings(value_terms.reshape(half, n, D)).astype(bf16)
-            value_grad, mix_grad = reduced([contract_rows(stream_low, value_low), mix_terms], False)
+            value_grad, mix_grad = reduced([contract_rows(stream_low, value_low), mix_terms])
             query_grad, key_grad = reduced(
-                [contract_rows(stream_low, query_low), contract_rows(stream_low, key_low)], True
+                [contract_rows(stream_low, query_low), contract_rows(stream_low, key_low)]
             )
             upstream = (
                 first_sum_grad
@@ -547,12 +1027,7 @@
             .reshape(device_count, layer_count * inner_held)
         )
         terms = jnp.concatenate([small_terms, wide_terms], axis=1)
-        if staged:
-            terms = jnp.pad(terms, ((0, 0), (0, 1024 - held))).reshape(device_count * 8, 128)
-            (own_terms,) = summed_shards(coords, [terms], True)
-            own_terms = own_terms.reshape(-1)[:held]
-        else:
-            own_terms = lax.psum_scatter(terms, AXES, scatter_dimension=0, tiled=False)
+        own_terms = lax.psum_scatter(terms, AXES, scatter_dimension=0, tiled=False)
         small_own = own_terms[:small_held].reshape(layer_count, len(small_vectors), rows_held)
         wide_own = own_terms[small_held:].reshape(layer_count, inner_held)
         query_g, key_g, value_g, mix_g, inner_g, outer_g = [
@@ -588,5 +1063,6 @@
     in_specs += (matrix, vector, matrix, vector, vector, vector)
     out_specs = (tokens, tokens) + (matrix,) * 4 + (vector,) * 5
     out_specs += (matrix, vector, matrix, vector, vector, vector)
-    body = make_body(mesh.shape["fsdp"], mesh.shape["seq"])
+    sizes = (mesh.shape["fsdp"], mesh.shape["seq"])
+    body = staged_body if sizes == (8, 4) else plain_body(*sizes)
     return jax.shard_map(body, mesh=mesh, in_specs=in_specs, out_specs=out_specs, check_vma=False)

time: 1210 us -> 818 us (0.68)
  matrix products: 336 us -> 125 us
  Pallas kernels: 57.9 us -> 186 us
  local copies, waits for them, and re-layouts: 148 us -> 47.3 us
  other arithmetic: 178 us -> 80.4 us
  waiting for transfers between devices: 322 us -> 246 us
  starting transfers between devices: 162 us -> 120 us
    dot_general x24 -> x13, matrix products: 225 us -> 18.2 us  [the longest x12 18 us: selected(): lax.dot_general(m, rows, (((0,), (1,)), ((), ())), preferred_element_type...]
    pallas_call x0 -> x10, Pallas kernels: none -> 152 us  [the longest x4 90.9 us: call_attention(): pl.pallas_call(kernel, grid=(pairs_count,), in_specs=in_specs, out_specs=...]
    ppermute x112 -> x108, waiting for transfers between devices: 318 us -> 246 us  [send(): return lax.ppermute(value, AXES, to)]
    convert_element_type x24, other arithmetic: 87.5 us -> 31.3 us  [the longest x7 14.6 us: local(): add = lambda a, b: (a.astype(f32) + b.astype(f32)).astype(bf16)]
    dynamic_slice x12 -> x3, local copies, waits for them, and re-layouts: 41.4 us -> 0.16 us  [the longest x1 0.08 us: window_bias(): keys = lax.dynamic_slice_in_dim(ids, window_start(s, slot), WINDOW)]
    ppermute x112 -> x108, starting transfers between devices: 158 us -> 120 us  [send(): return lax.ppermute(value, AXES, to)]
    another operation x22 -> x9, local copies, waits for them, and re-layouts: 38.3 us -> 0.66 us  [the longest x2 0.24 us: block_order(): return jnp.stack(order).astype(jnp.int32)]
    reduce_sum x4 -> x1, other arithmetic: 28.8 us -> 0.09 us  [staged_body(): jnp.sum((places[:, None] >= jnp.cumsum(lengths)[None, :]).astype(jnp.int3...]
  transfers between devices with their start and end apart: 116 -> 108, of which waited for: 42 -> 33; matrix products, arithmetic and copies ran while one was open for 40% -> 26% of each run, Pallas kernels for 5% -> 21%
where the time goes in v2:
time: 818 us; the launch traced here: 808 us
  waiting for transfers between devices  246 us (30%)
  Pallas kernels  186 us (23%)
  matrix products  125 us (15%)
  starting transfers between devices  120 us (15%)
  other arithmetic  80.4 us (10%)
  local copies, waits for them, and re-layouts  47.3 us (6%)
    ppermute x108, waiting for transfers between devices, send(): return lax.ppermute(value, AXES, to)  246 us
    ppermute x108, starting transfers between devices, send(): return lax.ppermute(value, AXES, to)  120 us
    pallas_call x4, Pallas kernels, call_attention(): pl.pallas_call(kernel, grid=(pairs_count,), in_specs=in_specs, out_specs=...  90.9 us
    dot_general x8, matrix products, dot(): return jnp.dot(left, right, preferred_element_type=f32)  57.4 us
    dot_general x8, matrix products, contract_cols(): lax.dot_general(left, right, (((1,), (1,)), ((), ())), preferred_element_...  49.2 us
    pallas_call x6, Pallas kernels, place(): pl.pallas_call(kernel, in_specs=[pl.BlockSpec(memory_space=pltpu.SMEM)] +...  33.5 us
    pallas_call x4, Pallas kernels, weight_terms(): pl.pallas_call(kernel, grid=(columns // tile,), in_specs=in_specs, out_sp...  32 us
    pallas_call x2, Pallas kernels, wide_terms_of(): pl.pallas_call(kernel, grid_spec=pltpu.PrefetchScalarGridSpec(num_scalar_...  29.5 us
  transfers between devices with their start and end apart: 108, of which 33 were waited for; matrix products, arithmetic and copies ran while one was open for 26% of the time, Pallas kernels for 21%

profile of v2, /device:TPU:0, one launch (start us, length us, event | category | flops | bytes accessed | tf_op | source)
XLA Modules:
  0.0 807.8 jit_solution(15405435896446316994)
XLA Ops:
  33.1 5.6 collective-permute-done.1
  38.8 16.1 %collective-permute-done.2 = bf16[128,1024]{1,0:T(8,128)(2,1)S(1)} collective-permute-done((bf16[128,1024]{1,0:T(8,128)(2,1)S(1)}, bf16[128,1024]{1,0:T(8,128)(2,1)S(1)}, u32[]{:S(2)}, u32[]{:S(2)}) %collective-permute-start.2) | collective-permute-done | bytes 262176 | tf_op jit(solution)/shard_map/ppermute | solution.py:56
  58.6 11.2 %collective-permute-done.7 = bf16[4,8,128]{2,1,0:T(8,128)(2,1)S(1)} collective-permute-done((bf16[4,8,128]{2,1,0:T(8,128)(2,1)S(1)}, bf16[4,8,128]{2,1,0:T(8,128)(2,1)S(1)}, u32[]{:S(2)}, u32[]{:S(2)}) %collective-permute-start.7) | collective-permute-done | bytes 8224 | tf_op jit(solution)/shard_map/ppermute | solution.py:56
  78.9 19.4 %collective-permute-done.9 = bf16[4,2,8,128]{3,2,1,0:T(8,128)(2,1)} collective-permute-done((bf16[4,2,8,128]{3,2,1,0:T(8,128)(2,1)S(1)}, bf16[4,2,8,128]{3,2,1,0:T(8,128)(2,1)}, u32[]{:S(2)}, u32[]{:S(2)}) %collective-permute-start.9) | collective-permute-done | bytes 16416 | tf_op jit(solution)/shard_map/ppermute | solution.py:56
  102.2 8.6 %collective-permute-done.13 = bf16[128,1024]{1,0:T(8,128)(2,1)} collective-permute-done((bf16[128,1024]{1,0:T(8,128)(2,1)}, bf16[128,1024]{1,0:T(8,128)(2,1)}, u32[]{:S(2)}, u32[]{:S(2)}) %collective-permute-start.13) | collective-permute-done | bytes 262176 | tf_op jit(solution)/shard_map/ppermute | solution.py:56
  119.3 6.7 shard_map.305
  126.1 7.2 add_convert_fusion.1.q_ref.km_ref.vm_ref
  138.5 9.8 %collective-permute-done.17 = bf16[4,128,1024]{2,1,0:T(8,128)(2,1)S(1)} collective-permute-done((bf16[4,128,1024]{2,1,0:T(8,128)(2,1)S(1)}, bf16[4,128,1024]{2,1,0:T(8,128)(2,1)S(1)}, u32[]{:S(2)}, u32[]{:S(2)}) %collective-permute-start.17) | collective-permute-done | bytes 1048608 | tf_op jit(solution)/shard_map/ppermute | solution.py:56
  168.8 21.0 %shard_map.306 = (bf16[512,1024]{1,0:T(8,128)(2,1)S(1)}, f32[8,2,512]{2,1,0:T(2,128)S(1)}) custom-call(s32[1]{0:T(128)} %bitcast.88.s_ref, bf16[512,3072]{1,0:T(8,128)(2,1)S(1)} %copy-done.4, bf16[512,3072]{1,0:T(8,128)(2,1)S(1)} %copy-done.4, bf16[512,3072]{1,0:T(8,128)(2,1)} %copy-done.117, bf16[512,3072]{1,0:T(8,128)(2,1)S(1)} %copy-done.4, ...), custom_call_target="tpu_custom_call" | custom-call | flops 12884901888 | bytes 16777216 | tf_op jit(solution)/shard_map/pallas_call | solution.py:425
  207.7 5.7 shard_map.307
  213.4 11.7 %fusion.4 = (bf16[512,4096]{1,0:T(8,128)(2,1)}, bf16[512,4096]{1,0:T(8,128)(2,1)}) fusion(f32[4096]{0:T(1024)S(1)} %bitcast.438, bf16[512,1024]{1,0:T(8,128)(2,1)S(1)} %get-tuple-element.426, bf16[1024,4096]{1,0:T(8,128)(2,1)} %bitcast.371), kind=kOutput, calls=%fused_computation.6 | convolution fusion | flops 4320133120 | bytes 17842176 | tf_op jit(solution)/shard_map/dot_general | solution.py:23
  225.1 7.3 collective-permute-done.29.refs_1_
  237.2 9.9 %collective-permute-done.31 = bf16[4,128,1024]{2,1,0:T(8,128)(2,1)S(1)} collective-permute-done((bf16[4,128,1024]{2,1,0:T(8,128)(2,1)S(1)}, bf16[4,128,1024]{2,1,0:T(8,128)(2,1)S(1)}, u32[]{:S(2)}, u32[]{:S(2)}) %collective-permute-start.31) | collective-permute-done | bytes 1048608 | tf_op jit(solution)/shard_map/ppermute | solution.py:56
  253.5 8.3 %fusion.46 = (f32[512]{0:T(512)S(1)}, f32[512,1024]{1,0:T(8,128)S(1)}) fusion(f32[512,1024]{1,0:T(8,128)S(1)} %copy-done.49, f32[1024]{0:T(1024)S(1)} %bitcast.448, bf16[512,4096]{1,0:T(8,128)(2,1)} %get-tuple-element.439.a1, bf16[4096,1024]{1,0:T(8,128)(2,1)} %bitcast.373), kind=kOutput, calls=%fused_computation.312 | convolution fusion | flops 4296539648 | bytes 16783360 | tf_op jit(solution)/shard_map/dot_general | solution.py:23
  263.8 9.6 %collective-permute-done.36.refs_1_ = bf16[2,4,128,1024]{3,2,1,0:T(8,128)(2,1)S(1)} collective-permute-done((bf16[2,4,128,1024]{3,2,1,0:T(8,128)(2,1)S(1)}, bf16[2,4,128,1024]{3,2,1,0:T(8,128)(2,1)S(1)}, u32[]{:S(2)}, u32[]{:S(2)}) %collective-permute-start.36) | collective-permute-done | bytes 2097184 | tf_op jit(solution)/shard_map/ppermute | solution.py:56
  277.6 5.8 shard_map.309
  283.5 7.2 add_convert_fusion.q_ref.km_ref.vm_ref
  292.4 13.3 %collective-permute-done.39 = bf16[4,128,1024]{2,1,0:T(8,128)(2,1)S(1)} collective-permute-done((bf16[4,128,1024]{2,1,0:T(8,128)(2,1)S(1)}, bf16[4,128,1024]{2,1,0:T(8,128)(2,1)S(1)}, u32[]{:S(2)}, u32[]{:S(2)}) %collective-permute-start.39) | collective-permute-done | bytes 1048608 | tf_op jit(solution)/shard_map/ppermute | solution.py:56
  310.4 6.7 collective-permute-done.41
  318.7 13.6 %collective-permute-done.42 = bf16[128,1024]{1,0:T(8,128)(2,1)S(1)} collective-permute-done((bf16[128,1024]{1,0:T(8,128)(2,1)S(1)}, bf16[128,1024]{1,0:T(8,128)(2,1)S(1)}, u32[]{:S(2)}, u32[]{:S(2)}) %collective-permute-start.42) | collective-permute-done | bytes 262176 | tf_op jit(solution)/shard_map/ppermute | solution.py:56
  335.5 21.2 %shard_map.310 = (bf16[512,1024]{1,0:T(8,128)(2,1)S(1)}, f32[8,2,512]{2,1,0:T(2,128)S(1)}) custom-call(s32[1]{0:T(128)} %bitcast.88.s_ref, bf16[512,3072]{1,0:T(8,128)(2,1)S(1)} %copy-done.6, bf16[512,3072]{1,0:T(8,128)(2,1)S(1)} %copy-done.6, bf16[512,3072]{1,0:T(8,128)(2,1)} %copy-done.118, bf16[512,3072]{1,0:T(8,128)(2,1)S(1)} %copy-done.6, ...), custom_call_target="tpu_custom_call" | custom-call | flops 12884901888 | bytes 16777216 | tf_op jit(solution)/shard_map/pallas_call | solution.py:425
  369.7 5.7 shard_map.311
  375.5 11.8 %fusion.9 = (bf16[512,4096]{1,0:T(8,128)(2,1)}, bf16[512,4096]{1,0:T(8,128)(2,1)}) fusion(f32[4096]{0:T(1024)S(1)} %bitcast.437, bf16[512,1024]{1,0:T(8,128)(2,1)S(1)} %copy-done.70, bf16[1024,4096]{1,0:T(8,128)(2,1)} %bitcast.375), kind=kOutput, calls=%fused_computation.11 | convolution fusion | flops 4320133120 | bytes 17842176 | tf_op jit(solution)/shard_map/dot_general | solution.py:23
  396.4 8.5 %fusion.48 = (f32[512]{0:T(512)S(1)}, f32[512,1024]{1,0:T(8,128)S(1)}) fusion(f32[512,1024]{1,0:T(8,128)S(1)} %get-tuple-element.490, f32[1024]{0:T(1024)S(1)} %bitcast.446, bf16[512,4096]{1,0:T(8,128)(2,1)} %get-tuple-element.499.a1, bf16[4096,1024]{1,0:T(8,128)(2,1)} %bitcast.377), kind=kOutput, calls=%fused_computation.314 | convolution fusion | flops 4296539648 | bytes 16783360 | tf_op jit(solution)/shard_map/dot_general | solution.py:23
  411.6 7.7 multiply_convert_fusion.1.refs_2_
  423.2 14.6 %shard_map.313 = (bf16[1024,1024]{1,0:T(8,128)(2,1)S(1)}, bf16[1024,1024]{1,0:T(8,128)(2,1)}) custom-call(s32[32]{0:T(128)S(1)} %stack.512.order_ref, bf16[512,4096]{1,0:T(8,128)(2,1)} %get-tuple-element.499.a1, bf16[512,4096]{1,0:T(8,128)(2,1)} %collective-permute-done.52.a2, bf16[512,1024]{1,0:T(8,128)(2,1)S(1)} %get-tuple-element.675.b1, ...), custom_call_target="tpu_custom_call" | custom-call | flops 4294967296 | bytes 6291456 | tf_op jit(solution)/shard_map/pallas_call | solution.py:283
  437.8 8.4 %fusion.49 = f32[512,1024]{1,0:T(8,128)S(1)} fusion(bf16[512,4096]{1,0:T(8,128)(2,1)} %multiply_convert_fusion.1.refs_2_, bf16[1024,4096]{1,0:T(8,128)(2,1)} %bitcast.376), kind=kOutput, calls=%fused_computation.315 | convolution fusion | flops 4294967296 | bytes 14680064 | tf_op jit(solution)/shard_map/dot_general | solution.py:31
  450.3 7.6 shard_map.314
  459.3 24.4 %shard_map.315 = (bf16[512,1024]{1,0:T(8,128)(2,1)S(1)}, f32[2,512,1024]{2,1,0:T(8,128)}, bf16[2,512,1024]{2,1,0:T(8,128)(2,1)}) custom-call(s32[1]{0:T(128)} %bitcast.88.s_ref, bf16[512,3072]{1,0:T(8,128)(2,1)} %copy-done.5, bf16[512,3072]{1,0:T(8,128)(2,1)} %copy-done.5, bf16[512,3072]{1,0:T(8,128)(2,1)} %copy-done.118, bf16[512,3072]{1,0:T(8,128)(2,1)} %copy-done.5, ...), custom_call_target="tpu_custom_call" | custom-call | flops 32212254720 | bytes 16777216 | tf_op jit(solution)/shard_map/pallas_call | solution.py:425
  497.8 11.9 %collective-permute-done.59 = bf16[256,4096]{1,0:T(8,128)(2,1)S(1)} collective-permute-done((bf16[256,4096]{1,0:T(8,128)(2,1)S(1)}, bf16[256,4096]{1,0:T(8,128)(2,1)S(1)}, u32[]{:S(2)}, u32[]{:S(2)}) %collective-permute-start.59) | collective-permute-done | bytes 2097184 | tf_op jit(solution)/shard_map/ppermute | solution.py:56
  517.6 8.5 %shard_map.316 = (bf16[256,4096]{1,0:T(8,128)(2,1)}, bf16[256,4096]{1,0:T(8,128)(2,1)}) custom-call(bf16[512,512]{1,0:T(8,128)(2,1)S(1)} %convolution_convert_fusion.7.refs_0_, bf16[512,512]{1,0:T(8,128)(2,1)S(1)} %collective-permute-done.60.refs_1_, bf16[512,3072]{1,0:T(8,128)(2,1)} %copy-done.27, bf16[512,3072]{1,0:T(8,128)(2,1)} %collective-permute-done.61.refs_3_, ...), custom_call_target="tpu_custom_call" | custom-call | flops 4294967296 | bytes 13631488 | tf_op jit(solution)/shard_map/pallas_call | solution.py:246
  531.1 10.3 %multiply_convert_fusion.refs_2_ = bf16[512,4096]{1,0:T(8,128)(2,1)} fusion(bf16[512,4096]{1,0:T(8,128)(2,1)} %get-tuple-element.544, bf16[512,1024]{1,0:T(8,128)(2,1)S(1)} %get-tuple-element.672.b1, bf16[4096,1024]{1,0:T(8,128)(2,1)} %bitcast.374), kind=kOutput, calls=%fused_computation.14 | convolution fusion | flops 4301258752 | bytes 17825792 | tf_op jit(solution)/shard_map/dot_general | solution.py:31
  548.3 14.9 %shard_map.317 = (bf16[1024,1024]{1,0:T(8,128)(2,1)S(1)}, bf16[1024,1024]{1,0:T(8,128)(2,1)}) custom-call(s32[32]{0:T(128)S(1)} %stack.512.order_ref, bf16[512,4096]{1,0:T(8,128)(2,1)} %get-tuple-element.439.a1, bf16[512,4096]{1,0:T(8,128)(2,1)} %collective-permute-done.65.a2, bf16[512,1024]{1,0:T(8,128)(2,1)S(1)} %get-tuple-element.672.b1, ...), custom_call_target="tpu_custom_call" | custom-call | flops 4294967296 | bytes 6291456 | tf_op jit(solution)/shard_map/pallas_call | solution.py:283
  567.4 7.7 multiply_reduce_fusion.2
  585.2 7.4 shard_map.318
  594.0 7.3 collective-permute-done.75
  606.8 24.3 %shard_map.319 = (bf16[512,1024]{1,0:T(8,128)(2,1)S(1)}, f32[2,512,1024]{2,1,0:T(8,128)}, bf16[2,512,1024]{2,1,0:T(8,128)(2,1)}) custom-call(s32[1]{0:T(128)} %bitcast.88.s_ref, bf16[512,3072]{1,0:T(8,128)(2,1)} %copy-done.3, bf16[512,3072]{1,0:T(8,128)(2,1)} %copy-done.3, bf16[512,3072]{1,0:T(8,128)(2,1)} %copy-done.117, bf16[512,3072]{1,0:T(8,128)(2,1)} %copy-done.3, ...), custom_call_target="tpu_custom_call" | custom-call | flops 32212254720 | bytes 16777216 | tf_op jit(solution)/shard_map/pallas_call | solution.py:425
  647.8 16.8 %collective-permute-done.80 = bf16[256,4096]{1,0:T(8,128)(2,1)S(1)} collective-permute-done((bf16[256,4096]{1,0:T(8,128)(2,1)S(1)}, bf16[256,4096]{1,0:T(8,128)(2,1)S(1)}, u32[]{:S(2)}, u32[]{:S(2)}) %collective-permute-start.80) | collective-permute-done | bytes 2097184 | tf_op jit(solution)/shard_map/ppermute | solution.py:56
  673.8 9.1 %convolution_add_fusion = f32[512,1024]{1,0:T(8,128)} fusion(f32[512,1024]{1,0:T(8,128)} %get-tuple-element.592, bf16[512,3072]{1,0:T(8,128)(2,1)} %pad_maximum_fusion.1.refs_2_, bf16[1024,3072]{1,0:T(8,128)(2,1)} %bitcast.462), kind=kOutput, calls=%fused_computation.95 | convolution fusion | flops 3221749760 | bytes 13631488 | tf_op jit(solution)/shard_map/dot_general | solution.py:31
  692.6 8.6 %shard_map.320 = (bf16[256,4096]{1,0:T(8,128)(2,1)}, bf16[256,4096]{1,0:T(8,128)(2,1)}) custom-call(bf16[512,512]{1,0:T(8,128)(2,1)S(1)} %copy-done.16, bf16[512,512]{1,0:T(8,128)(2,1)S(1)} %collective-permute-done.81.refs_1_, bf16[512,3072]{1,0:T(8,128)(2,1)} %pad_maximum_fusion.1.refs_2_, bf16[512,3072]{1,0:T(8,128)(2,1)} %collective-permute-done.82.refs_3_, ...), custom_call_target="tpu_custom_call" | custom-call | flops 4294967296 | bytes 13631488 | tf_op jit(solution)/shard_map/pallas_call | solution.py:246
  701.2 6.6 collective-permute-done.86
  710.3 6.1 collective-permute-start.102
  723.1 8.6 %collective-permute-done.103 = bf16[128,1024]{1,0:T(8,128)(2,1)S(1)} collective-permute-done((bf16[128,1024]{1,0:T(8,128)(2,1)S(1)}, bf16[128,1024]{1,0:T(8,128)(2,1)S(1)}, u32[]{:S(2)}, u32[]{:S(2)}) %collective-permute-start.103) | collective-permute-done | bytes 262176 | tf_op jit(solution)/shard_map/ppermute | solution.py:56
  733.3 6.1 collective-permute-start.105
  750.7 8.3 %collective-permute-done.106 = bf16[32,4096]{1,0:T(8,128)(2,1)S(1)} collective-permute-done((bf16[32,4096]{1,0:T(8,128)(2,1)S(1)}, bf16[32,4096]{1,0:T(8,128)(2,1)S(1)}, u32[]{:S(2)}, u32[]{:S(2)}) %collective-permute-start.106) | collective-permute-done | bytes 262176 | tf_op jit(solution)/shard_map/ppermute | solution.py:56
  763.0 11.6 %collective-permute-done.94 = bf16[32,128]{1,0:T(8,128)(2,1)S(1)} collective-permute-done((bf16[32,128]{1,0:T(8,128)(2,1)S(1)}, bf16[32,128]{1,0:T(8,128)(2,1)S(1)}, u32[]{:S(2)}, u32[]{:S(2)}) %collective-permute-start.94) | collective-permute-done | bytes 8224 | tf_op jit(solution)/shard_map/ppermute | solution.py:56
  774.8 6.1 collective-permute-start.95
  786.1 11.1 %collective-permute-done.98 = bf16[8,128]{1,0:T(8,128)(2,1)S(1)} collective-permute-done((bf16[8,128]{1,0:T(8,128)(2,1)S(1)}, bf16[8,128]{1,0:T(8,128)(2,1)S(1)}, u32[]{:S(2)}, u32[]{:S(2)}) %collective-permute-start.98) | collective-permute-done | bytes 2080 | tf_op jit(solution)/shard_map/ppermute | solution.py:56
  (650 shorter events, 298.3 us)
Async XLA Ops:
  5.1 24.0 %collective-permute-start.4 = (bf16[8,128]{1,0:T(8,128)(2,1)}, bf16[8,128]{1,0:T(8,128)(2,1)S(1)}, u32[]{:S(2)}, u32[]{:S(2)}) collective-permute-start(bf16[8,128]{1,0:T(8,128)(2,1)} %pad_bitcast_fusion), channel_id=1, source_target_pairs={{0,24},{1,25},{2,26},{3,27},{4,28},{5,29},{6,30},{7,31},{8,0},{9,1... | collective-permute-start | bytes 6152 | tf_op jit(solution)/shard_map/ppermute | solution.py:56
  71.7 43.2 %collective-permute-start.14 = (bf16[2,4,128,1024]{3,2,1,0:T(8,128)(2,1)S(1)}, bf16[2,4,128,1024]{3,2,1,0:T(8,128)(2,1)}, u32[]{:S(2)}, u32[]{:S(2)}) collective-permute-start(bf16[2,4,128,1024]{3,2,1,0:T(8,128)(2,1)S(1)} %pad_maximum_fusion.2.refs_0_), channel_id=1, source_target_pairs={{0,2},{1,5},{2,0},{3,7},{4,6},{5,1},{6,4},{7,3},{8,10},{9,13},{10,... | collective-permute-start | bytes 6291464 | tf_op jit(solution)/shard_map/ppermute | solution.py:56
  72.3 42.6 %collective-permute-start.15 = (bf16[2,4,128,1024]{3,2,1,0:T(8,128)(2,1)S(1)}, bf16[2,4,128,1024]{3,2,1,0:T(8,128)(2,1)}, u32[]{:S(2)}, u32[]{:S(2)}) collective-permute-start(bf16[2,4,128,1024]{3,2,1,0:T(8,128)(2,1)S(1)} %pad_maximum_fusion.2.refs_0_), channel_id=1, source_target_pairs={{0,1},{1,0},{2,3},{3,2},{4,5},{5,4},{6,7},{7,6},{8,9},{9,8},{10,11... | collective-permute-start | bytes 6291464 | tf_op jit(solution)/shard_map/ppermute | solution.py:56
  77.3 24.8 %collective-permute-start.11 = (bf16[128,1024]{1,0:T(8,128)(2,1)}, bf16[128,1024]{1,0:T(8,128)(2,1)S(1)}, u32[]{:S(2)}, u32[]{:S(2)}) collective-permute-start(bf16[128,1024]{1,0:T(8,128)(2,1)} %pad_maximum_fusion.17), channel_id=1, source_target_pairs={{0,24},{1,25},{2,26},{3,27},{4,28},{5,29},{6,30},{7,31},{8,0},{9,1... | collective-permute-start | bytes 786440 | tf_op jit(solution)/shard_map/ppermute | solution.py:56
  77.3 24.8 %collective-permute-start.12 = (bf16[128,1024]{1,0:T(8,128)(2,1)}, bf16[128,1024]{1,0:T(8,128)(2,1)}, u32[]{:S(2)}, u32[]{:S(2)}) collective-permute-start(bf16[128,1024]{1,0:T(8,128)(2,1)} %pad_maximum_fusion.17), channel_id=1, source_target_pairs={{0,16},{1,17},{2,18},{3,19},{4,20},{5,21},{6,22},{7,23},{8,24},{9,... | collective-permute-start | bytes 786440 | tf_op jit(solution)/shard_map/ppermute | solution.py:56
  133.3 33.8 %collective-permute-start.18 = (bf16[512,3072]{1,0:T(8,128)(2,1)S(1)}, bf16[512,3072]{1,0:T(8,128)(2,1)S(1)}, u32[]{:S(2)}, u32[]{:S(2)}) collective-permute-start(bf16[512,3072]{1,0:T(8,128)(2,1)S(1)} %add_convert_fusion.1.q_ref.km_ref.vm_ref), channel_id=1, source_target_pairs={{0,1},{1,0},{2,3},{3,2},{4,5},{5,4},{6,7},{7,6},{8,9},{9,8},{10,11... | collective-permute-start | bytes 9437192 | tf_op jit(solution)/shard_map/ppermute | solution.py:56
  148.5 41.3 %collective-permute-start.22 = (bf16[2,4,128,1024]{3,2,1,0:T(8,128)(2,1)S(1)}, bf16[2,4,128,1024]{3,2,1,0:T(8,128)(2,1)S(1)}, u32[]{:S(2)}, u32[]{:S(2)}) collective-permute-start(bf16[2,4,128,1024]{3,2,1,0:T(8,128)(2,1)S(1)} %pad_maximum_fusion.3.refs_0_), channel_id=1, source_target_pairs={{0,2},{1,5},{2,0},{3,7},{4,6},{5,1},{6,4},{7,3},{8,10},{9,13},{10,... | collective-permute-start | bytes 6291464 | tf_op jit(solution)/shard_map/ppermute | solution.py:56
  149.1 42.2 %collective-permute-start.23 = (bf16[2,4,128,1024]{3,2,1,0:T(8,128)(2,1)S(1)}, bf16[2,4,128,1024]{3,2,1,0:T(8,128)(2,1)S(1)}, u32[]{:S(2)}, u32[]{:S(2)}) collective-permute-start(bf16[2,4,128,1024]{3,2,1,0:T(8,128)(2,1)S(1)} %pad_maximum_fusion.3.refs_0_), channel_id=1, source_target_pairs={{0,1},{1,0},{2,3},{3,2},{4,5},{5,4},{6,7},{7,6},{8,9},{9,8},{10,11... | collective-permute-start | bytes 6291464 | tf_op jit(solution)/shard_map/ppermute | solution.py:56
  152.7 53.6 %collective-permute-start.25 = (bf16[128,1024]{1,0:T(8,128)(2,1)S(1)}, bf16[128,1024]{1,0:T(8,128)(2,1)S(1)}, u32[]{:S(2)}, u32[]{:S(2)}) collective-permute-start(bf16[128,1024]{1,0:T(8,128)(2,1)S(1)} %pad_maximum_fusion.18), channel_id=1, source_target_pairs={{0,24},{1,25},{2,26},{3,27},{4,28},{5,29},{6,30},{7,31},{8,0},{9,1... | collective-permute-start | bytes 786440 | tf_op jit(solution)/shard_map/ppermute | solution.py:56
  162.1 44.2 %collective-permute-start.26 = (bf16[128,1024]{1,0:T(8,128)(2,1)S(1)}, bf16[128,1024]{1,0:T(8,128)(2,1)S(1)}, u32[]{:S(2)}, u32[]{:S(2)}) collective-permute-start(bf16[128,1024]{1,0:T(8,128)(2,1)S(1)} %pad_maximum_fusion.18), channel_id=1, source_target_pairs={{0,16},{1,17},{2,18},{3,19},{4,20},{5,21},{6,22},{7,23},{8,24},{9,... | collective-permute-start | bytes 786440 | tf_op jit(solution)/shard_map/ppermute | solution.py:56
  167.1 24.1 %collective-permute-start.24 = (bf16[4,128,1024]{2,1,0:T(8,128)(2,1)S(1)}, bf16[4,128,1024]{2,1,0:T(8,128)(2,1)S(1)}, u32[]{:S(2)}, u32[]{:S(2)}) collective-permute-start(bf16[4,128,1024]{2,1,0:T(8,128)(2,1)S(1)} %bitcast.379), channel_id=1, source_target_pairs={{0,4},{1,3},{2,6},{3,1},{4,0},{5,7},{6,2},{7,5},{8,12},{9,11},{10,... | collective-permute-start | bytes 3145736 | tf_op jit(solution)/shard_map/ppermute | solution.py:56
  206.3 26.1 %collective-permute-start.29 = (bf16[2,4,128,1024]{3,2,1,0:T(8,128)(2,1)S(1)}, bf16[2,4,128,1024]{3,2,1,0:T(8,128)(2,1)S(1)}, u32[]{:S(2)}, u32[]{:S(2)}) collective-permute-start(bf16[2,4,128,1024]{3,2,1,0:T(8,128)(2,1)S(1)} %pad_maximum_fusion.4.refs_0_), channel_id=1, source_target_pairs={{0,2},{1,5},{2,0},{3,7},{4,6},{5,1},{6,4},{7,3},{8,10},{9,13},{10,... | collective-permute-start | bytes 6291464 | tf_op jit(solution)/shard_map/ppermute | solution.py:56
  207.6 24.8 %collective-permute-start.30 = (bf16[2,4,128,1024]{3,2,1,0:T(8,128)(2,1)S(1)}, bf16[2,4,128,1024]{3,2,1,0:T(8,128)(2,1)S(1)}, u32[]{:S(2)}, u32[]{:S(2)}) collective-permute-start(bf16[2,4,128,1024]{3,2,1,0:T(8,128)(2,1)S(1)} %pad_maximum_fusion.4.refs_0_), channel_id=1, source_target_pairs={{0,1},{1,0},{2,3},{3,2},{4,5},{5,4},{6,7},{7,6},{8,9},{9,8},{10,11... | collective-permute-start | bytes 6291464 | tf_op jit(solution)/shard_map/ppermute | solution.py:56
  233.9 29.3 %collective-permute-start.33 = (bf16[128,1024]{1,0:T(8,128)(2,1)}, bf16[128,1024]{1,0:T(8,128)(2,1)S(1)}, u32[]{:S(2)}, u32[]{:S(2)}) collective-permute-start(bf16[128,1024]{1,0:T(8,128)(2,1)} %pad_maximum_fusion.19), channel_id=1, source_target_pairs={{0,24},{1,25},{2,26},{3,27},{4,28},{5,29},{6,30},{7,31},{8,0},{9,1... | collective-permute-start | bytes 786440 | tf_op jit(solution)/shard_map/ppermute | solution.py:56
  236.3 26.9 %collective-permute-start.34 = (bf16[128,1024]{1,0:T(8,128)(2,1)}, bf16[128,1024]{1,0:T(8,128)(2,1)S(1)}, u32[]{:S(2)}, u32[]{:S(2)}) collective-permute-start(bf16[128,1024]{1,0:T(8,128)(2,1)} %pad_maximum_fusion.19), channel_id=1, source_target_pairs={{0,16},{1,17},{2,18},{3,19},{4,20},{5,21},{6,22},{7,23},{8,24},{9,... | collective-permute-start | bytes 786440 | tf_op jit(solution)/shard_map/ppermute | solution.py:56
  236.3 26.9 %collective-permute-start.35 = (bf16[128,1024]{1,0:T(8,128)(2,1)}, bf16[128,1024]{1,0:T(8,128)(2,1)S(1)}, u32[]{:S(2)}, u32[]{:S(2)}) collective-permute-start(bf16[128,1024]{1,0:T(8,128)(2,1)} %pad_maximum_fusion.19), channel_id=1, source_target_pairs={{0,8},{1,9},{2,10},{3,11},{4,12},{5,13},{6,14},{7,15},{8,16},{9,17... | collective-permute-start | bytes 786440 | tf_op jit(solution)/shard_map/ppermute | solution.py:56
  247.4 26.1 %collective-permute-start.36 = (bf16[2,4,128,1024]{3,2,1,0:T(8,128)(2,1)S(1)}, bf16[2,4,128,1024]{3,2,1,0:T(8,128)(2,1)S(1)}, u32[]{:S(2)}, u32[]{:S(2)}) collective-permute-start(bf16[2,4,128,1024]{3,2,1,0:T(8,128)(2,1)S(1)} %pad_maximum_fusion.5.refs_0_), channel_id=1, source_target_pairs={{0,2},{1,5},{2,0},{3,7},{4,6},{5,1},{6,4},{7,3},{8,10},{9,13},{10,... | collective-permute-start | bytes 6291464 | tf_op jit(solution)/shard_map/ppermute | solution.py:56
  248.7 24.8 %collective-permute-start.37 = (bf16[2,4,128,1024]{3,2,1,0:T(8,128)(2,1)S(1)}, bf16[2,4,128,1024]{3,2,1,0:T(8,128)(2,1)S(1)}, u32[]{:S(2)}, u32[]{:S(2)}) collective-permute-start(bf16[2,4,128,1024]{3,2,1,0:T(8,128)(2,1)S(1)} %pad_maximum_fusion.5.refs_0_), channel_id=1, source_target_pairs={{0,1},{1,0},{2,3},{3,2},{4,5},{5,4},{6,7},{7,6},{8,9},{9,8},{10,11... | collective-permute-start | bytes 6291464 | tf_op jit(solution)/shard_map/ppermute | solution.py:56
  290.7 41.6 %collective-permute-start.40 = (bf16[512,3072]{1,0:T(8,128)(2,1)S(1)}, bf16[512,3072]{1,0:T(8,128)(2,1)S(1)}, u32[]{:S(2)}, u32[]{:S(2)}) collective-permute-start(bf16[512,3072]{1,0:T(8,128)(2,1)S(1)} %add_convert_fusion.q_ref.km_ref.vm_ref), channel_id=1, source_target_pairs={{0,1},{1,0},{2,3},{3,2},{4,5},{5,4},{6,7},{7,6},{8,9},{9,8},{10,11... | collective-permute-start | bytes 9437192 | tf_op jit(solution)/shard_map/ppermute | solution.py:56
  305.9 50.8 %collective-permute-start.44 = (bf16[2,4,128,1024]{3,2,1,0:T(8,128)(2,1)S(1)}, bf16[2,4,128,1024]{3,2,1,0:T(8,128)(2,1)S(1)}, u32[]{:S(2)}, u32[]{:S(2)}) collective-permute-start(bf16[2,4,128,1024]{3,2,1,0:T(8,128)(2,1)S(1)} %pad_maximum_fusion.6.refs_0_), channel_id=1, source_target_pairs={{0,2},{1,5},{2,0},{3,7},{4,6},{5,1},{6,4},{7,3},{8,10},{9,13},{10,... | collective-permute-start | bytes 6291464 | tf_op jit(solution)/shard_map/ppermute | solution.py:56
  307.2 49.5 %collective-permute-start.45 = (bf16[2,4,128,1024]{3,2,1,0:T(8,128)(2,1)S(1)}, bf16[2,4,128,1024]{3,2,1,0:T(8,128)(2,1)S(1)}, u32[]{:S(2)}, u32[]{:S(2)}) collective-permute-start(bf16[2,4,128,1024]{3,2,1,0:T(8,128)(2,1)S(1)} %pad_maximum_fusion.6.refs_0_), channel_id=1, source_target_pairs={{0,1},{1,0},{2,3},{3,2},{4,5},{5,4},{6,7},{7,6},{8,9},{9,8},{10,11... | collective-permute-start | bytes 6291464 | tf_op jit(solution)/shard_map/ppermute | solution.py:56
  358.6 28.6 %collective-permute-start.48 = (bf16[2,4,128,1024]{3,2,1,0:T(8,128)(2,1)S(1)}, bf16[2,4,128,1024]{3,2,1,0:T(8,128)(2,1)S(1)}, u32[]{:S(2)}, u32[]{:S(2)}) collective-permute-start(bf16[2,4,128,1024]{3,2,1,0:T(8,128)(2,1)S(1)} %pad_maximum_fusion.7.refs_0_), channel_id=1, source_target_pairs={{0,2},{1,5},{2,0},{3,7},{4,6},{5,1},{6,4},{7,3},{8,10},{9,13},{10,... | collective-permute-start | bytes 6291464 | tf_op jit(solution)/shard_map/ppermute | solution.py:56
  359.6 27.7 %collective-permute-start.49 = (bf16[2,4,128,1024]{3,2,1,0:T(8,128)(2,1)S(1)}, bf16[2,4,128,1024]{3,2,1,0:T(8,128)(2,1)S(1)}, u32[]{:S(2)}, u32[]{:S(2)}) collective-permute-start(bf16[2,4,128,1024]{3,2,1,0:T(8,128)(2,1)S(1)} %pad_maximum_fusion.7.refs_0_), channel_id=1, source_target_pairs={{0,1},{1,0},{2,3},{3,2},{4,5},{5,4},{6,7},{7,6},{8,9},{9,8},{10,11... | collective-permute-start | bytes 6291464 | tf_op jit(solution)/shard_map/ppermute | solution.py:56
  389.1 34.1 %collective-permute-start.52 = (bf16[512,4096]{1,0:T(8,128)(2,1)}, bf16[512,4096]{1,0:T(8,128)(2,1)}, u32[]{:S(2)}, u32[]{:S(2)}) collective-permute-start(bf16[512,4096]{1,0:T(8,128)(2,1)} %get-tuple-element.499.a1), channel_id=1, source_target_pairs={{0,1},{1,0},{2,3},{3,2},{4,5},{5,4},{6,7},{7,6},{8,9},{9,8},{10,11... | collective-permute-start | bytes 12582920 | tf_op jit(solution)/shard_map/ppermute | solution.py:56
  419.3 31.1 %collective-permute-start.55 = (bf16[512,4096]{1,0:T(8,128)(2,1)}, bf16[512,4096]{1,0:T(8,128)(2,1)}, u32[]{:S(2)}, u32[]{:S(2)}) collective-permute-start(bf16[512,4096]{1,0:T(8,128)(2,1)} %multiply_convert_fusion.1.refs_2_), channel_id=1, source_target_pairs={{0,1},{1,0},{2,3},{3,2},{4,5},{5,4},{6,7},{7,6},{8,9},{9,8},{10,11... | collective-permute-start | bytes 12582920 | tf_op jit(solution)/shard_map/ppermute | solution.py:56
  419.8 30.6 %collective-permute-start.54 = (bf16[512,512]{1,0:T(8,128)(2,1)}, bf16[512,512]{1,0:T(8,128)(2,1)S(1)}, u32[]{:S(2)}, u32[]{:S(2)}) collective-permute-start(bf16[512,512]{1,0:T(8,128)(2,1)} %convolution_convert_fusion.2), channel_id=1, source_target_pairs={{0,1},{1,0},{2,3},{3,2},{4,5},{5,4},{6,7},{7,6},{8,9},{9,8},{10,11... | collective-permute-start | bytes 1572872 | tf_op jit(solution)/shard_map/ppermute | solution.py:56
  422.0 37.2 %collective-permute-start.56 = (bf16[256,1024]{1,0:T(8,128)(2,1)}, bf16[256,1024]{1,0:T(8,128)(2,1)}, u32[]{:S(2)}, u32[]{:S(2)}) collective-permute-start(bf16[256,1024]{1,0:T(8,128)(2,1)} %slice.940), channel_id=1, source_target_pairs={{0,2},{1,3},{2,0},{3,1},{4,6},{5,7},{6,4},{7,5},{8,10},{9,11},{10,... | collective-permute-start | bytes 1572872 | tf_op jit(solution)/shard_map/ppermute | solution.py:56
  449.4 35.5 %collective-permute-start.57 = (bf16[1024,1024]{1,0:T(8,128)(2,1)S(1)}, bf16[1024,1024]{1,0:T(8,128)(2,1)}, u32[]{:S(2)}, u32[]{:S(2)}) collective-permute-start(bf16[1024,1024]{1,0:T(8,128)(2,1)S(1)} %get-tuple-element.521), channel_id=1, source_target_pairs={{0,2},{1,5},{2,0},{3,7},{4,6},{5,1},{6,4},{7,3},{8,10},{9,13},{10,... | collective-permute-start | bytes 6291464 | tf_op jit(solution)/shard_map/ppermute | solution.py:56
  483.7 26.1 %collective-permute-start.59 = (bf16[256,4096]{1,0:T(8,128)(2,1)S(1)}, bf16[256,4096]{1,0:T(8,128)(2,1)S(1)}, u32[]{:S(2)}, u32[]{:S(2)}) collective-permute-start(bf16[256,4096]{1,0:T(8,128)(2,1)S(1)} %get-tuple-element.527), channel_id=1, source_target_pairs={{0,2},{1,5},{2,0},{3,7},{4,6},{5,1},{6,4},{7,3},{8,10},{9,13},{10,... | collective-permute-start | bytes 6291464 | tf_op jit(solution)/shard_map/ppermute | solution.py:56
  490.2 27.3 %collective-permute-start.61 = (bf16[512,3072]{1,0:T(8,128)(2,1)S(1)}, bf16[512,3072]{1,0:T(8,128)(2,1)}, u32[]{:S(2)}, u32[]{:S(2)}) collective-permute-start(bf16[512,3072]{1,0:T(8,128)(2,1)S(1)} %pad_maximum_fusion.refs_2_), channel_id=1, source_target_pairs={{0,1},{1,0},{2,3},{3,2},{4,5},{5,4},{6,7},{7,6},{8,9},{9,8},{10,11... | collective-permute-start | bytes 9437192 | tf_op jit(solution)/shard_map/ppermute | solution.py:56
  490.4 53.1 %collective-permute-start.65 = (bf16[512,4096]{1,0:T(8,128)(2,1)}, bf16[512,4096]{1,0:T(8,128)(2,1)}, u32[]{:S(2)}, u32[]{:S(2)}) collective-permute-start(bf16[512,4096]{1,0:T(8,128)(2,1)} %get-tuple-element.439.a1), channel_id=1, source_target_pairs={{0,1},{1,0},{2,3},{3,2},{4,5},{5,4},{6,7},{7,6},{8,9},{9,8},{10,11... | collective-permute-start | bytes 12582920 | tf_op jit(solution)/shard_map/ppermute | solution.py:56
  490.9 25.6 %collective-permute-start.62 = (bf16[512,512]{1,0:T(8,128)(2,1)S(1)}, bf16[512,512]{1,0:T(8,128)(2,1)S(1)}, u32[]{:S(2)}, u32[]{:S(2)}) collective-permute-start(bf16[512,512]{1,0:T(8,128)(2,1)S(1)} %copy-done.120), channel_id=1, source_target_pairs={{0,1},{1,0},{2,3},{3,2},{4,5},{5,4},{6,7},{7,6},{8,9},{9,8},{10,11... | collective-permute-start | bytes 1572872 | tf_op jit(solution)/shard_map/ppermute | solution.py:56
  516.5 46.7 %collective-permute-start.67 = (bf16[128,4096]{1,0:T(8,128)(2,1)}, bf16[128,4096]{1,0:T(8,128)(2,1)}, u32[]{:S(2)}, u32[]{:S(2)}) collective-permute-start(bf16[128,4096]{1,0:T(8,128)(2,1)} %get-tuple-element.550), channel_id=1, source_target_pairs={{0,4},{1,3},{2,6},{3,1},{4,0},{5,7},{6,2},{7,5},{8,12},{9,11},{10,... | collective-permute-start | bytes 3145736 | tf_op jit(solution)/shard_map/ppermute | solution.py:56
  541.4 43.8 %collective-permute-start.72 = (bf16[512,4096]{1,0:T(8,128)(2,1)}, bf16[512,4096]{1,0:T(8,128)(2,1)}, u32[]{:S(2)}, u32[]{:S(2)}) collective-permute-start(bf16[512,4096]{1,0:T(8,128)(2,1)} %multiply_convert_fusion.refs_2_), channel_id=1, source_target_pairs={{0,1},{1,0},{2,3},{3,2},{4,5},{5,4},{6,7},{7,6},{8,9},{9,8},{10,11... | collective-permute-start | bytes 12582920 | tf_op jit(solution)/shard_map/ppermute | solution.py:56
  563.2 120.4 %collective-permute-start.81 = (bf16[512,512]{1,0:T(8,128)(2,1)}, bf16[512,512]{1,0:T(8,128)(2,1)S(1)}, u32[]{:S(2)}, u32[]{:S(2)}) collective-permute-start(bf16[512,512]{1,0:T(8,128)(2,1)} %convolution_convert_fusion.12), channel_id=1, source_target_pairs={{0,1},{1,0},{2,3},{3,2},{4,5},{5,4},{6,7},{7,6},{8,9},{9,8},{10,11... | collective-permute-start | bytes 1572872 | tf_op jit(solution)/shard_map/ppermute | solution.py:56
  564.1 38.2 %collective-permute-start.73 = (bf16[256,4096]{1,0:T(8,128)(2,1)}, bf16[256,4096]{1,0:T(8,128)(2,1)}, u32[]{:S(2)}, u32[]{:S(2)}) collective-permute-start(bf16[256,4096]{1,0:T(8,128)(2,1)} %get-tuple-element.567), channel_id=1, source_target_pairs={{0,2},{1,5},{2,0},{3,7},{4,6},{5,1},{6,4},{7,3},{8,10},{9,13},{10,... | collective-permute-start | bytes 6291464 | tf_op jit(solution)/shard_map/ppermute | solution.py:56
  593.9 93.0 %collective-permute-start.83 = (bf16[512,512]{1,0:T(8,128)(2,1)}, bf16[512,512]{1,0:T(8,128)(2,1)}, u32[]{:S(2)}, u32[]{:S(2)}) collective-permute-start(bf16[512,512]{1,0:T(8,128)(2,1)} %convolution_convert_fusion.10), channel_id=1, source_target_pairs={{0,1},{1,0},{2,3},{3,2},{4,5},{5,4},{6,7},{7,6},{8,9},{9,8},{10,11... | collective-permute-start | bytes 1572872 | tf_op jit(solution)/shard_map/ppermute | solution.py:56
  601.3 37.3 %collective-permute-start.77 = (bf16[1024,1024]{1,0:T(8,128)(2,1)S(1)}, bf16[1024,1024]{1,0:T(8,128)(2,1)S(1)}, u32[]{:S(2)}, u32[]{:S(2)}) collective-permute-start(bf16[1024,1024]{1,0:T(8,128)(2,1)S(1)} %get-tuple-element.577), channel_id=1, source_target_pairs={{0,2},{1,5},{2,0},{3,7},{4,6},{5,1},{6,4},{7,3},{8,10},{9,13},{10,... | collective-permute-start | bytes 6291464 | tf_op jit(solution)/shard_map/ppermute | solution.py:56
  605.6 36.4 %collective-permute-start.78 = (bf16[128,4096]{1,0:T(8,128)(2,1)}, bf16[128,4096]{1,0:T(8,128)(2,1)}, u32[]{:S(2)}, u32[]{:S(2)}) collective-permute-start(bf16[128,4096]{1,0:T(8,128)(2,1)} %get-tuple-element.582), channel_id=1, source_target_pairs={{0,4},{1,3},{2,6},{3,1},{4,0},{5,7},{6,2},{7,5},{8,12},{9,11},{10,... | collective-permute-start | bytes 3145736 | tf_op jit(solution)/shard_map/ppermute | solution.py:56
  638.6 26.0 %collective-permute-start.80 = (bf16[256,4096]{1,0:T(8,128)(2,1)S(1)}, bf16[256,4096]{1,0:T(8,128)(2,1)S(1)}, u32[]{:S(2)}, u32[]{:S(2)}) collective-permute-start(bf16[256,4096]{1,0:T(8,128)(2,1)S(1)} %get-tuple-element.587), channel_id=1, source_target_pairs={{0,2},{1,5},{2,0},{3,7},{4,6},{5,1},{6,4},{7,3},{8,10},{9,13},{10,... | collective-permute-start | bytes 6291464 | tf_op jit(solution)/shard_map/ppermute | solution.py:56
  642.0 48.4 %collective-permute-start.84 = (bf16[512,1024]{1,0:T(8,128)(2,1)S(1)}, bf16[512,1024]{1,0:T(8,128)(2,1)S(1)}, u32[]{:S(2)}, u32[]{:S(2)}) collective-permute-start(bf16[512,1024]{1,0:T(8,128)(2,1)S(1)} %get-tuple-element.566.refs_6_), channel_id=1, source_target_pairs={{0,1},{1,0},{2,3},{3,2},{4,5},{5,4},{6,7},{7,6},{8,9},{9,8},{10,11... | collective-permute-start | bytes 3145736 | tf_op jit(solution)/shard_map/ppermute | solution.py:56
  647.3 43.2 %collective-permute-start.82 = (bf16[512,3072]{1,0:T(8,128)(2,1)}, bf16[512,3072]{1,0:T(8,128)(2,1)}, u32[]{:S(2)}, u32[]{:S(2)}) collective-permute-start(bf16[512,3072]{1,0:T(8,128)(2,1)} %pad_maximum_fusion.1.refs_2_), channel_id=1, source_target_pairs={{0,1},{1,0},{2,3},{3,2},{4,5},{5,4},{6,7},{7,6},{8,9},{9,8},{10,11... | collective-permute-start | bytes 9437192 | tf_op jit(solution)/shard_map/ppermute | solution.py:56
  672.8 35.0 %collective-permute-start.88 = (bf16[512,1024]{1,0:T(8,128)(2,1)}, bf16[512,1024]{1,0:T(8,128)(2,1)}, u32[]{:S(2)}, u32[]{:S(2)}) collective-permute-start(bf16[512,1024]{1,0:T(8,128)(2,1)} %get-tuple-element.604), channel_id=1, source_target_pairs={{0,4},{1,3},{2,6},{3,1},{4,0},{5,7},{6,2},{7,5},{8,12},{9,11},{10,... | collective-permute-start | bytes 3145736 | tf_op jit(solution)/shard_map/ppermute | solution.py:56
  690.4 29.6 %collective-permute-start.101 = (bf16[128,4096]{1,0:T(8,128)(2,1)}, bf16[128,4096]{1,0:T(8,128)(2,1)S(1)}, u32[]{:S(2)}, u32[]{:S(2)}) collective-permute-start(bf16[128,4096]{1,0:T(8,128)(2,1)} %get-tuple-element.631), channel_id=1, source_target_pairs={{0,4},{1,3},{2,6},{3,1},{4,0},{5,7},{6,2},{7,5},{8,12},{9,11},{10,... | collective-permute-start | bytes 3145736 | tf_op jit(solution)/shard_map/ppermute | solution.py:56
  709.3 49.6 %collective-permute-start.90 = (bf16[256,4096]{1,0:T(8,128)(2,1)}, bf16[256,4096]{1,0:T(8,128)(2,1)S(1)}, u32[]{:S(2)}, u32[]{:S(2)}) collective-permute-start(bf16[256,4096]{1,0:T(8,128)(2,1)} %get-tuple-element.609), channel_id=1, source_target_pairs={{0,2},{1,5},{2,0},{3,7},{4,6},{5,1},{6,4},{7,3},{8,10},{9,13},{10,... | collective-permute-start | bytes 6291464 | tf_op jit(solution)/shard_map/ppermute | solution.py:56
  720.0 38.9 %collective-permute-start.92 = (bf16[64,128]{1,0:T(8,128)(2,1)S(1)}, bf16[64,128]{1,0:T(8,128)(2,1)S(1)}, u32[]{:S(2)}, u32[]{:S(2)}) collective-permute-start(bf16[64,128]{1,0:T(8,128)(2,1)S(1)} %slice.736), channel_id=1, source_target_pairs={{0,2},{1,5},{2,0},{3,7},{4,6},{5,1},{6,4},{7,3},{8,10},{9,13},{10,... | collective-permute-start | bytes 49160 | tf_op jit(solution)/shard_map/ppermute | solution.py:56
  749.5 33.9 %collective-permute-start.89 = (bf16[256,1024]{1,0:T(8,128)(2,1)S(1)}, bf16[256,1024]{1,0:T(8,128)(2,1)S(1)}, u32[]{:S(2)}, u32[]{:S(2)}) collective-permute-start(bf16[256,1024]{1,0:T(8,128)(2,1)S(1)} %slice.939), channel_id=1, source_target_pairs={{0,2},{1,3},{2,0},{3,1},{4,6},{5,7},{6,4},{7,5},{8,10},{9,11},{10,... | collective-permute-start | bytes 1572872 | tf_op jit(solution)/shard_map/ppermute | solution.py:56
  774.8 30.1 %collective-permute-start.95 = (bf16[32,4096]{1,0:T(8,128)(2,1)S(1)}, bf16[32,4096]{1,0:T(8,128)(2,1)S(1)}, u32[]{:S(2)}, u32[]{:S(2)}) collective-permute-start(bf16[32,4096]{1,0:T(8,128)(2,1)S(1)} %get-tuple-element.616), channel_id=1, source_target_pairs={{0,8},{1,9},{2,10},{3,11},{4,12},{5,13},{6,14},{7,15},{8,16},{9,17... | collective-permute-start | bytes 786440 | tf_op jit(solution)/shard_map/ppermute | solution.py:56
  (184 other events, 2190.2 us)

commit v3 on v2

--- a/solution.py
+++ b/solution.py
@@ -1,3 +1,4 @@
+import collections
 import math
 
 import jax
@@ -31,6 +32,9 @@
     return lax.dot_general(left, right, (((1,), (1,)), ((), ())), preferred_element_type=f32)
 
 
+SMALL_COST = pl.CostEstimate(flops=1024, bytes_accessed=1024, transcendentals=0)
+
+
 def tie(value, *others):
     return lax.optimization_barrier((value, others))[0]
 
@@ -49,7 +53,8 @@
 TO_Y = pairs(lambda z, y, x, c: (z, 1 - y, x, c))
 TO_FAR = pairs(lambda z, y, x, c: (z, y if c == 0 else 1 - y, 1 - x if c == 0 else x, c))
 TO_NEAR = pairs(lambda z, y, x, c: (z, 1 - y if c == 0 else y, x if c == 0 else 1 - x, c))
-TO_Z = [pairs(lambda z, y, x, c, k=k: ((z + k) % 4, y, x, c)) for k in range(4)]
+TO_ODD = pairs(lambda z, y, x, c: (z ^ 1, y, x, c))
+TO_PAIR = pairs(lambda z, y, x, c: (z ^ 2, y, x, c))
 
 
 def send(value, to):
@@ -88,7 +93,6 @@
         for _, store in stores:
             store.wait()
 
-    size = sum(math.prod(shape) for shape in shapes) * 4
     return pl.pallas_call(
         kernel,
         in_specs=[pl.BlockSpec(memory_space=pltpu.SMEM)]
@@ -98,7 +102,7 @@
         scratch_shapes=[pltpu.VMEM(p.shape, bf16) for p in pieces]
         + [pltpu.SemaphoreType.DMA((total,)), pltpu.SemaphoreType.DMA((count,))],
         compiler_params=pltpu.CompilerParams(vmem_limit_bytes=40 << 20),
-        cost_estimate=pl.CostEstimate(flops=0, bytes_accessed=size, transcendentals=0),
+        cost_estimate=SMALL_COST,
     )(coords, *pieces)
 
 
@@ -110,8 +114,12 @@
     return jnp.where(at == 0, jnp.stack([own, other], axis), jnp.stack([other, own], axis))
 
 
-def phase(values, *units):
-    values, flights = lax.optimization_barrier((values, [u.flight for u in units]))
+def phase(values, *units, settle=()):
+    values, flights, ended = lax.optimization_barrier(
+        (values, [u.flight for u in units], [u.flight for u in settle])
+    )
+    for unit, flight in zip(settle, ended):
+        unit.flight = flight
     nexts = [u.local(flight) for u, flight in zip(units, flights)]
     values, sends = lax.optimization_barrier((values, [[v for v, _ in n] for n in nexts]))
     for unit, arrays, targets in zip(units, sends, nexts):
@@ -122,21 +130,18 @@
 class GatherUnit:
     def __init__(self, coords, pack, shapes, parts):
         self.coords, self.pack, self.shapes, self.parts = coords, pack, shapes, parts
-        self.flight, self.step = [], 0
+        self.flight, self.step = [pack], 0
 
     def local(self, got):
-        rows, width = self.pack.shape
         self.step += 1
         if self.step == 1:
-            return [(self.pack, TO_Z[4 - k]) for k in (1, 2, 3)]
-        if self.step == 2:
-            self.kept = jnp.concatenate([self.pack] + got).reshape(4, rows, width)
-            return [(self.kept, TO_NEAR)]
-        if self.step == 3:
-            self.kept = jnp.stack([self.kept, got[0]])
-            return [(self.kept, TO_FAR), (self.kept, TO_CORE)]
-        self.kept = [self.kept, got[0], got[1]]
-        return [(got[0], TO_CORE)]
+            self.kept = got[0][None]
+            return [(self.kept, TO_PAIR)]
+        if self.step < 5:
+            self.kept = jnp.concatenate([got[0], self.kept])
+            return [(self.kept, (TO_ODD, TO_NEAR, TO_FAR)[self.step - 2])]
+        self.kept = [self.kept, got[0]]
+        return [(blocks, TO_CORE) for blocks in self.kept]
 
     def result(self):
         width = self.pack.shape[1]
@@ -144,18 +149,19 @@
         def by_block(z, y, x, c, src, dst):
             out = []
             for n in range(4):
-                core = c if n < 2 else 1 - c
-                for near in range(2):
-                    far = n % 2
+                core, far = (c if n < 2 else 1 - c), n % 2
+                for near in (1, 0):
                     y2 = y ^ jnp.where(core == 0, near, far)
                     x2 = x ^ jnp.where(core == 0, far, near)
-                    for k in range(4):
-                        for lo, hi, target, column in self.parts:
-                            view = None
-                            if dst:
-                                spans = (slice(0, hi - lo), slice(column * width, (column + 1) * width))
-                                view = dst[target].at[((z + k) % 4, y2, x2, core) + spans]
-                            out.append((n, src and src[n].at[near, k, lo:hi], view))
+                    for odd in (1, 0):
+                        for pair in (1, 0):
+                            block = 4 * (1 - near) + 2 * (1 - odd) + 1 - pair
+                            for lo, hi, target, column in self.parts:
+                                view = None
+                                if dst:
+                                    spans = (slice(0, hi - lo), slice(column * width, (column + 1) * width))
+                                    view = dst[target].at[(z ^ odd ^ (2 * pair), y2, x2, core) + spans]
+                                out.append((n, src and src[n].at[block, lo:hi], view))
             return out
 
         return place(
@@ -165,28 +171,26 @@
 
 class SumUnit:
     def __init__(self, parts):
-        self.parts = parts
-        self.flight, self.step = [], 0
+        self.flight, self.step = list(parts), 0
 
     def local(self, got):
         self.step += 1
         if self.step == 1:
-            leaving, self.kept = self.parts
-            return [(leaving, TO_FAR)]
-        if self.step == 2:
+            leaving, self.kept = got
+        elif self.step < 5:
             half = self.kept.shape[0] // 2
-            add = lambda a, b: (a.astype(f32) + b.astype(f32)).astype(bf16)
-            leaving = add(self.kept[:half], got[0][:half])
+            add = lambda a, b: a.astype(f32) + b.astype(f32)
+            leaving = add(self.kept[:half], got[0][:half]).astype(bf16)
             self.kept = add(self.kept[half:], got[0][half:])
-            return [(leaving, TO_NEAR)]
-        if self.step == 3:
-            kept, rows = self.kept, self.kept.shape[0] // 4
-            cut = lambda array, k: array[k * rows : (k + 1) * rows].astype(f32)
-            add = lambda k: cut(kept, k) + cut(got[0], k)
-            self.kept = add(3)
-            return [(add(k - 1).astype(bf16), TO_Z[k]) for k in (1, 2, 3)]
-        self.kept = self.kept + (got[0].astype(f32) + got[1].astype(f32) + got[2].astype(f32))
-        return []
+            if self.step < 4:
+                self.kept = self.kept.astype(bf16)
+        else:
+            self.kept = self.kept + got[0].astype(f32)
+            return []
+        return [(leaving, (TO_FAR, TO_NEAR, TO_ODD, TO_PAIR)[self.step - 1])]
+
+
+Sums = collections.namedtuple("Sums", "o i a")
 
 
 def block_order(coords):
@@ -195,32 +199,44 @@
     for core in (c, 1 - c):
         for far in (1, 0):
             for near in (1, 0):
-                for k in (1, 2, 3, 0):
-                    y2 = y ^ jnp.where(core == 0, near, far)
-                    x2 = x ^ jnp.where(core == 0, far, near)
-                    order.append((z + k) % 4 * 8 + y2 * 4 + x2 * 2 + core)
+                y2 = y ^ jnp.where(core == 0, near, far)
+                x2 = x ^ jnp.where(core == 0, far, near)
+                for odd in (1, 0):
+                    for pair in (1, 0):
+                        order.append((z ^ odd ^ (2 * pair)) * 8 + y2 * 4 + x2 * 2 + core)
     return jnp.stack(order).astype(jnp.int32)
 
 
 def order_matrices(order):
     block = D // 32
-    wanted = (order[:, None] * block + lax.iota(jnp.int32, block)[None, :]).reshape(2, 1, D // 2)
-    rows = lax.broadcasted_iota(jnp.int32, (2, D, D // 2), 1)
-    chosen = (rows == wanted).astype(bf16)
+    wanted = (order[:, None] * block + lax.iota(jnp.int32, block)[None, :]).reshape(2, D // 2, 1)
+    columns = lax.broadcasted_iota(jnp.int32, (2, D // 2, D), 2)
+    chosen = (columns == wanted).astype(bf16)
     return chosen[0], chosen[1]
 
 
-def selected(matrices, rows):
-    return [
-        lax.dot_general(m, rows, (((0,), (1,)), ((), ())), preferred_element_type=f32).astype(bf16)
-        for m in matrices
-    ]
-
-
-def weight_terms(*pairs_of):
+def selected(matrices, *arrays):
+    count = len(arrays)
+
+    def kernel(mine, theirs, *refs):
+        for n in range(count):
+            rows = refs[n][...]
+            refs[count + 2 * n][...] = nt_dot(mine[...], rows).astype(bf16)
+            refs[count + 2 * n + 1][...] = nt_dot(theirs[...], rows).astype(bf16)
+
+    out = jax.ShapeDtypeStruct((D // 2, arrays[0].shape[0]), bf16)
+    outs = pl.pallas_call(
+        kernel,
+        out_shape=[out] * (2 * count),
+        compiler_params=pltpu.CompilerParams(vmem_limit_bytes=48 << 20),
+        cost_estimate=SMALL_COST,
+    )(*matrices, *arrays)
+    return [tuple(outs[2 * n : 2 * n + 2]) for n in range(count)]
+
+
+def weight_terms(*pairs_of, first=0, tile=1024):
     rows, tokens = pairs_of[0][0][0].shape
-    tile = (1 << 19) // rows
-    counts = [pair[1][0].shape[1] // tile for pair in pairs_of]
+    counts = [pair[2] // tile for pair in pairs_of]
     starts = [sum(counts[:n]) for n in range(len(counts))]
     columns, half = sum(counts) * tile, rows // 2
 
@@ -237,9 +253,9 @@
                 kept[...] = total[half:].astype(bf16)
 
     in_specs, args = [], []
-    for (left, right), start, count in zip(pairs_of, starts, counts):
+    for (left, right, _), start, count in zip(pairs_of, starts, counts):
         whole = pl.BlockSpec((rows, tokens), lambda j: (0, 0))
-        cut = pl.BlockSpec((tokens, tile), lambda j, s=start, n=count: (0, jnp.clip(j - s, 0, n - 1)))
+        cut = pl.BlockSpec((tokens, tile), lambda j, s=start, n=count: (0, jnp.clip(j - s, 0, n - 1) + first // tile))
         in_specs += [whole, whole, cut, cut]
         args += [*left, *right]
     out = jax.ShapeDtypeStruct((half, columns), bf16)
@@ -250,53 +266,50 @@
         out_specs=[pl.BlockSpec((half, tile), lambda j: (0, j))] * 2,
         out_shape=[out, out],
         compiler_params=pltpu.CompilerParams(vmem_limit_bytes=48 << 20),
-        cost_estimate=pl.CostEstimate(
-            flops=4 * rows * tokens * columns,
-            bytes_accessed=4 * rows * tokens + 4 * tokens * columns + 2 * rows * columns,
-            transcendentals=0,
-        ),
+        cost_estimate=SMALL_COST,
     )(*args)
 
 
 def wide_terms_of(order, left, right):
     tokens, width = left[0].shape
     block = width // 32
-
-    def kernel(order_ref, a1, a2, b1, b2, leaving, kept):
-        rows_dot = lambda a, b: lax.dot_general(
-            a[...], b[...], (((0,), (0,)), ((), ())), preferred_element_type=f32
-        )
-        total = (rows_dot(a1, b1) + rows_dot(a2, b2)).astype(bf16)
-
-        @pl.when(pl.program_id(0) < 8)
+    columns = right[0].shape[1]
+
+    def kernel(order_ref, *refs):
+        a1, a2, (b1, b2, leaving, kept) = refs[:2], refs[2:4], refs[4:]
+        one = (
+            lax.broadcasted_iota(jnp.int32, (block, block), 0) == lax.broadcasted_iota(jnp.int32, (block, block), 1)
+        ).astype(bf16)
+        turned = lambda refs: jnp.concatenate([nt_dot(one, r[...]).astype(bf16) for r in refs], axis=0)
+        total = jnp.dot(turned(a1), b1[...], preferred_element_type=f32)
+        total = (total + jnp.dot(turned(a2), b2[...], preferred_element_type=f32)).astype(bf16)
+
+        @pl.when(pl.program_id(0) < 4)
         def _():
             leaving[...] = total
 
-        @pl.when(pl.program_id(0) >= 8)
+        @pl.when(pl.program_id(0) >= 4)
         def _():
             kept[...] = total
 
-    columns = right[0].shape[1]
-    cut = pl.BlockSpec((tokens, block), lambda j, order: (0, order[j]))
+    cut = lambda n: pl.BlockSpec((tokens, block), lambda j, order: (0, order[2 * j + n]))
     whole = pl.BlockSpec((tokens, columns), lambda j, order: (0, 0))
     out = jax.ShapeDtypeStruct((width // 4, columns), bf16)
     return pl.pallas_call(
         kernel,
         grid_spec=pltpu.PrefetchScalarGridSpec(
             num_scalar_prefetch=1,
-            grid=(16,),
-            in_specs=[cut, cut, whole, whole],
+            grid=(8,),
+            in_specs=[cut(0), cut(1), cut(0), cut(1), whole, whole],
             out_specs=[
-                pl.BlockSpec((block, columns), lambda j, order: (jnp.minimum(j, 7), 0)),
-                pl.BlockSpec((block, columns), lambda j, order: (jnp.maximum(j - 8, 0), 0)),
+                pl.BlockSpec((2 * block, columns), lambda j, order: (jnp.minimum(j, 3), 0)),
+                pl.BlockSpec((2 * block, columns), lambda j, order: (jnp.maximum(j - 4, 0), 0)),
             ],
         ),
         out_shape=[out, out],
         compiler_params=pltpu.CompilerParams(vmem_limit_bytes=48 << 20),
-        cost_estimate=pl.CostEstimate(
-            flops=2 * tokens * width * columns, bytes_accessed=3 * tokens * width, transcendentals=0
-        ),
-    )(order, *left, *right)
+        cost_estimate=SMALL_COST,
+    )(order, left[0], left[0], left[1], left[1], *right)
 
 
 BLOCK = 256
@@ -330,26 +343,30 @@
     s = s_ref[0]
     in_order(s, km_ref, ko_ref, keys)
     in_order(s, vm_ref, vo_ref, values)
+    spans = [slice(h * HEAD_DIM, (h + 1) * HEAD_DIM) for h in range(2)]
+    rows = [slice(n * BLOCK, (n + 1) * BLOCK) for n in range(2)]
+    windows = [pl.ds(pl.multiple_of(window_start(s, n), BLOCK), WINDOW) for n in range(2)]
+    scores = []
     for slot in range(2):
-        start = pl.multiple_of(window_start(s, slot), BLOCK)
-        k = keys[pl.ds(start, WINDOW), :]
-        v_t = values[pl.ds(start, WINDOW), :].T
-        q = q_ref[slot * BLOCK : (slot + 1) * BLOCK, :] * jnp.asarray(HEAD_DIM**-0.5, bf16)
-        bias = bias_ref[slot]
-        halves = []
-        for head in range(2):
-            scores = nt_dot(k, only_head(q, head, 1)) + bias
-            top = jnp.max(scores, axis=0, keepdims=True)
-            raised = jnp.exp(scores - top)
-            total = jnp.sum(raised, axis=0, keepdims=True)
-            mixed = jnp.dot(
-                v_t[head * HEAD_DIM : (head + 1) * HEAD_DIM],
-                raised.astype(bf16),
-                preferred_element_type=f32,
-            )
-            halves.append(mixed / total)
-            total_ref[0, head : head + 1, slot * BLOCK : (slot + 1) * BLOCK] = top + jnp.log(total)
-        mixed_ref[slot * BLOCK : (slot + 1) * BLOCK, :] = jnp.concatenate(halves, axis=0).T.astype(bf16)
+        q = q_ref[rows[slot], :] * jnp.asarray(HEAD_DIM**-0.5, bf16)
+        k = keys[windows[slot], :]
+        scores += [nt_dot(k, only_head(q, head, 1)) for head in range(2)]
+    raised, totals = [], []
+    for n in range(4):
+        slot, head = divmod(n, 2)
+        biased = scores[n] + bias_ref[slot]
+        top = jnp.max(biased, axis=0, keepdims=True)
+        up = jnp.exp(biased - top)
+        totals.append(jnp.sum(up, axis=0, keepdims=True))
+        total_ref[0, head : head + 1, rows[slot]] = top + jnp.log(totals[n])
+        raised.append(up.astype(bf16))
+    for slot in range(2):
+        v_t = values[windows[slot], :].T
+        halves = [
+            jnp.dot(v_t[spans[h]], raised[2 * slot + h], preferred_element_type=f32) / totals[2 * slot + h]
+            for h in range(2)
+        ]
+        mixed_ref[rows[slot], :] = jnp.concatenate(halves, axis=0).T.astype(bf16)
 
 
 def attend_backward_kernel(
@@ -361,42 +378,45 @@
     in_order(s, vm_ref, vo_ref, values)
     key_sum[...] = jnp.zeros_like(key_sum)
     value_sum[...] = jnp.zeros_like(value_sum)
+    spans = [slice(h * HEAD_DIM, (h + 1) * HEAD_DIM) for h in range(2)]
+    rows = [slice(n * BLOCK, (n + 1) * BLOCK) for n in range(2)]
+    windows = [pl.ds(pl.multiple_of(window_start(s, n), BLOCK), WINDOW) for n in range(2)]
+    scores, share_grads, queries, grads, inner = [], [], [], [], []
     for slot in range(2):
-        rows = slice(slot * BLOCK, (slot + 1) * BLOCK)
-        start = pl.multiple_of(window_start(s, slot), BLOCK)
-        window = pl.ds(start, WINDOW)
-        k, v = keys[window, :], values[window, :]
-        k_t = k.T
-        q = q_ref[rows, :] * jnp.asarray(HEAD_DIM**-0.5, bf16)
-        g = grad_ref[rows, :]
-        bias = bias_ref[slot]
-        along = (g.astype(f32) * mixed_ref[rows, :].astype(f32)).T
-        shares_low, grads_low, queries, grads, query_grads = [], [], [], [], []
+        q = q_ref[rows[slot], :] * jnp.asarray(HEAD_DIM**-0.5, bf16)
+        g = grad_ref[rows[slot], :]
+        along = (g.astype(f32) * mixed_ref[rows[slot], :].astype(f32)).T
+        k, v = keys[windows[slot], :], values[windows[slot], :]
         for head in range(2):
-            span = slice(head * HEAD_DIM, (head + 1) * HEAD_DIM)
             queries.append(only_head(q, head, 1))
             grads.append(only_head(g, head, 1))
-            scores = nt_dot(k, queries[head]) + bias
-            shares = jnp.exp(scores - total_ref[0, head : head + 1, rows])
-            inner = jnp.sum(along[span], axis=0, keepdims=True)
-            score_grads = (shares * (nt_dot(v, grads[head]) - inner)).astype(bf16)
-            shares_low.append(shares.astype(bf16))
-            grads_low.append(score_grads)
-            query_grads.append(jnp.dot(k_t[span], score_grads, preferred_element_type=f32))
-        dq_ref[rows, :] = (jnp.concatenate(query_grads, axis=0).T * HEAD_DIM**-0.5).astype(bf16)
-        key_sum[window, :] += jnp.dot(
-            jnp.concatenate(grads_low, axis=1), jnp.concatenate(queries, axis=0), preferred_element_type=f32
-        )
-        value_sum[window, :] += jnp.dot(
-            jnp.concatenate(shares_low, axis=1), jnp.concatenate(grads, axis=0), preferred_element_type=f32
-        )
+            inner.append(jnp.sum(along[spans[head]], axis=0, keepdims=True))
+            scores.append(nt_dot(k, queries[-1]))
+            share_grads.append(nt_dot(v, grads[-1]))
+    shares_low, grads_low = [], []
+    for n in range(4):
+        slot, head = divmod(n, 2)
+        shares = jnp.exp(scores[n] + bias_ref[slot] - total_ref[0, head : head + 1, rows[slot]])
+        shares_low.append(shares.astype(bf16))
+        grads_low.append((shares * (share_grads[n] - inner[n])).astype(bf16))
+    both = lambda values, slot, axis: jnp.concatenate(values[2 * slot : 2 * slot + 2], axis=axis)
     for slot in range(2):
-        rows = slice(slot * BLOCK, (slot + 1) * BLOCK)
+        k_t = keys[windows[slot], :].T
+        query_grads = [
+            jnp.dot(k_t[spans[h]], grads_low[2 * slot + h], preferred_element_type=f32) for h in range(2)
+        ]
+        dq_ref[rows[slot], :] = (jnp.concatenate(query_grads, axis=0).T * HEAD_DIM**-0.5).astype(bf16)
+        key_sum[windows[slot], :] += jnp.dot(
+            both(grads_low, slot, 1), both(queries, slot, 0), preferred_element_type=f32
+        )
+        value_sum[windows[slot], :] += jnp.dot(
+            both(shares_low, slot, 1), both(grads, slot, 0), preferred_element_type=f32
+        )
+    for slot in range(2):
         mine, other = pl.ds((s ^ (2 * slot)) * BLOCK, BLOCK), pl.ds((s ^ (1 + 2 * slot)) * BLOCK, BLOCK)
-        mine_ref[0, rows, :] = key_sum[mine, :]
-        mine_ref[1, rows, :] = value_sum[mine, :]
-        sent_ref[0, rows, :] = key_sum[other, :].astype(bf16)
-        sent_ref[1, rows, :] = value_sum[other, :].astype(bf16)
+        for n, sums in ((0, key_sum), (1, value_sum)):
+            mine_ref[n, rows[slot], :] = sums[mine, :]
+            sent_ref[n, rows[slot], :] = sums[other, :].astype(bf16)
 
 
 def call_attention(kernel, s, own, other, bias, kept, outs, scratch):
@@ -421,7 +441,6 @@
             }[spec]
         )
         specs.append((cut, per_pair, double)[spec])
-    flops = 2 * (5 if kept else 2) * HEADS * 2 * BLOCK * WINDOW * HEAD_DIM
     return pl.pallas_call(
         kernel,
         grid=(pairs_count,),
@@ -430,9 +449,7 @@
         out_shape=shapes,
         scratch_shapes=scratch,
         compiler_params=pltpu.CompilerParams(vmem_limit_bytes=48 << 20),
-        cost_estimate=pl.CostEstimate(
-            flops=flops * 8, bytes_accessed=16 << 20, transcendentals=HEADS * 2 * BLOCK * WINDOW
-        ),
+        cost_estimate=SMALL_COST,
     )(*args)
 
 
@@ -513,6 +530,81 @@
     )
     flat = lambda a: a.reshape(a.shape[0], D)
     return flat(query_grad).astype(bf16), flat(key_grad), flat(value_grad)
+
+
+def product(rows, weight, tile, finish, outs, by_column=(), tiles=(), transposed=False, sums=0):
+    tokens, depth = rows.shape
+    width = weight.shape[0 if transposed else 1]
+
+    def kernel(rows_ref, weight_ref, *refs):
+        total = (nt_dot if transposed else lambda a, b: jnp.dot(a, b, preferred_element_type=f32))(
+            rows_ref[...], weight_ref[...]
+        )
+        inputs = [r[...] for r in refs[: len(by_column) + len(tiles)]]
+        for ref, value in zip(refs[len(inputs) :], finish(total, *inputs)):
+            ref[...] = value.astype(ref.dtype)
+
+    cut = pl.BlockSpec((tokens, tile), lambda j: (0, j))
+    if transposed:
+        weight_spec = pl.BlockSpec((tile, depth), lambda j: (j, 0))
+    else:
+        weight_spec = pl.BlockSpec((depth, tile), lambda j: (0, j))
+    return pl.pallas_call(
+        kernel,
+        grid=(width // tile,),
+        in_specs=[pl.BlockSpec((tokens, depth), lambda j: (0, 0)), weight_spec]
+        + [pl.BlockSpec((1, tile), lambda j: (0, j))] * len(by_column)
+        + [cut] * len(tiles),
+        out_specs=[cut] * len(outs) + [pl.BlockSpec((1, tile), lambda j: (0, j))] * sums,
+        out_shape=[jax.ShapeDtypeStruct((tokens, width), kind) for kind in outs]
+        + [jax.ShapeDtypeStruct((1, width), f32)] * sums,
+        compiler_params=pltpu.CompilerParams(vmem_limit_bytes=48 << 20),
+        cost_estimate=SMALL_COST,
+    )(rows, weight, *[v.reshape(1, width) for v in by_column], *tiles)
+
+
+def gelu_parts(total, bias):
+    inner = total + bias
+    below = 0.5 * (1.0 + lax.erf(inner * (0.5**0.5)))
+    slope = below + inner * jnp.exp(-0.5 * inner * inner) * (2 * math.pi) ** -0.5
+    return inner * below, slope
+
+
+def norm_backward_rows(total, gain, upstream):
+    tokens, width = total.shape
+    tile = 128
+
+    def kernel(total_ref, gain_ref, up_ref, grad_ref, low_ref, sums_ref):
+        unit, scale = norm_forward(total_ref[...])
+        up = up_ref[...]
+        lifted = up * gain_ref[...]
+        grad = scale * (
+            lifted
+            - jnp.mean(lifted, axis=-1, keepdims=True)
+            - unit * jnp.mean(lifted * unit, axis=-1, keepdims=True)
+        )
+        low = grad.astype(bf16)
+        grad_ref[...] = grad
+        low_ref[...] = low
+
+        @pl.when(pl.program_id(0) == 0)
+        def _():
+            sums_ref[...] = jnp.zeros_like(sums_ref)
+
+        for n, value in enumerate((up * unit, up, low.astype(f32))):
+            sums_ref[n : n + 1, :] += jnp.sum(value, axis=0, keepdims=True)
+
+    cut = pl.BlockSpec((tile, width), lambda j: (j, 0))
+    out = jax.ShapeDtypeStruct((tokens, width), f32)
+    return pl.pallas_call(
+        kernel,
+        grid=(tokens // tile,),
+        in_specs=[cut, pl.BlockSpec((1, width), lambda j: (0, 0)), cut],
+        out_specs=[cut, cut, pl.BlockSpec((8, width), lambda j: (0, 0))],
+        out_shape=[out, jax.ShapeDtypeStruct((tokens, width), bf16), jax.ShapeDtypeStruct((8, width), f32)],
+        compiler_params=pltpu.CompilerParams(vmem_limit_bytes=32 << 20),
+        cost_estimate=SMALL_COST,
+    )(total, gain.reshape(1, width), upstream)
 
 
 SMALL = 8
@@ -598,15 +690,12 @@
     held = mine.shape[0]
     padded = jnp.pad(mine, (0, 1024 - held)).reshape(8, 128)
 
-    tok = phase(token_got, units[0][0])
-    every = jnp.stack([padded] + [send(padded, TO_Z[4 - k]) for k in (1, 2, 3)])
-    every = jnp.roll(every, z, axis=0)
-    tok = phase(tok, units[0][0])
-    tok, every = phase((tok, every), units[0][1])
-    every = by_place(every, send(every, TO_Y), y, 1)
-    tok, every = phase((tok, every), units[0][0])
-    every = by_place(every, send(every, TO_X), x, 2)
-    every = by_place(every, send(every, TO_CORE), c, 3)
+    u = [unit for layer_units in units for unit in layer_units]
+    padded = phase(padded, u[0])
+    token_got = send(token_left, TO_X)
+    other = send(padded, TO_PAIR)
+    high, low_bit = z // 2, z % 2
+    every = by_place(padded, other, high, 0)
 
     lengths = pick(doc_lengths.reshape(2, NDOC), row, 0)
     places = lax.iota(jnp.int32, SEQ_LEN)
@@ -615,6 +704,14 @@
     order = block_order(coords)
     matrices = order_matrices(order)
 
+    token_got, every, upstream_left = phase((token_got, every, upstream_left), u[0], u[1])
+    every = by_place(every, send(every, TO_ODD), low_bit, 1).reshape(4, 8, 128)
+    upstream_got = send(upstream_left, TO_X)
+    token_got, every, matrices, bias = phase((token_got, every, matrices, bias), u[0], u[1], u[2])
+    every = by_place(every, send(every, TO_Y), y, 1)
+    token_got, every, upstream_got = phase((token_got, every, upstream_got), u[0], u[1], u[2], u[3])
+    every = by_place(every, send(every, TO_X), x, 2)
+    every = by_place(every, send(every, TO_CORE), c, 3)
     every = every.reshape(devices, 1024)[:, :held].astype(f32)
     small_all = (
         every[:, :small_held]
@@ -628,62 +725,57 @@
         .transpose(1, 0, 2)
         .reshape(layer_count, FF)
     )
-    tok, bias, matrices, small_all, wide_all = phase((tok, bias, matrices, small_all, wide_all), units[0][1])
-    tok = phase(tok, units[0][2])
-    tok = phase(tok, units[0][0])
-
-    stream = jnp.concatenate([token_kept, tok]).astype(f32)
+    stream = jnp.concatenate([token_kept, token_got]).astype(f32)
+    stream, small_all, wide_all = phase((stream, small_all, wide_all), u[0], u[2], u[3], u[4], settle=[u[1]])
     saved = []
     for layer in range(layer_count):
         a_unit, i_unit, o_unit = units[layer]
-        later = units[layer + 1] if layer + 1 < layer_count else None
+        next_a, next_i, next_o = units[layer + 1] if layer + 1 < layer_count else (None,) * 3
         q_bias, v_bias, m_bias, gain1, shift1, o_bias, gain2, shift2 = [small_all[layer, n] for n in range(SMALL)]
         w_three, w_mix = a_unit.result()
         w_three, w_mix = w_three.reshape(D, 3 * D), w_mix.reshape(D, D)
         stream_low = stream.astype(bf16)
-        three = (dot(stream_low, w_three) + jnp.concatenate([q_bias, jnp.zeros_like(q_bias), v_bias])).astype(bf16)
+        three_bias = jnp.concatenate([q_bias, jnp.zeros_like(q_bias), v_bias])
+        (three,) = product(stream_low, w_three, 1024, lambda total, b: (total + b,), (bf16,), (three_bias,))
+        if next_a:
+            three = phase(three, i_unit, next_i, next_o, settle=[o_unit, next_a])
+        else:
+            three = phase(three, i_unit)
         three_got = send(three, TO_CORE)
-        stream, stream_low, three = phase((stream, stream_low, three), i_unit)
-        if later:
-            stream_low = phase(stream_low, later[0])
-        left_stream = selected(matrices, stream_low)
-        left_stream, three, three_got = phase((left_stream, three, three_got), o_unit)
+        (left_stream,) = selected(matrices, tie(stream_low, three))
+        three, left_stream = lax.optimization_barrier((three, left_stream))
         left_stream = (left_stream[0], send(left_stream[1], TO_CORE))
         mixed, totals = attend_forward_blocks(place_of, three, three_got, bias)
-        mixed, totals = phase((mixed, totals), i_unit, o_unit)
-        left_mix = selected(matrices, mixed)
+        moving = [i_unit, o_unit] + ([next_a, next_o] if next_a else [])
+        mixed, totals, left_stream = phase(
+            (mixed, totals, left_stream), *moving, settle=[next_i] if next_a else []
+        )
         first_sum = stream + (dot(mixed, w_mix) + m_bias)
         first = norm_forward(first_sum)[0] * gain1 + shift1
         first_low = first.astype(bf16)
-        left_first = selected(matrices, first_low)
+        left_mix, left_first = selected(matrices, mixed, first_low)
+        if not next_a:
+            first_low = phase(first_low, o_unit)
         (w_inner,) = i_unit.result()
         w_inner = w_inner.reshape(D, FF)
-        first, first_low, left_mix, left_first = lax.optimization_barrier(
-            (first, first_low, left_mix, left_first)
-        )
+        first_low, left_mix, left_first = lax.optimization_barrier((first_low, left_mix, left_first))
         left_mix, left_first = [(m, send(t, TO_CORE)) for m, t in (left_mix, left_first)]
-        if later:
-            first, first_low = phase((first, first_low), later[0])
-            first, first_low = phase((first, first_low), later[1])
-        else:
-            (upstream_left,) = (tie(upstream_left, first_low),)
-            upstream_got = send(upstream_left, TO_X)
-        inner = dot(first_low, w_inner) + wide_all[layer]
-        below = 0.5 * (1.0 + lax.erf(inner * (0.5**0.5)))
-        active = (inner * below).astype(bf16)
-        slope = (below + inner * jnp.exp(-0.5 * inner * inner) * (2 * math.pi) ** -0.5).astype(bf16)
-        active, slope = phase((active, slope), o_unit)
-        if later:
-            active = phase(active, later[0])
+        active, slope = product(first_low, w_inner, 1024, gelu_parts, (bf16, bf16), (wide_all[layer],))
+        moving = [o_unit] + ([next_a] if next_a else [])
+        active, slope, left_mix, left_first = phase(
+            (active, slope, left_mix, left_first), *moving, settle=[next_o] if next_a else []
+        )
+        active_got = send(active, TO_CORE)
         (w_outer,) = o_unit.result()
         w_outer = w_outer.reshape(FF, D)
-        second_sum = first + (dot(active, w_outer) + o_bias)
-        left_active = (active, send(active, TO_CORE))
+        (second_sum,) = product(
+            active, w_outer, 256, lambda total, b, f: (f + (total + b),), (f32,), (o_bias,), (first,)
+        )
+        second_sum, active_got = lax.optimization_barrier((second_sum, active_got))
+        left_active = (active, active_got)
         stream = norm_forward(second_sum)[0] * gain2 + shift2
-        if later:
-            stream = phase(stream, later[1])
-            stream = phase(stream, later[2])
-            stream = phase(stream, later[0])
+        if next_a:
+            stream = phase(stream, next_a, next_i)
         saved.append(
             (
                 (w_three, w_mix, w_inner, w_outer, gain1, gain2),
@@ -710,59 +802,81 @@
         three, three_got, totals, mixed = kept
         first_sum, slope, second_sum = rest
         left_stream, left_mix, left_first, left_active = lefts
-        second_grad, gain2_grad, shift2_grad = norm_backward(second_sum, gain2, upstream)
-        second_low = second_grad.astype(bf16)
+
+        def with_sum(total, slopes):
+            low = (total * slopes).astype(bf16)
+            return low, jnp.sum(low.astype(f32), axis=0, keepdims=True)
+
+        second_grad, second_low, second_sums = norm_backward_rows(second_sum, gain2, upstream)
         second_got = send(second_low, TO_CORE)
-        inner_low = (contract_cols(second_low, w_outer) * slope).astype(bf16)
+        inner_low, inner_sum = product(
+            second_low, w_outer, 1024, with_sum, (bf16,), (), (slope,), transposed=True, sums=1
+        )
+        if before:
+            inner_low = phase(inner_low, before.o, before.i, before.a)
+        else:
+            inner_low, output_got = lax.optimization_barrier((inner_low, output_got))
         inner_got = send(inner_low, TO_CORE)
-        o_sum = SumUnit(wide_terms_of(order, left_active, (second_low, second_got)))
-        second_grad, inner_low = phase((second_grad, inner_low), o_sum)
+        o_sum = SumUnit(wide_terms_of(order, left_active, tie((second_low, second_got), inner_low)))
         if before:
-            second_grad, inner_low = phase((second_grad, inner_low), before[0], before[2])
-        first_grad = second_grad + contract_cols(inner_low, w_inner)
-        first_sum_grad, gain1_grad, shift1_grad = norm_backward(first_sum, gain1, first_grad)
-        branch_low = first_sum_grad.astype(bf16)
+            second_grad, inner_low = phase((second_grad, inner_low), o_sum, before.a, before.i, before.o)
+        else:
+            second_grad, inner_low = phase((second_grad, inner_low), o_sum)
+        (first_grad,) = product(
+            inner_low, w_inner, 256, lambda total, g: (g + total,), (f32,), (), (second_grad,), transposed=True
+        )
+        first_sum_grad, branch_low, first_sums = norm_backward_rows(first_sum, gain1, first_grad)
         branch_got = send(branch_low, TO_CORE)
-        i_sum = SumUnit(weight_terms((left_first, (inner_low, inner_got))))
-        first_sum_grad, branch_low = phase((first_sum_grad, branch_low), i_sum)
-        mixed_grad = contract_cols(branch_low, w_mix).astype(bf16)
+        (mixed_grad,) = product(branch_low, w_mix, 512, lambda total: (total,), (bf16,), transposed=True)
+        i_sum = SumUnit(
+            weight_terms(
+                (left_first, tie((inner_low, inner_got), mixed_grad), FF), (left_mix, (branch_low, branch_got), D)
+            )
+        )
         if before:
-            mixed_grad = phase(mixed_grad, before[1], before[0])
+            mixed_grad = phase(mixed_grad, i_sum, before.a, before.i, settle=[o_sum])
         else:
-            mixed_grad, output_got = lax.optimization_barrier((mixed_grad, output_got))
+            mixed_grad = phase(mixed_grad, i_sum, settle=[o_sum])
         query_low, own_grads, sent_grads = attend_backward_blocks(
             place_of, three, three_got, bias, mixed, totals, mixed_grad
         )
         grads_back = send(sent_grads, TO_CORE)
-        own_grads = phase(own_grads, o_sum)
-        if before:
-            own_grads = phase(own_grads, before[1])
+        if layer:
+            query_low, own_grads = phase((query_low, own_grads), o_sum, settle=[i_sum])
+        else:
+            moving = [o_sum, i_sum] + ([before.a] if before else [])
+            query_low, own_grads = phase((query_low, own_grads), *moving)
         sums_low = (own_grads + grads_back.astype(f32)).astype(bf16)
         low = jnp.concatenate([query_low, sums_low[0], sums_low[1]], axis=1)
         low_got = send(low, TO_CORE)
-        first_sum_grad, low = phase((first_sum_grad, low), i_sum)
-        upstream = first_sum_grad + contract_cols(low, w_three)
-        a_sum = SumUnit(weight_terms((left_stream, (low, low_got)), (left_mix, (branch_low, branch_got))))
-        upstream = phase(upstream, a_sum)
-        if before:
-            upstream = phase(upstream, before[1])
-        upstream = phase(upstream, o_sum)
+        if layer:
+            (upstream,) = product(
+                low, w_three, 256, lambda total, g: (g + total,), (f32,), (), (first_sum_grad,), transposed=True
+            )
+            a_sum = SumUnit(weight_terms((left_stream, tie((low, low_got), upstream), 3 * D)))
+        else:
+            a_sum = SumUnit(weight_terms((left_stream, (low, low_got), 3 * D)))
+            low = phase(low, a_sum, o_sum, i_sum)
+            (upstream,) = product(
+                low, w_three, 256, lambda total, g: (g + total,), (f32,), (), (first_sum_grad,), transposed=True
+            )
         small_grads[layer] = jnp.stack(
             [
                 column_sum(low[:, :D]),
                 column_sum(low[:, 2 * D :]),
-                column_sum(branch_low),
-                gain1_grad,
-                shift1_grad,
-                column_sum(second_low),
-                gain2_grad,
-                shift2_grad,
+                first_sums[2],
+                first_sums[0],
+                first_sums[1],
+                second_sums[2],
+                second_sums[0],
+                second_sums[1],
             ]
         )
-        wide_grads[layer] = column_sum(inner_low)
-        before = sums[layer] = (i_sum, a_sum, o_sum)
-
-    token_back = send(upstream[length:].astype(bf16), TO_X)
+        wide_grads[layer] = inner_sum[0]
+        if layer:
+            upstream, small_grads[layer] = phase((upstream, small_grads[layer]), o_sum, i_sum, settle=[a_sum])
+        sums[layer] = before = Sums(o_sum, i_sum, a_sum)
+
     small_terms = (
         jnp.stack(small_grads)
         .reshape(vector_count, devices, rows_held)
@@ -781,36 +895,34 @@
     terms = (terms[0] + send(terms[1].astype(bf16), TO_CORE).astype(f32)).astype(bf16)
     small_sum = SumUnit((terms[:64], terms[64:]))
 
-    i_sum, a_sum, o_sum = sums[0]
+    last = sums[0]
+    upstream = phase(upstream, last.a, last.o, last.i, small_sum)
+    upstream = phase(upstream, last.a, small_sum, settle=[last.o, last.i])
+    token_back = send(upstream[length:].astype(bf16), TO_X)
+    upstream, token_back = phase((upstream, token_back), last.a, small_sum)
+    phase((), last.a, small_sum)
     phase((), small_sum)
-    phase((), i_sum, o_sum)
-    phase((), a_sum, small_sum)
-    phase((), i_sum)
-    phase((), a_sum, small_sum)
-    phase((), a_sum, small_sum)
     own_terms = small_sum.kept.reshape(-1)[:held]
     small_own = own_terms[:small_held].reshape(layer_count, SMALL, rows_held)
     wide_own = own_terms[small_held:].reshape(layer_count, inner_held)
-    for layer in range(1, layer_count):
+    for layer in range(layer_count):
         for unit in sums[layer]:
-            while unit.step < 4:
+            while unit.step < 5:
                 phase((), unit)
-    i_all, a_all, o_all = [
-        jnp.stack([sums[layer][n].kept for layer in range(layer_count)]) for n in range(3)
-    ]
+    o_all, i_all, a_all = [jnp.stack([units_of[n].kept for units_of in sums]) for n in range(3)]
     return (
         both_rows(output[:length], output_got),
         both_rows(upstream[:length], token_back),
         a_all[:, :, :D],
         a_all[:, :, D : 2 * D],
         a_all[:, :, 2 * D : 3 * D],
-        a_all[:, :, 3 * D :],
+        i_all[:, :, FF:],
         small_own[:, 0],
         small_own[:, 1],
         small_own[:, 2],
         small_own[:, 3],
         small_own[:, 4],
-        i_all,
+        i_all[:, :, :FF],
         wide_own,
         o_all,
         small_own[:, 5],

time: 818 us -> 763 us (0.933)
  matrix products: 125 us -> 2.97 us
  Pallas kernels: 186 us -> 295 us
  starting transfers between devices: 120 us -> 83.6 us
  waiting for transfers between devices: 246 us -> 237 us
    pallas_call x0 -> x22, Pallas kernels: none -> 122 us  [the longest x14 104 us: product(): pl.pallas_call(kernel, grid=(width // tile,), in_specs=[pl.BlockSpec((tok...]
    dot_general x20 -> x0, matrix products: 67.2 us -> none  [the longest x8 49.2 us: contract_cols(): lax.dot_general(left, right, (((1,), (1,)), ((), ())), preferred_element_...]
    dot_general x8 -> x2, matrix products: 57.4 us -> 2.72 us  [dot(): return jnp.dot(left, right, preferred_element_type=f32)]
    ppermute x108 -> x94, starting transfers between devices: 120 us -> 83.6 us  [send(): return lax.ppermute(value, AXES, to)]
    concatenate x4 -> x19, other arithmetic: 3.41 us -> 19.5 us  [the longest x18 19.5 us: local(): self.kept = jnp.concatenate([got[0], self.kept])]
    convert_element_type x17 -> x24, other arithmetic: 26.5 us -> 39.9 us  [the longest x14 32.4 us: local(): self.kept = self.kept.astype(bf16)]
    pallas_call x4, Pallas kernels: 90.9 us -> 77.8 us  [call_attention(): pl.pallas_call(kernel, grid=(pairs_count,), in_specs=in_specs, out_specs=...]
    reduce_sum x8 -> x3, other arithmetic: 11.7 us -> 0.7 us  [column_sum(): return jnp.sum(values.astype(f32), axis=0)]
  transfers between devices with their start and end apart: 108 -> 94, of which waited for: 33 -> 45; matrix products, arithmetic and copies ran while one was open for 26% -> 8% of each run, Pallas kernels for 21% -> 39%
where the time goes in v3:
time: 763 us; the launch traced here: 756 us
  Pallas kernels  295 us (39%)
  waiting for transfers between devices  237 us (31%)
  starting transfers between devices  83.6 us (11%)
  other arithmetic  83.5 us (11%)
  local copies, waits for them, and re-layouts  50.4 us (7%)
    ppermute x94, waiting for transfers between devices, send(): return lax.ppermute(value, AXES, to)  237 us
    pallas_call x14, Pallas kernels, product(): pl.pallas_call(kernel, grid=(width // tile,), in_specs=[pl.BlockSpec((tok...  104 us
    ppermute x94, starting transfers between devices, send(): return lax.ppermute(value, AXES, to)  83.6 us
    pallas_call x4, Pallas kernels, call_attention(): pl.pallas_call(kernel, grid=(pairs_count,), in_specs=in_specs, out_specs=...  77.8 us
    pallas_call x6, Pallas kernels, place(): pl.pallas_call(kernel, in_specs=[pl.BlockSpec(memory_space=pltpu.SMEM)] +...  39.8 us
    pallas_call x4, Pallas kernels, weight_terms(): pl.pallas_call(kernel, grid=(columns // tile,), in_specs=in_specs, out_sp...  32.4 us
    convert_element_type x14, other arithmetic, local(): self.kept = self.kept.astype(bf16)  32.4 us
    unnamed x304, local copies, waits for them, and re-layouts  28.1 us
  transfers between devices with their start and end apart: 94, of which 45 were waited for; matrix products, arithmetic and copies ran while one was open for 8% of the time, Pallas kernels for 39%

profile of v3, /device:TPU:0, one launch (start us, length us, event | category | flops | bytes accessed | tf_op | source)
XLA Modules:
  0.0 755.8 jit_solution(8680610290627980452)
XLA Ops:
  21.2 4.9 collective-permute-done.2
  33.7 12.0 %collective-permute-done.3 = bf16[2,8,128]{2,1,0:T(8,128)(2,1)S(1)} collective-permute-done((bf16[2,8,128]{2,1,0:T(8,128)(2,1)S(1)}, bf16[2,8,128]{2,1,0:T(8,128)(2,1)S(1)}, u32[]{:S(2)}, u32[]{:S(2)}) %collective-permute-start.3) | collective-permute-done | bytes 4128 | tf_op jit(solution)/shard_map/ppermute | solution.py:61
  54.3 7.6 %collective-permute-done.6 = bf16[4,8,128]{2,1,0:T(8,128)(2,1)S(1)} collective-permute-done((bf16[4,8,128]{2,1,0:T(8,128)(2,1)S(1)}, bf16[4,8,128]{2,1,0:T(8,128)(2,1)S(1)}, u32[]{:S(2)}, u32[]{:S(2)}) %collective-permute-start.6) | collective-permute-done | bytes 8224 | tf_op jit(solution)/shard_map/ppermute | solution.py:61
  81.2 27.8 %collective-permute-done.11 = bf16[4,2,8,128]{3,2,0,1:T(8,128)(2,1)S(1)} collective-permute-done((bf16[4,2,8,128]{3,2,0,1:T(8,128)(2,1)S(1)}, bf16[4,2,8,128]{3,2,0,1:T(8,128)(2,1)S(1)}, u32[]{:S(2)}, u32[]{:S(2)}) %collective-permute-start.11) | collective-permute-done | bytes 16416 | tf_op jit(solution)/shard_map/ppermute | solution.py:61
  125.8 6.9 shard_map.305
  134.0 5.9 shard_map.306.q_ref.km_ref.vm_ref
  150.8 14.2 %shard_map.308 = (bf16[512,1024]{1,0:T(8,128)(2,1)S(1)}, f32[8,2,512]{2,1,0:T(2,128)S(1)}) custom-call(s32[1]{0:T(128)} %bitcast.87.s_ref, bf16[512,3072]{1,0:T(8,128)(2,1)S(1)} %shard_map.306.q_ref.km_ref.vm_ref, bf16[512,3072]{1,0:T(8,128)(2,1)S(1)} %shard_map.306.q_ref.km_ref.vm_ref, bf16[512,3072]{1,0:T(8,128)(2,1)} %collective-permute-done.22.ko_ref.vo_ref, ...), custom_call_target="tpu_custom_call" | custom-call | flops 1024 | bytes 1024 | tf_op jit(solution)/shard_map/pallas_call | solution.py:444
  193.9 6.6 shard_map.310
  200.5 11.0 %shard_map.311 = (bf16[512,4096]{1,0:T(8,128)(2,1)S(1)}, bf16[512,4096]{1,0:T(8,128)(2,1)}) custom-call(bf16[512,1024]{1,0:T(8,128)(2,1)S(1)} %copy-done.21, bf16[1024,4096]{1,0:T(8,128)(2,1)} %bitcast.291, f32[1,4096]{1,0:T(1,128)S(1)} %get-tuple-element.802.refs_0_), custom_call_target="tpu_custom_call" | custom-call | flops 1024 | bytes 1024 | tf_op jit(solution)/shard_map/pallas_call | solution.py:552
  220.5 8.6 %collective-permute-done.34.refs_2_ = bf16[8,128,1024]{2,1,0:T(8,128)(2,1)S(1)} collective-permute-done((bf16[8,128,1024]{2,1,0:T(8,128)(2,1)S(1)}, bf16[8,128,1024]{2,1,0:T(8,128)(2,1)S(1)}, u32[]{:S(2)}, u32[]{:S(2)}) %collective-permute-start.34) | collective-permute-done | bytes 2097184 | tf_op jit(solution)/shard_map/ppermute | solution.py:61
  232.0 6.0 shard_map.312
  238.0 8.5 %shard_map.313.total_ref = f32[512,1024]{1,0:T(8,128)S(1)} custom-call(bf16[512,4096]{1,0:T(8,128)(2,1)} %copy-done.9, bf16[4096,1024]{1,0:T(8,128)(2,1)} %bitcast.293, f32[1,1024]{1,0:T(1,128)S(1)} %get-tuple-element.792.refs_0_, f32[512,1024]{1,0:T(8,128)S(1)} %copy-done.22), custom_call_target="tpu_custom_call" | custom-call | flops 1024 | bytes 1024 | tf_op jit(solution)/shard_map/pallas_call | solution.py:552
  256.5 6.8 shard_map.314
  263.3 6.6 shard_map.315.q_ref.km_ref.vm_ref
  276.2 14.6 %shard_map.317 = (bf16[512,1024]{1,0:T(8,128)(2,1)S(1)}, f32[8,2,512]{2,1,0:T(2,128)S(1)}) custom-call(s32[1]{0:T(128)} %bitcast.87.s_ref, bf16[512,3072]{1,0:T(8,128)(2,1)S(1)} %shard_map.315.q_ref.km_ref.vm_ref, bf16[512,3072]{1,0:T(8,128)(2,1)S(1)} %shard_map.315.q_ref.km_ref.vm_ref, bf16[512,3072]{1,0:T(8,128)(2,1)} %collective-permute-done.41.ko_ref.vo_ref, ...), custom_call_target="tpu_custom_call" | custom-call | flops 1024 | bytes 1024 | tf_op jit(solution)/shard_map/pallas_call | solution.py:444
  290.8 6.0 collective-permute-done.43.refs_1_
  303.3 9.5 %collective-permute-done.44 = bf16[4,128,1024]{2,1,0:T(8,128)(2,1)S(1)} collective-permute-done((bf16[4,128,1024]{2,1,0:T(8,128)(2,1)S(1)}, bf16[4,128,1024]{2,1,0:T(8,128)(2,1)S(1)}, u32[]{:S(2)}, u32[]{:S(2)}) %collective-permute-start.44) | collective-permute-done | bytes 1048608 | tf_op jit(solution)/shard_map/ppermute | solution.py:61
  318.6 7.5 shard_map.319
  326.1 10.8 %shard_map.320 = (bf16[512,4096]{1,0:T(8,128)(2,1)S(1)}, bf16[512,4096]{1,0:T(8,128)(2,1)}) custom-call(bf16[512,1024]{1,0:T(8,128)(2,1)S(1)} %copy-done.20, bf16[1024,4096]{1,0:T(8,128)(2,1)} %bitcast.295, f32[1,4096]{1,0:T(1,128)S(1)} %get-tuple-element.801.refs_0_), custom_call_target="tpu_custom_call" | custom-call | flops 1024 | bytes 1024 | tf_op jit(solution)/shard_map/pallas_call | solution.py:552
  339.9 12.2 %collective-permute-done.50.refs_2_ = bf16[8,128,1024]{2,1,0:T(8,128)(2,1)S(1)} collective-permute-done((bf16[8,128,1024]{2,1,0:T(8,128)(2,1)S(1)}, bf16[8,128,1024]{2,1,0:T(8,128)(2,1)S(1)}, u32[]{:S(2)}, u32[]{:S(2)}) %collective-permute-start.50) | collective-permute-done | bytes 2097184 | tf_op jit(solution)/shard_map/ppermute | solution.py:61
  352.7 6.0 shard_map.321
  358.8 8.5 %shard_map.322.total_ref = f32[512,1024]{1,0:T(8,128)S(1)} custom-call(bf16[512,4096]{1,0:T(8,128)(2,1)} %copy-done.10, bf16[4096,1024]{1,0:T(8,128)(2,1)} %bitcast.297, f32[1,1024]{1,0:T(1,128)S(1)} %get-tuple-element.784.refs_0_, f32[512,1024]{1,0:T(8,128)S(1)} %get-tuple-element.718.refs_1_), custom_call_target="tpu_custom_call" | custom-call | flops 1024 | bytes 1024 | tf_op jit(solution)/shard_map/pallas_call | solution.py:552
  374.4 9.5 %shard_map.324 = (bf16[512,4096]{1,0:T(8,128)(2,1)}, f32[1,4096]{1,0:T(1,128)S(1)}) custom-call(bf16[512,1024]{1,0:T(8,128)(2,1)S(1)} %get-tuple-element.552.rows_ref.refs_4_, bf16[4096,1024]{1,0:T(8,128)(2,1)} %bitcast.298, bf16[512,4096]{1,0:T(8,128)(2,1)} %get-tuple-element.544.refs_0_), custom_call_target="tpu_custom_call" | custom-call | flops 1024 | bytes 1024 | tf_op jit(solution)/shard_map/pallas_call | solution.py:552
  384.8 7.4 collective-permute-done.54.refs_5_
  392.2 11.2 %shard_map.325 = (bf16[1024,1024]{1,0:T(8,128)(2,1)S(1)}, bf16[1024,1024]{1,0:T(8,128)(2,1)}) custom-call(s32[32]{0:T(128)S(1)} %stack.451.order_ref, bf16[512,4096]{1,0:T(8,128)(2,1)} %copy-done.10, bf16[512,4096]{1,0:T(8,128)(2,1)} %copy-done.10, bf16[512,4096]{1,0:T(8,128)(2,1)} %collective-permute-done.52.refs_2_.refs_3_, ...), custom_call_target="tpu_custom_call" | custom-call | flops 1024 | bytes 1024 | tf_op jit(solution)/shard_map/pallas_call | solution.py:298
  404.3 8.5 %shard_map.326.up_ref = f32[512,1024]{1,0:T(8,128)S(1)} custom-call(bf16[512,4096]{1,0:T(8,128)(2,1)} %get-tuple-element.564.rows_ref.refs_2_, bf16[1024,4096]{1,0:T(8,128)(2,1)} %bitcast.296, f32[512,1024]{1,0:T(8,128)S(1)} %copy-done.43), custom_call_target="tpu_custom_call" | custom-call | flops 1024 | bytes 1024 | tf_op jit(solution)/shard_map/pallas_call | solution.py:552
  418.4 9.9 %shard_map.329 = (bf16[256,5120]{1,0:T(8,128)(2,1)}, bf16[256,5120]{1,0:T(8,128)(2,1)}) custom-call(bf16[512,512]{1,0:T(8,128)(2,1)S(1)} %copy-done.64, bf16[512,512]{1,0:T(8,128)(2,1)S(1)} %copy-done.68, bf16[512,4096]{1,0:T(8,128)(2,1)} %get-tuple-element.564.rows_ref.refs_2_, bf16[512,4096]{1,0:T(8,128)(2,1)} %collective-permute-done.55.refs_3_, ...), custom_call_target="tpu_custom_call" | custom-call | flops 1024 | bytes 1024 | tf_op jit(solution)/shard_map/pallas_call | solution.py:262
  430.4 24.5 %shard_map.330 = (bf16[512,1024]{1,0:T(8,128)(2,1)S(1)}, f32[2,512,1024]{2,1,0:T(8,128)}, bf16[2,512,1024]{2,1,0:T(8,128)(2,1)}) custom-call(s32[1]{0:T(128)} %bitcast.87.s_ref, bf16[512,3072]{1,0:T(8,128)(2,1)} %copy-done.3, bf16[512,3072]{1,0:T(8,128)(2,1)} %copy-done.3, bf16[512,3072]{1,0:T(8,128)(2,1)} %collective-permute-done.41.ko_ref.vo_ref, ...), custom_call_target="tpu_custom_call" | custom-call | flops 1024 | bytes 1024 | tf_op jit(solution)/shard_map/pallas_call | solution.py:444
  454.9 6.6 collective-permute-done.58
  470.1 7.1 shard_map.331.up_ref
  479.7 6.0 shard_map.332
  497.4 8.3 %shard_map.334 = (bf16[512,4096]{1,0:T(8,128)(2,1)S(1)}, f32[1,4096]{1,0:T(1,128)S(1)}) custom-call(bf16[512,1024]{1,0:T(8,128)(2,1)S(1)} %get-tuple-element.616.rows_ref.refs_4_, bf16[4096,1024]{1,0:T(8,128)(2,1)} %bitcast.294, bf16[512,4096]{1,0:T(8,128)(2,1)} %get-tuple-element.604.refs_0_), custom_call_target="tpu_custom_call" | custom-call | flops 1024 | bytes 1024 | tf_op jit(solution)/shard_map/pallas_call | solution.py:552
  517.5 11.6 %shard_map.335 = (bf16[1024,1024]{1,0:T(8,128)(2,1)}, bf16[1024,1024]{1,0:T(8,128)(2,1)}) custom-call(s32[32]{0:T(128)S(1)} %stack.451.order_ref, bf16[512,4096]{1,0:T(8,128)(2,1)} %copy-done.9, bf16[512,4096]{1,0:T(8,128)(2,1)} %copy-done.9, bf16[512,4096]{1,0:T(8,128)(2,1)} %collective-permute-done.36.refs_2_.refs_3_, ...), custom_call_target="tpu_custom_call" | custom-call | flops 1024 | bytes 1024 | tf_op jit(solution)/shard_map/pallas_call | solution.py:298
  529.1 6.5 collective-permute-done.67
  543.0 8.5 %shard_map.336.up_ref = f32[512,1024]{1,0:T(8,128)S(1)} custom-call(bf16[512,4096]{1,0:T(8,128)(2,1)} %copy-done.19, bf16[1024,4096]{1,0:T(8,128)(2,1)} %bitcast.292, f32[512,1024]{1,0:T(8,128)S(1)} %copy-done.41), custom_call_target="tpu_custom_call" | custom-call | flops 1024 | bytes 1024 | tf_op jit(solution)/shard_map/pallas_call | solution.py:552
  558.4 9.8 %shard_map.339 = (bf16[256,5120]{1,0:T(8,128)(2,1)}, bf16[256,5120]{1,0:T(8,128)(2,1)}) custom-call(bf16[512,512]{1,0:T(8,128)(2,1)S(1)} %copy-done.56, bf16[512,512]{1,0:T(8,128)(2,1)S(1)} %copy-done.60, bf16[512,4096]{1,0:T(8,128)(2,1)} %copy-done.19, bf16[512,4096]{1,0:T(8,128)(2,1)} %collective-permute-done.68.refs_3_, bf16[512,512]{1,0:T(8,128)(2,1)S(1)} %copy-done.54, ...), custom_call_target="tpu_custom_call" | custom-call | flops 1024 | bytes 1024 | tf_op jit(solution)/shard_map/pallas_call | solution.py:262
  568.3 5.5 collective-permute-done.71
  579.3 24.6 %shard_map.340 = (bf16[512,1024]{1,0:T(8,128)(2,1)S(1)}, f32[2,512,1024]{2,1,0:T(8,128)}, bf16[2,512,1024]{2,1,0:T(8,128)(2,1)}) custom-call(s32[1]{0:T(128)} %bitcast.87.s_ref, bf16[512,3072]{1,0:T(8,128)(2,1)} %copy-done.2, bf16[512,3072]{1,0:T(8,128)(2,1)} %copy-done.2, bf16[512,3072]{1,0:T(8,128)(2,1)} %collective-permute-done.22.ko_ref.vo_ref, ...), custom_call_target="tpu_custom_call" | custom-call | flops 1024 | bytes 1024 | tf_op jit(solution)/shard_map/pallas_call | solution.py:444
  608.7 4.8 add_convert_fusion.6
  627.0 6.7 shard_map.341
  633.7 15.2 %collective-permute-done.77 = bf16[512,1024]{1,0:T(8,128)(2,1)} collective-permute-done((bf16[512,1024]{1,0:T(8,128)(2,1)}, bf16[512,1024]{1,0:T(8,128)(2,1)}, u32[]{:S(2)}, u32[]{:S(2)}) %collective-permute-start.77) | collective-permute-done | bytes 1048608 | tf_op jit(solution)/shard_map/ppermute | solution.py:61
  660.8 7.4 shard_map.342
  668.3 6.0 collective-permute-done.80
  674.3 13.6 %collective-permute-done.81 = bf16[64,5120]{1,0:T(8,128)(2,1)} collective-permute-done((bf16[64,5120]{1,0:T(8,128)(2,1)}, bf16[64,5120]{1,0:T(8,128)(2,1)}, u32[]{:S(2)}, u32[]{:S(2)}) %collective-permute-start.81) | collective-permute-done | bytes 655392 | tf_op jit(solution)/shard_map/ppermute | solution.py:61
  698.1 16.6 %collective-permute-done.85 = bf16[128,1024]{1,0:T(8,128)(2,1)S(1)} collective-permute-done((bf16[128,1024]{1,0:T(8,128)(2,1)S(1)}, bf16[128,1024]{1,0:T(8,128)(2,1)S(1)}, u32[]{:S(2)}, u32[]{:S(2)}) %collective-permute-start.85) | collective-permute-done | bytes 262176 | tf_op jit(solution)/shard_map/ppermute | solution.py:61
  714.7 6.9 collective-permute-done.86
  729.7 5.1 collective-permute-done.88
  741.9 7.6 %collective-permute-done.90 = bf16[32,3072]{1,0:T(8,128)(2,1)S(1)} collective-permute-done((bf16[32,3072]{1,0:T(8,128)(2,1)S(1)}, bf16[32,3072]{1,0:T(8,128)(2,1)S(1)}, u32[]{:S(2)}, u32[]{:S(2)}) %collective-permute-start.90) | collective-permute-done | bytes 196640 | tf_op jit(solution)/shard_map/ppermute | solution.py:61
  (657 shorter events, 288.8 us)
Async XLA Ops:
  27.4 18.3 %collective-permute-start.4 = (bf16[2,128,1024]{2,1,0:T(8,128)(2,1)S(1)}, bf16[2,128,1024]{2,1,0:T(8,128)(2,1)S(1)}, u32[]{:S(2)}, u32[]{:S(2)}) collective-permute-start(bf16[2,128,1024]{2,1,0:T(8,128)(2,1)S(1)} %pad_maximum_fusion.17), channel_id=1, source_target_pairs={{0,8},{1,9},{2,10},{3,11},{4,12},{5,13},{6,14},{7,15},{8,0},{9,1},... | collective-permute-start | bytes 1572872 | tf_op jit(solution)/shard_map/ppermute | solution.py:61
  46.8 19.1 %collective-permute-start.8 = (bf16[4,128,1024]{2,1,0:T(8,128)(2,1)S(1)}, bf16[4,128,1024]{2,1,0:T(8,128)(2,1)}, u32[]{:S(2)}, u32[]{:S(2)}) collective-permute-start(bf16[4,128,1024]{2,1,0:T(8,128)(2,1)S(1)} %pad_maximum_fusion.10), channel_id=1, source_target_pairs={{0,4},{1,3},{2,6},{3,1},{4,0},{5,7},{6,2},{7,5},{8,12},{9,11},{10,... | collective-permute-start | bytes 3145736 | tf_op jit(solution)/shard_map/ppermute | solution.py:61
  71.4 44.8 %collective-permute-start.13 = (bf16[8,128,1024]{2,1,0:T(8,128)(2,1)S(1)}, bf16[8,128,1024]{2,1,0:T(8,128)(2,1)}, u32[]{:S(2)}, u32[]{:S(2)}) collective-permute-start(bf16[8,128,1024]{2,1,0:T(8,128)(2,1)S(1)} %pad_maximum_fusion.2.refs_0_), channel_id=1, source_target_pairs={{0,2},{1,5},{2,0},{3,7},{4,6},{5,1},{6,4},{7,3},{8,10},{9,13},{10,... | collective-permute-start | bytes 6291464 | tf_op jit(solution)/shard_map/ppermute | solution.py:61
  72.9 43.3 %collective-permute-start.16 = (bf16[4,128,1024]{2,1,0:T(8,128)(2,1)}, bf16[4,128,1024]{2,1,0:T(8,128)(2,1)}, u32[]{:S(2)}, u32[]{:S(2)}) collective-permute-start(bf16[4,128,1024]{2,1,0:T(8,128)(2,1)} %pad_maximum_fusion.11), channel_id=1, source_target_pairs={{0,4},{1,3},{2,6},{3,1},{4,0},{5,7},{6,2},{7,5},{8,12},{9,11},{10,... | collective-permute-start | bytes 3145736 | tf_op jit(solution)/shard_map/ppermute | solution.py:61
  74.5 34.6 %collective-permute-start.11 = (bf16[4,2,8,128]{3,2,0,1:T(8,128)(2,1)S(1)}, bf16[4,2,8,128]{3,2,0,1:T(8,128)(2,1)S(1)}, u32[]{:S(2)}, u32[]{:S(2)}) collective-permute-start(bf16[4,2,8,128]{3,2,0,1:T(8,128)(2,1)S(1)} %maximum_select_fusion.5), channel_id=1, source_target_pairs={{0,2},{1,3},{2,0},{3,1},{4,6},{5,7},{6,4},{7,5},{8,10},{9,11},{10,... | collective-permute-start | bytes 49160 | tf_op jit(solution)/shard_map/ppermute | solution.py:61
  75.1 41.1 %collective-permute-start.15 = (bf16[1,128,1024]{2,1,0:T(8,128)(2,1)S(1)}, bf16[1,128,1024]{2,1,0:T(8,128)(2,1)S(1)}, u32[]{:S(2)}, u32[]{:S(2)}) collective-permute-start(bf16[1,128,1024]{2,1,0:T(8,128)(2,1)S(1)} %bitcast.315), channel_id=1, source_target_pairs={{0,16},{1,17},{2,18},{3,19},{4,20},{5,21},{6,22},{7,23},{8,24},{9,... | collective-permute-start | bytes 786440 | tf_op jit(solution)/shard_map/ppermute | solution.py:61
  77.8 38.4 %collective-permute-start.14 = (bf16[2,128,1024]{2,1,0:T(8,128)(2,1)}, bf16[2,128,1024]{2,1,0:T(8,128)(2,1)}, u32[]{:S(2)}, u32[]{:S(2)}) collective-permute-start(bf16[2,128,1024]{2,1,0:T(8,128)(2,1)} %pad_maximum_fusion.19), channel_id=1, source_target_pairs={{0,8},{1,9},{2,10},{3,11},{4,12},{5,13},{6,14},{7,15},{8,0},{9,1},... | collective-permute-start | bytes 1572872 | tf_op jit(solution)/shard_map/ppermute | solution.py:61
  118.9 21.1 %collective-permute-start.20 = (bf16[4,128,1024]{2,1,0:T(8,128)(2,1)S(1)}, bf16[4,128,1024]{2,1,0:T(8,128)(2,1)S(1)}, u32[]{:S(2)}, u32[]{:S(2)}) collective-permute-start(bf16[4,128,1024]{2,1,0:T(8,128)(2,1)S(1)} %pad_maximum_fusion.12), channel_id=1, source_target_pairs={{0,4},{1,3},{2,6},{3,1},{4,0},{5,7},{6,2},{7,5},{8,12},{9,11},{10,... | collective-permute-start | bytes 3145736 | tf_op jit(solution)/shard_map/ppermute | solution.py:61
  120.4 19.6 %collective-permute-start.21 = (bf16[2,128,1024]{2,1,0:T(8,128)(2,1)}, bf16[2,128,1024]{2,1,0:T(8,128)(2,1)S(1)}, u32[]{:S(2)}, u32[]{:S(2)}) collective-permute-start(bf16[2,128,1024]{2,1,0:T(8,128)(2,1)} %pad_maximum_fusion.20), channel_id=1, source_target_pairs={{0,8},{1,9},{2,10},{3,11},{4,12},{5,13},{6,14},{7,15},{8,0},{9,1},... | collective-permute-start | bytes 1572872 | tf_op jit(solution)/shard_map/ppermute | solution.py:61
  144.4 26.0 %collective-permute-start.24 = (bf16[8,128,1024]{2,1,0:T(8,128)(2,1)S(1)}, bf16[8,128,1024]{2,1,0:T(8,128)(2,1)S(1)}, u32[]{:S(2)}, u32[]{:S(2)}) collective-permute-start(bf16[8,128,1024]{2,1,0:T(8,128)(2,1)S(1)} %pad_maximum_fusion.3.refs_0_), channel_id=1, source_target_pairs={{0,2},{1,5},{2,0},{3,7},{4,6},{5,1},{6,4},{7,3},{8,10},{9,13},{10,... | collective-permute-start | bytes 6291464 | tf_op jit(solution)/shard_map/ppermute | solution.py:61
  147.2 19.9 %collective-permute-start.23 = (bf16[512,512]{1,0:T(8,128)(2,1)S(1)}, bf16[512,512]{1,0:T(8,128)(2,1)S(1)}, u32[]{:S(2)}, u32[]{:S(2)}) collective-permute-start(bf16[512,512]{1,0:T(8,128)(2,1)S(1)} %get-tuple-element.437), channel_id=1, source_target_pairs={{0,1},{1,0},{2,3},{3,2},{4,5},{5,4},{6,7},{7,6},{8,9},{9,8},{10,11... | collective-permute-start | bytes 1572872 | tf_op jit(solution)/shard_map/ppermute | solution.py:61
  147.3 20.6 %collective-permute-start.26 = (bf16[2,128,1024]{2,1,0:T(8,128)(2,1)}, bf16[2,128,1024]{2,1,0:T(8,128)(2,1)S(1)}, u32[]{:S(2)}, u32[]{:S(2)}) collective-permute-start(bf16[2,128,1024]{2,1,0:T(8,128)(2,1)} %pad_maximum_fusion.21), channel_id=1, source_target_pairs={{0,8},{1,9},{2,10},{3,11},{4,12},{5,13},{6,14},{7,15},{8,0},{9,1},... | collective-permute-start | bytes 1572872 | tf_op jit(solution)/shard_map/ppermute | solution.py:61
  176.5 35.1 %collective-permute-start.33 = (bf16[2,128,1024]{2,1,0:T(8,128)(2,1)}, bf16[2,128,1024]{2,1,0:T(8,128)(2,1)S(1)}, u32[]{:S(2)}, u32[]{:S(2)}) collective-permute-start(bf16[2,128,1024]{2,1,0:T(8,128)(2,1)} %pad_maximum_fusion.22), channel_id=1, source_target_pairs={{0,8},{1,9},{2,10},{3,11},{4,12},{5,13},{6,14},{7,15},{8,0},{9,1},... | collective-permute-start | bytes 1572872 | tf_op jit(solution)/shard_map/ppermute | solution.py:61
  178.9 34.8 %collective-permute-start.32 = (bf16[4,128,1024]{2,1,0:T(8,128)(2,1)}, bf16[4,128,1024]{2,1,0:T(8,128)(2,1)}, u32[]{:S(2)}, u32[]{:S(2)}) collective-permute-start(bf16[4,128,1024]{2,1,0:T(8,128)(2,1)} %pad_maximum_fusion.13), channel_id=1, source_target_pairs={{0,4},{1,3},{2,6},{3,1},{4,0},{5,7},{6,2},{7,5},{8,12},{9,11},{10,... | collective-permute-start | bytes 3145736 | tf_op jit(solution)/shard_map/ppermute | solution.py:61
  180.5 35.2 %collective-permute-start.31 = (bf16[8,128,1024]{2,1,0:T(8,128)(2,1)S(1)}, bf16[8,128,1024]{2,1,0:T(8,128)(2,1)}, u32[]{:S(2)}, u32[]{:S(2)}) collective-permute-start(bf16[8,128,1024]{2,1,0:T(8,128)(2,1)S(1)} %pad_maximum_fusion.4.refs_0_), channel_id=1, source_target_pairs={{0,2},{1,5},{2,0},{3,7},{4,6},{5,1},{6,4},{7,3},{8,10},{9,13},{10,... | collective-permute-start | bytes 6291464 | tf_op jit(solution)/shard_map/ppermute | solution.py:61
  191.8 19.8 %collective-permute-start.29 = (bf16[512,512]{1,0:T(8,128)(2,1)S(1)}, bf16[512,512]{1,0:T(8,128)(2,1)S(1)}, u32[]{:S(2)}, u32[]{:S(2)}) collective-permute-start(bf16[512,512]{1,0:T(8,128)(2,1)S(1)} %get-tuple-element.464), channel_id=1, source_target_pairs={{0,1},{1,0},{2,3},{3,2},{4,5},{5,4},{6,7},{7,6},{8,9},{9,8},{10,11... | collective-permute-start | bytes 1572872 | tf_op jit(solution)/shard_map/ppermute | solution.py:61
  191.8 20.6 %collective-permute-start.30 = (bf16[512,512]{1,0:T(8,128)(2,1)S(1)}, bf16[512,512]{1,0:T(8,128)(2,1)S(1)}, u32[]{:S(2)}, u32[]{:S(2)}) collective-permute-start(bf16[512,512]{1,0:T(8,128)(2,1)S(1)} %get-tuple-element.466), channel_id=1, source_target_pairs={{0,1},{1,0},{2,3},{3,2},{4,5},{5,4},{6,7},{7,6},{8,9},{9,8},{10,11... | collective-permute-start | bytes 1572872 | tf_op jit(solution)/shard_map/ppermute | solution.py:61
  218.6 27.9 %collective-permute-start.36 = (bf16[512,4096]{1,0:T(8,128)(2,1)S(1)}, bf16[512,4096]{1,0:T(8,128)(2,1)}, u32[]{:S(2)}, u32[]{:S(2)}) collective-permute-start(bf16[512,4096]{1,0:T(8,128)(2,1)S(1)} %get-tuple-element.478.rows_ref.refs_0_.refs_1_), channel_id=1, source_target_pairs={{0,1},{1,0},{2,3},{3,2},{4,5},{5,4},{6,7},{7,6},{8,9},{9,8},{10,11... | collective-permute-start | bytes 12582920 | tf_op jit(solution)/shard_map/ppermute | solution.py:61
  219.4 28.9 %collective-permute-start.37 = (bf16[8,128,1024]{2,1,0:T(8,128)(2,1)}, bf16[8,128,1024]{2,1,0:T(8,128)(2,1)}, u32[]{:S(2)}, u32[]{:S(2)}) collective-permute-start(bf16[8,128,1024]{2,1,0:T(8,128)(2,1)} %pad_maximum_fusion.5.refs_0_), channel_id=1, source_target_pairs={{0,2},{1,5},{2,0},{3,7},{4,6},{5,1},{6,4},{7,3},{8,10},{9,13},{10,... | collective-permute-start | bytes 6291464 | tf_op jit(solution)/shard_map/ppermute | solution.py:61
  249.7 20.3 %collective-permute-start.40 = (bf16[4,128,1024]{2,1,0:T(8,128)(2,1)S(1)}, bf16[4,128,1024]{2,1,0:T(8,128)(2,1)S(1)}, u32[]{:S(2)}, u32[]{:S(2)}) collective-permute-start(bf16[4,128,1024]{2,1,0:T(8,128)(2,1)S(1)} %pad_maximum_fusion.14), channel_id=1, source_target_pairs={{0,4},{1,3},{2,6},{3,1},{4,0},{5,7},{6,2},{7,5},{8,12},{9,11},{10,... | collective-permute-start | bytes 3145736 | tf_op jit(solution)/shard_map/ppermute | solution.py:61
  270.6 26.1 %collective-permute-start.43 = (bf16[8,128,1024]{2,1,0:T(8,128)(2,1)S(1)}, bf16[8,128,1024]{2,1,0:T(8,128)(2,1)}, u32[]{:S(2)}, u32[]{:S(2)}) collective-permute-start(bf16[8,128,1024]{2,1,0:T(8,128)(2,1)S(1)} %pad_maximum_fusion.6.refs_0_), channel_id=1, source_target_pairs={{0,2},{1,5},{2,0},{3,7},{4,6},{5,1},{6,4},{7,3},{8,10},{9,13},{10,... | collective-permute-start | bytes 6291464 | tf_op jit(solution)/shard_map/ppermute | solution.py:61
  299.6 18.9 %collective-permute-start.45 = (bf16[8,128,1024]{2,1,0:T(8,128)(2,1)S(1)}, bf16[8,128,1024]{2,1,0:T(8,128)(2,1)}, u32[]{:S(2)}, u32[]{:S(2)}) collective-permute-start(bf16[8,128,1024]{2,1,0:T(8,128)(2,1)S(1)} %pad_maximum_fusion.6.refs_0_), channel_id=1, source_target_pairs={{0,1},{1,0},{2,3},{3,2},{4,5},{5,4},{6,7},{7,6},{8,9},{9,8},{10,11... | collective-permute-start | bytes 6291464 | tf_op jit(solution)/shard_map/ppermute | solution.py:61
  299.6 18.9 %collective-permute-start.46 = (bf16[8,128,1024]{2,1,0:T(8,128)(2,1)}, bf16[8,128,1024]{2,1,0:T(8,128)(2,1)}, u32[]{:S(2)}, u32[]{:S(2)}) collective-permute-start(bf16[8,128,1024]{2,1,0:T(8,128)(2,1)} %collective-permute-done.43.refs_1_), channel_id=1, source_target_pairs={{0,1},{1,0},{2,3},{3,2},{4,5},{5,4},{6,7},{7,6},{8,9},{9,8},{10,11... | collective-permute-start | bytes 6291464 | tf_op jit(solution)/shard_map/ppermute | solution.py:61
  313.1 26.2 %collective-permute-start.49 = (bf16[8,128,1024]{2,1,0:T(8,128)(2,1)S(1)}, bf16[8,128,1024]{2,1,0:T(8,128)(2,1)}, u32[]{:S(2)}, u32[]{:S(2)}) collective-permute-start(bf16[8,128,1024]{2,1,0:T(8,128)(2,1)S(1)} %pad_maximum_fusion.7.refs_0_), channel_id=1, source_target_pairs={{0,2},{1,5},{2,0},{3,7},{4,6},{5,1},{6,4},{7,3},{8,10},{9,13},{10,... | collective-permute-start | bytes 6291464 | tf_op jit(solution)/shard_map/ppermute | solution.py:61
  318.0 18.9 %collective-permute-start.47 = (bf16[512,512]{1,0:T(8,128)(2,1)S(1)}, bf16[512,512]{1,0:T(8,128)(2,1)S(1)}, u32[]{:S(2)}, u32[]{:S(2)}) collective-permute-start(bf16[512,512]{1,0:T(8,128)(2,1)S(1)} %get-tuple-element.527), channel_id=1, source_target_pairs={{0,1},{1,0},{2,3},{3,2},{4,5},{5,4},{6,7},{7,6},{8,9},{9,8},{10,11... | collective-permute-start | bytes 1572872 | tf_op jit(solution)/shard_map/ppermute | solution.py:61
  318.1 18.8 %collective-permute-start.48 = (bf16[512,512]{1,0:T(8,128)(2,1)S(1)}, bf16[512,512]{1,0:T(8,128)(2,1)S(1)}, u32[]{:S(2)}, u32[]{:S(2)}) collective-permute-start(bf16[512,512]{1,0:T(8,128)(2,1)S(1)} %get-tuple-element.529), channel_id=1, source_target_pairs={{0,1},{1,0},{2,3},{3,2},{4,5},{5,4},{6,7},{7,6},{8,9},{9,8},{10,11... | collective-permute-start | bytes 1572872 | tf_op jit(solution)/shard_map/ppermute | solution.py:61
  339.3 27.9 %collective-permute-start.52 = (bf16[512,4096]{1,0:T(8,128)(2,1)S(1)}, bf16[512,4096]{1,0:T(8,128)(2,1)}, u32[]{:S(2)}, u32[]{:S(2)}) collective-permute-start(bf16[512,4096]{1,0:T(8,128)(2,1)S(1)} %get-tuple-element.538.rows_ref.refs_0_.refs_1_), channel_id=1, source_target_pairs={{0,1},{1,0},{2,3},{3,2},{4,5},{5,4},{6,7},{7,6},{8,9},{9,8},{10,11... | collective-permute-start | bytes 12582920 | tf_op jit(solution)/shard_map/ppermute | solution.py:61
  383.8 33.8 %collective-permute-start.55 = (bf16[512,4096]{1,0:T(8,128)(2,1)}, bf16[512,4096]{1,0:T(8,128)(2,1)}, u32[]{:S(2)}, u32[]{:S(2)}) collective-permute-start(bf16[512,4096]{1,0:T(8,128)(2,1)} %get-tuple-element.564.rows_ref.refs_2_), channel_id=1, source_target_pairs={{0,1},{1,0},{2,3},{3,2},{4,5},{5,4},{6,7},{7,6},{8,9},{9,8},{10,11... | collective-permute-start | bytes 12582920 | tf_op jit(solution)/shard_map/ppermute | solution.py:61
  403.4 26.1 %collective-permute-start.57 = (bf16[1024,1024]{1,0:T(8,128)(2,1)S(1)}, bf16[1024,1024]{1,0:T(8,128)(2,1)}, u32[]{:S(2)}, u32[]{:S(2)}) collective-permute-start(bf16[1024,1024]{1,0:T(8,128)(2,1)S(1)} %get-tuple-element.570), channel_id=1, source_target_pairs={{0,2},{1,5},{2,0},{3,7},{4,6},{5,1},{6,4},{7,3},{8,10},{9,13},{10,... | collective-permute-start | bytes 6291464 | tf_op jit(solution)/shard_map/ppermute | solution.py:61
  429.5 32.0 %collective-permute-start.58 = (bf16[256,5120]{1,0:T(8,128)(2,1)}, bf16[256,5120]{1,0:T(8,128)(2,1)}, u32[]{:S(2)}, u32[]{:S(2)}) collective-permute-start(bf16[256,5120]{1,0:T(8,128)(2,1)} %get-tuple-element.577), channel_id=1, source_target_pairs={{0,2},{1,5},{2,0},{3,7},{4,6},{5,1},{6,4},{7,3},{8,10},{9,13},{10,... | collective-permute-start | bytes 7864328 | tf_op jit(solution)/shard_map/ppermute | solution.py:61
  513.9 23.9 %collective-permute-start.65 = (bf16[256,3072]{1,0:T(8,128)(2,1)S(1)}, bf16[256,3072]{1,0:T(8,128)(2,1)}, u32[]{:S(2)}, u32[]{:S(2)}) collective-permute-start(bf16[256,3072]{1,0:T(8,128)(2,1)S(1)} %copy-done.70), channel_id=1, source_target_pairs={{0,2},{1,5},{2,0},{3,7},{4,6},{5,1},{6,4},{7,3},{8,10},{9,13},{10,... | collective-permute-start | bytes 4718600 | tf_op jit(solution)/shard_map/ppermute | solution.py:61
  514.8 23.0 %collective-permute-start.66 = (bf16[64,5120]{1,0:T(8,128)(2,1)}, bf16[64,5120]{1,0:T(8,128)(2,1)S(1)}, u32[]{:S(2)}, u32[]{:S(2)}) collective-permute-start(bf16[64,5120]{1,0:T(8,128)(2,1)} %get-tuple-element.621), channel_id=1, source_target_pairs={{0,8},{1,9},{2,10},{3,11},{4,12},{5,13},{6,14},{7,15},{8,0},{9,1},... | collective-permute-start | bytes 1966088 | tf_op jit(solution)/shard_map/ppermute | solution.py:61
  515.1 20.5 %collective-permute-start.67 = (bf16[128,1024]{1,0:T(8,128)(2,1)S(1)}, bf16[128,1024]{1,0:T(8,128)(2,1)S(1)}, u32[]{:S(2)}, u32[]{:S(2)}) collective-permute-start(bf16[128,1024]{1,0:T(8,128)(2,1)S(1)} %add_convert_fusion.29), channel_id=1, source_target_pairs={{0,16},{1,17},{2,18},{3,19},{4,20},{5,21},{6,22},{7,23},{8,24},{9,... | collective-permute-start | bytes 786440 | tf_op jit(solution)/shard_map/ppermute | solution.py:61
  517.5 40.9 %collective-permute-start.68 = (bf16[512,4096]{1,0:T(8,128)(2,1)S(1)}, bf16[512,4096]{1,0:T(8,128)(2,1)}, u32[]{:S(2)}, u32[]{:S(2)}) collective-permute-start(bf16[512,4096]{1,0:T(8,128)(2,1)S(1)} %get-tuple-element.634.rows_ref.refs_2_), channel_id=1, source_target_pairs={{0,1},{1,0},{2,3},{3,2},{4,5},{5,4},{6,7},{7,6},{8,9},{9,8},{10,11... | collective-permute-start | bytes 12582920 | tf_op jit(solution)/shard_map/ppermute | solution.py:61
  541.7 34.8 %collective-permute-start.72 = (bf16[1024,1024]{1,0:T(8,128)(2,1)}, bf16[1024,1024]{1,0:T(8,128)(2,1)}, u32[]{:S(2)}, u32[]{:S(2)}) collective-permute-start(bf16[1024,1024]{1,0:T(8,128)(2,1)} %get-tuple-element.642), channel_id=1, source_target_pairs={{0,2},{1,5},{2,0},{3,7},{4,6},{5,1},{6,4},{7,3},{8,10},{9,13},{10,... | collective-permute-start | bytes 6291464 | tf_op jit(solution)/shard_map/ppermute | solution.py:61
  555.2 20.0 %collective-permute-start.70 = (bf16[128,3072]{1,0:T(8,128)(2,1)}, bf16[128,3072]{1,0:T(8,128)(2,1)S(1)}, u32[]{:S(2)}, u32[]{:S(2)}) collective-permute-start(bf16[128,3072]{1,0:T(8,128)(2,1)} %get-tuple-element.640), channel_id=1, source_target_pairs={{0,4},{1,3},{2,6},{3,1},{4,0},{5,7},{6,2},{7,5},{8,12},{9,11},{10,... | collective-permute-start | bytes 2359304 | tf_op jit(solution)/shard_map/ppermute | solution.py:61
  555.6 18.2 %collective-permute-start.71 = (bf16[32,5120]{1,0:T(8,128)(2,1)S(1)}, bf16[32,5120]{1,0:T(8,128)(2,1)S(1)}, u32[]{:S(2)}, u32[]{:S(2)}) collective-permute-start(bf16[32,5120]{1,0:T(8,128)(2,1)S(1)} %add_convert_fusion.27), channel_id=1, source_target_pairs={{0,16},{1,17},{2,18},{3,19},{4,20},{5,21},{6,22},{7,23},{8,24},{9,... | collective-permute-start | bytes 983048 | tf_op jit(solution)/shard_map/ppermute | solution.py:61
  576.8 31.9 %collective-permute-start.73 = (bf16[256,5120]{1,0:T(8,128)(2,1)}, bf16[256,5120]{1,0:T(8,128)(2,1)S(1)}, u32[]{:S(2)}, u32[]{:S(2)}) collective-permute-start(bf16[256,5120]{1,0:T(8,128)(2,1)} %get-tuple-element.650), channel_id=1, source_target_pairs={{0,2},{1,5},{2,0},{3,7},{4,6},{5,1},{6,4},{7,3},{8,10},{9,13},{10,... | collective-permute-start | bytes 7864328 | tf_op jit(solution)/shard_map/ppermute | solution.py:61
  578.1 25.9 %collective-permute-start.74 = (bf16[64,3072]{1,0:T(8,128)(2,1)S(1)}, bf16[64,3072]{1,0:T(8,128)(2,1)S(1)}, u32[]{:S(2)}, u32[]{:S(2)}) collective-permute-start(bf16[64,3072]{1,0:T(8,128)(2,1)S(1)} %get-tuple-element.651), channel_id=1, source_target_pairs={{0,8},{1,9},{2,10},{3,11},{4,12},{5,13},{6,14},{7,15},{8,0},{9,1},... | collective-permute-start | bytes 1179656 | tf_op jit(solution)/shard_map/ppermute | solution.py:61
  619.7 29.2 %collective-permute-start.78 = (bf16[128,5120]{1,0:T(8,128)(2,1)}, bf16[128,5120]{1,0:T(8,128)(2,1)S(1)}, u32[]{:S(2)}, u32[]{:S(2)}) collective-permute-start(bf16[128,5120]{1,0:T(8,128)(2,1)} %get-tuple-element.667), channel_id=1, source_target_pairs={{0,4},{1,3},{2,6},{3,1},{4,0},{5,7},{6,2},{7,5},{8,12},{9,11},{10,... | collective-permute-start | bytes 3932168 | tf_op jit(solution)/shard_map/ppermute | solution.py:61
  620.1 28.8 %collective-permute-start.77 = (bf16[512,1024]{1,0:T(8,128)(2,1)}, bf16[512,1024]{1,0:T(8,128)(2,1)}, u32[]{:S(2)}, u32[]{:S(2)}) collective-permute-start(bf16[512,1024]{1,0:T(8,128)(2,1)} %get-tuple-element.666), channel_id=1, source_target_pairs={{0,4},{1,3},{2,6},{3,1},{4,0},{5,7},{6,2},{7,5},{8,12},{9,11},{10,... | collective-permute-start | bytes 3145736 | tf_op jit(solution)/shard_map/ppermute | solution.py:61
  652.5 35.5 %collective-permute-start.79 = (bf16[256,3072]{1,0:T(8,128)(2,1)}, bf16[256,3072]{1,0:T(8,128)(2,1)}, u32[]{:S(2)}, u32[]{:S(2)}) collective-permute-start(bf16[256,3072]{1,0:T(8,128)(2,1)} %get-tuple-element.674), channel_id=1, source_target_pairs={{0,2},{1,5},{2,0},{3,7},{4,6},{5,1},{6,4},{7,3},{8,10},{9,13},{10,... | collective-permute-start | bytes 4718600 | tf_op jit(solution)/shard_map/ppermute | solution.py:61
  655.0 19.3 %collective-permute-start.80 = (bf16[256,1024]{1,0:T(8,128)(2,1)}, bf16[256,1024]{1,0:T(8,128)(2,1)}, u32[]{:S(2)}, u32[]{:S(2)}) collective-permute-start(bf16[256,1024]{1,0:T(8,128)(2,1)} %get-tuple-element.675), channel_id=1, source_target_pairs={{0,8},{1,9},{2,10},{3,11},{4,12},{5,13},{6,14},{7,15},{8,0},{9,1},... | collective-permute-start | bytes 1572872 | tf_op jit(solution)/shard_map/ppermute | solution.py:61
  656.3 31.6 %collective-permute-start.81 = (bf16[64,5120]{1,0:T(8,128)(2,1)}, bf16[64,5120]{1,0:T(8,128)(2,1)}, u32[]{:S(2)}, u32[]{:S(2)}) collective-permute-start(bf16[64,5120]{1,0:T(8,128)(2,1)} %get-tuple-element.676), channel_id=1, source_target_pairs={{0,8},{1,9},{2,10},{3,11},{4,12},{5,13},{6,14},{7,15},{8,0},{9,1},... | collective-permute-start | bytes 1966088 | tf_op jit(solution)/shard_map/ppermute | solution.py:61
  658.0 35.2 %collective-permute-start.92 = (bf16[32,3072]{1,0:T(8,128)(2,1)}, bf16[32,3072]{1,0:T(8,128)(2,1)}, u32[]{:S(2)}, u32[]{:S(2)}) collective-permute-start(bf16[32,3072]{1,0:T(8,128)(2,1)} %add_convert_fusion.31), channel_id=1, source_target_pairs={{0,16},{1,17},{2,18},{3,19},{4,20},{5,21},{6,22},{7,23},{8,24},{9,... | collective-permute-start | bytes 589832 | tf_op jit(solution)/shard_map/ppermute | solution.py:61
  692.7 29.0 %collective-permute-start.83 = (bf16[128,3072]{1,0:T(8,128)(2,1)S(1)}, bf16[128,3072]{1,0:T(8,128)(2,1)S(1)}, u32[]{:S(2)}, u32[]{:S(2)}) collective-permute-start(bf16[128,3072]{1,0:T(8,128)(2,1)S(1)} %get-tuple-element.689), channel_id=1, source_target_pairs={{0,4},{1,3},{2,6},{3,1},{4,0},{5,7},{6,2},{7,5},{8,12},{9,11},{10,... | collective-permute-start | bytes 2359304 | tf_op jit(solution)/shard_map/ppermute | solution.py:61
  694.2 20.5 %collective-permute-start.85 = (bf16[128,1024]{1,0:T(8,128)(2,1)S(1)}, bf16[128,1024]{1,0:T(8,128)(2,1)S(1)}, u32[]{:S(2)}, u32[]{:S(2)}) collective-permute-start(bf16[128,1024]{1,0:T(8,128)(2,1)S(1)} %add_convert_fusion.28), channel_id=1, source_target_pairs={{0,16},{1,17},{2,18},{3,19},{4,20},{5,21},{6,22},{7,23},{8,24},{9,... | collective-permute-start | bytes 786440 | tf_op jit(solution)/shard_map/ppermute | solution.py:61
  694.5 27.1 %collective-permute-start.86 = (bf16[32,5120]{1,0:T(8,128)(2,1)S(1)}, bf16[32,5120]{1,0:T(8,128)(2,1)S(1)}, u32[]{:S(2)}, u32[]{:S(2)}) collective-permute-start(bf16[32,5120]{1,0:T(8,128)(2,1)S(1)} %add_convert_fusion.26), channel_id=1, source_target_pairs={{0,16},{1,17},{2,18},{3,19},{4,20},{5,21},{6,22},{7,23},{8,24},{9,... | collective-permute-start | bytes 983048 | tf_op jit(solution)/shard_map/ppermute | solution.py:61
  (197 other events, 1820.2 us)

commit v4 on v3

--- a/solution.py
+++ b/solution.py
@@ -55,6 +55,8 @@
 TO_NEAR = pairs(lambda z, y, x, c: (z, 1 - y if c == 0 else y, x if c == 0 else 1 - x, c))
 TO_ODD = pairs(lambda z, y, x, c: (z ^ 1, y, x, c))
 TO_PAIR = pairs(lambda z, y, x, c: (z ^ 2, y, x, c))
+TO_BOTH = pairs(lambda z, y, x, c: (z ^ 3, y, x, c))
+TO_Z = [pairs(lambda z, y, x, c, k=k: ((z + k) % 4, y, x, c)) for k in range(4)]
 
 
 def send(value, to):
@@ -139,9 +141,10 @@
             return [(self.kept, TO_PAIR)]
         if self.step < 5:
             self.kept = jnp.concatenate([got[0], self.kept])
-            return [(self.kept, (TO_ODD, TO_NEAR, TO_FAR)[self.step - 2])]
-        self.kept = [self.kept, got[0]]
-        return [(blocks, TO_CORE) for blocks in self.kept]
+            sends = [(self.kept, (TO_ODD, TO_NEAR, TO_FAR)[self.step - 2])]
+            return sends + [(self.kept, TO_CORE)] * (self.step == 4)
+        self.kept = [self.kept, *got]
+        return [(got[0], TO_CORE)]
 
     def result(self):
         width = self.pack.shape[1]
@@ -169,9 +172,13 @@
         )
 
 
+FAR_FIRST = (TO_FAR, TO_NEAR, TO_ODD, TO_PAIR)
+Z_FIRST = (TO_ODD, TO_PAIR, TO_FAR, TO_NEAR)
+
+
 class SumUnit:
-    def __init__(self, parts):
-        self.flight, self.step = list(parts), 0
+    def __init__(self, parts, route=FAR_FIRST):
+        self.flight, self.step, self.route = list(parts), 0, route
 
     def local(self, got):
         self.step += 1
@@ -187,23 +194,39 @@
         else:
             self.kept = self.kept + got[0].astype(f32)
             return []
-        return [(leaving, (TO_FAR, TO_NEAR, TO_ODD, TO_PAIR)[self.step - 1])]
+        return [(leaving, self.route[self.step - 1])]
 
 
 Sums = collections.namedtuple("Sums", "o i a")
 
 
-def block_order(coords):
+class SmallUnit(SumUnit):
+    def local(self, got):
+        if self.step < 2:
+            return super().local(got)
+        self.step += 1
+        if self.step > 3:
+            self.kept = self.kept + sum(value.astype(f32) for value in got)
+            return []
+        rows = self.kept.shape[0] // 4
+        total = self.kept.astype(f32) + got[0].astype(f32)
+        blocks = [total[n * rows : (n + 1) * rows] for n in range(4)]
+        self.kept = blocks[3]
+        return [(b.astype(bf16), to) for b, to in zip(blocks, (TO_BOTH, TO_ODD, TO_PAIR))]
+
+
+def block_order(coords, z_first=False):
     z, y, x, c = coords[0], coords[1], coords[2], coords[3]
     order = []
     for core in (c, 1 - c):
-        for far in (1, 0):
-            for near in (1, 0):
+        for first in range(4):
+            for second in range(4):
+                across, along = (second, first) if z_first else (first, second)
+                far, near = 1 - across // 2, 1 - across % 2
+                odd, pair = 1 - along // 2, 1 - along % 2
                 y2 = y ^ jnp.where(core == 0, near, far)
                 x2 = x ^ jnp.where(core == 0, far, near)
-                for odd in (1, 0):
-                    for pair in (1, 0):
-                        order.append((z ^ odd ^ (2 * pair)) * 8 + y2 * 4 + x2 * 2 + core)
+                order.append((z ^ odd ^ (2 * pair)) * 8 + y2 * 4 + x2 * 2 + core)
     return jnp.stack(order).astype(jnp.int32)
 
 
@@ -270,10 +293,10 @@
     )(*args)
 
 
-def wide_terms_of(order, left, right):
+def wide_terms_of(order, left, right, part=0, parts=1):
     tokens, width = left[0].shape
     block = width // 32
-    columns = right[0].shape[1]
+    columns = right[0].shape[1] // parts
 
     def kernel(order_ref, *refs):
         a1, a2, (b1, b2, leaving, kept) = refs[:2], refs[2:4], refs[4:]
@@ -293,7 +316,7 @@
             kept[...] = total
 
     cut = lambda n: pl.BlockSpec((tokens, block), lambda j, order: (0, order[2 * j + n]))
-    whole = pl.BlockSpec((tokens, columns), lambda j, order: (0, 0))
+    whole = pl.BlockSpec((tokens, columns), lambda j, order: (0, part))
     out = jax.ShapeDtypeStruct((width // 4, columns), bf16)
     return pl.pallas_call(
         kernel,
@@ -313,13 +336,17 @@
 
 
 BLOCK = 256
-WINDOW = 3 * BLOCK
+WINDOWS = (2 * BLOCK, 3 * BLOCK)
 PAIR = 2 * HEAD_DIM
 
 
-def window_start(s, slot):
-    block = s ^ (2 * slot)
-    return jnp.clip(block - 1, 0, 1) * BLOCK
+def query_starts(s):
+    edge = (s // 2) ^ (s % 2)
+    return edge * BLOCK, (1 - edge) * BLOCK
+
+
+def window_starts(s):
+    return (s % 2) * (2 * BLOCK), (1 - s % 2) * BLOCK
 
 
 def nt_dot(left, right):
@@ -337,40 +364,46 @@
             scratch[pl.ds((s ^ (n + 2 * slot)) * BLOCK, BLOCK), :] = ref[slot * BLOCK : (slot + 1) * BLOCK, :]
 
 
+def attention_views(s):
+    rows = [pl.ds(pl.multiple_of(start, BLOCK), BLOCK) for start in query_starts(s)]
+    windows = [pl.ds(pl.multiple_of(start, BLOCK), width) for start, width in zip(window_starts(s), WINDOWS)]
+    spans = [slice(h * HEAD_DIM, (h + 1) * HEAD_DIM) for h in range(2)]
+    return rows, windows, spans, [slice(n * BLOCK, (n + 1) * BLOCK) for n in range(2)]
+
+
 def attend_forward_kernel(
-    s_ref, q_ref, km_ref, ko_ref, vm_ref, vo_ref, bias_ref, mixed_ref, total_ref, keys, values
+    s_ref, q_ref, km_ref, ko_ref, vm_ref, vo_ref, edge_ref, inner_ref, mixed_ref, total_ref, keys, values
 ):
     s = s_ref[0]
     in_order(s, km_ref, ko_ref, keys)
     in_order(s, vm_ref, vo_ref, values)
-    spans = [slice(h * HEAD_DIM, (h + 1) * HEAD_DIM) for h in range(2)]
-    rows = [slice(n * BLOCK, (n + 1) * BLOCK) for n in range(2)]
-    windows = [pl.ds(pl.multiple_of(window_start(s, n), BLOCK), WINDOW) for n in range(2)]
+    rows, windows, spans, kinds = attention_views(s)
+    biases = (edge_ref, inner_ref)
     scores = []
-    for slot in range(2):
-        q = q_ref[rows[slot], :] * jnp.asarray(HEAD_DIM**-0.5, bf16)
-        k = keys[windows[slot], :]
+    for n in range(2):
+        q = q_ref[rows[n], :] * jnp.asarray(HEAD_DIM**-0.5, bf16)
+        k = keys[windows[n], :]
         scores += [nt_dot(k, only_head(q, head, 1)) for head in range(2)]
     raised, totals = [], []
-    for n in range(4):
-        slot, head = divmod(n, 2)
-        biased = scores[n] + bias_ref[slot]
+    for m in range(4):
+        n, head = divmod(m, 2)
+        biased = scores[m] + biases[n][...]
         top = jnp.max(biased, axis=0, keepdims=True)
         up = jnp.exp(biased - top)
         totals.append(jnp.sum(up, axis=0, keepdims=True))
-        total_ref[0, head : head + 1, rows[slot]] = top + jnp.log(totals[n])
+        total_ref[0, head : head + 1, kinds[n]] = top + jnp.log(totals[m])
         raised.append(up.astype(bf16))
-    for slot in range(2):
-        v_t = values[windows[slot], :].T
+    for n in range(2):
+        v_t = values[windows[n], :].T
         halves = [
-            jnp.dot(v_t[spans[h]], raised[2 * slot + h], preferred_element_type=f32) / totals[2 * slot + h]
+            jnp.dot(v_t[spans[h]], raised[2 * n + h], preferred_element_type=f32) / totals[2 * n + h]
             for h in range(2)
         ]
-        mixed_ref[rows[slot], :] = jnp.concatenate(halves, axis=0).T.astype(bf16)
+        mixed_ref[rows[n], :] = jnp.concatenate(halves, axis=0).T.astype(bf16)
 
 
 def attend_backward_kernel(
-    s_ref, q_ref, km_ref, ko_ref, vm_ref, vo_ref, bias_ref, mixed_ref, total_ref, grad_ref,
+    s_ref, q_ref, km_ref, ko_ref, vm_ref, vo_ref, edge_ref, inner_ref, mixed_ref, total_ref, grad_ref,
     dq_ref, mine_ref, sent_ref, keys, values, key_sum, value_sum,
 ):
     s = s_ref[0]
@@ -378,15 +411,14 @@
     in_order(s, vm_ref, vo_ref, values)
     key_sum[...] = jnp.zeros_like(key_sum)
     value_sum[...] = jnp.zeros_like(value_sum)
-    spans = [slice(h * HEAD_DIM, (h + 1) * HEAD_DIM) for h in range(2)]
-    rows = [slice(n * BLOCK, (n + 1) * BLOCK) for n in range(2)]
-    windows = [pl.ds(pl.multiple_of(window_start(s, n), BLOCK), WINDOW) for n in range(2)]
+    rows, windows, spans, kinds = attention_views(s)
+    biases = (edge_ref, inner_ref)
     scores, share_grads, queries, grads, inner = [], [], [], [], []
-    for slot in range(2):
-        q = q_ref[rows[slot], :] * jnp.asarray(HEAD_DIM**-0.5, bf16)
-        g = grad_ref[rows[slot], :]
-        along = (g.astype(f32) * mixed_ref[rows[slot], :].astype(f32)).T
-        k, v = keys[windows[slot], :], values[windows[slot], :]
+    for n in range(2):
+        q = q_ref[rows[n], :] * jnp.asarray(HEAD_DIM**-0.5, bf16)
+        g = grad_ref[rows[n], :]
+        along = (g.astype(f32) * mixed_ref[rows[n], :].astype(f32)).T
+        k, v = keys[windows[n], :], values[windows[n], :]
         for head in range(2):
             queries.append(only_head(q, head, 1))
             grads.append(only_head(g, head, 1))
@@ -394,29 +426,24 @@
             scores.append(nt_dot(k, queries[-1]))
             share_grads.append(nt_dot(v, grads[-1]))
     shares_low, grads_low = [], []
-    for n in range(4):
-        slot, head = divmod(n, 2)
-        shares = jnp.exp(scores[n] + bias_ref[slot] - total_ref[0, head : head + 1, rows[slot]])
+    for m in range(4):
+        n, head = divmod(m, 2)
+        shares = jnp.exp(scores[m] + biases[n][...] - total_ref[0, head : head + 1, kinds[n]])
         shares_low.append(shares.astype(bf16))
-        grads_low.append((shares * (share_grads[n] - inner[n])).astype(bf16))
-    both = lambda values, slot, axis: jnp.concatenate(values[2 * slot : 2 * slot + 2], axis=axis)
+        grads_low.append((shares * (share_grads[m] - inner[m])).astype(bf16))
+    both = lambda values, n, axis: jnp.concatenate(values[2 * n : 2 * n + 2], axis=axis)
+    for n in range(2):
+        k_t = keys[windows[n], :].T
+        query_grads = [jnp.dot(k_t[spans[h]], grads_low[2 * n + h], preferred_element_type=f32) for h in range(2)]
+        dq_ref[rows[n], :] = (jnp.concatenate(query_grads, axis=0).T * HEAD_DIM**-0.5).astype(bf16)
+        key_sum[windows[n], :] += jnp.dot(both(grads_low, n, 1), both(queries, n, 0), preferred_element_type=f32)
+        value_sum[windows[n], :] += jnp.dot(both(shares_low, n, 1), both(grads, n, 0), preferred_element_type=f32)
     for slot in range(2):
-        k_t = keys[windows[slot], :].T
-        query_grads = [
-            jnp.dot(k_t[spans[h]], grads_low[2 * slot + h], preferred_element_type=f32) for h in range(2)
-        ]
-        dq_ref[rows[slot], :] = (jnp.concatenate(query_grads, axis=0).T * HEAD_DIM**-0.5).astype(bf16)
-        key_sum[windows[slot], :] += jnp.dot(
-            both(grads_low, slot, 1), both(queries, slot, 0), preferred_element_type=f32
-        )
-        value_sum[windows[slot], :] += jnp.dot(
-            both(shares_low, slot, 1), both(grads, slot, 0), preferred_element_type=f32
-        )
-    for slot in range(2):
+        here = slice(slot * BLOCK, (slot + 1) * BLOCK)
         mine, other = pl.ds((s ^ (2 * slot)) * BLOCK, BLOCK), pl.ds((s ^ (1 + 2 * slot)) * BLOCK, BLOCK)
         for n, sums in ((0, key_sum), (1, value_sum)):
-            mine_ref[n, rows[slot], :] = sums[mine, :]
-            sent_ref[n, rows[slot], :] = sums[other, :].astype(bf16)
+            mine_ref[n, here, :] = sums[mine, :]
+            sent_ref[n, here, :] = sums[other, :].astype(bf16)
 
 
 def call_attention(kernel, s, own, other, bias, kept, outs, scratch):
@@ -425,9 +452,9 @@
     cut = third(0)
     double = pl.BlockSpec((2, 2 * BLOCK, PAIR), lambda h: (0, 0, h))
     per_pair = pl.BlockSpec((1, 2, 2 * BLOCK), lambda h: (h, 0, 0))
-    whole = pl.BlockSpec(bias.shape, lambda h: (0, 0, 0))
-    in_specs = [pl.BlockSpec(memory_space=pltpu.SMEM), third(0), third(1), third(1), third(2), third(2), whole]
-    args = [s, own, own, other, own, other, bias]
+    whole = [pl.BlockSpec(b.shape, lambda h: (0, 0)) for b in bias]
+    in_specs = [pl.BlockSpec(memory_space=pltpu.SMEM), third(0), third(1), third(1), third(2), third(2), *whole]
+    args = [s, own, own, other, own, other, *bias]
     if kept:
         in_specs += [cut, per_pair, cut]
         args += kept
@@ -467,11 +494,12 @@
 
 def window_bias(s, ids):
     out = []
-    for slot in range(2):
-        keys = lax.dynamic_slice_in_dim(ids, window_start(s, slot), WINDOW)
-        queries = lax.dynamic_slice_in_dim(ids, (s ^ (2 * slot)) * BLOCK, BLOCK)
-        out.append(jnp.where(keys[:, None] == queries[None, :], 0.0, -1e30))
-    return jnp.stack(out).astype(f32)
+    for start, width, first in zip(window_starts(s), WINDOWS, query_starts(s)):
+        keys = lax.dynamic_slice_in_dim(ids, start, width)
+        block = s ^ (2 * (first // BLOCK))
+        queries = lax.dynamic_slice_in_dim(ids, block * BLOCK, BLOCK)
+        out.append(jnp.where(keys[:, None] == queries[None, :], 0.0, -1e30).astype(f32))
+    return tuple(out)
 
 
 def norm_forward(total):
@@ -605,6 +633,35 @@
         compiler_params=pltpu.CompilerParams(vmem_limit_bytes=32 << 20),
         cost_estimate=SMALL_COST,
     )(total, gain.reshape(1, width), upstream)
+
+
+def merged(query_low, own, back):
+    tokens = query_low.shape[0]
+    tile = D // 2
+
+    def kernel(query_ref, own_ref, back_ref, low_ref, sum_ref):
+        def put(low):
+            low_ref[...] = low
+            sum_ref[...] = jnp.sum(low.astype(f32), axis=0, keepdims=True)
+
+        @pl.when(pl.program_id(0) < 2)
+        def _():
+            put(query_ref[...])
+
+        @pl.when(pl.program_id(0) >= 2)
+        def _():
+            put((own_ref[0] + back_ref[0].astype(f32)).astype(bf16))
+
+    part = pl.BlockSpec((1, tokens, tile), lambda j: (jnp.maximum(j - 2, 0) // 2, 0, jnp.maximum(j - 2, 0) % 2))
+    return pl.pallas_call(
+        kernel,
+        grid=(6,),
+        in_specs=[pl.BlockSpec((tokens, tile), lambda j: (0, jnp.minimum(j, 1))), part, part],
+        out_specs=[pl.BlockSpec((tokens, tile), lambda j: (0, j)), pl.BlockSpec((1, tile), lambda j: (0, j))],
+        out_shape=[jax.ShapeDtypeStruct((tokens, 3 * D), bf16), jax.ShapeDtypeStruct((1, 3 * D), f32)],
+        compiler_params=pltpu.CompilerParams(vmem_limit_bytes=32 << 20),
+        cost_estimate=SMALL_COST,
+    )(query_low, own, back)
 
 
 SMALL = 8
@@ -644,27 +701,22 @@
 
     token_kept, token_left = split_rows(tokens)
     upstream_kept, upstream_left = split_rows(cotangent)
-    token_got = send(token_left, TO_X)
 
     def unit_a(layer):
         r = rows_held
-        parts = [w[layer] for w in (query_weight, key_weight, value_weight, mix_weight)]
-        outs = (((0, 0), (0, 1), (0, 2), (1, 0)))
-        return GatherUnit(
-            coords,
-            jnp.concatenate(parts),
-            [(r, 3 * D), (r, D)],
-            [(r * n, r * (n + 1), target, column) for n, (target, column) in enumerate(outs)],
-        )
+        parts = [w[layer] for w in (query_weight, key_weight, value_weight)]
+        rows, outs = [(r * n, r * (n + 1), 0, n) for n in range(3)], [(r, 3 * D)]
+        if layer:
+            parts, rows, outs = parts + [mix_weight[layer]], rows + [(3 * r, 4 * r, 1, 0)], outs + [(r, D)]
+        return GatherUnit(coords, jnp.concatenate(parts), outs, rows)
 
     def unit_i(layer):
         r, inner = rows_held, inner_weight[layer]
-        return GatherUnit(
-            coords,
-            jnp.concatenate([inner[:, D * n : D * (n + 1)] for n in range(4)]),
-            [(r, FF)],
-            [(r * n, r * (n + 1), 0, n) for n in range(4)],
-        )
+        parts = [inner[:, D * n : D * (n + 1)] for n in range(4)]
+        rows, outs = [(r * n, r * (n + 1), 0, n) for n in range(4)], [(r, FF)]
+        if not layer:
+            parts, rows, outs = parts + [mix_weight[layer]], rows + [(4 * r, 5 * r, 1, 0)], outs + [(r, D)]
+        return GatherUnit(coords, jnp.concatenate(parts), outs, rows)
 
     def unit_o(layer):
         return GatherUnit(coords, outer_weight[layer], [(inner_held, D)], [(0, inner_held, 0, 0)])
@@ -693,24 +745,20 @@
     u = [unit for layer_units in units for unit in layer_units]
     padded = phase(padded, u[0])
     token_got = send(token_left, TO_X)
-    other = send(padded, TO_PAIR)
-    high, low_bit = z // 2, z % 2
-    every = by_place(padded, other, high, 0)
+    every = jnp.roll(jnp.stack([padded] + [send(padded, TO_Z[4 - k]) for k in (1, 2, 3)]), z, axis=0)
 
     lengths = pick(doc_lengths.reshape(2, NDOC), row, 0)
     places = lax.iota(jnp.int32, SEQ_LEN)
     segment = jnp.sum((places[:, None] >= jnp.cumsum(lengths)[None, :]).astype(jnp.int32), axis=1)
     bias = window_bias(seq, jnp.where(segment == NDOC - 1, NDOC + places, segment))
-    order = block_order(coords)
+    order, order_z = block_order(coords), block_order(coords, True)
     matrices = order_matrices(order)
 
-    token_got, every, upstream_left = phase((token_got, every, upstream_left), u[0], u[1])
-    every = by_place(every, send(every, TO_ODD), low_bit, 1).reshape(4, 8, 128)
-    upstream_got = send(upstream_left, TO_X)
-    token_got, every, matrices, bias = phase((token_got, every, matrices, bias), u[0], u[1], u[2])
+    token_got, every = phase((token_got, every), u[0])
     every = by_place(every, send(every, TO_Y), y, 1)
-    token_got, every, upstream_got = phase((token_got, every, upstream_got), u[0], u[1], u[2], u[3])
+    every, bias = phase((every, bias), u[0], u[1])
     every = by_place(every, send(every, TO_X), x, 2)
+    every, matrices = phase((every, matrices), u[0], u[1], u[2])
     every = by_place(every, send(every, TO_CORE), c, 3)
     every = every.reshape(devices, 1024)[:, :held].astype(f32)
     small_all = (
@@ -726,19 +774,19 @@
         .reshape(layer_count, FF)
     )
     stream = jnp.concatenate([token_kept, token_got]).astype(f32)
-    stream, small_all, wide_all = phase((stream, small_all, wide_all), u[0], u[2], u[3], u[4], settle=[u[1]])
+    stream, small_all, wide_all = phase((stream, small_all, wide_all), u[0], u[1], u[2], u[3])
     saved = []
     for layer in range(layer_count):
         a_unit, i_unit, o_unit = units[layer]
         next_a, next_i, next_o = units[layer + 1] if layer + 1 < layer_count else (None,) * 3
         q_bias, v_bias, m_bias, gain1, shift1, o_bias, gain2, shift2 = [small_all[layer, n] for n in range(SMALL)]
-        w_three, w_mix = a_unit.result()
-        w_three, w_mix = w_three.reshape(D, 3 * D), w_mix.reshape(D, D)
+        w_three, *w_rest = a_unit.result()
+        w_three = w_three.reshape(D, 3 * D)
         stream_low = stream.astype(bf16)
         three_bias = jnp.concatenate([q_bias, jnp.zeros_like(q_bias), v_bias])
         (three,) = product(stream_low, w_three, 1024, lambda total, b: (total + b,), (bf16,), (three_bias,))
         if next_a:
-            three = phase(three, i_unit, next_i, next_o, settle=[o_unit, next_a])
+            three = phase(three, i_unit, next_a, next_i, settle=[o_unit])
         else:
             three = phase(three, i_unit)
         three_got = send(three, TO_CORE)
@@ -746,32 +794,45 @@
         three, left_stream = lax.optimization_barrier((three, left_stream))
         left_stream = (left_stream[0], send(left_stream[1], TO_CORE))
         mixed, totals = attend_forward_blocks(place_of, three, three_got, bias)
-        moving = [i_unit, o_unit] + ([next_a, next_o] if next_a else [])
-        mixed, totals, left_stream = phase(
-            (mixed, totals, left_stream), *moving, settle=[next_i] if next_a else []
-        )
+        if next_a:
+            mixed, totals, left_stream = phase(
+                (mixed, totals, left_stream), i_unit, o_unit, next_a, next_i, next_o
+            )
+        else:
+            mixed, totals, left_stream = phase((mixed, totals, left_stream), i_unit, o_unit)
+        w_inner, *w_more = i_unit.result()
+        (w_mix,) = w_rest + w_more
+        w_inner, w_mix = w_inner.reshape(D, FF), w_mix.reshape(D, D)
         first_sum = stream + (dot(mixed, w_mix) + m_bias)
         first = norm_forward(first_sum)[0] * gain1 + shift1
         first_low = first.astype(bf16)
+        if next_a:
+            first_low = phase(first_low, o_unit, next_o, settle=[next_a, next_i])
+        else:
+            first_low = phase(first_low, o_unit)
         left_mix, left_first = selected(matrices, mixed, first_low)
-        if not next_a:
-            first_low = phase(first_low, o_unit)
-        (w_inner,) = i_unit.result()
-        w_inner = w_inner.reshape(D, FF)
         first_low, left_mix, left_first = lax.optimization_barrier((first_low, left_mix, left_first))
         left_mix, left_first = [(m, send(t, TO_CORE)) for m, t in (left_mix, left_first)]
         active, slope = product(first_low, w_inner, 1024, gelu_parts, (bf16, bf16), (wide_all[layer],))
-        moving = [o_unit] + ([next_a] if next_a else [])
-        active, slope, left_mix, left_first = phase(
-            (active, slope, left_mix, left_first), *moving, settle=[next_o] if next_a else []
-        )
-        active_got = send(active, TO_CORE)
+        if next_a:
+            active, slope, left_mix, left_first = phase(
+                (active, slope, left_mix, left_first), o_unit, next_a, settle=[next_o]
+            )
+        else:
+            active, slope, left_mix, left_first = phase((active, slope, left_mix, left_first), o_unit)
+        if not next_a:
+            upstream_left, active = lax.optimization_barrier((upstream_left, active))
+            upstream_got = send(upstream_left, TO_X)
         (w_outer,) = o_unit.result()
+        active_got = send(tie(active, w_outer), TO_CORE)
         w_outer = w_outer.reshape(FF, D)
         (second_sum,) = product(
             active, w_outer, 256, lambda total, b, f: (f + (total + b),), (f32,), (o_bias,), (first,)
         )
-        second_sum, active_got = lax.optimization_barrier((second_sum, active_got))
+        if next_a:
+            second_sum, active_got = lax.optimization_barrier((second_sum, active_got))
+        else:
+            second_sum, active_got, upstream_got = lax.optimization_barrier((second_sum, active_got, upstream_got))
         left_active = (active, active_got)
         stream = norm_forward(second_sum)[0] * gain2 + shift2
         if next_a:
@@ -813,41 +874,45 @@
             second_low, w_outer, 1024, with_sum, (bf16,), (), (slope,), transposed=True, sums=1
         )
         if before:
-            inner_low = phase(inner_low, before.o, before.i, before.a)
+            inner_low, second_got = phase((inner_low, second_got), before.o[0], before.i, before.a)
         else:
-            inner_low, output_got = lax.optimization_barrier((inner_low, output_got))
+            inner_low, second_got, output_got = lax.optimization_barrier((inner_low, second_got, output_got))
         inner_got = send(inner_low, TO_CORE)
-        o_sum = SumUnit(wide_terms_of(order, left_active, tie((second_low, second_got), inner_low)))
+        second_pair = (second_low, second_got)
         if before:
-            second_grad, inner_low = phase((second_grad, inner_low), o_sum, before.a, before.i, before.o)
+            o_sums = (
+                SumUnit(wide_terms_of(order_z, left_active, second_pair, 0, 2), Z_FIRST),
+                SumUnit(wide_terms_of(order, left_active, second_pair, 1, 2)),
+            )
+            second_grad, inner_low = phase(
+                (second_grad, inner_low), *o_sums, before.a, before.i, settle=before.o
+            )
         else:
-            second_grad, inner_low = phase((second_grad, inner_low), o_sum)
+            o_sums = (SumUnit(wide_terms_of(order, left_active, second_pair)),)
+            second_grad, inner_low = phase((second_grad, inner_low), *o_sums)
         (first_grad,) = product(
             inner_low, w_inner, 256, lambda total, g: (g + total,), (f32,), (), (second_grad,), transposed=True
         )
         first_sum_grad, branch_low, first_sums = norm_backward_rows(first_sum, gain1, first_grad)
         branch_got = send(branch_low, TO_CORE)
         (mixed_grad,) = product(branch_low, w_mix, 512, lambda total: (total,), (bf16,), transposed=True)
+        mixed_grad, inner_got, branch_got = lax.optimization_barrier((mixed_grad, inner_got, branch_got))
         i_sum = SumUnit(
-            weight_terms(
-                (left_first, tie((inner_low, inner_got), mixed_grad), FF), (left_mix, (branch_low, branch_got), D)
-            )
+            weight_terms((left_first, (inner_low, inner_got), FF), (left_mix, (branch_low, branch_got), D))
         )
         if before:
-            mixed_grad = phase(mixed_grad, i_sum, before.a, before.i, settle=[o_sum])
+            mixed_grad = phase(mixed_grad, i_sum, *o_sums, before.a, settle=[before.i])
         else:
-            mixed_grad = phase(mixed_grad, i_sum, settle=[o_sum])
+            mixed_grad = phase(mixed_grad, i_sum, settle=o_sums)
         query_low, own_grads, sent_grads = attend_backward_blocks(
             place_of, three, three_got, bias, mixed, totals, mixed_grad
         )
         grads_back = send(sent_grads, TO_CORE)
-        if layer:
-            query_low, own_grads = phase((query_low, own_grads), o_sum, settle=[i_sum])
+        if before:
+            query_low, own_grads = phase((query_low, own_grads), i_sum, *o_sums, before.a)
         else:
-            moving = [o_sum, i_sum] + ([before.a] if before else [])
-            query_low, own_grads = phase((query_low, own_grads), *moving)
-        sums_low = (own_grads + grads_back.astype(f32)).astype(bf16)
-        low = jnp.concatenate([query_low, sums_low[0], sums_low[1]], axis=1)
+            query_low, own_grads = phase((query_low, own_grads), *o_sums, settle=[i_sum])
+        low, low_sums = merged(query_low, own_grads, grads_back)
         low_got = send(low, TO_CORE)
         if layer:
             (upstream,) = product(
@@ -856,14 +921,14 @@
             a_sum = SumUnit(weight_terms((left_stream, tie((low, low_got), upstream), 3 * D)))
         else:
             a_sum = SumUnit(weight_terms((left_stream, (low, low_got), 3 * D)))
-            low = phase(low, a_sum, o_sum, i_sum)
+            low, low_sums = phase((low, low_sums), a_sum, settle=[before.a] if before else [])
             (upstream,) = product(
                 low, w_three, 256, lambda total, g: (g + total,), (f32,), (), (first_sum_grad,), transposed=True
             )
         small_grads[layer] = jnp.stack(
             [
-                column_sum(low[:, :D]),
-                column_sum(low[:, 2 * D :]),
+                low_sums[0, :D],
+                low_sums[0, 2 * D :],
                 first_sums[2],
                 first_sums[0],
                 first_sums[1],
@@ -874,8 +939,8 @@
         )
         wide_grads[layer] = inner_sum[0]
         if layer:
-            upstream, small_grads[layer] = phase((upstream, small_grads[layer]), o_sum, i_sum, settle=[a_sum])
-        sums[layer] = before = Sums(o_sum, i_sum, a_sum)
+            upstream, small_grads[layer] = phase((upstream, small_grads[layer]), *o_sums, i_sum, settle=[a_sum])
+        sums[layer] = before = Sums(o_sums, i_sum, a_sum)
 
     small_terms = (
         jnp.stack(small_grads)
@@ -893,23 +958,25 @@
     chosen = (order[:, None] == lax.iota(jnp.int32, devices)[None, :]).astype(f32)
     terms = jnp.dot(chosen, terms, precision=lax.Precision.HIGHEST).reshape(2, 128, 128)
     terms = (terms[0] + send(terms[1].astype(bf16), TO_CORE).astype(f32)).astype(bf16)
-    small_sum = SumUnit((terms[:64], terms[64:]))
+    small_sum = SmallUnit((terms[:64], terms[64:]))
 
     last = sums[0]
-    upstream = phase(upstream, last.a, last.o, last.i, small_sum)
-    upstream = phase(upstream, last.a, small_sum, settle=[last.o, last.i])
-    token_back = send(upstream[length:].astype(bf16), TO_X)
-    upstream, token_back = phase((upstream, token_back), last.a, small_sum)
+    done = [unit for layer in range(1, layer_count) for unit in (*sums[layer].o, sums[layer].i, sums[layer].a)]
+    upstream, output_got = phase((upstream, output_got), last.a, last.i, *last.o, small_sum, *done)
+    token_left = upstream[length:].astype(bf16)
+    upstream, token_left = phase((upstream, token_left), last.a, last.i, *last.o, small_sum)
+    token_back = send(token_left, TO_X)
+    upstream, token_back = phase((upstream, token_back), last.a, last.i, small_sum)
     phase((), last.a, small_sum)
-    phase((), small_sum)
     own_terms = small_sum.kept.reshape(-1)[:held]
     small_own = own_terms[:small_held].reshape(layer_count, SMALL, rows_held)
     wide_own = own_terms[small_held:].reshape(layer_count, inner_held)
     for layer in range(layer_count):
-        for unit in sums[layer]:
+        for unit in (*sums[layer].o, sums[layer].i, sums[layer].a):
             while unit.step < 5:
                 phase((), unit)
-    o_all, i_all, a_all = [jnp.stack([units_of[n].kept for units_of in sums]) for n in range(3)]
+    o_all = jnp.stack([jnp.concatenate([unit.kept for unit in group.o], axis=1) for group in sums])
+    i_all, a_all = [jnp.stack([group[n].kept for group in sums]) for n in (1, 2)]
     return (
         both_rows(output[:length], output_got),
         both_rows(upstream[:length], token_back),

time: 763 us -> 739 us (0.969)
  waiting for transfers between devices: 237 us -> 207 us
  other arithmetic: 83.5 us -> 72.3 us
  starting transfers between devices: 83.6 us -> 94.2 us
    ppermute x94 -> x100, waiting for transfers between devices: 237 us -> 207 us  [send(): return lax.ppermute(value, AXES, to)]
    pallas_call x4, Pallas kernels: 77.8 us -> 66.4 us  [call_attention(): pl.pallas_call(kernel, grid=(pairs_count,), in_specs=in_specs, out_specs=...]
    ppermute x94 -> x100, starting transfers between devices: 83.6 us -> 94.2 us  [send(): return lax.ppermute(value, AXES, to)]
    convert_element_type x14, other arithmetic: 32.4 us -> 22.7 us  [local(): self.kept = self.kept.astype(bf16)]
    pallas_call x2 -> x3, Pallas kernels: 22.8 us -> 28.5 us  [wide_terms_of(): pl.pallas_call(kernel, grid_spec=pltpu.PrefetchScalarGridSpec(num_scalar_...]
    unnamed x304 -> x306, local copies, waits for them, and re-layouts: 28.1 us -> 31.5 us
  transfers between devices with their start and end apart: 94 -> 100, of which waited for: 45 -> 43; matrix products, arithmetic and copies ran while one was open for 8% -> 8% of each run, Pallas kernels for 39% -> 38%
where the time goes in v4:
time: 739 us; the launch traced here: 732 us
  Pallas kernels  295 us (40%)
  waiting for transfers between devices  207 us (28%)
  starting transfers between devices  94.2 us (13%)
  other arithmetic  72.3 us (10%)
  local copies, waits for them, and re-layouts  55.6 us (8%)
    ppermute x100, waiting for transfers between devices, send(): return lax.ppermute(value, AXES, to)  207 us
    pallas_call x14, Pallas kernels, product(): pl.pallas_call(kernel, grid=(width // tile,), in_specs=[pl.BlockSpec((tok...  104 us
    ppermute x100, starting transfers between devices, send(): return lax.ppermute(value, AXES, to)  94.2 us
    pallas_call x4, Pallas kernels, call_attention(): pl.pallas_call(kernel, grid=(pairs_count,), in_specs=in_specs, out_specs=...  66.4 us
    pallas_call x6, Pallas kernels, place(): pl.pallas_call(kernel, in_specs=[pl.BlockSpec(memory_space=pltpu.SMEM)] +...  38.2 us
    pallas_call x4, Pallas kernels, weight_terms(): pl.pallas_call(kernel, grid=(columns // tile,), in_specs=in_specs, out_sp...  33 us
    unnamed x306, local copies, waits for them, and re-layouts  31.5 us
    pallas_call x3, Pallas kernels, wide_terms_of(): pl.pallas_call(kernel, grid_spec=pltpu.PrefetchScalarGridSpec(num_scalar_...  28.5 us
  transfers between devices with their start and end apart: 100, of which 43 were waited for; matrix products, arithmetic and copies ran while one was open for 8% of the time, Pallas kernels for 38%

profile of v4, /device:TPU:0, one launch (start us, length us, event | category | flops | bytes accessed | tf_op | source)
XLA Modules:
  0.0 732.4 jit_solution(8930324704367966304)
XLA Ops:
  24.9 4.2 collective-permute-done
  34.5 4.5 collective-permute-done.6
  47.1 9.8 %collective-permute-done.9 = bf16[1,160,1024]{2,1,0:T(8,128)(2,1)} collective-permute-done((bf16[1,160,1024]{2,1,0:T(8,128)(2,1)S(1)}, bf16[1,160,1024]{2,1,0:T(8,128)(2,1)}, u32[]{:S(2)}, u32[]{:S(2)}) %collective-permute-start.9) | collective-permute-done | bytes 327712 | tf_op jit(solution)/shard_map/ppermute | solution.py:63
  72.1 11.3 %collective-permute-done.14 = bf16[1,128,1024]{2,1,0:T(8,128)(2,1)} collective-permute-done((bf16[1,128,1024]{2,1,0:T(8,128)(2,1)S(1)}, bf16[1,128,1024]{2,1,0:T(8,128)(2,1)}, u32[]{:S(2)}, u32[]{:S(2)}) %collective-permute-start.14) | collective-permute-done | bytes 262176 | tf_op jit(solution)/shard_map/ppermute | solution.py:63
  94.5 4.5 shard_map.305
  101.7 5.9 shard_map.306.q_ref.km_ref.vm_ref
  120.5 12.5 %shard_map.308 = (bf16[512,1024]{1,0:T(8,128)(2,1)S(1)}, f32[8,2,512]{2,1,0:T(2,128)S(1)}) custom-call(s32[1]{0:T(128)} %bitcast.83.s_ref, bf16[512,3072]{1,0:T(8,128)(2,1)S(1)} %shard_map.306.q_ref.km_ref.vm_ref, bf16[512,3072]{1,0:T(8,128)(2,1)S(1)} %shard_map.306.q_ref.km_ref.vm_ref, bf16[512,3072]{1,0:T(8,128)(2,1)} %collective-permute-done.19.ko_ref.vo_ref, ...), custom_call_target="tpu_custom_call" | custom-call | flops 1024 | bytes 1024 | tf_op jit(solution)/shard_map/pallas_call | solution.py:471
  135.7 8.5 %collective-permute-done.21.refs_1_ = bf16[8,160,1024]{2,1,0:T(8,128)(2,1)S(1)} collective-permute-done((bf16[8,160,1024]{2,1,0:T(8,128)(2,1)S(1)}, bf16[8,160,1024]{2,1,0:T(8,128)(2,1)S(1)}, u32[]{:S(2)}, u32[]{:S(2)}) %collective-permute-start.21) | collective-permute-done | bytes 2621472 | tf_op jit(solution)/shard_map/ppermute | solution.py:63
  152.8 7.6 %shard_map.309 = (bf16[4,2,2,2,32,4096]{5,4,3,2,1,0:T(8,128)(2,1)}, bf16[4,2,2,2,32,1024]{5,4,3,2,1,0:T(8,128)(2,1)S(1)}) custom-call(s32[4]{0:T(128)S(1)} %pad_add_fusion.coords_ref, bf16[8,160,1024]{2,1,0:T(8,128)(2,1)S(1)} %pad_maximum_fusion.refs_0_, bf16[8,160,1024]{2,1,0:T(8,128)(2,1)S(1)} %collective-permute-done.21.refs_1_, ...), custom_call_target="tpu_custom_call" | custom-call | flops 1024 | bytes 1024 | tf_op jit(solution)/shard_map/pallas_call | solution.py:98
  163.7 5.1 collective-permute-done.29
  168.8 8.3 %collective-permute-done.28 = bf16[4,128,1024]{2,1,0:T(8,128)(2,1)S(1)} collective-permute-done((bf16[4,128,1024]{2,1,0:T(8,128)(2,1)S(1)}, bf16[4,128,1024]{2,1,0:T(8,128)(2,1)S(1)}, u32[]{:S(2)}, u32[]{:S(2)}) %collective-permute-start.28) | collective-permute-done | bytes 1048608 | tf_op jit(solution)/shard_map/ppermute | solution.py:63
  188.4 11.3 %shard_map.311 = (bf16[512,4096]{1,0:T(8,128)(2,1)S(1)}, bf16[512,4096]{1,0:T(8,128)(2,1)}) custom-call(bf16[512,1024]{1,0:T(8,128)(2,1)S(1)} %copy-done.24, bf16[1024,4096]{1,0:T(8,128)(2,1)} %bitcast.291, f32[1,4096]{1,0:T(1,128)S(1)} %get-tuple-element.866.refs_0_), custom_call_target="tpu_custom_call" | custom-call | flops 1024 | bytes 1024 | tf_op jit(solution)/shard_map/pallas_call | solution.py:580
  213.2 5.9 shard_map.312
  221.0 8.4 %shard_map.313.total_ref = f32[512,1024]{1,0:T(8,128)S(1)} custom-call(bf16[512,4096]{1,0:T(8,128)(2,1)} %copy-done.4, bf16[4096,1024]{1,0:T(8,128)(2,1)} %bitcast.285, f32[1,1024]{1,0:T(1,128)S(1)} %get-tuple-element.858.refs_0_, f32[512,1024]{1,0:T(8,128)S(1)} %get-tuple-element.792.refs_1_), custom_call_target="tpu_custom_call" | custom-call | flops 1024 | bytes 1024 | tf_op jit(solution)/shard_map/pallas_call | solution.py:580
  231.2 14.4 %collective-permute-done.37.refs_1_ = bf16[8,128,1024]{2,1,0:T(8,128)(2,1)} collective-permute-done((bf16[8,128,1024]{2,1,0:T(8,128)(2,1)}, bf16[8,128,1024]{2,1,0:T(8,128)(2,1)}, u32[]{:S(2)}, u32[]{:S(2)}) %collective-permute-start.37) | collective-permute-done | bytes 2097184 | tf_op jit(solution)/shard_map/ppermute | solution.py:63
  250.2 7.2 shard_map.314
  258.8 5.9 shard_map.315.q_ref.km_ref.vm_ref
  270.9 12.7 %shard_map.317 = (bf16[512,1024]{1,0:T(8,128)(2,1)S(1)}, f32[8,2,512]{2,1,0:T(2,128)S(1)}) custom-call(s32[1]{0:T(128)} %bitcast.83.s_ref, bf16[512,3072]{1,0:T(8,128)(2,1)S(1)} %shard_map.315.q_ref.km_ref.vm_ref, bf16[512,3072]{1,0:T(8,128)(2,1)S(1)} %shard_map.315.q_ref.km_ref.vm_ref, bf16[512,3072]{1,0:T(8,128)(2,1)} %collective-permute-done.41.ko_ref.vo_ref, ...), custom_call_target="tpu_custom_call" | custom-call | flops 1024 | bytes 1024 | tf_op jit(solution)/shard_map/pallas_call | solution.py:471
  283.7 7.7 %collective-permute-done.43.refs_1_ = bf16[8,128,1024]{2,1,0:T(8,128)(2,1)} collective-permute-done((bf16[8,128,1024]{2,1,0:T(8,128)(2,1)S(1)}, bf16[8,128,1024]{2,1,0:T(8,128)(2,1)}, u32[]{:S(2)}, u32[]{:S(2)}) %collective-permute-start.43) | collective-permute-done | bytes 2097184 | tf_op jit(solution)/shard_map/ppermute | solution.py:63
  298.0 8.4 %collective-permute-done.45 = bf16[4,128,1024]{2,1,0:T(8,128)(2,1)S(1)} collective-permute-done((bf16[4,128,1024]{2,1,0:T(8,128)(2,1)S(1)}, bf16[4,128,1024]{2,1,0:T(8,128)(2,1)S(1)}, u32[]{:S(2)}, u32[]{:S(2)}) %collective-permute-start.45) | collective-permute-done | bytes 1048608 | tf_op jit(solution)/shard_map/ppermute | solution.py:63
  314.3 6.9 shard_map.319
  321.2 10.9 %shard_map.320 = (bf16[512,4096]{1,0:T(8,128)(2,1)S(1)}, bf16[512,4096]{1,0:T(8,128)(2,1)}) custom-call(bf16[512,1024]{1,0:T(8,128)(2,1)S(1)} %copy-done.25, bf16[1024,4096]{1,0:T(8,128)(2,1)} %bitcast.287, f32[1,4096]{1,0:T(1,128)S(1)} %get-tuple-element.865.refs_0_), custom_call_target="tpu_custom_call" | custom-call | flops 1024 | bytes 1024 | tf_op jit(solution)/shard_map/pallas_call | solution.py:580
  337.4 6.1 shard_map.321
  345.1 8.4 %shard_map.322.total_ref = f32[512,1024]{1,0:T(8,128)S(1)} custom-call(bf16[512,4096]{1,0:T(8,128)(2,1)} %copy-done.8, bf16[4096,1024]{1,0:T(8,128)(2,1)} %bitcast.289, f32[1,1024]{1,0:T(1,128)S(1)} %get-tuple-element.850.refs_0_, f32[512,1024]{1,0:T(8,128)S(1)} %get-tuple-element.790.refs_1_), custom_call_target="tpu_custom_call" | custom-call | flops 1024 | bytes 1024 | tf_op jit(solution)/shard_map/pallas_call | solution.py:580
  353.6 4.3 collective-permute-done.53
  367.5 9.4 %shard_map.324 = (bf16[512,4096]{1,0:T(8,128)(2,1)}, f32[1,4096]{1,0:T(1,128)S(1)}) custom-call(bf16[512,1024]{1,0:T(8,128)(2,1)S(1)} %get-tuple-element.588.rows_ref.refs_4_, bf16[4096,1024]{1,0:T(8,128)(2,1)} %bitcast.290, bf16[512,4096]{1,0:T(8,128)(2,1)} %get-tuple-element.589.refs_0_), custom_call_target="tpu_custom_call" | custom-call | flops 1024 | bytes 1024 | tf_op jit(solution)/shard_map/pallas_call | solution.py:580
  383.7 11.3 %shard_map.325 = (bf16[1024,1024]{1,0:T(8,128)(2,1)S(1)}, bf16[1024,1024]{1,0:T(8,128)(2,1)}) custom-call(s32[32]{0:T(128)S(1)} %stack.436.order_ref, bf16[512,4096]{1,0:T(8,128)(2,1)} %copy-done.8, bf16[512,4096]{1,0:T(8,128)(2,1)} %copy-done.8, bf16[512,4096]{1,0:T(8,128)(2,1)} %collective-permute-done.52.refs_2_.refs_3_, ...), custom_call_target="tpu_custom_call" | custom-call | flops 1024 | bytes 1024 | tf_op jit(solution)/shard_map/pallas_call | solution.py:321
  396.5 8.5 %shard_map.326.up_ref = f32[512,1024]{1,0:T(8,128)S(1)} custom-call(bf16[512,4096]{1,0:T(8,128)(2,1)} %get-tuple-element.599.rows_ref.refs_2_, bf16[1024,4096]{1,0:T(8,128)(2,1)} %bitcast.288, f32[512,1024]{1,0:T(8,128)S(1)} %copy-done.49), custom_call_target="tpu_custom_call" | custom-call | flops 1024 | bytes 1024 | tf_op jit(solution)/shard_map/pallas_call | solution.py:580
  410.1 9.8 %shard_map.329 = (bf16[256,5120]{1,0:T(8,128)(2,1)}, bf16[256,5120]{1,0:T(8,128)(2,1)}) custom-call(bf16[512,512]{1,0:T(8,128)(2,1)S(1)} %copy-done.75, bf16[512,512]{1,0:T(8,128)(2,1)S(1)} %copy-done.79, bf16[512,4096]{1,0:T(8,128)(2,1)} %get-tuple-element.599.rows_ref.refs_2_, bf16[512,4096]{1,0:T(8,128)(2,1)} %collective-permute-done.56.refs_3_, ...), custom_call_target="tpu_custom_call" | custom-call | flops 1024 | bytes 1024 | tf_op jit(solution)/shard_map/pallas_call | solution.py:285
  422.7 20.5 %shard_map.330 = (bf16[512,1024]{1,0:T(8,128)(2,1)S(1)}, f32[2,512,1024]{2,1,0:T(8,128)}, bf16[2,512,1024]{2,1,0:T(8,128)(2,1)}) custom-call(s32[1]{0:T(128)} %bitcast.83.s_ref, bf16[512,3072]{1,0:T(8,128)(2,1)} %copy-done.3, bf16[512,3072]{1,0:T(8,128)(2,1)} %copy-done.3, bf16[512,3072]{1,0:T(8,128)(2,1)} %collective-permute-done.41.ko_ref.vo_ref, ...), custom_call_target="tpu_custom_call" | custom-call | flops 1024 | bytes 1024 | tf_op jit(solution)/shard_map/pallas_call | solution.py:471
  443.2 9.8 %collective-permute-done.59 = bf16[256,5120]{1,0:T(8,128)(2,1)S(1)} collective-permute-done((bf16[256,5120]{1,0:T(8,128)(2,1)}, bf16[256,5120]{1,0:T(8,128)(2,1)S(1)}, u32[]{:S(2)}, u32[]{:S(2)}) %collective-permute-start.59) | collective-permute-done | bytes 2621472 | tf_op jit(solution)/shard_map/ppermute | solution.py:63
  453.0 4.8 add_convert_fusion.4
  463.2 7.2 shard_map.332.up_ref
  471.8 6.8 shard_map.333
  489.0 9.5 %shard_map.335 = (bf16[512,4096]{1,0:T(8,128)(2,1)}, f32[1,4096]{1,0:T(1,128)S(1)}) custom-call(bf16[512,1024]{1,0:T(8,128)(2,1)S(1)} %get-tuple-element.646.rows_ref.refs_4_, bf16[4096,1024]{1,0:T(8,128)(2,1)} %bitcast.286, bf16[512,4096]{1,0:T(8,128)(2,1)} %get-tuple-element.647.refs_0_), custom_call_target="tpu_custom_call" | custom-call | flops 1024 | bytes 1024 | tf_op jit(solution)/shard_map/pallas_call | solution.py:580
  507.6 8.6 %shard_map.337 = (bf16[1024,512]{1,0:T(8,128)(2,1)S(1)}, bf16[1024,512]{1,0:T(8,128)(2,1)S(1)}) custom-call(s32[32]{0:T(128)S(1)} %stack.436.order_ref, bf16[512,4096]{1,0:T(8,128)(2,1)} %copy-done.4, bf16[512,4096]{1,0:T(8,128)(2,1)} %copy-done.4, bf16[512,4096]{1,0:T(8,128)(2,1)} %collective-permute-done.36.refs_2_.refs_3_, ...), custom_call_target="tpu_custom_call" | custom-call | flops 1024 | bytes 1024 | tf_op jit(solution)/shard_map/pallas_call | solution.py:321
  516.2 8.6 %shard_map.336 = (bf16[1024,512]{1,0:T(8,128)(2,1)S(1)}, bf16[1024,512]{1,0:T(8,128)(2,1)S(1)}) custom-call(s32[32]{0:T(128)S(1)} %stack.438.order_ref, bf16[512,4096]{1,0:T(8,128)(2,1)} %copy-done.4, bf16[512,4096]{1,0:T(8,128)(2,1)} %copy-done.4, bf16[512,4096]{1,0:T(8,128)(2,1)} %collective-permute-done.36.refs_2_.refs_3_, ...), custom_call_target="tpu_custom_call" | custom-call | flops 1024 | bytes 1024 | tf_op jit(solution)/shard_map/pallas_call | solution.py:321
  533.3 8.6 %shard_map.338.up_ref = f32[512,1024]{1,0:T(8,128)S(1)} custom-call(bf16[512,4096]{1,0:T(8,128)(2,1)} %get-tuple-element.675.rows_ref.refs_2_, bf16[1024,4096]{1,0:T(8,128)(2,1)} %bitcast.292, f32[512,1024]{1,0:T(8,128)S(1)} %copy-done.47), custom_call_target="tpu_custom_call" | custom-call | flops 1024 | bytes 1024 | tf_op jit(solution)/shard_map/pallas_call | solution.py:580
  552.0 9.8 %shard_map.341 = (bf16[256,5120]{1,0:T(8,128)(2,1)}, bf16[256,5120]{1,0:T(8,128)(2,1)}) custom-call(bf16[512,512]{1,0:T(8,128)(2,1)S(1)} %copy-done.67, bf16[512,512]{1,0:T(8,128)(2,1)S(1)} %copy-done.71, bf16[512,4096]{1,0:T(8,128)(2,1)} %get-tuple-element.675.rows_ref.refs_2_, bf16[512,4096]{1,0:T(8,128)(2,1)} %collective-permute-done.69.refs_3_, ...), custom_call_target="tpu_custom_call" | custom-call | flops 1024 | bytes 1024 | tf_op jit(solution)/shard_map/pallas_call | solution.py:285
  561.8 15.1 %collective-permute-done.74 = bf16[32,5120]{1,0:T(8,128)(2,1)S(1)} collective-permute-done((bf16[32,5120]{1,0:T(8,128)(2,1)}, bf16[32,5120]{1,0:T(8,128)(2,1)S(1)}, u32[]{:S(2)}, u32[]{:S(2)}) %collective-permute-start.74) | collective-permute-done | bytes 327712 | tf_op jit(solution)/shard_map/ppermute | solution.py:63
  586.9 20.7 %shard_map.342 = (bf16[512,1024]{1,0:T(8,128)(2,1)S(1)}, f32[2,512,1024]{2,1,0:T(8,128)}, bf16[2,512,1024]{2,1,0:T(8,128)(2,1)}) custom-call(s32[1]{0:T(128)} %bitcast.83.s_ref, bf16[512,3072]{1,0:T(8,128)(2,1)} %copy-done.2, bf16[512,3072]{1,0:T(8,128)(2,1)} %copy-done.2, bf16[512,3072]{1,0:T(8,128)(2,1)} %collective-permute-done.19.ko_ref.vo_ref, ...), custom_call_target="tpu_custom_call" | custom-call | flops 1024 | bytes 1024 | tf_op jit(solution)/shard_map/pallas_call | solution.py:471
  608.8 11.2 %collective-permute-done.75 = bf16[256,5120]{1,0:T(8,128)(2,1)S(1)} collective-permute-done((bf16[256,5120]{1,0:T(8,128)(2,1)S(1)}, bf16[256,5120]{1,0:T(8,128)(2,1)S(1)}, u32[]{:S(2)}, u32[]{:S(2)}) %collective-permute-start.75) | collective-permute-done | bytes 2621472 | tf_op jit(solution)/shard_map/ppermute | solution.py:63
  634.2 6.6 shard_map.344
  650.0 7.1 shard_map.345
  659.5 6.1 collective-permute-done.84
  684.9 11.2 %collective-permute-done.88 = bf16[64,5120]{1,0:T(8,128)(2,1)S(1)} collective-permute-done((bf16[64,5120]{1,0:T(8,128)(2,1)S(1)}, bf16[64,5120]{1,0:T(8,128)(2,1)S(1)}, u32[]{:S(2)}, u32[]{:S(2)}) %collective-permute-start.88) | collective-permute-done | bytes 655392 | tf_op jit(solution)/shard_map/ppermute | solution.py:63
  705.8 8.7 %collective-permute-done.94 = bf16[32,5120]{1,0:T(8,128)(2,1)S(1)} collective-permute-done((bf16[32,5120]{1,0:T(8,128)(2,1)S(1)}, bf16[32,5120]{1,0:T(8,128)(2,1)S(1)}, u32[]{:S(2)}, u32[]{:S(2)}) %collective-permute-start.94) | collective-permute-done | bytes 327712 | tf_op jit(solution)/shard_map/ppermute | solution.py:63
  724.2 5.8 collective-permute-done.96
  (673 shorter events, 302.5 us)
Async XLA Ops:
  61.1 24.6 %collective-permute-start.11 = (bf16[8,96,1024]{2,1,0:T(8,128)(2,1)S(1)}, bf16[8,96,1024]{2,1,0:T(8,128)(2,1)S(1)}, u32[]{:S(2)}, u32[]{:S(2)}) collective-permute-start(bf16[8,96,1024]{2,1,0:T(8,128)(2,1)S(1)} %pad_maximum_fusion.5.refs_0_), channel_id=1, source_target_pairs={{0,2},{1,5},{2,0},{3,7},{4,6},{5,1},{6,4},{7,3},{8,10},{9,13},{10,... | collective-permute-start | bytes 4718600 | tf_op jit(solution)/shard_map/ppermute | solution.py:63
  62.6 23.1 %collective-permute-start.12 = (bf16[8,96,1024]{2,1,0:T(8,128)(2,1)S(1)}, bf16[8,96,1024]{2,1,0:T(8,128)(2,1)}, u32[]{:S(2)}, u32[]{:S(2)}) collective-permute-start(bf16[8,96,1024]{2,1,0:T(8,128)(2,1)S(1)} %pad_maximum_fusion.5.refs_0_), channel_id=1, source_target_pairs={{0,1},{1,0},{2,3},{3,2},{4,5},{5,4},{6,7},{7,6},{8,9},{9,8},{10,11... | collective-permute-start | bytes 4718600 | tf_op jit(solution)/shard_map/ppermute | solution.py:63
  62.6 23.1 %collective-permute-start.13 = (bf16[2,160,1024]{2,1,0:T(8,128)(2,1)}, bf16[2,160,1024]{2,1,0:T(8,128)(2,1)}, u32[]{:S(2)}, u32[]{:S(2)}) collective-permute-start(bf16[2,160,1024]{2,1,0:T(8,128)(2,1)} %pad_maximum_fusion.14), channel_id=1, source_target_pairs={{0,8},{1,9},{2,10},{3,11},{4,12},{5,13},{6,14},{7,15},{8,0},{9,1},... | collective-permute-start | bytes 1966088 | tf_op jit(solution)/shard_map/ppermute | solution.py:63
  65.4 18.0 %collective-permute-start.14 = (bf16[1,128,1024]{2,1,0:T(8,128)(2,1)S(1)}, bf16[1,128,1024]{2,1,0:T(8,128)(2,1)}, u32[]{:S(2)}, u32[]{:S(2)}) collective-permute-start(bf16[1,128,1024]{2,1,0:T(8,128)(2,1)S(1)} %bitcast.303), channel_id=1, source_target_pairs={{0,16},{1,17},{2,18},{3,19},{4,20},{5,21},{6,22},{7,23},{8,24},{9,... | collective-permute-start | bytes 786440 | tf_op jit(solution)/shard_map/ppermute | solution.py:63
  88.4 20.3 %collective-permute-start.16 = (bf16[4,160,1024]{2,1,0:T(8,128)(2,1)S(1)}, bf16[4,160,1024]{2,1,0:T(8,128)(2,1)S(1)}, u32[]{:S(2)}, u32[]{:S(2)}) collective-permute-start(bf16[4,160,1024]{2,1,0:T(8,128)(2,1)S(1)} %pad_maximum_fusion.6), channel_id=1, source_target_pairs={{0,4},{1,3},{2,6},{3,1},{4,0},{5,7},{6,2},{7,5},{8,12},{9,11},{10,... | collective-permute-start | bytes 3932168 | tf_op jit(solution)/shard_map/ppermute | solution.py:63
  90.0 18.7 %collective-permute-start.18 = (bf16[2,128,1024]{2,1,0:T(8,128)(2,1)S(1)}, bf16[2,128,1024]{2,1,0:T(8,128)(2,1)S(1)}, u32[]{:S(2)}, u32[]{:S(2)}) collective-permute-start(bf16[2,128,1024]{2,1,0:T(8,128)(2,1)S(1)} %pad_maximum_fusion.15), channel_id=1, source_target_pairs={{0,8},{1,9},{2,10},{3,11},{4,12},{5,13},{6,14},{7,15},{8,0},{9,1},... | collective-permute-start | bytes 1572872 | tf_op jit(solution)/shard_map/ppermute | solution.py:63
  112.5 31.7 %collective-permute-start.21 = (bf16[8,160,1024]{2,1,0:T(8,128)(2,1)S(1)}, bf16[8,160,1024]{2,1,0:T(8,128)(2,1)S(1)}, u32[]{:S(2)}, u32[]{:S(2)}) collective-permute-start(bf16[8,160,1024]{2,1,0:T(8,128)(2,1)S(1)} %pad_maximum_fusion.refs_0_), channel_id=1, source_target_pairs={{0,2},{1,5},{2,0},{3,7},{4,6},{5,1},{6,4},{7,3},{8,10},{9,13},{10,... | collective-permute-start | bytes 7864328 | tf_op jit(solution)/shard_map/ppermute | solution.py:63
  113.9 30.3 %collective-permute-start.22 = (bf16[8,160,1024]{2,1,0:T(8,128)(2,1)S(1)}, bf16[8,160,1024]{2,1,0:T(8,128)(2,1)}, u32[]{:S(2)}, u32[]{:S(2)}) collective-permute-start(bf16[8,160,1024]{2,1,0:T(8,128)(2,1)S(1)} %pad_maximum_fusion.refs_0_), channel_id=1, source_target_pairs={{0,1},{1,0},{2,3},{3,2},{4,5},{5,4},{6,7},{7,6},{8,9},{9,8},{10,11... | collective-permute-start | bytes 7864328 | tf_op jit(solution)/shard_map/ppermute | solution.py:63
  115.4 19.2 %collective-permute-start.20 = (bf16[512,512]{1,0:T(8,128)(2,1)S(1)}, bf16[512,512]{1,0:T(8,128)(2,1)S(1)}, u32[]{:S(2)}, u32[]{:S(2)}) collective-permute-start(bf16[512,512]{1,0:T(8,128)(2,1)S(1)} %get-tuple-element.461), channel_id=1, source_target_pairs={{0,1},{1,0},{2,3},{3,2},{4,5},{5,4},{6,7},{7,6},{8,9},{9,8},{10,11... | collective-permute-start | bytes 1572872 | tf_op jit(solution)/shard_map/ppermute | solution.py:63
  115.8 19.9 %collective-permute-start.23 = (bf16[2,128,1024]{2,1,0:T(8,128)(2,1)}, bf16[2,128,1024]{2,1,0:T(8,128)(2,1)}, u32[]{:S(2)}, u32[]{:S(2)}) collective-permute-start(bf16[2,128,1024]{2,1,0:T(8,128)(2,1)} %pad_maximum_fusion.16), channel_id=1, source_target_pairs={{0,8},{1,9},{2,10},{3,11},{4,12},{5,13},{6,14},{7,15},{8,0},{9,1},... | collective-permute-start | bytes 1572872 | tf_op jit(solution)/shard_map/ppermute | solution.py:63
  150.0 18.8 %collective-permute-start.29 = (bf16[2,128,1024]{2,1,0:T(8,128)(2,1)S(1)}, bf16[2,128,1024]{2,1,0:T(8,128)(2,1)S(1)}, u32[]{:S(2)}, u32[]{:S(2)}) collective-permute-start(bf16[2,128,1024]{2,1,0:T(8,128)(2,1)S(1)} %pad_maximum_fusion.17), channel_id=1, source_target_pairs={{0,8},{1,9},{2,10},{3,11},{4,12},{5,13},{6,14},{7,15},{8,0},{9,1},... | collective-permute-start | bytes 1572872 | tf_op jit(solution)/shard_map/ppermute | solution.py:63
  150.8 18.0 %collective-permute-start.26 = (bf16[4,128,1024]{2,1,0:T(8,128)(2,1)}, bf16[4,128,1024]{2,1,0:T(8,128)(2,1)}, u32[]{:S(2)}, u32[]{:S(2)}) collective-permute-start(bf16[4,128,1024]{2,1,0:T(8,128)(2,1)} %pad_maximum_fusion.8), channel_id=1, source_target_pairs={{0,4},{1,3},{2,6},{3,1},{4,0},{5,7},{6,2},{7,5},{8,12},{9,11},{10,... | collective-permute-start | bytes 3145736 | tf_op jit(solution)/shard_map/ppermute | solution.py:63
  152.3 24.7 %collective-permute-start.28 = (bf16[4,128,1024]{2,1,0:T(8,128)(2,1)S(1)}, bf16[4,128,1024]{2,1,0:T(8,128)(2,1)S(1)}, u32[]{:S(2)}, u32[]{:S(2)}) collective-permute-start(bf16[4,128,1024]{2,1,0:T(8,128)(2,1)S(1)} %pad_maximum_fusion.9), channel_id=1, source_target_pairs={{0,4},{1,3},{2,6},{3,1},{4,0},{5,7},{6,2},{7,5},{8,12},{9,11},{10,... | collective-permute-start | bytes 3145736 | tf_op jit(solution)/shard_map/ppermute | solution.py:63
  179.8 26.1 %collective-permute-start.32 = (bf16[8,128,1024]{2,1,0:T(8,128)(2,1)S(1)}, bf16[8,128,1024]{2,1,0:T(8,128)(2,1)S(1)}, u32[]{:S(2)}, u32[]{:S(2)}) collective-permute-start(bf16[8,128,1024]{2,1,0:T(8,128)(2,1)S(1)} %pad_maximum_fusion.1.refs_0_), channel_id=1, source_target_pairs={{0,2},{1,5},{2,0},{3,7},{4,6},{5,1},{6,4},{7,3},{8,10},{9,13},{10,... | collective-permute-start | bytes 6291464 | tf_op jit(solution)/shard_map/ppermute | solution.py:63
  181.4 24.5 %collective-permute-start.33 = (bf16[8,128,1024]{2,1,0:T(8,128)(2,1)S(1)}, bf16[8,128,1024]{2,1,0:T(8,128)(2,1)}, u32[]{:S(2)}, u32[]{:S(2)}) collective-permute-start(bf16[8,128,1024]{2,1,0:T(8,128)(2,1)S(1)} %pad_maximum_fusion.1.refs_0_), channel_id=1, source_target_pairs={{0,1},{1,0},{2,3},{3,2},{4,5},{5,4},{6,7},{7,6},{8,9},{9,8},{10,11... | collective-permute-start | bytes 6291464 | tf_op jit(solution)/shard_map/ppermute | solution.py:63
  181.4 18.4 %collective-permute-start.34 = (bf16[2,128,1024]{2,1,0:T(8,128)(2,1)S(1)}, bf16[2,128,1024]{2,1,0:T(8,128)(2,1)S(1)}, u32[]{:S(2)}, u32[]{:S(2)}) collective-permute-start(bf16[2,128,1024]{2,1,0:T(8,128)(2,1)S(1)} %pad_maximum_fusion.18), channel_id=1, source_target_pairs={{0,8},{1,9},{2,10},{3,11},{4,12},{5,13},{6,14},{7,15},{8,0},{9,1},... | collective-permute-start | bytes 1572872 | tf_op jit(solution)/shard_map/ppermute | solution.py:63
  219.3 26.4 %collective-permute-start.37 = (bf16[8,128,1024]{2,1,0:T(8,128)(2,1)}, bf16[8,128,1024]{2,1,0:T(8,128)(2,1)}, u32[]{:S(2)}, u32[]{:S(2)}) collective-permute-start(bf16[8,128,1024]{2,1,0:T(8,128)(2,1)} %pad_maximum_fusion.2.refs_0_), channel_id=1, source_target_pairs={{0,2},{1,5},{2,0},{3,7},{4,6},{5,1},{6,4},{7,3},{8,10},{9,13},{10,... | collective-permute-start | bytes 6291464 | tf_op jit(solution)/shard_map/ppermute | solution.py:63
  220.8 24.9 %collective-permute-start.38 = (bf16[8,128,1024]{2,1,0:T(8,128)(2,1)}, bf16[8,128,1024]{2,1,0:T(8,128)(2,1)}, u32[]{:S(2)}, u32[]{:S(2)}) collective-permute-start(bf16[8,128,1024]{2,1,0:T(8,128)(2,1)} %pad_maximum_fusion.2.refs_0_), channel_id=1, source_target_pairs={{0,1},{1,0},{2,3},{3,2},{4,5},{5,4},{6,7},{7,6},{8,9},{9,8},{10,11... | collective-permute-start | bytes 6291464 | tf_op jit(solution)/shard_map/ppermute | solution.py:63
  245.8 18.9 %collective-permute-start.40 = (bf16[4,128,1024]{2,1,0:T(8,128)(2,1)S(1)}, bf16[4,128,1024]{2,1,0:T(8,128)(2,1)S(1)}, u32[]{:S(2)}, u32[]{:S(2)}) collective-permute-start(bf16[4,128,1024]{2,1,0:T(8,128)(2,1)S(1)} %pad_maximum_fusion.10), channel_id=1, source_target_pairs={{0,4},{1,3},{2,6},{3,1},{4,0},{5,7},{6,2},{7,5},{8,12},{9,11},{10,... | collective-permute-start | bytes 3145736 | tf_op jit(solution)/shard_map/ppermute | solution.py:63
  265.3 26.1 %collective-permute-start.43 = (bf16[8,128,1024]{2,1,0:T(8,128)(2,1)S(1)}, bf16[8,128,1024]{2,1,0:T(8,128)(2,1)}, u32[]{:S(2)}, u32[]{:S(2)}) collective-permute-start(bf16[8,128,1024]{2,1,0:T(8,128)(2,1)S(1)} %pad_maximum_fusion.3.refs_0_), channel_id=1, source_target_pairs={{0,2},{1,5},{2,0},{3,7},{4,6},{5,1},{6,4},{7,3},{8,10},{9,13},{10,... | collective-permute-start | bytes 6291464 | tf_op jit(solution)/shard_map/ppermute | solution.py:63
  266.8 24.7 %collective-permute-start.44 = (bf16[8,128,1024]{2,1,0:T(8,128)(2,1)S(1)}, bf16[8,128,1024]{2,1,0:T(8,128)(2,1)S(1)}, u32[]{:S(2)}, u32[]{:S(2)}) collective-permute-start(bf16[8,128,1024]{2,1,0:T(8,128)(2,1)S(1)} %pad_maximum_fusion.3.refs_0_), channel_id=1, source_target_pairs={{0,1},{1,0},{2,3},{3,2},{4,5},{5,4},{6,7},{7,6},{8,9},{9,8},{10,11... | collective-permute-start | bytes 6291464 | tf_op jit(solution)/shard_map/ppermute | solution.py:63
  293.2 19.4 %collective-permute-start.46 = (bf16[8,128,1024]{2,1,0:T(8,128)(2,1)}, bf16[8,128,1024]{2,1,0:T(8,128)(2,1)S(1)}, u32[]{:S(2)}, u32[]{:S(2)}) collective-permute-start(bf16[8,128,1024]{2,1,0:T(8,128)(2,1)} %collective-permute-done.43.refs_1_), channel_id=1, source_target_pairs={{0,1},{1,0},{2,3},{3,2},{4,5},{5,4},{6,7},{7,6},{8,9},{9,8},{10,11... | collective-permute-start | bytes 6291464 | tf_op jit(solution)/shard_map/ppermute | solution.py:63
  306.8 26.2 %collective-permute-start.49 = (bf16[8,128,1024]{2,1,0:T(8,128)(2,1)S(1)}, bf16[8,128,1024]{2,1,0:T(8,128)(2,1)}, u32[]{:S(2)}, u32[]{:S(2)}) collective-permute-start(bf16[8,128,1024]{2,1,0:T(8,128)(2,1)S(1)} %pad_maximum_fusion.4.refs_0_), channel_id=1, source_target_pairs={{0,2},{1,5},{2,0},{3,7},{4,6},{5,1},{6,4},{7,3},{8,10},{9,13},{10,... | collective-permute-start | bytes 6291464 | tf_op jit(solution)/shard_map/ppermute | solution.py:63
  308.3 24.7 %collective-permute-start.50 = (bf16[8,128,1024]{2,1,0:T(8,128)(2,1)S(1)}, bf16[8,128,1024]{2,1,0:T(8,128)(2,1)}, u32[]{:S(2)}, u32[]{:S(2)}) collective-permute-start(bf16[8,128,1024]{2,1,0:T(8,128)(2,1)S(1)} %pad_maximum_fusion.4.refs_0_), channel_id=1, source_target_pairs={{0,1},{1,0},{2,3},{3,2},{4,5},{5,4},{6,7},{7,6},{8,9},{9,8},{10,11... | collective-permute-start | bytes 6291464 | tf_op jit(solution)/shard_map/ppermute | solution.py:63
  312.0 20.1 %collective-permute-start.47 = (bf16[512,512]{1,0:T(8,128)(2,1)}, bf16[512,512]{1,0:T(8,128)(2,1)S(1)}, u32[]{:S(2)}, u32[]{:S(2)}) collective-permute-start(bf16[512,512]{1,0:T(8,128)(2,1)} %get-tuple-element.565), channel_id=1, source_target_pairs={{0,1},{1,0},{2,3},{3,2},{4,5},{5,4},{6,7},{7,6},{8,9},{9,8},{10,11... | collective-permute-start | bytes 1572872 | tf_op jit(solution)/shard_map/ppermute | solution.py:63
  312.6 19.6 %collective-permute-start.48 = (bf16[512,512]{1,0:T(8,128)(2,1)S(1)}, bf16[512,512]{1,0:T(8,128)(2,1)S(1)}, u32[]{:S(2)}, u32[]{:S(2)}) collective-permute-start(bf16[512,512]{1,0:T(8,128)(2,1)S(1)} %get-tuple-element.567), channel_id=1, source_target_pairs={{0,1},{1,0},{2,3},{3,2},{4,5},{5,4},{6,7},{7,6},{8,9},{9,8},{10,11... | collective-permute-start | bytes 1572872 | tf_op jit(solution)/shard_map/ppermute | solution.py:63
  381.0 29.0 %collective-permute-start.56 = (bf16[512,4096]{1,0:T(8,128)(2,1)}, bf16[512,4096]{1,0:T(8,128)(2,1)}, u32[]{:S(2)}, u32[]{:S(2)}) collective-permute-start(bf16[512,4096]{1,0:T(8,128)(2,1)} %get-tuple-element.599.rows_ref.refs_2_), channel_id=1, source_target_pairs={{0,1},{1,0},{2,3},{3,2},{4,5},{5,4},{6,7},{7,6},{8,9},{9,8},{10,11... | collective-permute-start | bytes 12582920 | tf_op jit(solution)/shard_map/ppermute | solution.py:63
  395.0 26.1 %collective-permute-start.58 = (bf16[1024,1024]{1,0:T(8,128)(2,1)S(1)}, bf16[1024,1024]{1,0:T(8,128)(2,1)}, u32[]{:S(2)}, u32[]{:S(2)}) collective-permute-start(bf16[1024,1024]{1,0:T(8,128)(2,1)S(1)} %get-tuple-element.611), channel_id=1, source_target_pairs={{0,2},{1,5},{2,0},{3,7},{4,6},{5,1},{6,4},{7,3},{8,10},{9,13},{10,... | collective-permute-start | bytes 6291464 | tf_op jit(solution)/shard_map/ppermute | solution.py:63
  421.2 31.9 %collective-permute-start.59 = (bf16[256,5120]{1,0:T(8,128)(2,1)}, bf16[256,5120]{1,0:T(8,128)(2,1)S(1)}, u32[]{:S(2)}, u32[]{:S(2)}) collective-permute-start(bf16[256,5120]{1,0:T(8,128)(2,1)} %get-tuple-element.618), channel_id=1, source_target_pairs={{0,2},{1,5},{2,0},{3,7},{4,6},{5,1},{6,4},{7,3},{8,10},{9,13},{10,... | collective-permute-start | bytes 7864328 | tf_op jit(solution)/shard_map/ppermute | solution.py:63
  482.2 19.7 %collective-permute-start.65 = (bf16[128,5120]{1,0:T(8,128)(2,1)S(1)}, bf16[128,5120]{1,0:T(8,128)(2,1)S(1)}, u32[]{:S(2)}, u32[]{:S(2)}) collective-permute-start(bf16[128,5120]{1,0:T(8,128)(2,1)S(1)} %get-tuple-element.650), channel_id=1, source_target_pairs={{0,4},{1,3},{2,6},{3,1},{4,0},{5,7},{6,2},{7,5},{8,12},{9,11},{10,... | collective-permute-start | bytes 3932168 | tf_op jit(solution)/shard_map/ppermute | solution.py:63
  504.2 24.4 %collective-permute-start.66 = (bf16[256,3072]{1,0:T(8,128)(2,1)}, bf16[256,3072]{1,0:T(8,128)(2,1)}, u32[]{:S(2)}, u32[]{:S(2)}) collective-permute-start(bf16[256,3072]{1,0:T(8,128)(2,1)} %get-tuple-element.665), channel_id=1, source_target_pairs={{0,2},{1,5},{2,0},{3,7},{4,6},{5,1},{6,4},{7,3},{8,10},{9,13},{10,... | collective-permute-start | bytes 4718600 | tf_op jit(solution)/shard_map/ppermute | solution.py:63
  505.4 46.5 %collective-permute-start.69 = (bf16[512,4096]{1,0:T(8,128)(2,1)}, bf16[512,4096]{1,0:T(8,128)(2,1)}, u32[]{:S(2)}, u32[]{:S(2)}) collective-permute-start(bf16[512,4096]{1,0:T(8,128)(2,1)} %get-tuple-element.675.rows_ref.refs_2_), channel_id=1, source_target_pairs={{0,1},{1,0},{2,3},{3,2},{4,5},{5,4},{6,7},{7,6},{8,9},{9,8},{10,11... | collective-permute-start | bytes 12582920 | tf_op jit(solution)/shard_map/ppermute | solution.py:63
  505.5 23.1 %collective-permute-start.67 = (bf16[64,5120]{1,0:T(8,128)(2,1)}, bf16[64,5120]{1,0:T(8,128)(2,1)}, u32[]{:S(2)}, u32[]{:S(2)}) collective-permute-start(bf16[64,5120]{1,0:T(8,128)(2,1)} %get-tuple-element.666), channel_id=1, source_target_pairs={{0,8},{1,9},{2,10},{3,11},{4,12},{5,13},{6,14},{7,15},{8,0},{9,1},... | collective-permute-start | bytes 1966088 | tf_op jit(solution)/shard_map/ppermute | solution.py:63
  506.6 20.6 %collective-permute-start.68 = (bf16[128,1024]{1,0:T(8,128)(2,1)}, bf16[128,1024]{1,0:T(8,128)(2,1)}, u32[]{:S(2)}, u32[]{:S(2)}) collective-permute-start(bf16[128,1024]{1,0:T(8,128)(2,1)} %add_convert_fusion.30), channel_id=1, source_target_pairs={{0,16},{1,17},{2,18},{3,19},{4,20},{5,21},{6,22},{7,23},{8,24},{9,... | collective-permute-start | bytes 786440 | tf_op jit(solution)/shard_map/ppermute | solution.py:63
  545.6 32.7 %collective-permute-start.71 = (bf16[1024,512]{1,0:T(8,128)(2,1)S(1)}, bf16[1024,512]{1,0:T(8,128)(2,1)}, u32[]{:S(2)}, u32[]{:S(2)}) collective-permute-start(bf16[1024,512]{1,0:T(8,128)(2,1)S(1)} %get-tuple-element.687), channel_id=1, source_target_pairs={{0,8},{1,9},{2,10},{3,11},{4,12},{5,13},{6,14},{7,15},{8,0},{9,1},... | collective-permute-start | bytes 3145736 | tf_op jit(solution)/shard_map/ppermute | solution.py:63
  546.8 31.6 %collective-permute-start.72 = (bf16[1024,512]{1,0:T(8,128)(2,1)S(1)}, bf16[1024,512]{1,0:T(8,128)(2,1)S(1)}, u32[]{:S(2)}, u32[]{:S(2)}) collective-permute-start(bf16[1024,512]{1,0:T(8,128)(2,1)S(1)} %get-tuple-element.688), channel_id=1, source_target_pairs={{0,2},{1,5},{2,0},{3,7},{4,6},{5,1},{6,4},{7,3},{8,10},{9,13},{10,... | collective-permute-start | bytes 3145736 | tf_op jit(solution)/shard_map/ppermute | solution.py:63
  547.7 29.2 %collective-permute-start.73 = (bf16[128,3072]{1,0:T(8,128)(2,1)}, bf16[128,3072]{1,0:T(8,128)(2,1)S(1)}, u32[]{:S(2)}, u32[]{:S(2)}) collective-permute-start(bf16[128,3072]{1,0:T(8,128)(2,1)} %get-tuple-element.689), channel_id=1, source_target_pairs={{0,4},{1,3},{2,6},{3,1},{4,0},{5,7},{6,2},{7,5},{8,12},{9,11},{10,... | collective-permute-start | bytes 2359304 | tf_op jit(solution)/shard_map/ppermute | solution.py:63
  548.5 28.4 %collective-permute-start.74 = (bf16[32,5120]{1,0:T(8,128)(2,1)}, bf16[32,5120]{1,0:T(8,128)(2,1)S(1)}, u32[]{:S(2)}, u32[]{:S(2)}) collective-permute-start(bf16[32,5120]{1,0:T(8,128)(2,1)} %add_convert_fusion.25), channel_id=1, source_target_pairs={{0,16},{1,17},{2,18},{3,19},{4,20},{5,21},{6,22},{7,23},{8,24},{9,... | collective-permute-start | bytes 983048 | tf_op jit(solution)/shard_map/ppermute | solution.py:63
  582.8 37.3 %collective-permute-start.75 = (bf16[256,5120]{1,0:T(8,128)(2,1)S(1)}, bf16[256,5120]{1,0:T(8,128)(2,1)S(1)}, u32[]{:S(2)}, u32[]{:S(2)}) collective-permute-start(bf16[256,5120]{1,0:T(8,128)(2,1)S(1)} %copy-done.146), channel_id=1, source_target_pairs={{0,2},{1,5},{2,0},{3,7},{4,6},{5,1},{6,4},{7,3},{8,10},{9,13},{10,... | collective-permute-start | bytes 7864328 | tf_op jit(solution)/shard_map/ppermute | solution.py:63
  583.5 25.3 %collective-permute-start.76 = (bf16[512,512]{1,0:T(8,128)(2,1)S(1)}, bf16[512,512]{1,0:T(8,128)(2,1)S(1)}, u32[]{:S(2)}, u32[]{:S(2)}) collective-permute-start(bf16[512,512]{1,0:T(8,128)(2,1)S(1)} %get-tuple-element.702), channel_id=1, source_target_pairs={{0,16},{1,17},{2,18},{3,19},{4,20},{5,21},{6,22},{7,23},{8,24},{9,... | collective-permute-start | bytes 1572872 | tf_op jit(solution)/shard_map/ppermute | solution.py:63
  585.6 23.2 %collective-permute-start.77 = (bf16[512,512]{1,0:T(8,128)(2,1)S(1)}, bf16[512,512]{1,0:T(8,128)(2,1)S(1)}, u32[]{:S(2)}, u32[]{:S(2)}) collective-permute-start(bf16[512,512]{1,0:T(8,128)(2,1)S(1)} %get-tuple-element.703), channel_id=1, source_target_pairs={{0,4},{1,3},{2,6},{3,1},{4,0},{5,7},{6,2},{7,5},{8,12},{9,11},{10,... | collective-permute-start | bytes 1572872 | tf_op jit(solution)/shard_map/ppermute | solution.py:63
  586.4 21.2 %collective-permute-start.78 = (bf16[64,3072]{1,0:T(8,128)(2,1)S(1)}, bf16[64,3072]{1,0:T(8,128)(2,1)S(1)}, u32[]{:S(2)}, u32[]{:S(2)}) collective-permute-start(bf16[64,3072]{1,0:T(8,128)(2,1)S(1)} %get-tuple-element.704), channel_id=1, source_target_pairs={{0,8},{1,9},{2,10},{3,11},{4,12},{5,13},{6,14},{7,15},{8,0},{9,1},... | collective-permute-start | bytes 1179656 | tf_op jit(solution)/shard_map/ppermute | solution.py:63
  628.6 37.0 %collective-permute-start.83 = (bf16[128,5120]{1,0:T(8,128)(2,1)}, bf16[128,5120]{1,0:T(8,128)(2,1)}, u32[]{:S(2)}, u32[]{:S(2)}) collective-permute-start(bf16[128,5120]{1,0:T(8,128)(2,1)} %get-tuple-element.729), channel_id=1, source_target_pairs={{0,4},{1,3},{2,6},{3,1},{4,0},{5,7},{6,2},{7,5},{8,12},{9,11},{10,... | collective-permute-start | bytes 3932168 | tf_op jit(solution)/shard_map/ppermute | solution.py:63
  642.1 23.6 %collective-permute-start.82 = (bf16[256,3072]{1,0:T(8,128)(2,1)}, bf16[256,3072]{1,0:T(8,128)(2,1)}, u32[]{:S(2)}, u32[]{:S(2)}) collective-permute-start(bf16[256,3072]{1,0:T(8,128)(2,1)} %get-tuple-element.728), channel_id=1, source_target_pairs={{0,2},{1,5},{2,0},{3,7},{4,6},{5,1},{6,4},{7,3},{8,10},{9,13},{10,... | collective-permute-start | bytes 4718600 | tf_op jit(solution)/shard_map/ppermute | solution.py:63
  645.6 20.0 %collective-permute-start.84 = (bf16[256,512]{1,0:T(8,128)(2,1)}, bf16[256,512]{1,0:T(8,128)(2,1)}, u32[]{:S(2)}, u32[]{:S(2)}) collective-permute-start(bf16[256,512]{1,0:T(8,128)(2,1)} %get-tuple-element.730), channel_id=1, source_target_pairs={{0,2},{1,5},{2,0},{3,7},{4,6},{5,1},{6,4},{7,3},{8,10},{9,13},{10,... | collective-permute-start | bytes 786440 | tf_op jit(solution)/shard_map/ppermute | solution.py:63
  647.0 18.6 %collective-permute-start.85 = (bf16[256,512]{1,0:T(8,128)(2,1)}, bf16[256,512]{1,0:T(8,128)(2,1)}, u32[]{:S(2)}, u32[]{:S(2)}) collective-permute-start(bf16[256,512]{1,0:T(8,128)(2,1)} %get-tuple-element.731), channel_id=1, source_target_pairs={{0,8},{1,9},{2,10},{3,11},{4,12},{5,13},{6,14},{7,15},{8,0},{9,1},... | collective-permute-start | bytes 786440 | tf_op jit(solution)/shard_map/ppermute | solution.py:63
  677.7 18.4 %collective-permute-start.88 = (bf16[64,5120]{1,0:T(8,128)(2,1)S(1)}, bf16[64,5120]{1,0:T(8,128)(2,1)S(1)}, u32[]{:S(2)}, u32[]{:S(2)}) collective-permute-start(bf16[64,5120]{1,0:T(8,128)(2,1)S(1)} %get-tuple-element.752), channel_id=1, source_target_pairs={{0,8},{1,9},{2,10},{3,11},{4,12},{5,13},{6,14},{7,15},{8,0},{9,1},... | collective-permute-start | bytes 1966088 | tf_op jit(solution)/shard_map/ppermute | solution.py:63
  696.4 18.7 %collective-permute-start.92 = (bf16[256,1024]{1,0:T(8,128)(2,1)S(1)}, bf16[256,1024]{1,0:T(8,128)(2,1)S(1)}, u32[]{:S(2)}, u32[]{:S(2)}) collective-permute-start(bf16[256,1024]{1,0:T(8,128)(2,1)S(1)} %slice.977), channel_id=1, source_target_pairs={{0,2},{1,3},{2,0},{3,1},{4,6},{5,7},{6,4},{7,5},{8,10},{9,11},{10,... | collective-permute-start | bytes 1572872 | tf_op jit(solution)/shard_map/ppermute | solution.py:63
  (199 other events, 1906.2 us)

commit v5 on v4

--- a/solution.py
+++ b/solution.py
@@ -55,7 +55,6 @@
 TO_NEAR = pairs(lambda z, y, x, c: (z, 1 - y if c == 0 else y, x if c == 0 else 1 - x, c))
 TO_ODD = pairs(lambda z, y, x, c: (z ^ 1, y, x, c))
 TO_PAIR = pairs(lambda z, y, x, c: (z ^ 2, y, x, c))
-TO_BOTH = pairs(lambda z, y, x, c: (z ^ 3, y, x, c))
 TO_Z = [pairs(lambda z, y, x, c, k=k: ((z + k) % 4, y, x, c)) for k in range(4)]
 
 
@@ -99,13 +98,17 @@
         kernel,
         in_specs=[pl.BlockSpec(memory_space=pltpu.SMEM)]
         + [pl.BlockSpec(memory_space=pl.ANY)] * len(pieces),
-        out_specs=[pl.BlockSpec(memory_space=pl.ANY)] * len(shapes),
+        out_specs=[pl.BlockSpec(memory_space=pltpu.HBM)] * len(shapes),
         out_shape=[jax.ShapeDtypeStruct(shape, bf16) for shape in shapes],
         scratch_shapes=[pltpu.VMEM(p.shape, bf16) for p in pieces]
         + [pltpu.SemaphoreType.DMA((total,)), pltpu.SemaphoreType.DMA((count,))],
         compiler_params=pltpu.CompilerParams(vmem_limit_bytes=40 << 20),
         cost_estimate=SMALL_COST,
     )(coords, *pieces)
+
+
+def in_hbm(value):
+    return pltpu.with_memory_space_constraint(value, pltpu.HBM)
 
 
 def pick(value, index, axis):
@@ -200,21 +203,6 @@
 Sums = collections.namedtuple("Sums", "o i a")
 
 
-class SmallUnit(SumUnit):
-    def local(self, got):
-        if self.step < 2:
-            return super().local(got)
-        self.step += 1
-        if self.step > 3:
-            self.kept = self.kept + sum(value.astype(f32) for value in got)
-            return []
-        rows = self.kept.shape[0] // 4
-        total = self.kept.astype(f32) + got[0].astype(f32)
-        blocks = [total[n * rows : (n + 1) * rows] for n in range(4)]
-        self.kept = blocks[3]
-        return [(b.astype(bf16), to) for b, to in zip(blocks, (TO_BOTH, TO_ODD, TO_PAIR))]
-
-
 def block_order(coords, z_first=False):
     z, y, x, c = coords[0], coords[1], coords[2], coords[3]
     order = []
@@ -280,7 +268,7 @@
         whole = pl.BlockSpec((rows, tokens), lambda j: (0, 0))
         cut = pl.BlockSpec((tokens, tile), lambda j, s=start, n=count: (0, jnp.clip(j - s, 0, n - 1) + first // tile))
         in_specs += [whole, whole, cut, cut]
-        args += [*left, *right]
+        args += [*map(in_hbm, left), *right]
     out = jax.ShapeDtypeStruct((half, columns), bf16)
     return pl.pallas_call(
         kernel,
@@ -332,7 +320,7 @@
         out_shape=[out, out],
         compiler_params=pltpu.CompilerParams(vmem_limit_bytes=48 << 20),
         cost_estimate=SMALL_COST,
-    )(order, left[0], left[0], left[1], left[1], *right)
+    )(order, *map(in_hbm, (left[0], left[0], left[1], left[1])), *right)
 
 
 BLOCK = 256
@@ -588,7 +576,7 @@
         + [jax.ShapeDtypeStruct((1, width), f32)] * sums,
         compiler_params=pltpu.CompilerParams(vmem_limit_bytes=48 << 20),
         cost_estimate=SMALL_COST,
-    )(rows, weight, *[v.reshape(1, width) for v in by_column], *tiles)
+    )(rows, in_hbm(weight), *[v.reshape(1, width) for v in by_column], *tiles)
 
 
 def gelu_parts(total, bias):
@@ -754,11 +742,13 @@
     order, order_z = block_order(coords), block_order(coords, True)
     matrices = order_matrices(order)
 
-    token_got, every = phase((token_got, every), u[0])
+    token_got, every = phase((token_got, every), u[0], u[1])
+    every, upstream_left = lax.optimization_barrier((every, upstream_left))
+    upstream_got = send(upstream_left, TO_X)
     every = by_place(every, send(every, TO_Y), y, 1)
-    every, bias = phase((every, bias), u[0], u[1])
+    every, bias, upstream_got = phase((every, bias, upstream_got), u[0], settle=[u[1]])
     every = by_place(every, send(every, TO_X), x, 2)
-    every, matrices = phase((every, matrices), u[0], u[1], u[2])
+    every, matrices = phase((every, matrices), u[0], u[1])
     every = by_place(every, send(every, TO_CORE), c, 3)
     every = every.reshape(devices, 1024)[:, :held].astype(f32)
     small_all = (
@@ -775,7 +765,7 @@
     )
     stream = jnp.concatenate([token_kept, token_got]).astype(f32)
     stream, small_all, wide_all = phase((stream, small_all, wide_all), u[0], u[1], u[2], u[3])
-    saved = []
+    saved, active_gots = [], []
     for layer in range(layer_count):
         a_unit, i_unit, o_unit = units[layer]
         next_a, next_i, next_o = units[layer + 1] if layer + 1 < layer_count else (None,) * 3
@@ -786,9 +776,9 @@
         three_bias = jnp.concatenate([q_bias, jnp.zeros_like(q_bias), v_bias])
         (three,) = product(stream_low, w_three, 1024, lambda total, b: (total + b,), (bf16,), (three_bias,))
         if next_a:
-            three = phase(three, i_unit, next_a, next_i, settle=[o_unit])
+            three = phase(three, i_unit, o_unit, next_a)
         else:
-            three = phase(three, i_unit)
+            three = phase(three, i_unit, settle=[o_unit])
         three_got = send(three, TO_CORE)
         (left_stream,) = selected(matrices, tie(stream_low, three))
         three, left_stream = lax.optimization_barrier((three, left_stream))
@@ -796,10 +786,12 @@
         mixed, totals = attend_forward_blocks(place_of, three, three_got, bias)
         if next_a:
             mixed, totals, left_stream = phase(
-                (mixed, totals, left_stream), i_unit, o_unit, next_a, next_i, next_o
+                (mixed, totals, left_stream), i_unit, o_unit, next_a, next_i
             )
         else:
-            mixed, totals, left_stream = phase((mixed, totals, left_stream), i_unit, o_unit)
+            mixed, totals, left_stream, active_gots = phase(
+                (mixed, totals, left_stream, active_gots), i_unit, o_unit
+            )
         w_inner, *w_more = i_unit.result()
         (w_mix,) = w_rest + w_more
         w_inner, w_mix = w_inner.reshape(D, FF), w_mix.reshape(D, D)
@@ -807,7 +799,7 @@
         first = norm_forward(first_sum)[0] * gain1 + shift1
         first_low = first.astype(bf16)
         if next_a:
-            first_low = phase(first_low, o_unit, next_o, settle=[next_a, next_i])
+            first_low = phase(first_low, o_unit, next_i, settle=[next_a])
         else:
             first_low = phase(first_low, o_unit)
         left_mix, left_first = selected(matrices, mixed, first_low)
@@ -816,33 +808,28 @@
         active, slope = product(first_low, w_inner, 1024, gelu_parts, (bf16, bf16), (wide_all[layer],))
         if next_a:
             active, slope, left_mix, left_first = phase(
-                (active, slope, left_mix, left_first), o_unit, next_a, settle=[next_o]
+                (active, slope, left_mix, left_first), o_unit, next_a, next_o, settle=[next_i]
             )
         else:
             active, slope, left_mix, left_first = phase((active, slope, left_mix, left_first), o_unit)
-        if not next_a:
-            upstream_left, active = lax.optimization_barrier((upstream_left, active))
-            upstream_got = send(upstream_left, TO_X)
         (w_outer,) = o_unit.result()
         active_got = send(tie(active, w_outer), TO_CORE)
         w_outer = w_outer.reshape(FF, D)
         (second_sum,) = product(
             active, w_outer, 256, lambda total, b, f: (f + (total + b),), (f32,), (o_bias,), (first,)
         )
-        if next_a:
+        if not next_a:
             second_sum, active_got = lax.optimization_barrier((second_sum, active_got))
-        else:
-            second_sum, active_got, upstream_got = lax.optimization_barrier((second_sum, active_got, upstream_got))
-        left_active = (active, active_got)
+        active_gots.append(active_got)
         stream = norm_forward(second_sum)[0] * gain2 + shift2
         if next_a:
-            stream = phase(stream, next_a, next_i)
+            stream = phase(stream, next_a, next_i, next_o)
         saved.append(
             (
                 (w_three, w_mix, w_inner, w_outer, gain1, gain2),
                 (three, three_got, totals, mixed),
                 (first_sum, slope, second_sum),
-                (left_stream, left_mix, left_first, left_active),
+                (left_stream, left_mix, left_first, active),
             )
         )
 
@@ -862,7 +849,8 @@
         w_three, w_mix, w_inner, w_outer, gain1, gain2 = weights
         three, three_got, totals, mixed = kept
         first_sum, slope, second_sum = rest
-        left_stream, left_mix, left_first, left_active = lefts
+        left_stream, left_mix, left_first, active = lefts
+        left_active = (active, active_gots[layer])
 
         def with_sum(total, slopes):
             low = (total * slopes).astype(bf16)
@@ -876,7 +864,7 @@
         if before:
             inner_low, second_got = phase((inner_low, second_got), before.o[0], before.i, before.a)
         else:
-            inner_low, second_got, output_got = lax.optimization_barrier((inner_low, second_got, output_got))
+            inner_low, second_got = lax.optimization_barrier((inner_low, second_got))
         inner_got = send(inner_low, TO_CORE)
         second_pair = (second_low, second_got)
         if before:
@@ -884,44 +872,45 @@
                 SumUnit(wide_terms_of(order_z, left_active, second_pair, 0, 2), Z_FIRST),
                 SumUnit(wide_terms_of(order, left_active, second_pair, 1, 2)),
             )
-            second_grad, inner_low = phase(
-                (second_grad, inner_low), *o_sums, before.a, before.i, settle=before.o
+            second_grad, inner_low, inner_got = phase(
+                (second_grad, inner_low, inner_got), *o_sums, before.a, before.i, settle=before.o
             )
         else:
             o_sums = (SumUnit(wide_terms_of(order, left_active, second_pair)),)
-            second_grad, inner_low = phase((second_grad, inner_low), *o_sums)
+            second_grad, inner_low, inner_got, output_got = phase(
+                (second_grad, inner_low, inner_got, output_got), *o_sums
+            )
         (first_grad,) = product(
             inner_low, w_inner, 256, lambda total, g: (g + total,), (f32,), (), (second_grad,), transposed=True
         )
         first_sum_grad, branch_low, first_sums = norm_backward_rows(first_sum, gain1, first_grad)
         branch_got = send(branch_low, TO_CORE)
         (mixed_grad,) = product(branch_low, w_mix, 512, lambda total: (total,), (bf16,), transposed=True)
-        mixed_grad, inner_got, branch_got = lax.optimization_barrier((mixed_grad, inner_got, branch_got))
-        i_sum = SumUnit(
-            weight_terms((left_first, (inner_low, inner_got), FF), (left_mix, (branch_low, branch_got), D))
-        )
+        i_sum = SumUnit(weight_terms((left_first, tie((inner_low, inner_got), mixed_grad), FF)))
         if before:
             mixed_grad = phase(mixed_grad, i_sum, *o_sums, before.a, settle=[before.i])
         else:
             mixed_grad = phase(mixed_grad, i_sum, settle=o_sums)
         query_low, own_grads, sent_grads = attend_backward_blocks(
-            place_of, three, three_got, bias, mixed, totals, mixed_grad
+            place_of, in_hbm(three), in_hbm(three_got), bias, in_hbm(mixed), in_hbm(totals), mixed_grad
         )
         grads_back = send(sent_grads, TO_CORE)
         if before:
-            query_low, own_grads = phase((query_low, own_grads), i_sum, *o_sums, before.a)
+            query_low, own_grads, branch_got = phase((query_low, own_grads, branch_got), i_sum, *o_sums, before.a)
         else:
-            query_low, own_grads = phase((query_low, own_grads), *o_sums, settle=[i_sum])
+            query_low, own_grads, branch_got = phase((query_low, own_grads, branch_got), *o_sums, settle=[i_sum])
         low, low_sums = merged(query_low, own_grads, grads_back)
         low_got = send(low, TO_CORE)
         if layer:
             (upstream,) = product(
                 low, w_three, 256, lambda total, g: (g + total,), (f32,), (), (first_sum_grad,), transposed=True
             )
-            a_sum = SumUnit(weight_terms((left_stream, tie((low, low_got), upstream), 3 * D)))
+            mix_pair = (left_mix, (branch_low, branch_got), D)
+            a_sum = SumUnit(weight_terms((left_stream, tie((low, low_got), upstream), 3 * D), mix_pair))
         else:
-            a_sum = SumUnit(weight_terms((left_stream, (low, low_got), 3 * D)))
-            low, low_sums = phase((low, low_sums), a_sum, settle=[before.a] if before else [])
+            mix_pair = (left_mix, (branch_low, branch_got), D)
+            a_sum = SumUnit(weight_terms((left_stream, (low, low_got), 3 * D), mix_pair))
+            low, low_sums = phase((low, low_sums), a_sum, settle=[i_sum, before.a] if before else [i_sum])
             (upstream,) = product(
                 low, w_three, 256, lambda total, g: (g + total,), (f32,), (), (first_sum_grad,), transposed=True
             )
@@ -958,8 +947,9 @@
     chosen = (order[:, None] == lax.iota(jnp.int32, devices)[None, :]).astype(f32)
     terms = jnp.dot(chosen, terms, precision=lax.Precision.HIGHEST).reshape(2, 128, 128)
     terms = (terms[0] + send(terms[1].astype(bf16), TO_CORE).astype(f32)).astype(bf16)
-    small_sum = SmallUnit((terms[:64], terms[64:]))
-
+    small_sum = SumUnit((terms[:64], terms[64:]))
+
+    phase((), small_sum)
     last = sums[0]
     done = [unit for layer in range(1, layer_count) for unit in (*sums[layer].o, sums[layer].i, sums[layer].a)]
     upstream, output_got = phase((upstream, output_got), last.a, last.i, *last.o, small_sum, *done)
@@ -983,13 +973,13 @@
         a_all[:, :, :D],
         a_all[:, :, D : 2 * D],
         a_all[:, :, 2 * D : 3 * D],
-        i_all[:, :, FF:],
+        a_all[:, :, 3 * D :],
         small_own[:, 0],
         small_own[:, 1],
         small_own[:, 2],
         small_own[:, 3],
         small_own[:, 4],
-        i_all[:, :, :FF],
+        i_all,
         wide_own,
         o_all,
         small_own[:, 5],

time: 739 us -> 715 us (0.968)
  waiting for transfers between devices: 207 us -> 181 us
  local copies, waits for them, and re-layouts: 55.6 us -> 45.8 us
    ppermute x100 -> x99, waiting for transfers between devices: 207 us -> 181 us  [send(): return lax.ppermute(value, AXES, to)]
    unnamed x306 -> x274, local copies, waits for them, and re-layouts: 31.5 us -> 21.6 us
    convert_element_type x14 -> x16, other arithmetic: 22.7 us -> 26.2 us  [local(): self.kept = self.kept.astype(bf16)]
    ppermute x100 -> x99, starting transfers between devices: 94.2 us -> 92.8 us  [send(): return lax.ppermute(value, AXES, to)]
  transfers between devices with their start and end apart: 100 -> 99, of which waited for: 43 -> 44; matrix products, arithmetic and copies ran while one was open for 8% -> 8% of each run, Pallas kernels for 38% -> 40%
where the time goes in v5:
time: 715 us; the launch traced here: 704 us
  Pallas kernels  301 us (42%)
  waiting for transfers between devices  181 us (25%)
  starting transfers between devices  92.8 us (13%)
  other arithmetic  76.4 us (11%)
  local copies, waits for them, and re-layouts  45.8 us (6%)
    ppermute x99, waiting for transfers between devices, send(): return lax.ppermute(value, AXES, to)  181 us
    pallas_call x14, Pallas kernels, product(): pl.pallas_call(kernel, grid=(width // tile,), in_specs=[pl.BlockSpec((tok...  107 us
    ppermute x99, starting transfers between devices, send(): return lax.ppermute(value, AXES, to)  92.8 us
    pallas_call x4, Pallas kernels, call_attention(): pl.pallas_call(kernel, grid=(pairs_count,), in_specs=in_specs, out_specs=...  66.7 us
    pallas_call x6, Pallas kernels, place(): pl.pallas_call(kernel, in_specs=[pl.BlockSpec(memory_space=pltpu.SMEM)] +...  38.3 us
    pallas_call x4, Pallas kernels, weight_terms(): pl.pallas_call(kernel, grid=(columns // tile,), in_specs=in_specs, out_sp...  34.3 us
    pallas_call x3, Pallas kernels, wide_terms_of(): pl.pallas_call(kernel, grid_spec=pltpu.PrefetchScalarGridSpec(num_scalar_...  30.1 us
    convert_element_type x16, other arithmetic, local(): self.kept = self.kept.astype(bf16)  26.2 us
  transfers between devices with their start and end apart: 99, of which 44 were waited for; matrix products, arithmetic and copies ran while one was open for 8% of the time, Pallas kernels for 40%

profile of v5, /device:TPU:0, one launch (start us, length us, event | category | flops | bytes accessed | tf_op | source)
XLA Modules:
  0.0 704.5 jit_solution(10262674966345382521)
XLA Ops:
  20.6 4.3 collective-permute-done.4
  24.9 4.7 collective-permute-done
  40.3 7.2 %collective-permute-done.8 = bf16[1,160,1024]{2,1,0:T(8,128)(2,1)S(1)} collective-permute-done((bf16[1,160,1024]{2,1,0:T(8,128)(2,1)S(1)}, bf16[1,160,1024]{2,1,0:T(8,128)(2,1)S(1)}, u32[]{:S(2)}, u32[]{:S(2)}) %collective-permute-start.8) | collective-permute-done | bytes 327712 | tf_op jit(solution)/shard_map/ppermute | solution.py:62
  56.1 6.0 collective-permute-done.10
  76.6 7.7 %collective-permute-done.14 = bf16[2,160,1024]{2,1,0:T(8,128)(2,1)} collective-permute-done((bf16[2,160,1024]{2,1,0:T(8,128)(2,1)}, bf16[2,160,1024]{2,1,0:T(8,128)(2,1)}, u32[]{:S(2)}, u32[]{:S(2)}) %collective-permute-start.14) | collective-permute-done | bytes 655392 | tf_op jit(solution)/shard_map/ppermute | solution.py:62
  99.0 5.9 shard_map.306.q_ref.km_ref.vm_ref
  108.6 5.5 collective-permute-done.18
  126.0 12.5 %shard_map.308 = (bf16[512,1024]{1,0:T(8,128)(2,1)S(1)}, f32[8,2,512]{2,1,0:T(2,128)S(1)}) custom-call(s32[1]{0:T(128)} %bitcast.83.s_ref, bf16[512,3072]{1,0:T(8,128)(2,1)S(1)} %shard_map.306.q_ref.km_ref.vm_ref, bf16[512,3072]{1,0:T(8,128)(2,1)S(1)} %shard_map.306.q_ref.km_ref.vm_ref, bf16[512,3072]{1,0:T(8,128)(2,1)} %collective-permute-done.19.ko_ref.vo_ref, ...), custom_call_target="tpu_custom_call" | custom-call | flops 1024 | bytes 1024 | tf_op jit(solution)/shard_map/pallas_call | solution.py:459
  138.5 10.5 %collective-permute-done.24 = bf16[2,128,1024]{2,1,0:T(8,128)(2,1)S(1)} collective-permute-done((bf16[2,128,1024]{2,1,0:T(8,128)(2,1)}, bf16[2,128,1024]{2,1,0:T(8,128)(2,1)S(1)}, u32[]{:S(2)}, u32[]{:S(2)}) %collective-permute-start.24) | collective-permute-done | bytes 524320 | tf_op jit(solution)/shard_map/ppermute | solution.py:62
  159.0 7.6 %shard_map.309 = (bf16[4,2,2,2,32,4096]{5,4,3,2,1,0:T(8,128)(2,1)}, bf16[4,2,2,2,32,1024]{5,4,3,2,1,0:T(8,128)(2,1)S(1)}) custom-call(s32[4]{0:T(128)S(1)} %pad_add_fusion.coords_ref, bf16[8,160,1024]{2,1,0:T(8,128)(2,1)S(1)} %pad_maximum_fusion.refs_0_, bf16[8,160,1024]{2,1,0:T(8,128)(2,1)S(1)} %collective-permute-done.21.refs_1_, ...), custom_call_target="tpu_custom_call" | custom-call | flops 1024 | bytes 1024 | tf_op jit(solution)/shard_map/pallas_call | solution.py:97
  169.8 10.5 %collective-permute-done.28 = bf16[4,128,1024]{2,1,0:T(8,128)(2,1)S(1)} collective-permute-done((bf16[4,128,1024]{2,1,0:T(8,128)(2,1)S(1)}, bf16[4,128,1024]{2,1,0:T(8,128)(2,1)S(1)}, u32[]{:S(2)}, u32[]{:S(2)}) %collective-permute-start.28) | collective-permute-done | bytes 1048608 | tf_op jit(solution)/shard_map/ppermute | solution.py:62
  192.4 11.0 %shard_map.311 = (bf16[512,4096]{1,0:T(8,128)(2,1)S(1)}, bf16[512,4096]{1,0:T(8,128)(2,1)}) custom-call(bf16[512,1024]{1,0:T(8,128)(2,1)S(1)} %copy-done.25, bf16[1024,4096]{1,0:T(8,128)(2,1)} %bitcast.291, f32[1,4096]{1,0:T(1,128)S(1)} %get-tuple-element.879.refs_0_), custom_call_target="tpu_custom_call" | custom-call | flops 1024 | bytes 1024 | tf_op jit(solution)/shard_map/pallas_call | solution.py:568
  203.4 6.5 collective-permute-done.31.refs_1_
  217.2 5.9 shard_map.312
  223.1 8.5 %shard_map.313.total_ref = f32[512,1024]{1,0:T(8,128)S(1)} custom-call(bf16[512,4096]{1,0:T(8,128)(2,1)} %copy-done.4, bf16[4096,1024]{1,0:T(8,128)(2,1)} %bitcast.285, f32[1,1024]{1,0:T(1,128)S(1)} %get-tuple-element.869.refs_0_, f32[512,1024]{1,0:T(8,128)S(1)} %get-tuple-element.802.refs_1_), custom_call_target="tpu_custom_call" | custom-call | flops 1024 | bytes 1024 | tf_op jit(solution)/shard_map/pallas_call | solution.py:568
  233.4 5.6 collective-permute-done.35.refs_1_
  245.5 7.2 %shard_map.314 = (bf16[4,2,2,2,32,3072]{5,4,3,2,1,0:T(8,128)(2,1)}, bf16[4,2,2,2,32,1024]{5,4,3,2,1,0:T(8,128)(2,1)S(1)}) custom-call(s32[4]{0:T(128)S(1)} %pad_add_fusion.coords_ref, bf16[8,128,1024]{2,1,0:T(8,128)(2,1)} %pad_maximum_fusion.2.refs_0_, bf16[8,128,1024]{2,1,0:T(8,128)(2,1)} %collective-permute-done.35.refs_1_, ...), custom_call_target="tpu_custom_call" | custom-call | flops 1024 | bytes 1024 | tf_op jit(solution)/shard_map/pallas_call | solution.py:97
  254.1 6.0 shard_map.315.q_ref.km_ref.vm_ref
  260.2 4.4 pad_maximum_fusion.3.refs_0_
  270.3 12.6 %shard_map.317 = (bf16[512,1024]{1,0:T(8,128)(2,1)S(1)}, f32[8,2,512]{2,1,0:T(2,128)S(1)}) custom-call(s32[1]{0:T(128)} %bitcast.83.s_ref, bf16[512,3072]{1,0:T(8,128)(2,1)S(1)} %shard_map.315.q_ref.km_ref.vm_ref, bf16[512,3072]{1,0:T(8,128)(2,1)S(1)} %shard_map.315.q_ref.km_ref.vm_ref, bf16[512,3072]{1,0:T(8,128)(2,1)} %collective-permute-done.41.ko_ref.vo_ref, ...), custom_call_target="tpu_custom_call" | custom-call | flops 1024 | bytes 1024 | tf_op jit(solution)/shard_map/pallas_call | solution.py:459
  283.0 8.0 %collective-permute-done.44.refs_1_ = bf16[8,128,1024]{2,1,0:T(8,128)(2,1)} collective-permute-done((bf16[8,128,1024]{2,1,0:T(8,128)(2,1)}, bf16[8,128,1024]{2,1,0:T(8,128)(2,1)}, u32[]{:S(2)}, u32[]{:S(2)}) %collective-permute-start.44) | collective-permute-done | bytes 2097184 | tf_op jit(solution)/shard_map/ppermute | solution.py:62
  297.6 8.5 %collective-permute-done.46 = bf16[4,128,1024]{2,1,0:T(8,128)(2,1)S(1)} collective-permute-done((bf16[4,128,1024]{2,1,0:T(8,128)(2,1)S(1)}, bf16[4,128,1024]{2,1,0:T(8,128)(2,1)S(1)}, u32[]{:S(2)}, u32[]{:S(2)}) %collective-permute-start.46) | collective-permute-done | bytes 1048608 | tf_op jit(solution)/shard_map/ppermute | solution.py:62
  312.2 7.3 %shard_map.319 = bf16[4,2,2,2,32,4096]{5,4,3,2,1,0:T(8,128)(2,1)} custom-call(s32[4]{0:T(128)S(1)} %pad_add_fusion.coords_ref, bf16[8,128,1024]{2,1,0:T(8,128)(2,1)} %pad_maximum_fusion.3.refs_0_, bf16[8,128,1024]{2,1,0:T(8,128)(2,1)} %collective-permute-done.44.refs_1_, bf16[8,128,1024]{2,1,0:T(8,128)(2,1)} %collective-permute-done.45.refs_2_, ...), custom_call_target="tpu_custom_call" | custom-call | flops 1024 | bytes 1024 | tf_op jit(solution)/shard_map/pallas_call | solution.py:97
  319.6 10.9 %shard_map.320 = (bf16[512,4096]{1,0:T(8,128)(2,1)S(1)}, bf16[512,4096]{1,0:T(8,128)(2,1)}) custom-call(bf16[512,1024]{1,0:T(8,128)(2,1)S(1)} %copy-done.26, bf16[1024,4096]{1,0:T(8,128)(2,1)} %bitcast.287, f32[1,4096]{1,0:T(1,128)S(1)} %get-tuple-element.878.refs_0_), custom_call_target="tpu_custom_call" | custom-call | flops 1024 | bytes 1024 | tf_op jit(solution)/shard_map/pallas_call | solution.py:568
  332.6 4.4 collective-permute-done.52.refs_3_
  337.0 6.0 shard_map.321
  344.6 8.9 %shard_map.322.total_ref = f32[512,1024]{1,0:T(8,128)S(1)} custom-call(bf16[512,4096]{1,0:T(8,128)(2,1)} %copy-done.9, bf16[4096,1024]{1,0:T(8,128)(2,1)} %bitcast.289, f32[1,1024]{1,0:T(1,128)S(1)} %get-tuple-element.861.refs_0_, f32[512,1024]{1,0:T(8,128)S(1)} %get-tuple-element.800.refs_1_), custom_call_target="tpu_custom_call" | custom-call | flops 1024 | bytes 1024 | tf_op jit(solution)/shard_map/pallas_call | solution.py:568
  357.3 9.5 %shard_map.324 = (bf16[512,4096]{1,0:T(8,128)(2,1)}, f32[1,4096]{1,0:T(1,128)S(1)}) custom-call(bf16[512,1024]{1,0:T(8,128)(2,1)S(1)} %get-tuple-element.595.rows_ref.refs_4_, bf16[4096,1024]{1,0:T(8,128)(2,1)} %bitcast.290, bf16[512,4096]{1,0:T(8,128)(2,1)} %get-tuple-element.596.refs_0_), custom_call_target="tpu_custom_call" | custom-call | flops 1024 | bytes 1024 | tf_op jit(solution)/shard_map/pallas_call | solution.py:568
  374.6 11.1 %shard_map.325 = (bf16[1024,1024]{1,0:T(8,128)(2,1)S(1)}, bf16[1024,1024]{1,0:T(8,128)(2,1)}) custom-call(s32[32]{0:T(128)S(1)} %stack.436.order_ref, bf16[512,4096]{1,0:T(8,128)(2,1)} %copy-done.9, bf16[512,4096]{1,0:T(8,128)(2,1)} %copy-done.9, bf16[512,4096]{1,0:T(8,128)(2,1)} %copy-done.56, bf16[512,4096]{1,0:T(8,128)(2,1)} %copy-done.56, ...), custom_call_target="tpu_custom_call" | custom-call | flops 1024 | bytes 1024 | tf_op jit(solution)/shard_map/pallas_call | solution.py:309
  387.4 8.5 %shard_map.326.up_ref = f32[512,1024]{1,0:T(8,128)S(1)} custom-call(bf16[512,4096]{1,0:T(8,128)(2,1)} %get-tuple-element.614.rows_ref.refs_2_, bf16[1024,4096]{1,0:T(8,128)(2,1)} %bitcast.288, f32[512,1024]{1,0:T(8,128)S(1)} %copy-done.45), custom_call_target="tpu_custom_call" | custom-call | flops 1024 | bytes 1024 | tf_op jit(solution)/shard_map/pallas_call | solution.py:568
  401.0 7.6 %shard_map.329 = (bf16[256,4096]{1,0:T(8,128)(2,1)S(1)}, bf16[256,4096]{1,0:T(8,128)(2,1)S(1)}) custom-call(bf16[512,512]{1,0:T(8,128)(2,1)} %copy-done.53, bf16[512,512]{1,0:T(8,128)(2,1)} %copy-done.115, bf16[512,4096]{1,0:T(8,128)(2,1)} %get-tuple-element.614.rows_ref.refs_2_, bf16[512,4096]{1,0:T(8,128)(2,1)} %collective-permute-done.55.refs_3_), custom_call_target="tpu_custom_call" | custom-call | flops 1024 | bytes 1024 | tf_op jit(solution)/shard_map/pallas_call | solution.py:273
  413.5 20.9 %shard_map.330 = (bf16[512,1024]{1,0:T(8,128)(2,1)S(1)}, f32[2,512,1024]{2,1,0:T(8,128)}, bf16[2,512,1024]{2,1,0:T(8,128)(2,1)S(1)}) custom-call(s32[1]{0:T(128)} %bitcast.83.s_ref, bf16[512,3072]{1,0:T(8,128)(2,1)} %copy-done.3, bf16[512,3072]{1,0:T(8,128)(2,1)} %copy-done.3, bf16[512,3072]{1,0:T(8,128)(2,1)} %collective-permute-done.41.ko_ref.vo_ref, ...), custom_call_target="tpu_custom_call" | custom-call | flops 1024 | bytes 1024 | tf_op jit(solution)/shard_map/pallas_call | solution.py:459
  434.9 5.1 collective-permute-done.58.refs_7_
  440.1 4.6 add_convert_fusion.8
  450.3 7.1 %shard_map.332.up_ref = f32[512,1024]{1,0:T(8,128)S(1)} custom-call(bf16[512,3072]{1,0:T(8,128)(2,1)} %get-tuple-element.643.rows_ref.refs_2_, bf16[1024,3072]{1,0:T(8,128)(2,1)} %bitcast.294, f32[512,1024]{1,0:T(8,128)S(1)} %get-tuple-element.635.refs_0_), custom_call_target="tpu_custom_call" | custom-call | flops 1024 | bytes 1024 | tf_op jit(solution)/shard_map/pallas_call | solution.py:568
  458.8 9.2 %shard_map.333 = (bf16[256,4096]{1,0:T(8,128)(2,1)}, bf16[256,4096]{1,0:T(8,128)(2,1)}) custom-call(bf16[512,512]{1,0:T(8,128)(2,1)} %copy-done.51, bf16[512,512]{1,0:T(8,128)(2,1)} %copy-done.111, bf16[512,3072]{1,0:T(8,128)(2,1)} %get-tuple-element.643.rows_ref.refs_2_, bf16[512,3072]{1,0:T(8,128)(2,1)} %collective-permute-done.62.refs_3_, ...), custom_call_target="tpu_custom_call" | custom-call | flops 1024 | bytes 1024 | tf_op jit(solution)/shard_map/pallas_call | solution.py:273
  477.8 9.5 %shard_map.335 = (bf16[512,4096]{1,0:T(8,128)(2,1)}, f32[1,4096]{1,0:T(1,128)S(1)}) custom-call(bf16[512,1024]{1,0:T(8,128)(2,1)S(1)} %get-tuple-element.657.rows_ref.refs_4_, bf16[4096,1024]{1,0:T(8,128)(2,1)} %bitcast.286, bf16[512,4096]{1,0:T(8,128)(2,1)} %get-tuple-element.658.refs_0_), custom_call_target="tpu_custom_call" | custom-call | flops 1024 | bytes 1024 | tf_op jit(solution)/shard_map/pallas_call | solution.py:568
  497.2 9.5 %shard_map.337 = (bf16[1024,512]{1,0:T(8,128)(2,1)}, bf16[1024,512]{1,0:T(8,128)(2,1)S(1)}) custom-call(s32[32]{0:T(128)S(1)} %stack.436.order_ref, bf16[512,4096]{1,0:T(8,128)(2,1)} %copy-done.4, bf16[512,4096]{1,0:T(8,128)(2,1)} %copy-done.4, bf16[512,4096]{1,0:T(8,128)(2,1)} %collective-permute-done.43.refs_2_.refs_3_, ...), custom_call_target="tpu_custom_call" | custom-call | flops 1024 | bytes 1024 | tf_op jit(solution)/shard_map/pallas_call | solution.py:309
  506.6 9.5 %shard_map.336 = (bf16[1024,512]{1,0:T(8,128)(2,1)}, bf16[1024,512]{1,0:T(8,128)(2,1)S(1)}) custom-call(s32[32]{0:T(128)S(1)} %stack.438.order_ref, bf16[512,4096]{1,0:T(8,128)(2,1)} %copy-done.4, bf16[512,4096]{1,0:T(8,128)(2,1)} %copy-done.4, bf16[512,4096]{1,0:T(8,128)(2,1)} %collective-permute-done.43.refs_2_.refs_3_, ...), custom_call_target="tpu_custom_call" | custom-call | flops 1024 | bytes 1024 | tf_op jit(solution)/shard_map/pallas_call | solution.py:309
  528.6 8.5 %shard_map.338.up_ref = f32[512,1024]{1,0:T(8,128)S(1)} custom-call(bf16[512,4096]{1,0:T(8,128)(2,1)} %get-tuple-element.693.rows_ref.refs_2_, bf16[1024,4096]{1,0:T(8,128)(2,1)} %bitcast.292, f32[512,1024]{1,0:T(8,128)S(1)} %copy-done.43), custom_call_target="tpu_custom_call" | custom-call | flops 1024 | bytes 1024 | tf_op jit(solution)/shard_map/pallas_call | solution.py:568
  543.5 8.5 %shard_map.341 = (bf16[256,4096]{1,0:T(8,128)(2,1)}, bf16[256,4096]{1,0:T(8,128)(2,1)S(1)}) custom-call(bf16[512,512]{1,0:T(8,128)(2,1)} %copy-done.50, bf16[512,512]{1,0:T(8,128)(2,1)} %copy-done.106, bf16[512,4096]{1,0:T(8,128)(2,1)} %get-tuple-element.693.rows_ref.refs_2_, bf16[512,4096]{1,0:T(8,128)(2,1)} %collective-permute-done.66.refs_3_), custom_call_target="tpu_custom_call" | custom-call | flops 1024 | bytes 1024 | tf_op jit(solution)/shard_map/pallas_call | solution.py:273
  565.5 20.8 %shard_map.342 = (bf16[512,1024]{1,0:T(8,128)(2,1)S(1)}, f32[2,512,1024]{2,1,0:T(8,128)}, bf16[2,512,1024]{2,1,0:T(8,128)(2,1)S(1)}) custom-call(s32[1]{0:T(128)} %bitcast.83.s_ref, bf16[512,3072]{1,0:T(8,128)(2,1)} %copy-done.2, bf16[512,3072]{1,0:T(8,128)(2,1)} %copy-done.2, bf16[512,3072]{1,0:T(8,128)(2,1)} %collective-permute-done.19.ko_ref.vo_ref, ...), custom_call_target="tpu_custom_call" | custom-call | flops 1024 | bytes 1024 | tf_op jit(solution)/shard_map/pallas_call | solution.py:459
  607.7 8.9 %shard_map.344 = (bf16[256,4096]{1,0:T(8,128)(2,1)}, bf16[256,4096]{1,0:T(8,128)(2,1)}) custom-call(bf16[512,512]{1,0:T(8,128)(2,1)} %copy-done.48, bf16[512,512]{1,0:T(8,128)(2,1)} %copy-done.104, bf16[512,3072]{1,0:T(8,128)(2,1)} %copy-done.24, bf16[512,3072]{1,0:T(8,128)(2,1)} %copy-done.68, bf16[512,512]{1,0:T(8,128)(2,1)} %copy-done.49, ...), custom_call_target="tpu_custom_call" | custom-call | flops 1024 | bytes 1024 | tf_op jit(solution)/shard_map/pallas_call | solution.py:273
  625.4 7.5 %shard_map.345 = f32[512,1024]{1,0:T(8,128)S(1)} custom-call(bf16[512,3072]{1,0:T(8,128)(2,1)} %copy-done.24, bf16[1024,3072]{1,0:T(8,128)(2,1)} %bitcast.278, f32[512,1024]{1,0:T(8,128)S(1)} %copy-done.41), custom_call_target="tpu_custom_call" | custom-call | flops 1024 | bytes 1024 | tf_op jit(solution)/shard_map/pallas_call | solution.py:568
  632.9 13.0 %collective-permute-done.84 = bf16[256,512]{1,0:T(8,128)(2,1)S(1)} collective-permute-done((bf16[256,512]{1,0:T(8,128)(2,1)}, bf16[256,512]{1,0:T(8,128)(2,1)S(1)}, u32[]{:S(2)}, u32[]{:S(2)}) %collective-permute-start.84) | collective-permute-done | bytes 262176 | tf_op jit(solution)/shard_map/ppermute | solution.py:62
  659.9 5.8 collective-permute-done.92
  676.0 11.7 %collective-permute-done.96 = bf16[16,128]{1,0:T(8,128)(2,1)S(1)} collective-permute-done((bf16[16,128]{1,0:T(8,128)(2,1)S(1)}, bf16[16,128]{1,0:T(8,128)(2,1)S(1)}, u32[]{:S(2)}, u32[]{:S(2)}) %collective-permute-start.96) | collective-permute-done | bytes 4128 | tf_op jit(solution)/shard_map/ppermute | solution.py:62
  693.8 7.9 %collective-permute-done.97 = bf16[32,4096]{1,0:T(8,128)(2,1)S(1)} collective-permute-done((bf16[32,4096]{1,0:T(8,128)(2,1)S(1)}, bf16[32,4096]{1,0:T(8,128)(2,1)S(1)}, u32[]{:S(2)}, u32[]{:S(2)}) %collective-permute-start.97) | collective-permute-done | bytes 262176 | tf_op jit(solution)/shard_map/ppermute | solution.py:62
  (638 shorter events, 292.7 us)
Async XLA Ops:
  29.7 20.3 %collective-permute-start.6 = (bf16[256,1024]{1,0:T(8,128)(2,1)}, bf16[256,1024]{1,0:T(8,128)(2,1)}, u32[]{:S(2)}, u32[]{:S(2)}) collective-permute-start(bf16[256,1024]{1,0:T(8,128)(2,1)} %get-tuple-element.419), channel_id=1, source_target_pairs={{0,2},{1,3},{2,0},{3,1},{4,6},{5,7},{6,4},{7,5},{8,10},{9,11},{10,... | collective-permute-start | bytes 1572872 | tf_op jit(solution)/shard_map/ppermute | solution.py:62
  65.4 20.5 %collective-permute-start.12 = (bf16[8,96,1024]{2,1,0:T(8,128)(2,1)S(1)}, bf16[8,96,1024]{2,1,0:T(8,128)(2,1)S(1)}, u32[]{:S(2)}, u32[]{:S(2)}) collective-permute-start(bf16[8,96,1024]{2,1,0:T(8,128)(2,1)S(1)} %pad_maximum_fusion.5.refs_0_), channel_id=1, source_target_pairs={{0,2},{1,5},{2,0},{3,7},{4,6},{5,1},{6,4},{7,3},{8,10},{9,13},{10,... | collective-permute-start | bytes 4718600 | tf_op jit(solution)/shard_map/ppermute | solution.py:62
  66.0 19.9 %collective-permute-start.13 = (bf16[8,96,1024]{2,1,0:T(8,128)(2,1)S(1)}, bf16[8,96,1024]{2,1,0:T(8,128)(2,1)}, u32[]{:S(2)}, u32[]{:S(2)}) collective-permute-start(bf16[8,96,1024]{2,1,0:T(8,128)(2,1)S(1)} %pad_maximum_fusion.5.refs_0_), channel_id=1, source_target_pairs={{0,1},{1,0},{2,3},{3,2},{4,5},{5,4},{6,7},{7,6},{8,9},{9,8},{10,11... | collective-permute-start | bytes 4718600 | tf_op jit(solution)/shard_map/ppermute | solution.py:62
  87.3 26.9 %collective-permute-start.16 = (bf16[4,160,1024]{2,1,0:T(8,128)(2,1)S(1)}, bf16[4,160,1024]{2,1,0:T(8,128)(2,1)S(1)}, u32[]{:S(2)}, u32[]{:S(2)}) collective-permute-start(bf16[4,160,1024]{2,1,0:T(8,128)(2,1)S(1)} %pad_maximum_fusion.6), channel_id=1, source_target_pairs={{0,4},{1,3},{2,6},{3,1},{4,0},{5,7},{6,2},{7,5},{8,12},{9,11},{10,... | collective-permute-start | bytes 3932168 | tf_op jit(solution)/shard_map/ppermute | solution.py:62
  89.0 19.7 %collective-permute-start.17 = (bf16[1,128,1024]{2,1,0:T(8,128)(2,1)}, bf16[1,128,1024]{2,1,0:T(8,128)(2,1)S(1)}, u32[]{:S(2)}, u32[]{:S(2)}) collective-permute-start(bf16[1,128,1024]{2,1,0:T(8,128)(2,1)} %bitcast.81), channel_id=1, source_target_pairs={{0,16},{1,17},{2,18},{3,19},{4,20},{5,21},{6,22},{7,23},{8,24},{9,... | collective-permute-start | bytes 786440 | tf_op jit(solution)/shard_map/ppermute | solution.py:62
  89.0 25.2 %collective-permute-start.18 = (bf16[1,128,1024]{2,1,0:T(8,128)(2,1)}, bf16[1,128,1024]{2,1,0:T(8,128)(2,1)S(1)}, u32[]{:S(2)}, u32[]{:S(2)}) collective-permute-start(bf16[1,128,1024]{2,1,0:T(8,128)(2,1)} %bitcast.82), channel_id=1, source_target_pairs={{0,16},{1,17},{2,18},{3,19},{4,20},{5,21},{6,22},{7,23},{8,24},{9,... | collective-permute-start | bytes 786440 | tf_op jit(solution)/shard_map/ppermute | solution.py:62
  120.1 31.7 %collective-permute-start.21 = (bf16[8,160,1024]{2,1,0:T(8,128)(2,1)S(1)}, bf16[8,160,1024]{2,1,0:T(8,128)(2,1)S(1)}, u32[]{:S(2)}, u32[]{:S(2)}) collective-permute-start(bf16[8,160,1024]{2,1,0:T(8,128)(2,1)S(1)} %pad_maximum_fusion.refs_0_), channel_id=1, source_target_pairs={{0,2},{1,5},{2,0},{3,7},{4,6},{5,1},{6,4},{7,3},{8,10},{9,13},{10,... | collective-permute-start | bytes 7864328 | tf_op jit(solution)/shard_map/ppermute | solution.py:62
  121.6 30.2 %collective-permute-start.22 = (bf16[8,160,1024]{2,1,0:T(8,128)(2,1)S(1)}, bf16[8,160,1024]{2,1,0:T(8,128)(2,1)}, u32[]{:S(2)}, u32[]{:S(2)}) collective-permute-start(bf16[8,160,1024]{2,1,0:T(8,128)(2,1)S(1)} %pad_maximum_fusion.refs_0_), channel_id=1, source_target_pairs={{0,1},{1,0},{2,3},{3,2},{4,5},{5,4},{6,7},{7,6},{8,9},{9,8},{10,11... | collective-permute-start | bytes 7864328 | tf_op jit(solution)/shard_map/ppermute | solution.py:62
  125.9 23.1 %collective-permute-start.24 = (bf16[2,128,1024]{2,1,0:T(8,128)(2,1)}, bf16[2,128,1024]{2,1,0:T(8,128)(2,1)S(1)}, u32[]{:S(2)}, u32[]{:S(2)}) collective-permute-start(bf16[2,128,1024]{2,1,0:T(8,128)(2,1)} %pad_maximum_fusion.16), channel_id=1, source_target_pairs={{0,8},{1,9},{2,10},{3,11},{4,12},{5,13},{6,14},{7,15},{8,0},{9,1},... | collective-permute-start | bytes 1572872 | tf_op jit(solution)/shard_map/ppermute | solution.py:62
  155.8 24.5 %collective-permute-start.28 = (bf16[4,128,1024]{2,1,0:T(8,128)(2,1)S(1)}, bf16[4,128,1024]{2,1,0:T(8,128)(2,1)S(1)}, u32[]{:S(2)}, u32[]{:S(2)}) collective-permute-start(bf16[4,128,1024]{2,1,0:T(8,128)(2,1)S(1)} %pad_maximum_fusion.8), channel_id=1, source_target_pairs={{0,4},{1,3},{2,6},{3,1},{4,0},{5,7},{6,2},{7,5},{8,12},{9,11},{10,... | collective-permute-start | bytes 3145736 | tf_op jit(solution)/shard_map/ppermute | solution.py:62
  183.8 26.1 %collective-permute-start.31 = (bf16[8,128,1024]{2,1,0:T(8,128)(2,1)S(1)}, bf16[8,128,1024]{2,1,0:T(8,128)(2,1)S(1)}, u32[]{:S(2)}, u32[]{:S(2)}) collective-permute-start(bf16[8,128,1024]{2,1,0:T(8,128)(2,1)S(1)} %pad_maximum_fusion.1.refs_0_), channel_id=1, source_target_pairs={{0,2},{1,5},{2,0},{3,7},{4,6},{5,1},{6,4},{7,3},{8,10},{9,13},{10,... | collective-permute-start | bytes 6291464 | tf_op jit(solution)/shard_map/ppermute | solution.py:62
  185.4 24.5 %collective-permute-start.32 = (bf16[8,128,1024]{2,1,0:T(8,128)(2,1)S(1)}, bf16[8,128,1024]{2,1,0:T(8,128)(2,1)}, u32[]{:S(2)}, u32[]{:S(2)}) collective-permute-start(bf16[8,128,1024]{2,1,0:T(8,128)(2,1)S(1)} %pad_maximum_fusion.1.refs_0_), channel_id=1, source_target_pairs={{0,1},{1,0},{2,3},{3,2},{4,5},{5,4},{6,7},{7,6},{8,9},{9,8},{10,11... | collective-permute-start | bytes 6291464 | tf_op jit(solution)/shard_map/ppermute | solution.py:62
  185.4 18.0 %collective-permute-start.33 = (bf16[2,128,1024]{2,1,0:T(8,128)(2,1)}, bf16[2,128,1024]{2,1,0:T(8,128)(2,1)}, u32[]{:S(2)}, u32[]{:S(2)}) collective-permute-start(bf16[2,128,1024]{2,1,0:T(8,128)(2,1)} %pad_maximum_fusion.17), channel_id=1, source_target_pairs={{0,8},{1,9},{2,10},{3,11},{4,12},{5,13},{6,14},{7,15},{8,0},{9,1},... | collective-permute-start | bytes 1572872 | tf_op jit(solution)/shard_map/ppermute | solution.py:62
  212.6 26.4 %collective-permute-start.35 = (bf16[8,128,1024]{2,1,0:T(8,128)(2,1)}, bf16[8,128,1024]{2,1,0:T(8,128)(2,1)}, u32[]{:S(2)}, u32[]{:S(2)}) collective-permute-start(bf16[8,128,1024]{2,1,0:T(8,128)(2,1)} %pad_maximum_fusion.2.refs_0_), channel_id=1, source_target_pairs={{0,2},{1,5},{2,0},{3,7},{4,6},{5,1},{6,4},{7,3},{8,10},{9,13},{10,... | collective-permute-start | bytes 6291464 | tf_op jit(solution)/shard_map/ppermute | solution.py:62
  214.1 24.9 %collective-permute-start.36 = (bf16[8,128,1024]{2,1,0:T(8,128)(2,1)}, bf16[8,128,1024]{2,1,0:T(8,128)(2,1)}, u32[]{:S(2)}, u32[]{:S(2)}) collective-permute-start(bf16[8,128,1024]{2,1,0:T(8,128)(2,1)} %pad_maximum_fusion.2.refs_0_), channel_id=1, source_target_pairs={{0,1},{1,0},{2,3},{3,2},{4,5},{5,4},{6,7},{7,6},{8,9},{9,8},{10,11... | collective-permute-start | bytes 6291464 | tf_op jit(solution)/shard_map/ppermute | solution.py:62
  214.3 19.0 %collective-permute-start.37 = (bf16[1,128,1024]{2,1,0:T(8,128)(2,1)S(1)}, bf16[1,128,1024]{2,1,0:T(8,128)(2,1)S(1)}, u32[]{:S(2)}, u32[]{:S(2)}) collective-permute-start(bf16[1,128,1024]{2,1,0:T(8,128)(2,1)S(1)} %bitcast.299), channel_id=1, source_target_pairs={{0,16},{1,17},{2,18},{3,19},{4,20},{5,21},{6,22},{7,23},{8,24},{9,... | collective-permute-start | bytes 786440 | tf_op jit(solution)/shard_map/ppermute | solution.py:62
  241.1 19.0 %collective-permute-start.39 = (bf16[4,128,1024]{2,1,0:T(8,128)(2,1)}, bf16[4,128,1024]{2,1,0:T(8,128)(2,1)}, u32[]{:S(2)}, u32[]{:S(2)}) collective-permute-start(bf16[4,128,1024]{2,1,0:T(8,128)(2,1)} %pad_maximum_fusion.9), channel_id=1, source_target_pairs={{0,4},{1,3},{2,6},{3,1},{4,0},{5,7},{6,2},{7,5},{8,12},{9,11},{10,... | collective-permute-start | bytes 3145736 | tf_op jit(solution)/shard_map/ppermute | solution.py:62
  242.7 48.4 %collective-permute-start.43 = (bf16[512,4096]{1,0:T(8,128)(2,1)S(1)}, bf16[512,4096]{1,0:T(8,128)(2,1)}, u32[]{:S(2)}, u32[]{:S(2)}) collective-permute-start(bf16[512,4096]{1,0:T(8,128)(2,1)S(1)} %copy-done.5), channel_id=1, source_target_pairs={{0,1},{1,0},{2,3},{3,2},{4,5},{5,4},{6,7},{7,6},{8,9},{9,8},{10,11... | collective-permute-start | bytes 12582920 | tf_op jit(solution)/shard_map/ppermute | solution.py:62
  264.7 26.4 %collective-permute-start.44 = (bf16[8,128,1024]{2,1,0:T(8,128)(2,1)}, bf16[8,128,1024]{2,1,0:T(8,128)(2,1)}, u32[]{:S(2)}, u32[]{:S(2)}) collective-permute-start(bf16[8,128,1024]{2,1,0:T(8,128)(2,1)} %pad_maximum_fusion.3.refs_0_), channel_id=1, source_target_pairs={{0,2},{1,5},{2,0},{3,7},{4,6},{5,1},{6,4},{7,3},{8,10},{9,13},{10,... | collective-permute-start | bytes 6291464 | tf_op jit(solution)/shard_map/ppermute | solution.py:62
  266.2 24.8 %collective-permute-start.45 = (bf16[8,128,1024]{2,1,0:T(8,128)(2,1)}, bf16[8,128,1024]{2,1,0:T(8,128)(2,1)}, u32[]{:S(2)}, u32[]{:S(2)}) collective-permute-start(bf16[8,128,1024]{2,1,0:T(8,128)(2,1)} %pad_maximum_fusion.3.refs_0_), channel_id=1, source_target_pairs={{0,1},{1,0},{2,3},{3,2},{4,5},{5,4},{6,7},{7,6},{8,9},{9,8},{10,11... | collective-permute-start | bytes 6291464 | tf_op jit(solution)/shard_map/ppermute | solution.py:62
  292.8 19.4 %collective-permute-start.47 = (bf16[8,128,1024]{2,1,0:T(8,128)(2,1)}, bf16[8,128,1024]{2,1,0:T(8,128)(2,1)S(1)}, u32[]{:S(2)}, u32[]{:S(2)}) collective-permute-start(bf16[8,128,1024]{2,1,0:T(8,128)(2,1)} %collective-permute-done.44.refs_1_), channel_id=1, source_target_pairs={{0,1},{1,0},{2,3},{3,2},{4,5},{5,4},{6,7},{7,6},{8,9},{9,8},{10,11... | collective-permute-start | bytes 6291464 | tf_op jit(solution)/shard_map/ppermute | solution.py:62
  306.4 26.2 %collective-permute-start.50 = (bf16[8,128,1024]{2,1,0:T(8,128)(2,1)S(1)}, bf16[8,128,1024]{2,1,0:T(8,128)(2,1)}, u32[]{:S(2)}, u32[]{:S(2)}) collective-permute-start(bf16[8,128,1024]{2,1,0:T(8,128)(2,1)S(1)} %pad_maximum_fusion.4.refs_0_), channel_id=1, source_target_pairs={{0,2},{1,5},{2,0},{3,7},{4,6},{5,1},{6,4},{7,3},{8,10},{9,13},{10,... | collective-permute-start | bytes 6291464 | tf_op jit(solution)/shard_map/ppermute | solution.py:62
  307.9 24.6 %collective-permute-start.51 = (bf16[8,128,1024]{2,1,0:T(8,128)(2,1)S(1)}, bf16[8,128,1024]{2,1,0:T(8,128)(2,1)}, u32[]{:S(2)}, u32[]{:S(2)}) collective-permute-start(bf16[8,128,1024]{2,1,0:T(8,128)(2,1)S(1)} %pad_maximum_fusion.4.refs_0_), channel_id=1, source_target_pairs={{0,1},{1,0},{2,3},{3,2},{4,5},{5,4},{6,7},{7,6},{8,9},{9,8},{10,11... | collective-permute-start | bytes 6291464 | tf_op jit(solution)/shard_map/ppermute | solution.py:62
  311.6 18.9 %collective-permute-start.48 = (bf16[512,512]{1,0:T(8,128)(2,1)S(1)}, bf16[512,512]{1,0:T(8,128)(2,1)S(1)}, u32[]{:S(2)}, u32[]{:S(2)}) collective-permute-start(bf16[512,512]{1,0:T(8,128)(2,1)S(1)} %get-tuple-element.574), channel_id=1, source_target_pairs={{0,1},{1,0},{2,3},{3,2},{4,5},{5,4},{6,7},{7,6},{8,9},{9,8},{10,11... | collective-permute-start | bytes 1572872 | tf_op jit(solution)/shard_map/ppermute | solution.py:62
  312.2 18.3 %collective-permute-start.49 = (bf16[512,512]{1,0:T(8,128)(2,1)S(1)}, bf16[512,512]{1,0:T(8,128)(2,1)S(1)}, u32[]{:S(2)}, u32[]{:S(2)}) collective-permute-start(bf16[512,512]{1,0:T(8,128)(2,1)S(1)} %get-tuple-element.576), channel_id=1, source_target_pairs={{0,1},{1,0},{2,3},{3,2},{4,5},{5,4},{6,7},{7,6},{8,9},{9,8},{10,11... | collective-permute-start | bytes 1572872 | tf_op jit(solution)/shard_map/ppermute | solution.py:62
  367.8 18.0 %collective-permute-start.55 = (bf16[512,4096]{1,0:T(8,128)(2,1)}, bf16[512,4096]{1,0:T(8,128)(2,1)}, u32[]{:S(2)}, u32[]{:S(2)}) collective-permute-start(bf16[512,4096]{1,0:T(8,128)(2,1)} %get-tuple-element.614.rows_ref.refs_2_), channel_id=1, source_target_pairs={{0,1},{1,0},{2,3},{3,2},{4,5},{5,4},{6,7},{7,6},{8,9},{9,8},{10,11... | collective-permute-start | bytes 12582920 | tf_op jit(solution)/shard_map/ppermute | solution.py:62
  385.8 26.2 %collective-permute-start.57 = (bf16[1024,1024]{1,0:T(8,128)(2,1)S(1)}, bf16[1024,1024]{1,0:T(8,128)(2,1)}, u32[]{:S(2)}, u32[]{:S(2)}) collective-permute-start(bf16[1024,1024]{1,0:T(8,128)(2,1)S(1)} %get-tuple-element.618), channel_id=1, source_target_pairs={{0,2},{1,5},{2,0},{3,7},{4,6},{5,1},{6,4},{7,3},{8,10},{9,13},{10,... | collective-permute-start | bytes 6291464 | tf_op jit(solution)/shard_map/ppermute | solution.py:62
  412.0 28.1 %collective-permute-start.59 = (bf16[256,4096]{1,0:T(8,128)(2,1)S(1)}, bf16[256,4096]{1,0:T(8,128)(2,1)S(1)}, u32[]{:S(2)}, u32[]{:S(2)}) collective-permute-start(bf16[256,4096]{1,0:T(8,128)(2,1)S(1)} %get-tuple-element.625), channel_id=1, source_target_pairs={{0,2},{1,5},{2,0},{3,7},{4,6},{5,1},{6,4},{7,3},{8,10},{9,13},{10,... | collective-permute-start | bytes 6291464 | tf_op jit(solution)/shard_map/ppermute | solution.py:62
  448.8 19.1 %collective-permute-start.61 = (bf16[512,1024]{1,0:T(8,128)(2,1)}, bf16[512,1024]{1,0:T(8,128)(2,1)}, u32[]{:S(2)}, u32[]{:S(2)}) collective-permute-start(bf16[512,1024]{1,0:T(8,128)(2,1)} %get-tuple-element.639), channel_id=1, source_target_pairs={{0,4},{1,3},{2,6},{3,1},{4,0},{5,7},{6,2},{7,5},{8,12},{9,11},{10,... | collective-permute-start | bytes 3145736 | tf_op jit(solution)/shard_map/ppermute | solution.py:62
  492.6 26.4 %collective-permute-start.66 = (bf16[512,4096]{1,0:T(8,128)(2,1)}, bf16[512,4096]{1,0:T(8,128)(2,1)}, u32[]{:S(2)}, u32[]{:S(2)}) collective-permute-start(bf16[512,4096]{1,0:T(8,128)(2,1)} %get-tuple-element.693.rows_ref.refs_2_), channel_id=1, source_target_pairs={{0,1},{1,0},{2,3},{3,2},{4,5},{5,4},{6,7},{7,6},{8,9},{9,8},{10,11... | collective-permute-start | bytes 12582920 | tf_op jit(solution)/shard_map/ppermute | solution.py:62
  492.6 26.4 %collective-permute-start.67 = (bf16[256,4096]{1,0:T(8,128)(2,1)}, bf16[256,4096]{1,0:T(8,128)(2,1)}, u32[]{:S(2)}, u32[]{:S(2)}) collective-permute-start(bf16[256,4096]{1,0:T(8,128)(2,1)} %get-tuple-element.676), channel_id=1, source_target_pairs={{0,2},{1,5},{2,0},{3,7},{4,6},{5,1},{6,4},{7,3},{8,10},{9,13},{10,... | collective-permute-start | bytes 6291464 | tf_op jit(solution)/shard_map/ppermute | solution.py:62
  493.9 22.2 %collective-permute-start.68 = (bf16[64,4096]{1,0:T(8,128)(2,1)}, bf16[64,4096]{1,0:T(8,128)(2,1)}, u32[]{:S(2)}, u32[]{:S(2)}) collective-permute-start(bf16[64,4096]{1,0:T(8,128)(2,1)} %get-tuple-element.677), channel_id=1, source_target_pairs={{0,8},{1,9},{2,10},{3,11},{4,12},{5,13},{6,14},{7,15},{8,0},{9,1},... | collective-permute-start | bytes 1572872 | tf_op jit(solution)/shard_map/ppermute | solution.py:62
  495.0 21.2 %collective-permute-start.69 = (bf16[128,1024]{1,0:T(8,128)(2,1)}, bf16[128,1024]{1,0:T(8,128)(2,1)}, u32[]{:S(2)}, u32[]{:S(2)}) collective-permute-start(bf16[128,1024]{1,0:T(8,128)(2,1)} %add_convert_fusion.32), channel_id=1, source_target_pairs={{0,16},{1,17},{2,18},{3,19},{4,20},{5,21},{6,22},{7,23},{8,24},{9,... | collective-permute-start | bytes 786440 | tf_op jit(solution)/shard_map/ppermute | solution.py:62
  523.5 30.7 %collective-permute-start.70 = (bf16[1024,512]{1,0:T(8,128)(2,1)}, bf16[1024,512]{1,0:T(8,128)(2,1)}, u32[]{:S(2)}, u32[]{:S(2)}) collective-permute-start(bf16[1024,512]{1,0:T(8,128)(2,1)} %get-tuple-element.697), channel_id=1, source_target_pairs={{0,8},{1,9},{2,10},{3,11},{4,12},{5,13},{6,14},{7,15},{8,0},{9,1},... | collective-permute-start | bytes 3145736 | tf_op jit(solution)/shard_map/ppermute | solution.py:62
  524.7 29.5 %collective-permute-start.71 = (bf16[1024,512]{1,0:T(8,128)(2,1)}, bf16[1024,512]{1,0:T(8,128)(2,1)}, u32[]{:S(2)}, u32[]{:S(2)}) collective-permute-start(bf16[1024,512]{1,0:T(8,128)(2,1)} %get-tuple-element.698), channel_id=1, source_target_pairs={{0,2},{1,5},{2,0},{3,7},{4,6},{5,1},{6,4},{7,3},{8,10},{9,13},{10,... | collective-permute-start | bytes 3145736 | tf_op jit(solution)/shard_map/ppermute | solution.py:62
  525.9 28.3 %collective-permute-start.72 = (bf16[128,4096]{1,0:T(8,128)(2,1)}, bf16[128,4096]{1,0:T(8,128)(2,1)}, u32[]{:S(2)}, u32[]{:S(2)}) collective-permute-start(bf16[128,4096]{1,0:T(8,128)(2,1)} %get-tuple-element.699), channel_id=1, source_target_pairs={{0,4},{1,3},{2,6},{3,1},{4,0},{5,7},{6,2},{7,5},{8,12},{9,11},{10,... | collective-permute-start | bytes 3145736 | tf_op jit(solution)/shard_map/ppermute | solution.py:62
  526.7 26.0 %collective-permute-start.73 = (bf16[32,4096]{1,0:T(8,128)(2,1)S(1)}, bf16[32,4096]{1,0:T(8,128)(2,1)S(1)}, u32[]{:S(2)}, u32[]{:S(2)}) collective-permute-start(bf16[32,4096]{1,0:T(8,128)(2,1)S(1)} %add_convert_fusion.31), channel_id=1, source_target_pairs={{0,16},{1,17},{2,18},{3,19},{4,20},{5,21},{6,22},{7,23},{8,24},{9,... | collective-permute-start | bytes 786440 | tf_op jit(solution)/shard_map/ppermute | solution.py:62
  560.2 32.0 %collective-permute-start.75 = (bf16[256,4096]{1,0:T(8,128)(2,1)}, bf16[256,4096]{1,0:T(8,128)(2,1)}, u32[]{:S(2)}, u32[]{:S(2)}) collective-permute-start(bf16[256,4096]{1,0:T(8,128)(2,1)} %get-tuple-element.711), channel_id=1, source_target_pairs={{0,2},{1,5},{2,0},{3,7},{4,6},{5,1},{6,4},{7,3},{8,10},{9,13},{10,... | collective-permute-start | bytes 6291464 | tf_op jit(solution)/shard_map/ppermute | solution.py:62
  561.5 24.8 %collective-permute-start.74 = (bf16[512,1024]{1,0:T(8,128)(2,1)S(1)}, bf16[512,1024]{1,0:T(8,128)(2,1)S(1)}, u32[]{:S(2)}, u32[]{:S(2)}) collective-permute-start(bf16[512,1024]{1,0:T(8,128)(2,1)S(1)} %get-tuple-element.689.rows_ref.refs_6_), channel_id=1, source_target_pairs={{0,1},{1,0},{2,3},{3,2},{4,5},{5,4},{6,7},{7,6},{8,9},{9,8},{10,11... | collective-permute-start | bytes 3145736 | tf_op jit(solution)/shard_map/ppermute | solution.py:62
  561.5 26.5 %collective-permute-start.76 = (bf16[512,512]{1,0:T(8,128)(2,1)S(1)}, bf16[512,512]{1,0:T(8,128)(2,1)S(1)}, u32[]{:S(2)}, u32[]{:S(2)}) collective-permute-start(bf16[512,512]{1,0:T(8,128)(2,1)S(1)} %get-tuple-element.712), channel_id=1, source_target_pairs={{0,16},{1,17},{2,18},{3,19},{4,20},{5,21},{6,22},{7,23},{8,24},{9,... | collective-permute-start | bytes 1572872 | tf_op jit(solution)/shard_map/ppermute | solution.py:62
  563.5 24.5 %collective-permute-start.77 = (bf16[512,512]{1,0:T(8,128)(2,1)}, bf16[512,512]{1,0:T(8,128)(2,1)S(1)}, u32[]{:S(2)}, u32[]{:S(2)}) collective-permute-start(bf16[512,512]{1,0:T(8,128)(2,1)} %get-tuple-element.713), channel_id=1, source_target_pairs={{0,4},{1,3},{2,6},{3,1},{4,0},{5,7},{6,2},{7,5},{8,12},{9,11},{10,... | collective-permute-start | bytes 1572872 | tf_op jit(solution)/shard_map/ppermute | solution.py:62
  564.3 23.7 %collective-permute-start.78 = (bf16[64,4096]{1,0:T(8,128)(2,1)}, bf16[64,4096]{1,0:T(8,128)(2,1)S(1)}, u32[]{:S(2)}, u32[]{:S(2)}) collective-permute-start(bf16[64,4096]{1,0:T(8,128)(2,1)} %get-tuple-element.714), channel_id=1, source_target_pairs={{0,8},{1,9},{2,10},{3,11},{4,12},{5,13},{6,14},{7,15},{8,0},{9,1},... | collective-permute-start | bytes 1572872 | tf_op jit(solution)/shard_map/ppermute | solution.py:62
  616.8 29.3 %collective-permute-start.83 = (bf16[256,4096]{1,0:T(8,128)(2,1)}, bf16[256,4096]{1,0:T(8,128)(2,1)}, u32[]{:S(2)}, u32[]{:S(2)}) collective-permute-start(bf16[256,4096]{1,0:T(8,128)(2,1)} %get-tuple-element.743), channel_id=1, source_target_pairs={{0,2},{1,5},{2,0},{3,7},{4,6},{5,1},{6,4},{7,3},{8,10},{9,13},{10,... | collective-permute-start | bytes 6291464 | tf_op jit(solution)/shard_map/ppermute | solution.py:62
  619.0 26.9 %collective-permute-start.84 = (bf16[256,512]{1,0:T(8,128)(2,1)}, bf16[256,512]{1,0:T(8,128)(2,1)S(1)}, u32[]{:S(2)}, u32[]{:S(2)}) collective-permute-start(bf16[256,512]{1,0:T(8,128)(2,1)} %get-tuple-element.745), channel_id=1, source_target_pairs={{0,2},{1,5},{2,0},{3,7},{4,6},{5,1},{6,4},{7,3},{8,10},{9,13},{10,... | collective-permute-start | bytes 786440 | tf_op jit(solution)/shard_map/ppermute | solution.py:62
  619.9 26.0 %collective-permute-start.85 = (bf16[256,512]{1,0:T(8,128)(2,1)}, bf16[256,512]{1,0:T(8,128)(2,1)S(1)}, u32[]{:S(2)}, u32[]{:S(2)}) collective-permute-start(bf16[256,512]{1,0:T(8,128)(2,1)} %get-tuple-element.746), channel_id=1, source_target_pairs={{0,8},{1,9},{2,10},{3,11},{4,12},{5,13},{6,14},{7,15},{8,0},{9,1},... | collective-permute-start | bytes 786440 | tf_op jit(solution)/shard_map/ppermute | solution.py:62
  622.8 23.2 %collective-permute-start.87 = (bf16[64,128]{1,0:T(8,128)(2,1)S(1)}, bf16[64,128]{1,0:T(8,128)(2,1)S(1)}, u32[]{:S(2)}, u32[]{:S(2)}) collective-permute-start(bf16[64,128]{1,0:T(8,128)(2,1)S(1)} %get-tuple-element.753), channel_id=1, source_target_pairs={{0,2},{1,5},{2,0},{3,7},{4,6},{5,1},{6,4},{7,3},{8,10},{9,13},{10,... | collective-permute-start | bytes 49160 | tf_op jit(solution)/shard_map/ppermute | solution.py:62
  650.7 18.2 %collective-permute-start.88 = (bf16[128,4096]{1,0:T(8,128)(2,1)S(1)}, bf16[128,4096]{1,0:T(8,128)(2,1)S(1)}, u32[]{:S(2)}, u32[]{:S(2)}) collective-permute-start(bf16[128,4096]{1,0:T(8,128)(2,1)S(1)} %get-tuple-element.768), channel_id=1, source_target_pairs={{0,4},{1,3},{2,6},{3,1},{4,0},{5,7},{6,2},{7,5},{8,12},{9,11},{10,... | collective-permute-start | bytes 3145736 | tf_op jit(solution)/shard_map/ppermute | solution.py:62
  669.2 18.5 %collective-permute-start.93 = (bf16[256,1024]{1,0:T(8,128)(2,1)S(1)}, bf16[256,1024]{1,0:T(8,128)(2,1)S(1)}, u32[]{:S(2)}, u32[]{:S(2)}) collective-permute-start(bf16[256,1024]{1,0:T(8,128)(2,1)S(1)} %slice.1001), channel_id=1, source_target_pairs={{0,2},{1,3},{2,0},{3,1},{4,6},{5,7},{6,4},{7,5},{8,10},{9,11},{10,... | collective-permute-start | bytes 1572872 | tf_op jit(solution)/shard_map/ppermute | solution.py:62
  (182 other events, 1831.0 us)

commit v6 on v5

--- a/solution.py
+++ b/solution.py
@@ -99,7 +99,7 @@
         in_specs=[pl.BlockSpec(memory_space=pltpu.SMEM)]
         + [pl.BlockSpec(memory_space=pl.ANY)] * len(pieces),
         out_specs=[pl.BlockSpec(memory_space=pltpu.HBM)] * len(shapes),
-        out_shape=[jax.ShapeDtypeStruct(shape, bf16) for shape in shapes],
+        out_shape=[pltpu.HBM(shape, bf16) for shape in shapes],
         scratch_shapes=[pltpu.VMEM(p.shape, bf16) for p in pieces]
         + [pltpu.SemaphoreType.DMA((total,)), pltpu.SemaphoreType.DMA((count,))],
         compiler_params=pltpu.CompilerParams(vmem_limit_bytes=40 << 20),
@@ -281,10 +281,10 @@
     )(*args)
 
 
-def wide_terms_of(order, left, right, part=0, parts=1):
+def wide_terms_of(order, left, right):
     tokens, width = left[0].shape
     block = width // 32
-    columns = right[0].shape[1] // parts
+    columns = right[0].shape[1]
 
     def kernel(order_ref, *refs):
         a1, a2, (b1, b2, leaving, kept) = refs[:2], refs[2:4], refs[4:]
@@ -304,7 +304,7 @@
             kept[...] = total
 
     cut = lambda n: pl.BlockSpec((tokens, block), lambda j, order: (0, order[2 * j + n]))
-    whole = pl.BlockSpec((tokens, columns), lambda j, order: (0, part))
+    whole = pl.BlockSpec((tokens, columns), lambda j, order: (0, 0))
     out = jax.ShapeDtypeStruct((width // 4, columns), bf16)
     return pl.pallas_call(
         kernel,
@@ -321,6 +321,44 @@
         compiler_params=pltpu.CompilerParams(vmem_limit_bytes=48 << 20),
         cost_estimate=SMALL_COST,
     )(order, *map(in_hbm, (left[0], left[0], left[1], left[1])), *right)
+
+
+def wide_terms_split(order, order_z, left, right):
+    tokens, width = left[0].shape
+    block, columns = width // 32, right[0].shape[1] // 2
+    same = order_z[:16, None] == order[None, :16]
+    places = jnp.sum(jnp.where(same, lax.broadcasted_iota(jnp.int32, (16, 16), 1), 0), axis=1)
+
+    def kernel(order_ref, place_ref, a1, a2, b1, b2, first, second):
+        one = (
+            lax.broadcasted_iota(jnp.int32, (block, block), 0) == lax.broadcasted_iota(jnp.int32, (block, block), 1)
+        ).astype(bf16)
+        total = sum(
+            jnp.dot(nt_dot(one, a[...]).astype(bf16), b[...], preferred_element_type=f32)
+            for a, b in ((a1, b1), (a2, b2))
+        ).astype(bf16)
+        first[0, 0] = total[:, :columns]
+        second[0, 0] = total[:, columns:]
+
+    cut = pl.BlockSpec((tokens, block), lambda j, order, place: (0, order[j]))
+    whole = pl.BlockSpec((tokens, 2 * columns), lambda j, order, place: (0, 0))
+    out = jax.ShapeDtypeStruct((2, 8, block, columns), bf16)
+    outs = pl.pallas_call(
+        kernel,
+        grid_spec=pltpu.PrefetchScalarGridSpec(
+            num_scalar_prefetch=2,
+            grid=(16,),
+            in_specs=[cut, cut, whole, whole],
+            out_specs=[
+                pl.BlockSpec((1, 1, block, columns), lambda j, order, place: (j // 8, j % 8, 0, 0)),
+                pl.BlockSpec((1, 1, block, columns), lambda j, order, place: (place[j] // 8, place[j] % 8, 0, 0)),
+            ],
+        ),
+        out_shape=[out, out],
+        compiler_params=pltpu.CompilerParams(vmem_limit_bytes=48 << 20),
+        cost_estimate=SMALL_COST,
+    )(order_z, places, *map(in_hbm, left), *right)
+    return [[part.reshape(8 * block, columns) for part in (o[0], o[1])] for o in outs]
 
 
 BLOCK = 256
@@ -586,6 +624,32 @@
     return inner * below, slope
 
 
+def mixed_norm(mixed, weight, stream, bias, gain, shift):
+    tokens, width = stream.shape
+    tile = 256
+
+    def kernel(mixed_ref, weight_ref, stream_ref, bias_ref, gain_ref, shift_ref, sum_ref, first_ref, low_ref):
+        total = jnp.dot(mixed_ref[...], weight_ref[...], preferred_element_type=f32)
+        total = stream_ref[...] + (total + bias_ref[...])
+        first = norm_forward(total)[0] * gain_ref[...] + shift_ref[...]
+        sum_ref[...] = total
+        first_ref[...] = first
+        low_ref[...] = first.astype(bf16)
+
+    cut = pl.BlockSpec((tile, width), lambda j: (j, 0))
+    vector = pl.BlockSpec((1, width), lambda j: (0, 0))
+    out = jax.ShapeDtypeStruct((tokens, width), f32)
+    return pl.pallas_call(
+        kernel,
+        grid=(tokens // tile,),
+        in_specs=[cut, pl.BlockSpec(weight.shape, lambda j: (0, 0)), cut, vector, vector, vector],
+        out_specs=[cut] * 3,
+        out_shape=[out, out, jax.ShapeDtypeStruct((tokens, width), bf16)],
+        compiler_params=pltpu.CompilerParams(vmem_limit_bytes=48 << 20),
+        cost_estimate=SMALL_COST,
+    )(mixed, in_hbm(weight), stream, *[v.reshape(1, width) for v in (bias, gain, shift)])
+
+
 def norm_backward_rows(total, gain, upstream):
     tokens, width = total.shape
     tile = 128
@@ -764,7 +828,7 @@
         .reshape(layer_count, FF)
     )
     stream = jnp.concatenate([token_kept, token_got]).astype(f32)
-    stream, small_all, wide_all = phase((stream, small_all, wide_all), u[0], u[1], u[2], u[3])
+    stream, small_all, wide_all = phase((stream, small_all, wide_all), u[0], u[1], u[2])
     saved, active_gots = [], []
     for layer in range(layer_count):
         a_unit, i_unit, o_unit = units[layer]
@@ -795,11 +859,9 @@
         w_inner, *w_more = i_unit.result()
         (w_mix,) = w_rest + w_more
         w_inner, w_mix = w_inner.reshape(D, FF), w_mix.reshape(D, D)
-        first_sum = stream + (dot(mixed, w_mix) + m_bias)
-        first = norm_forward(first_sum)[0] * gain1 + shift1
-        first_low = first.astype(bf16)
+        first_sum, first, first_low = mixed_norm(mixed, w_mix, stream, m_bias, gain1, shift1)
         if next_a:
-            first_low = phase(first_low, o_unit, next_i, settle=[next_a])
+            first_low = phase(first_low, o_unit, next_a, next_i)
         else:
             first_low = phase(first_low, o_unit)
         left_mix, left_first = selected(matrices, mixed, first_low)
@@ -868,10 +930,8 @@
         inner_got = send(inner_low, TO_CORE)
         second_pair = (second_low, second_got)
         if before:
-            o_sums = (
-                SumUnit(wide_terms_of(order_z, left_active, second_pair, 0, 2), Z_FIRST),
-                SumUnit(wide_terms_of(order, left_active, second_pair, 1, 2)),
-            )
+            by_z, by_far = wide_terms_split(order, order_z, left_active, second_pair)
+            o_sums = (SumUnit(by_z, Z_FIRST), SumUnit(by_far))
             second_grad, inner_low, inner_got = phase(
                 (second_grad, inner_low, inner_got), *o_sums, before.a, before.i, settle=before.o
             )
@@ -896,10 +956,11 @@
         )
         grads_back = send(sent_grads, TO_CORE)
         if before:
-            query_low, own_grads, branch_got = phase((query_low, own_grads, branch_got), i_sum, *o_sums, before.a)
+            query_low, own_grads = phase((query_low, own_grads), i_sum, *o_sums, before.a)
         else:
-            query_low, own_grads, branch_got = phase((query_low, own_grads, branch_got), *o_sums, settle=[i_sum])
+            query_low, own_grads = phase((query_low, own_grads), *o_sums, settle=[i_sum])
         low, low_sums = merged(query_low, own_grads, grads_back)
+        low, branch_got = lax.optimization_barrier((low, branch_got))
         low_got = send(low, TO_CORE)
         if layer:
             (upstream,) = product(

time: 715 us -> 697 us (0.975)
  starting transfers between devices: 92.8 us -> 75.3 us
  other arithmetic: 76.4 us -> 67.3 us
    pallas_call x0 -> x3, Pallas kernels: none -> 25.2 us  [the longest x1 15.1 us: wide_terms_split(): pl.pallas_call(kernel, grid_spec=pltpu.PrefetchScalarGridSpec(num_scalar_...]
    pallas_call x3 -> x1, Pallas kernels: 30.1 us -> 11.1 us  [wide_terms_of(): pl.pallas_call(kernel, grid_spec=pltpu.PrefetchScalarGridSpec(num_scalar_...]
    ppermute x99, starting transfers between devices: 92.8 us -> 75.3 us  [send(): return lax.ppermute(value, AXES, to)]
  transfers between devices with their start and end apart: 99 -> 99, of which waited for: 44 -> 46; matrix products, arithmetic and copies ran while one was open for 8% -> 8% of each run, Pallas kernels for 40% -> 43%
where the time goes in v6:
time: 697 us; the launch traced here: 690 us
  Pallas kernels  308 us (44%)
  waiting for transfers between devices  184 us (26%)
  starting transfers between devices  75.3 us (11%)
  other arithmetic  67.3 us (10%)
  local copies, waits for them, and re-layouts  52.1 us (7%)
    ppermute x99, waiting for transfers between devices, send(): return lax.ppermute(value, AXES, to)  184 us
    pallas_call x14, Pallas kernels, product(): pl.pallas_call(kernel, grid=(width // tile,), in_specs=[pl.BlockSpec((tok...  107 us
    ppermute x99, starting transfers between devices, send(): return lax.ppermute(value, AXES, to)  75.3 us
    pallas_call x4, Pallas kernels, call_attention(): pl.pallas_call(kernel, grid=(pairs_count,), in_specs=in_specs, out_specs=...  66.6 us
    pallas_call x6, Pallas kernels, place(): pl.pallas_call(kernel, in_specs=[pl.BlockSpec(memory_space=pltpu.SMEM)] +...  39.2 us
    pallas_call x4, Pallas kernels, weight_terms(): pl.pallas_call(kernel, grid=(columns // tile,), in_specs=in_specs, out_sp...  34.2 us
    convert_element_type x16, other arithmetic, local(): self.kept = self.kept.astype(bf16)  26.4 us
    unnamed x274, local copies, waits for them, and re-layouts  24.8 us
  transfers between devices with their start and end apart: 99, of which 46 were waited for; matrix products, arithmetic and copies ran while one was open for 8% of the time, Pallas kernels for 43%

profile of v6, /device:TPU:0, one launch (start us, length us, event | category | flops | bytes accessed | tf_op | source)
XLA Modules:
  0.0 690.1 jit_solution(5129402783579571713)
XLA Ops:
  21.2 4.3 collective-permute-done.4
  25.5 4.7 collective-permute-done
  40.9 7.2 %collective-permute-done.8 = bf16[1,160,1024]{2,1,0:T(8,128)(2,1)S(1)} collective-permute-done((bf16[1,160,1024]{2,1,0:T(8,128)(2,1)S(1)}, bf16[1,160,1024]{2,1,0:T(8,128)(2,1)S(1)}, u32[]{:S(2)}, u32[]{:S(2)}) %collective-permute-start.8) | collective-permute-done | bytes 327712 | tf_op jit(solution)/shard_map/ppermute | solution.py:62
  56.8 6.0 collective-permute-done.10
  76.4 7.6 %collective-permute-done.14 = bf16[2,160,1024]{2,1,0:T(8,128)(2,1)} collective-permute-done((bf16[2,160,1024]{2,1,0:T(8,128)(2,1)}, bf16[2,160,1024]{2,1,0:T(8,128)(2,1)}, u32[]{:S(2)}, u32[]{:S(2)}) %collective-permute-start.14) | collective-permute-done | bytes 655392 | tf_op jit(solution)/shard_map/ppermute | solution.py:62
  91.3 5.9 shard_map.305
  97.2 5.9 shard_map.306.q_ref.km_ref.vm_ref
  114.7 12.4 %shard_map.308 = (bf16[512,1024]{1,0:T(8,128)(2,1)S(1)}, f32[8,2,512]{2,1,0:T(2,128)S(1)}) custom-call(s32[1]{0:T(128)} %bitcast.s_ref, bf16[512,3072]{1,0:T(8,128)(2,1)S(1)} %shard_map.306.q_ref.km_ref.vm_ref, bf16[512,3072]{1,0:T(8,128)(2,1)S(1)} %shard_map.306.q_ref.km_ref.vm_ref, bf16[512,3072]{1,0:T(8,128)(2,1)} %collective-permute-done.18.ko_ref.vo_ref, ...), custom_call_target="tpu_custom_call" | custom-call | flops 1024 | bytes 1024 | tf_op jit(solution)/shard_map/pallas_call | solution.py:497
  131.9 8.7 %collective-permute-done.20.refs_1_ = bf16[8,160,1024]{2,1,0:T(8,128)(2,1)} collective-permute-done((bf16[8,160,1024]{2,1,0:T(8,128)(2,1)S(1)}, bf16[8,160,1024]{2,1,0:T(8,128)(2,1)}, u32[]{:S(2)}, u32[]{:S(2)}) %collective-permute-start.20) | collective-permute-done | bytes 2621472 | tf_op jit(solution)/shard_map/ppermute | solution.py:62
  146.9 7.9 %shard_map.309 = (bf16[4,2,2,2,32,4096]{5,4,3,2,1,0:T(8,128)(2,1)}, bf16[4,2,2,2,32,1024]{5,4,3,2,1,0:T(8,128)(2,1)}) custom-call(s32[4]{0:T(128)S(1)} %pad_add_fusion.coords_ref, bf16[8,160,1024]{2,1,0:T(8,128)(2,1)S(1)} %pad_maximum_fusion.refs_0_, bf16[8,160,1024]{2,1,0:T(8,128)(2,1)} %collective-permute-done.20.refs_1_, ...), custom_call_target="tpu_custom_call" | custom-call | flops 1024 | bytes 1024 | tf_op jit(solution)/shard_map/pallas_call | solution.py:97
  154.9 5.0 shard_map.310
  171.8 8.7 %collective-permute-done.33 = bf16[2,128,1024]{2,1,0:T(8,128)(2,1)S(1)} collective-permute-done((bf16[2,128,1024]{2,1,0:T(8,128)(2,1)S(1)}, bf16[2,128,1024]{2,1,0:T(8,128)(2,1)S(1)}, u32[]{:S(2)}, u32[]{:S(2)}) %collective-permute-start.33) | collective-permute-done | bytes 524320 | tf_op jit(solution)/shard_map/ppermute | solution.py:62
  181.3 11.3 %shard_map.312 = (bf16[512,4096]{1,0:T(8,128)(2,1)S(1)}, bf16[512,4096]{1,0:T(8,128)(2,1)}) custom-call(bf16[512,1024]{1,0:T(8,128)(2,1)S(1)} %copy-done.27, bf16[1024,4096]{1,0:T(8,128)(2,1)} %bitcast.289, f32[1,4096]{1,0:T(1,128)S(1)} %get-tuple-element.884.refs_0_), custom_call_target="tpu_custom_call" | custom-call | flops 1024 | bytes 1024 | tf_op jit(solution)/shard_map/pallas_call | solution.py:606
  192.7 9.3 %collective-permute-done.30.refs_1_ = bf16[8,128,1024]{2,1,0:T(8,128)(2,1)S(1)} collective-permute-done((bf16[8,128,1024]{2,1,0:T(8,128)(2,1)S(1)}, bf16[8,128,1024]{2,1,0:T(8,128)(2,1)S(1)}, u32[]{:S(2)}, u32[]{:S(2)}) %collective-permute-start.30) | collective-permute-done | bytes 2097184 | tf_op jit(solution)/shard_map/ppermute | solution.py:62
  209.0 4.8 shard_map.313
  213.8 8.5 %shard_map.314.total_ref = f32[512,1024]{1,0:T(8,128)S(1)} custom-call(bf16[512,4096]{1,0:T(8,128)(2,1)} %copy-done.14, bf16[4096,1024]{1,0:T(8,128)(2,1)} %bitcast.281, f32[1,1024]{1,0:T(1,128)S(1)} %get-tuple-element.873.refs_0_, f32[512,1024]{1,0:T(8,128)S(1)} %copy-done.32), custom_call_target="tpu_custom_call" | custom-call | flops 1024 | bytes 1024 | tf_op jit(solution)/shard_map/pallas_call | solution.py:606
  224.1 7.2 %collective-permute-done.35.refs_1_ = bf16[8,128,1024]{2,1,0:T(8,128)(2,1)} collective-permute-done((bf16[8,128,1024]{2,1,0:T(8,128)(2,1)}, bf16[8,128,1024]{2,1,0:T(8,128)(2,1)}, u32[]{:S(2)}, u32[]{:S(2)}) %collective-permute-start.35) | collective-permute-done | bytes 2097184 | tf_op jit(solution)/shard_map/ppermute | solution.py:62
  237.8 7.3 %shard_map.315 = (bf16[4,2,2,2,32,3072]{5,4,3,2,1,0:T(8,128)(2,1)}, bf16[4,2,2,2,32,1024]{5,4,3,2,1,0:T(8,128)(2,1)}) custom-call(s32[4]{0:T(128)S(1)} %pad_add_fusion.coords_ref, bf16[8,128,1024]{2,1,0:T(8,128)(2,1)} %pad_maximum_fusion.2.refs_0_, bf16[8,128,1024]{2,1,0:T(8,128)(2,1)} %collective-permute-done.35.refs_1_, ...), custom_call_target="tpu_custom_call" | custom-call | flops 1024 | bytes 1024 | tf_op jit(solution)/shard_map/pallas_call | solution.py:97
  245.1 5.9 shard_map.316.q_ref.km_ref.vm_ref
  262.2 12.4 %shard_map.318 = (bf16[512,1024]{1,0:T(8,128)(2,1)S(1)}, f32[8,2,512]{2,1,0:T(2,128)S(1)}) custom-call(s32[1]{0:T(128)} %bitcast.s_ref, bf16[512,3072]{1,0:T(8,128)(2,1)S(1)} %shard_map.316.q_ref.km_ref.vm_ref, bf16[512,3072]{1,0:T(8,128)(2,1)S(1)} %shard_map.316.q_ref.km_ref.vm_ref, bf16[512,3072]{1,0:T(8,128)(2,1)} %copy-done.58, ...), custom_call_target="tpu_custom_call" | custom-call | flops 1024 | bytes 1024 | tf_op jit(solution)/shard_map/pallas_call | solution.py:497
  274.6 6.7 collective-permute-done.44.refs_1_
  284.1 5.1 shard_map.319
  290.5 6.9 collective-permute-done.46
  305.3 8.6 %shard_map.321 = bf16[4,2,2,2,32,4096]{5,4,3,2,1,0:T(8,128)(2,1)} custom-call(s32[4]{0:T(128)S(1)} %pad_add_fusion.coords_ref, bf16[8,128,1024]{2,1,0:T(8,128)(2,1)} %pad_maximum_fusion.3.refs_0_, bf16[8,128,1024]{2,1,0:T(8,128)(2,1)} %collective-permute-done.44.refs_1_, bf16[8,128,1024]{2,1,0:T(8,128)(2,1)} %collective-permute-done.45.refs_2_, ...), custom_call_target="tpu_custom_call" | custom-call | flops 1024 | bytes 1024 | tf_op jit(solution)/shard_map/pallas_call | solution.py:97
  314.0 10.9 %shard_map.322 = (bf16[512,4096]{1,0:T(8,128)(2,1)S(1)}, bf16[512,4096]{1,0:T(8,128)(2,1)}) custom-call(bf16[512,1024]{1,0:T(8,128)(2,1)S(1)} %copy-done.29, bf16[1024,4096]{1,0:T(8,128)(2,1)} %bitcast.283, f32[1,4096]{1,0:T(1,128)S(1)} %get-tuple-element.883.refs_0_), custom_call_target="tpu_custom_call" | custom-call | flops 1024 | bytes 1024 | tf_op jit(solution)/shard_map/pallas_call | solution.py:606
  329.4 4.8 shard_map.323
  336.1 8.5 %shard_map.324.total_ref = f32[512,1024]{1,0:T(8,128)S(1)} custom-call(bf16[512,4096]{1,0:T(8,128)(2,1)} %copy-done.6, bf16[4096,1024]{1,0:T(8,128)(2,1)} %bitcast.285, f32[1,1024]{1,0:T(1,128)S(1)} %get-tuple-element.865.refs_0_, f32[512,1024]{1,0:T(8,128)S(1)} %copy-done.35), custom_call_target="tpu_custom_call" | custom-call | flops 1024 | bytes 1024 | tf_op jit(solution)/shard_map/pallas_call | solution.py:606
  348.3 9.4 %shard_map.326 = (bf16[512,4096]{1,0:T(8,128)(2,1)}, f32[1,4096]{1,0:T(1,128)S(1)}) custom-call(bf16[512,1024]{1,0:T(8,128)(2,1)S(1)} %get-tuple-element.603.rows_ref.refs_4_, bf16[4096,1024]{1,0:T(8,128)(2,1)} %bitcast.286, bf16[512,4096]{1,0:T(8,128)(2,1)} %get-tuple-element.604.refs_0_), custom_call_target="tpu_custom_call" | custom-call | flops 1024 | bytes 1024 | tf_op jit(solution)/shard_map/pallas_call | solution.py:606
  365.0 11.1 %shard_map.327 = (bf16[1024,1024]{1,0:T(8,128)(2,1)S(1)}, bf16[1024,1024]{1,0:T(8,128)(2,1)}) custom-call(s32[32]{0:T(128)S(1)} %stack.442.order_ref, bf16[512,4096]{1,0:T(8,128)(2,1)} %copy-done.6, bf16[512,4096]{1,0:T(8,128)(2,1)} %copy-done.6, bf16[512,4096]{1,0:T(8,128)(2,1)} %copy-done.61, bf16[512,4096]{1,0:T(8,128)(2,1)} %copy-done.61, ...), custom_call_target="tpu_custom_call" | custom-call | flops 1024 | bytes 1024 | tf_op jit(solution)/shard_map/pallas_call | solution.py:309
  377.9 8.5 %shard_map.328.up_ref = f32[512,1024]{1,0:T(8,128)S(1)} custom-call(bf16[512,4096]{1,0:T(8,128)(2,1)} %get-tuple-element.622.rows_ref.refs_2_, bf16[1024,4096]{1,0:T(8,128)(2,1)} %bitcast.284, f32[512,1024]{1,0:T(8,128)S(1)} %copy-done.45), custom_call_target="tpu_custom_call" | custom-call | flops 1024 | bytes 1024 | tf_op jit(solution)/shard_map/pallas_call | solution.py:606
  392.1 8.4 %shard_map.331 = (bf16[256,4096]{1,0:T(8,128)(2,1)}, bf16[256,4096]{1,0:T(8,128)(2,1)S(1)}) custom-call(bf16[512,512]{1,0:T(8,128)(2,1)} %copy-done.55, bf16[512,512]{1,0:T(8,128)(2,1)} %copy-done.112, bf16[512,4096]{1,0:T(8,128)(2,1)} %get-tuple-element.622.rows_ref.refs_2_, bf16[512,4096]{1,0:T(8,128)(2,1)} %collective-permute-done.55.refs_3_), custom_call_target="tpu_custom_call" | custom-call | flops 1024 | bytes 1024 | tf_op jit(solution)/shard_map/pallas_call | solution.py:273
  404.0 20.9 %shard_map.332 = (bf16[512,1024]{1,0:T(8,128)(2,1)S(1)}, f32[2,512,1024]{2,1,0:T(8,128)}, bf16[2,512,1024]{2,1,0:T(8,128)(2,1)S(1)}) custom-call(s32[1]{0:T(128)} %bitcast.s_ref, bf16[512,3072]{1,0:T(8,128)(2,1)} %copy-done.3, bf16[512,3072]{1,0:T(8,128)(2,1)} %copy-done.3, bf16[512,3072]{1,0:T(8,128)(2,1)} %copy-done.58, bf16[512,3072]{1,0:T(8,128)(2,1)} %copy-done.3, ...), custom_call_target="tpu_custom_call" | custom-call | flops 1024 | bytes 1024 | tf_op jit(solution)/shard_map/pallas_call | solution.py:497
  429.1 5.3 add_convert_fusion.8
  440.5 7.1 %shard_map.334.up_ref = f32[512,1024]{1,0:T(8,128)S(1)} custom-call(bf16[512,3072]{1,0:T(8,128)(2,1)} %get-tuple-element.651.rows_ref.refs_2_, bf16[1024,3072]{1,0:T(8,128)(2,1)} %bitcast.292, f32[512,1024]{1,0:T(8,128)S(1)} %get-tuple-element.643.refs_0_), custom_call_target="tpu_custom_call" | custom-call | flops 1024 | bytes 1024 | tf_op jit(solution)/shard_map/pallas_call | solution.py:606
  450.1 9.2 %shard_map.335 = (bf16[256,4096]{1,0:T(8,128)(2,1)}, bf16[256,4096]{1,0:T(8,128)(2,1)}) custom-call(bf16[512,512]{1,0:T(8,128)(2,1)} %copy-done.53, bf16[512,512]{1,0:T(8,128)(2,1)} %collective-permute-done.42.refs_1_, bf16[512,3072]{1,0:T(8,128)(2,1)} %get-tuple-element.651.rows_ref.refs_2_, bf16[512,3072]{1,0:T(8,128)(2,1)} %collective-permute-done.62.refs_3_, ...), custom_call_target="tpu_custom_call" | custom-call | flops 1024 | bytes 1024 | tf_op jit(solution)/shard_map/pallas_call | solution.py:273
  467.9 9.8 %shard_map.337 = (bf16[512,4096]{1,0:T(8,128)(2,1)}, f32[1,4096]{1,0:T(1,128)S(1)}) custom-call(bf16[512,1024]{1,0:T(8,128)(2,1)S(1)} %get-tuple-element.665.rows_ref.b1, bf16[4096,1024]{1,0:T(8,128)(2,1)} %bitcast.282, bf16[512,4096]{1,0:T(8,128)(2,1)} %get-tuple-element.666.refs_0_), custom_call_target="tpu_custom_call" | custom-call | flops 1024 | bytes 1024 | tf_op jit(solution)/shard_map/pallas_call | solution.py:606
  477.7 4.0 collective-permute-done.64
  486.9 15.1 %shard_map.338 = (bf16[2,8,128,512]{3,2,1,0:T(8,128)(2,1)S(1)}, bf16[2,8,128,512]{3,2,1,0:T(8,128)(2,1)}) custom-call(s32[32]{0:T(128)S(1)} %stack.444.order_ref, s32[16]{0:T(128)S(1)} %select_reduce_fusion.place_ref, bf16[512,4096]{1,0:T(8,128)(2,1)} %copy-done.14, bf16[512,4096]{1,0:T(8,128)(2,1)} %collective-permute-done.43.a2, ...), custom_call_target="tpu_custom_call" | custom-call | flops 1024 | bytes 1024 | tf_op jit(solution)/shard_map/pallas_call | solution.py:346
  517.2 8.5 %shard_map.339.up_ref = f32[512,1024]{1,0:T(8,128)S(1)} custom-call(bf16[512,4096]{1,0:T(8,128)(2,1)} %get-tuple-element.699.rows_ref.refs_2_, bf16[1024,4096]{1,0:T(8,128)(2,1)} %bitcast.290, f32[512,1024]{1,0:T(8,128)S(1)} %copy-done.43), custom_call_target="tpu_custom_call" | custom-call | flops 1024 | bytes 1024 | tf_op jit(solution)/shard_map/pallas_call | solution.py:606
  532.1 7.5 %shard_map.342 = (bf16[256,4096]{1,0:T(8,128)(2,1)S(1)}, bf16[256,4096]{1,0:T(8,128)(2,1)S(1)}) custom-call(bf16[512,512]{1,0:T(8,128)(2,1)} %copy-done.52, bf16[512,512]{1,0:T(8,128)(2,1)} %copy-done.102, bf16[512,4096]{1,0:T(8,128)(2,1)} %get-tuple-element.699.rows_ref.refs_2_, bf16[512,4096]{1,0:T(8,128)(2,1)} %collective-permute-done.66.refs_3_), custom_call_target="tpu_custom_call" | custom-call | flops 1024 | bytes 1024 | tf_op jit(solution)/shard_map/pallas_call | solution.py:273
  553.5 20.9 %shard_map.343 = (bf16[512,1024]{1,0:T(8,128)(2,1)S(1)}, f32[2,512,1024]{2,1,0:T(8,128)}, bf16[2,512,1024]{2,1,0:T(8,128)(2,1)S(1)}) custom-call(s32[1]{0:T(128)} %bitcast.s_ref, bf16[512,3072]{1,0:T(8,128)(2,1)} %copy-done.2, bf16[512,3072]{1,0:T(8,128)(2,1)} %copy-done.2, bf16[512,3072]{1,0:T(8,128)(2,1)} %collective-permute-done.18.ko_ref.vo_ref, ...), custom_call_target="tpu_custom_call" | custom-call | flops 1024 | bytes 1024 | tf_op jit(solution)/shard_map/pallas_call | solution.py:497
  575.6 5.9 collective-permute-done.74
  596.3 9.1 %shard_map.345 = (bf16[256,4096]{1,0:T(8,128)(2,1)}, bf16[256,4096]{1,0:T(8,128)(2,1)}) custom-call(bf16[512,512]{1,0:T(8,128)(2,1)} %copy-done.50, bf16[512,512]{1,0:T(8,128)(2,1)} %copy-done.100, bf16[512,3072]{1,0:T(8,128)(2,1)} %copy-done.19, bf16[512,3072]{1,0:T(8,128)(2,1)} %copy-done.70, bf16[512,512]{1,0:T(8,128)(2,1)} %copy-done.51, ...), custom_call_target="tpu_custom_call" | custom-call | flops 1024 | bytes 1024 | tf_op jit(solution)/shard_map/pallas_call | solution.py:273
  611.4 7.2 %shard_map.346 = f32[512,1024]{1,0:T(8,128)S(1)} custom-call(bf16[512,3072]{1,0:T(8,128)(2,1)} %copy-done.19, bf16[1024,3072]{1,0:T(8,128)(2,1)} %bitcast.288, f32[512,1024]{1,0:T(8,128)S(1)} %copy-done.41), custom_call_target="tpu_custom_call" | custom-call | flops 1024 | bytes 1024 | tf_op jit(solution)/shard_map/pallas_call | solution.py:606
  618.6 15.9 %collective-permute-done.84 = bf16[256,512]{1,0:T(8,128)(2,1)S(1)} collective-permute-done((bf16[256,512]{1,0:T(8,128)(2,1)}, bf16[256,512]{1,0:T(8,128)(2,1)S(1)}, u32[]{:S(2)}, u32[]{:S(2)}) %collective-permute-start.84) | collective-permute-done | bytes 262176 | tf_op jit(solution)/shard_map/ppermute | solution.py:62
  645.6 7.8 %collective-permute-done.92 = bf16[32,128]{1,0:T(8,128)(2,1)S(1)} collective-permute-done((bf16[32,128]{1,0:T(8,128)(2,1)S(1)}, bf16[32,128]{1,0:T(8,128)(2,1)S(1)}, u32[]{:S(2)}, u32[]{:S(2)}) %collective-permute-start.92) | collective-permute-done | bytes 8224 | tf_op jit(solution)/shard_map/ppermute | solution.py:62
  661.4 12.9 %collective-permute-done.96 = bf16[16,128]{1,0:T(8,128)(2,1)S(1)} collective-permute-done((bf16[16,128]{1,0:T(8,128)(2,1)S(1)}, bf16[16,128]{1,0:T(8,128)(2,1)S(1)}, u32[]{:S(2)}, u32[]{:S(2)}) %collective-permute-start.96) | collective-permute-done | bytes 4128 | tf_op jit(solution)/shard_map/ppermute | solution.py:62
  680.4 7.2 %collective-permute-done.97 = bf16[32,4096]{1,0:T(8,128)(2,1)S(1)} collective-permute-done((bf16[32,4096]{1,0:T(8,128)(2,1)S(1)}, bf16[32,4096]{1,0:T(8,128)(2,1)S(1)}, u32[]{:S(2)}, u32[]{:S(2)}) %collective-permute-start.97) | collective-permute-done | bytes 262176 | tf_op jit(solution)/shard_map/ppermute | solution.py:62
  (633 shorter events, 273.3 us)
Async XLA Ops:
  30.3 20.3 %collective-permute-start.6 = (bf16[256,1024]{1,0:T(8,128)(2,1)}, bf16[256,1024]{1,0:T(8,128)(2,1)}, u32[]{:S(2)}, u32[]{:S(2)}) collective-permute-start(bf16[256,1024]{1,0:T(8,128)(2,1)} %get-tuple-element.422), channel_id=1, source_target_pairs={{0,2},{1,3},{2,0},{3,1},{4,6},{5,7},{6,4},{7,5},{8,10},{9,11},{10,... | collective-permute-start | bytes 1572872 | tf_op jit(solution)/shard_map/ppermute | solution.py:62
  66.0 20.5 %collective-permute-start.12 = (bf16[8,96,1024]{2,1,0:T(8,128)(2,1)S(1)}, bf16[8,96,1024]{2,1,0:T(8,128)(2,1)S(1)}, u32[]{:S(2)}, u32[]{:S(2)}) collective-permute-start(bf16[8,96,1024]{2,1,0:T(8,128)(2,1)S(1)} %pad_maximum_fusion.5.refs_0_), channel_id=1, source_target_pairs={{0,2},{1,5},{2,0},{3,7},{4,6},{5,1},{6,4},{7,3},{8,10},{9,13},{10,... | collective-permute-start | bytes 4718600 | tf_op jit(solution)/shard_map/ppermute | solution.py:62
  66.6 19.9 %collective-permute-start.13 = (bf16[8,96,1024]{2,1,0:T(8,128)(2,1)S(1)}, bf16[8,96,1024]{2,1,0:T(8,128)(2,1)}, u32[]{:S(2)}, u32[]{:S(2)}) collective-permute-start(bf16[8,96,1024]{2,1,0:T(8,128)(2,1)S(1)} %pad_maximum_fusion.5.refs_0_), channel_id=1, source_target_pairs={{0,1},{1,0},{2,3},{3,2},{4,5},{5,4},{6,7},{7,6},{8,9},{9,8},{10,11... | collective-permute-start | bytes 4718600 | tf_op jit(solution)/shard_map/ppermute | solution.py:62
  87.9 17.7 %collective-permute-start.16 = (bf16[4,160,1024]{2,1,0:T(8,128)(2,1)S(1)}, bf16[4,160,1024]{2,1,0:T(8,128)(2,1)S(1)}, u32[]{:S(2)}, u32[]{:S(2)}) collective-permute-start(bf16[4,160,1024]{2,1,0:T(8,128)(2,1)S(1)} %pad_maximum_fusion.6), channel_id=1, source_target_pairs={{0,4},{1,3},{2,6},{3,1},{4,0},{5,7},{6,2},{7,5},{8,12},{9,11},{10,... | collective-permute-start | bytes 3932168 | tf_op jit(solution)/shard_map/ppermute | solution.py:62
  108.8 31.8 %collective-permute-start.20 = (bf16[8,160,1024]{2,1,0:T(8,128)(2,1)S(1)}, bf16[8,160,1024]{2,1,0:T(8,128)(2,1)}, u32[]{:S(2)}, u32[]{:S(2)}) collective-permute-start(bf16[8,160,1024]{2,1,0:T(8,128)(2,1)S(1)} %pad_maximum_fusion.refs_0_), channel_id=1, source_target_pairs={{0,2},{1,5},{2,0},{3,7},{4,6},{5,1},{6,4},{7,3},{8,10},{9,13},{10,... | collective-permute-start | bytes 7864328 | tf_op jit(solution)/shard_map/ppermute | solution.py:62
  109.4 31.2 %collective-permute-start.21 = (bf16[8,160,1024]{2,1,0:T(8,128)(2,1)S(1)}, bf16[8,160,1024]{2,1,0:T(8,128)(2,1)}, u32[]{:S(2)}, u32[]{:S(2)}) collective-permute-start(bf16[8,160,1024]{2,1,0:T(8,128)(2,1)S(1)} %pad_maximum_fusion.refs_0_), channel_id=1, source_target_pairs={{0,1},{1,0},{2,3},{3,2},{4,5},{5,4},{6,7},{7,6},{8,9},{9,8},{10,11... | collective-permute-start | bytes 7864328 | tf_op jit(solution)/shard_map/ppermute | solution.py:62
  111.9 18.0 %collective-permute-start.19 = (bf16[512,512]{1,0:T(8,128)(2,1)S(1)}, bf16[512,512]{1,0:T(8,128)(2,1)S(1)}, u32[]{:S(2)}, u32[]{:S(2)}) collective-permute-start(bf16[512,512]{1,0:T(8,128)(2,1)S(1)} %get-tuple-element.470), channel_id=1, source_target_pairs={{0,1},{1,0},{2,3},{3,2},{4,5},{5,4},{6,7},{7,6},{8,9},{9,8},{10,11... | collective-permute-start | bytes 1572872 | tf_op jit(solution)/shard_map/ppermute | solution.py:62
  111.9 20.0 %collective-permute-start.22 = (bf16[2,128,1024]{2,1,0:T(8,128)(2,1)S(1)}, bf16[2,128,1024]{2,1,0:T(8,128)(2,1)S(1)}, u32[]{:S(2)}, u32[]{:S(2)}) collective-permute-start(bf16[2,128,1024]{2,1,0:T(8,128)(2,1)S(1)} %pad_maximum_fusion.15), channel_id=1, source_target_pairs={{0,8},{1,9},{2,10},{3,11},{4,12},{5,13},{6,14},{7,15},{8,0},{9,1},... | collective-permute-start | bytes 1572872 | tf_op jit(solution)/shard_map/ppermute | solution.py:62
  141.8 20.2 %collective-permute-start.25 = (bf16[4,128,1024]{2,1,0:T(8,128)(2,1)S(1)}, bf16[4,128,1024]{2,1,0:T(8,128)(2,1)S(1)}, u32[]{:S(2)}, u32[]{:S(2)}) collective-permute-start(bf16[4,128,1024]{2,1,0:T(8,128)(2,1)S(1)} %pad_maximum_fusion.7), channel_id=1, source_target_pairs={{0,4},{1,3},{2,6},{3,1},{4,0},{5,7},{6,2},{7,5},{8,12},{9,11},{10,... | collective-permute-start | bytes 3145736 | tf_op jit(solution)/shard_map/ppermute | solution.py:62
  143.4 18.6 %collective-permute-start.26 = (bf16[2,128,1024]{2,1,0:T(8,128)(2,1)S(1)}, bf16[2,128,1024]{2,1,0:T(8,128)(2,1)S(1)}, u32[]{:S(2)}, u32[]{:S(2)}) collective-permute-start(bf16[2,128,1024]{2,1,0:T(8,128)(2,1)S(1)} %pad_maximum_fusion.16), channel_id=1, source_target_pairs={{0,8},{1,9},{2,10},{3,11},{4,12},{5,13},{6,14},{7,15},{8,0},{9,1},... | collective-permute-start | bytes 1572872 | tf_op jit(solution)/shard_map/ppermute | solution.py:62
  164.6 37.3 %collective-permute-start.30 = (bf16[8,128,1024]{2,1,0:T(8,128)(2,1)S(1)}, bf16[8,128,1024]{2,1,0:T(8,128)(2,1)S(1)}, u32[]{:S(2)}, u32[]{:S(2)}) collective-permute-start(bf16[8,128,1024]{2,1,0:T(8,128)(2,1)S(1)} %pad_maximum_fusion.1.refs_0_), channel_id=1, source_target_pairs={{0,2},{1,5},{2,0},{3,7},{4,6},{5,1},{6,4},{7,3},{8,10},{9,13},{10,... | collective-permute-start | bytes 6291464 | tf_op jit(solution)/shard_map/ppermute | solution.py:62
  166.1 35.8 %collective-permute-start.31 = (bf16[8,128,1024]{2,1,0:T(8,128)(2,1)S(1)}, bf16[8,128,1024]{2,1,0:T(8,128)(2,1)S(1)}, u32[]{:S(2)}, u32[]{:S(2)}) collective-permute-start(bf16[8,128,1024]{2,1,0:T(8,128)(2,1)S(1)} %pad_maximum_fusion.1.refs_0_), channel_id=1, source_target_pairs={{0,1},{1,0},{2,3},{3,2},{4,5},{5,4},{6,7},{7,6},{8,9},{9,8},{10,11... | collective-permute-start | bytes 6291464 | tf_op jit(solution)/shard_map/ppermute | solution.py:62
  166.1 26.5 %collective-permute-start.32 = (bf16[4,128,1024]{2,1,0:T(8,128)(2,1)}, bf16[4,128,1024]{2,1,0:T(8,128)(2,1)}, u32[]{:S(2)}, u32[]{:S(2)}) collective-permute-start(bf16[4,128,1024]{2,1,0:T(8,128)(2,1)} %pad_maximum_fusion.8), channel_id=1, source_target_pairs={{0,4},{1,3},{2,6},{3,1},{4,0},{5,7},{6,2},{7,5},{8,12},{9,11},{10,... | collective-permute-start | bytes 3145736 | tf_op jit(solution)/shard_map/ppermute | solution.py:62
  171.8 20.8 %collective-permute-start.28 = (bf16[512,512]{1,0:T(8,128)(2,1)}, bf16[512,512]{1,0:T(8,128)(2,1)S(1)}, u32[]{:S(2)}, u32[]{:S(2)}) collective-permute-start(bf16[512,512]{1,0:T(8,128)(2,1)} %get-tuple-element.506), channel_id=1, source_target_pairs={{0,1},{1,0},{2,3},{3,2},{4,5},{5,4},{6,7},{7,6},{8,9},{9,8},{10,11... | collective-permute-start | bytes 1572872 | tf_op jit(solution)/shard_map/ppermute | solution.py:62
  204.9 26.4 %collective-permute-start.35 = (bf16[8,128,1024]{2,1,0:T(8,128)(2,1)}, bf16[8,128,1024]{2,1,0:T(8,128)(2,1)}, u32[]{:S(2)}, u32[]{:S(2)}) collective-permute-start(bf16[8,128,1024]{2,1,0:T(8,128)(2,1)} %pad_maximum_fusion.2.refs_0_), channel_id=1, source_target_pairs={{0,2},{1,5},{2,0},{3,7},{4,6},{5,1},{6,4},{7,3},{8,10},{9,13},{10,... | collective-permute-start | bytes 6291464 | tf_op jit(solution)/shard_map/ppermute | solution.py:62
  206.4 24.9 %collective-permute-start.36 = (bf16[8,128,1024]{2,1,0:T(8,128)(2,1)}, bf16[8,128,1024]{2,1,0:T(8,128)(2,1)}, u32[]{:S(2)}, u32[]{:S(2)}) collective-permute-start(bf16[8,128,1024]{2,1,0:T(8,128)(2,1)} %pad_maximum_fusion.2.refs_0_), channel_id=1, source_target_pairs={{0,1},{1,0},{2,3},{3,2},{4,5},{5,4},{6,7},{7,6},{8,9},{9,8},{10,11... | collective-permute-start | bytes 6291464 | tf_op jit(solution)/shard_map/ppermute | solution.py:62
  233.4 17.6 %collective-permute-start.39 = (bf16[4,128,1024]{2,1,0:T(8,128)(2,1)}, bf16[4,128,1024]{2,1,0:T(8,128)(2,1)}, u32[]{:S(2)}, u32[]{:S(2)}) collective-permute-start(bf16[4,128,1024]{2,1,0:T(8,128)(2,1)} %pad_maximum_fusion.9), channel_id=1, source_target_pairs={{0,4},{1,3},{2,6},{3,1},{4,0},{5,7},{6,2},{7,5},{8,12},{9,11},{10,... | collective-permute-start | bytes 3145736 | tf_op jit(solution)/shard_map/ppermute | solution.py:62
  234.9 46.4 %collective-permute-start.43 = (bf16[512,4096]{1,0:T(8,128)(2,1)S(1)}, bf16[512,4096]{1,0:T(8,128)(2,1)}, u32[]{:S(2)}, u32[]{:S(2)}) collective-permute-start(bf16[512,4096]{1,0:T(8,128)(2,1)S(1)} %copy-done.15), channel_id=1, source_target_pairs={{0,1},{1,0},{2,3},{3,2},{4,5},{5,4},{6,7},{7,6},{8,9},{9,8},{10,11... | collective-permute-start | bytes 12582920 | tf_op jit(solution)/shard_map/ppermute | solution.py:62
  254.9 26.4 %collective-permute-start.44 = (bf16[8,128,1024]{2,1,0:T(8,128)(2,1)}, bf16[8,128,1024]{2,1,0:T(8,128)(2,1)}, u32[]{:S(2)}, u32[]{:S(2)}) collective-permute-start(bf16[8,128,1024]{2,1,0:T(8,128)(2,1)} %pad_maximum_fusion.3.refs_0_), channel_id=1, source_target_pairs={{0,2},{1,5},{2,0},{3,7},{4,6},{5,1},{6,4},{7,3},{8,10},{9,13},{10,... | collective-permute-start | bytes 6291464 | tf_op jit(solution)/shard_map/ppermute | solution.py:62
  256.4 24.9 %collective-permute-start.45 = (bf16[8,128,1024]{2,1,0:T(8,128)(2,1)}, bf16[8,128,1024]{2,1,0:T(8,128)(2,1)}, u32[]{:S(2)}, u32[]{:S(2)}) collective-permute-start(bf16[8,128,1024]{2,1,0:T(8,128)(2,1)} %pad_maximum_fusion.3.refs_0_), channel_id=1, source_target_pairs={{0,1},{1,0},{2,3},{3,2},{4,5},{5,4},{6,7},{7,6},{8,9},{9,8},{10,11... | collective-permute-start | bytes 6291464 | tf_op jit(solution)/shard_map/ppermute | solution.py:62
  284.1 21.2 %collective-permute-start.47 = (bf16[8,128,1024]{2,1,0:T(8,128)(2,1)}, bf16[8,128,1024]{2,1,0:T(8,128)(2,1)}, u32[]{:S(2)}, u32[]{:S(2)}) collective-permute-start(bf16[8,128,1024]{2,1,0:T(8,128)(2,1)} %collective-permute-done.44.refs_1_), channel_id=1, source_target_pairs={{0,1},{1,0},{2,3},{3,2},{4,5},{5,4},{6,7},{7,6},{8,9},{9,8},{10,11... | collective-permute-start | bytes 6291464 | tf_op jit(solution)/shard_map/ppermute | solution.py:62
  298.9 26.1 %collective-permute-start.50 = (bf16[8,128,1024]{2,1,0:T(8,128)(2,1)S(1)}, bf16[8,128,1024]{2,1,0:T(8,128)(2,1)S(1)}, u32[]{:S(2)}, u32[]{:S(2)}) collective-permute-start(bf16[8,128,1024]{2,1,0:T(8,128)(2,1)S(1)} %pad_maximum_fusion.4.refs_0_), channel_id=1, source_target_pairs={{0,2},{1,5},{2,0},{3,7},{4,6},{5,1},{6,4},{7,3},{8,10},{9,13},{10,... | collective-permute-start | bytes 6291464 | tf_op jit(solution)/shard_map/ppermute | solution.py:62
  300.4 24.6 %collective-permute-start.51 = (bf16[8,128,1024]{2,1,0:T(8,128)(2,1)S(1)}, bf16[8,128,1024]{2,1,0:T(8,128)(2,1)S(1)}, u32[]{:S(2)}, u32[]{:S(2)}) collective-permute-start(bf16[8,128,1024]{2,1,0:T(8,128)(2,1)S(1)} %pad_maximum_fusion.4.refs_0_), channel_id=1, source_target_pairs={{0,1},{1,0},{2,3},{3,2},{4,5},{5,4},{6,7},{7,6},{8,9},{9,8},{10,11... | collective-permute-start | bytes 6291464 | tf_op jit(solution)/shard_map/ppermute | solution.py:62
  304.8 20.0 %collective-permute-start.48 = (bf16[512,512]{1,0:T(8,128)(2,1)S(1)}, bf16[512,512]{1,0:T(8,128)(2,1)S(1)}, u32[]{:S(2)}, u32[]{:S(2)}) collective-permute-start(bf16[512,512]{1,0:T(8,128)(2,1)S(1)} %get-tuple-element.579), channel_id=1, source_target_pairs={{0,1},{1,0},{2,3},{3,2},{4,5},{5,4},{6,7},{7,6},{8,9},{9,8},{10,11... | collective-permute-start | bytes 1572872 | tf_op jit(solution)/shard_map/ppermute | solution.py:62
  305.3 19.5 %collective-permute-start.49 = (bf16[512,512]{1,0:T(8,128)(2,1)S(1)}, bf16[512,512]{1,0:T(8,128)(2,1)S(1)}, u32[]{:S(2)}, u32[]{:S(2)}) collective-permute-start(bf16[512,512]{1,0:T(8,128)(2,1)S(1)} %get-tuple-element.581), channel_id=1, source_target_pairs={{0,1},{1,0},{2,3},{3,2},{4,5},{5,4},{6,7},{7,6},{8,9},{9,8},{10,11... | collective-permute-start | bytes 1572872 | tf_op jit(solution)/shard_map/ppermute | solution.py:62
  358.7 18.0 %collective-permute-start.55 = (bf16[512,4096]{1,0:T(8,128)(2,1)}, bf16[512,4096]{1,0:T(8,128)(2,1)}, u32[]{:S(2)}, u32[]{:S(2)}) collective-permute-start(bf16[512,4096]{1,0:T(8,128)(2,1)} %get-tuple-element.622.rows_ref.refs_2_), channel_id=1, source_target_pairs={{0,1},{1,0},{2,3},{3,2},{4,5},{5,4},{6,7},{7,6},{8,9},{9,8},{10,11... | collective-permute-start | bytes 12582920 | tf_op jit(solution)/shard_map/ppermute | solution.py:62
  376.6 26.2 %collective-permute-start.57 = (bf16[1024,1024]{1,0:T(8,128)(2,1)S(1)}, bf16[1024,1024]{1,0:T(8,128)(2,1)}, u32[]{:S(2)}, u32[]{:S(2)}) collective-permute-start(bf16[1024,1024]{1,0:T(8,128)(2,1)S(1)} %get-tuple-element.626), channel_id=1, source_target_pairs={{0,2},{1,5},{2,0},{3,7},{4,6},{5,1},{6,4},{7,3},{8,10},{9,13},{10,... | collective-permute-start | bytes 6291464 | tf_op jit(solution)/shard_map/ppermute | solution.py:62
  402.8 26.2 %collective-permute-start.58 = (bf16[256,4096]{1,0:T(8,128)(2,1)}, bf16[256,4096]{1,0:T(8,128)(2,1)S(1)}, u32[]{:S(2)}, u32[]{:S(2)}) collective-permute-start(bf16[256,4096]{1,0:T(8,128)(2,1)} %get-tuple-element.633), channel_id=1, source_target_pairs={{0,2},{1,5},{2,0},{3,7},{4,6},{5,1},{6,4},{7,3},{8,10},{9,13},{10,... | collective-permute-start | bytes 6291464 | tf_op jit(solution)/shard_map/ppermute | solution.py:62
  439.2 20.1 %collective-permute-start.61 = (bf16[512,1024]{1,0:T(8,128)(2,1)}, bf16[512,1024]{1,0:T(8,128)(2,1)}, u32[]{:S(2)}, u32[]{:S(2)}) collective-permute-start(bf16[512,1024]{1,0:T(8,128)(2,1)} %get-tuple-element.647), channel_id=1, source_target_pairs={{0,4},{1,3},{2,6},{3,1},{4,0},{5,7},{6,2},{7,5},{8,12},{9,11},{10,... | collective-permute-start | bytes 3145736 | tf_op jit(solution)/shard_map/ppermute | solution.py:62
  483.8 26.4 %collective-permute-start.66 = (bf16[512,4096]{1,0:T(8,128)(2,1)}, bf16[512,4096]{1,0:T(8,128)(2,1)}, u32[]{:S(2)}, u32[]{:S(2)}) collective-permute-start(bf16[512,4096]{1,0:T(8,128)(2,1)} %get-tuple-element.699.rows_ref.refs_2_), channel_id=1, source_target_pairs={{0,1},{1,0},{2,3},{3,2},{4,5},{5,4},{6,7},{7,6},{8,9},{9,8},{10,11... | collective-permute-start | bytes 12582920 | tf_op jit(solution)/shard_map/ppermute | solution.py:62
  483.8 26.4 %collective-permute-start.67 = (bf16[256,4096]{1,0:T(8,128)(2,1)}, bf16[256,4096]{1,0:T(8,128)(2,1)}, u32[]{:S(2)}, u32[]{:S(2)}) collective-permute-start(bf16[256,4096]{1,0:T(8,128)(2,1)} %get-tuple-element.682), channel_id=1, source_target_pairs={{0,2},{1,5},{2,0},{3,7},{4,6},{5,1},{6,4},{7,3},{8,10},{9,13},{10,... | collective-permute-start | bytes 6291464 | tf_op jit(solution)/shard_map/ppermute | solution.py:62
  485.1 20.0 %collective-permute-start.69 = (bf16[128,1024]{1,0:T(8,128)(2,1)}, bf16[128,1024]{1,0:T(8,128)(2,1)S(1)}, u32[]{:S(2)}, u32[]{:S(2)}) collective-permute-start(bf16[128,1024]{1,0:T(8,128)(2,1)} %add_convert_fusion.32), channel_id=1, source_target_pairs={{0,16},{1,17},{2,18},{3,19},{4,20},{5,21},{6,22},{7,23},{8,24},{9,... | collective-permute-start | bytes 786440 | tf_op jit(solution)/shard_map/ppermute | solution.py:62
  486.6 19.7 %collective-permute-start.68 = (bf16[64,4096]{1,0:T(8,128)(2,1)}, bf16[64,4096]{1,0:T(8,128)(2,1)S(1)}, u32[]{:S(2)}, u32[]{:S(2)}) collective-permute-start(bf16[64,4096]{1,0:T(8,128)(2,1)} %get-tuple-element.683), channel_id=1, source_target_pairs={{0,8},{1,9},{2,10},{3,11},{4,12},{5,13},{6,14},{7,15},{8,0},{9,1},... | collective-permute-start | bytes 1572872 | tf_op jit(solution)/shard_map/ppermute | solution.py:62
  513.7 30.7 %collective-permute-start.70 = (bf16[1024,512]{1,0:T(8,128)(2,1)}, bf16[1024,512]{1,0:T(8,128)(2,1)}, u32[]{:S(2)}, u32[]{:S(2)}) collective-permute-start(bf16[1024,512]{1,0:T(8,128)(2,1)} %bitcast.154), channel_id=1, source_target_pairs={{0,8},{1,9},{2,10},{3,11},{4,12},{5,13},{6,14},{7,15},{8,0},{9,1},... | collective-permute-start | bytes 3145736 | tf_op jit(solution)/shard_map/ppermute | solution.py:62
  514.0 30.4 %collective-permute-start.71 = (bf16[1024,512]{1,0:T(8,128)(2,1)}, bf16[1024,512]{1,0:T(8,128)(2,1)}, u32[]{:S(2)}, u32[]{:S(2)}) collective-permute-start(bf16[1024,512]{1,0:T(8,128)(2,1)} %bitcast.156), channel_id=1, source_target_pairs={{0,2},{1,5},{2,0},{3,7},{4,6},{5,1},{6,4},{7,3},{8,10},{9,13},{10,... | collective-permute-start | bytes 3145736 | tf_op jit(solution)/shard_map/ppermute | solution.py:62
  514.9 29.5 %collective-permute-start.72 = (bf16[128,4096]{1,0:T(8,128)(2,1)}, bf16[128,4096]{1,0:T(8,128)(2,1)S(1)}, u32[]{:S(2)}, u32[]{:S(2)}) collective-permute-start(bf16[128,4096]{1,0:T(8,128)(2,1)} %get-tuple-element.705), channel_id=1, source_target_pairs={{0,4},{1,3},{2,6},{3,1},{4,0},{5,7},{6,2},{7,5},{8,12},{9,11},{10,... | collective-permute-start | bytes 3145736 | tf_op jit(solution)/shard_map/ppermute | solution.py:62
  515.8 26.3 %collective-permute-start.73 = (bf16[32,4096]{1,0:T(8,128)(2,1)S(1)}, bf16[32,4096]{1,0:T(8,128)(2,1)S(1)}, u32[]{:S(2)}, u32[]{:S(2)}) collective-permute-start(bf16[32,4096]{1,0:T(8,128)(2,1)S(1)} %add_convert_fusion.31), channel_id=1, source_target_pairs={{0,16},{1,17},{2,18},{3,19},{4,20},{5,21},{6,22},{7,23},{8,24},{9,... | collective-permute-start | bytes 786440 | tf_op jit(solution)/shard_map/ppermute | solution.py:62
  550.0 31.5 %collective-permute-start.74 = (bf16[256,4096]{1,0:T(8,128)(2,1)S(1)}, bf16[256,4096]{1,0:T(8,128)(2,1)}, u32[]{:S(2)}, u32[]{:S(2)}) collective-permute-start(bf16[256,4096]{1,0:T(8,128)(2,1)S(1)} %get-tuple-element.717), channel_id=1, source_target_pairs={{0,2},{1,5},{2,0},{3,7},{4,6},{5,1},{6,4},{7,3},{8,10},{9,13},{10,... | collective-permute-start | bytes 6291464 | tf_op jit(solution)/shard_map/ppermute | solution.py:62
  550.9 24.7 %collective-permute-start.75 = (bf16[512,512]{1,0:T(8,128)(2,1)}, bf16[512,512]{1,0:T(8,128)(2,1)S(1)}, u32[]{:S(2)}, u32[]{:S(2)}) collective-permute-start(bf16[512,512]{1,0:T(8,128)(2,1)} %get-tuple-element.718), channel_id=1, source_target_pairs={{0,16},{1,17},{2,18},{3,19},{4,20},{5,21},{6,22},{7,23},{8,24},{9,... | collective-permute-start | bytes 1572872 | tf_op jit(solution)/shard_map/ppermute | solution.py:62
  552.1 23.5 %collective-permute-start.76 = (bf16[512,512]{1,0:T(8,128)(2,1)}, bf16[512,512]{1,0:T(8,128)(2,1)S(1)}, u32[]{:S(2)}, u32[]{:S(2)}) collective-permute-start(bf16[512,512]{1,0:T(8,128)(2,1)} %get-tuple-element.719), channel_id=1, source_target_pairs={{0,4},{1,3},{2,6},{3,1},{4,0},{5,7},{6,2},{7,5},{8,12},{9,11},{10,... | collective-permute-start | bytes 1572872 | tf_op jit(solution)/shard_map/ppermute | solution.py:62
  553.0 22.6 %collective-permute-start.77 = (bf16[64,4096]{1,0:T(8,128)(2,1)}, bf16[64,4096]{1,0:T(8,128)(2,1)S(1)}, u32[]{:S(2)}, u32[]{:S(2)}) collective-permute-start(bf16[64,4096]{1,0:T(8,128)(2,1)} %get-tuple-element.720), channel_id=1, source_target_pairs={{0,8},{1,9},{2,10},{3,11},{4,12},{5,13},{6,14},{7,15},{8,0},{9,1},... | collective-permute-start | bytes 1572872 | tf_op jit(solution)/shard_map/ppermute | solution.py:62
  553.5 35.3 %collective-permute-start.79 = (bf16[512,1024]{1,0:T(8,128)(2,1)S(1)}, bf16[512,1024]{1,0:T(8,128)(2,1)S(1)}, u32[]{:S(2)}, u32[]{:S(2)}) collective-permute-start(bf16[512,1024]{1,0:T(8,128)(2,1)S(1)} %get-tuple-element.695.rows_ref.refs_6_), channel_id=1, source_target_pairs={{0,1},{1,0},{2,3},{3,2},{4,5},{5,4},{6,7},{7,6},{8,9},{9,8},{10,11... | collective-permute-start | bytes 3145736 | tf_op jit(solution)/shard_map/ppermute | solution.py:62
  605.4 29.3 %collective-permute-start.83 = (bf16[256,4096]{1,0:T(8,128)(2,1)}, bf16[256,4096]{1,0:T(8,128)(2,1)}, u32[]{:S(2)}, u32[]{:S(2)}) collective-permute-start(bf16[256,4096]{1,0:T(8,128)(2,1)} %get-tuple-element.749), channel_id=1, source_target_pairs={{0,2},{1,5},{2,0},{3,7},{4,6},{5,1},{6,4},{7,3},{8,10},{9,13},{10,... | collective-permute-start | bytes 6291464 | tf_op jit(solution)/shard_map/ppermute | solution.py:62
  607.4 27.1 %collective-permute-start.84 = (bf16[256,512]{1,0:T(8,128)(2,1)}, bf16[256,512]{1,0:T(8,128)(2,1)S(1)}, u32[]{:S(2)}, u32[]{:S(2)}) collective-permute-start(bf16[256,512]{1,0:T(8,128)(2,1)} %get-tuple-element.751), channel_id=1, source_target_pairs={{0,2},{1,5},{2,0},{3,7},{4,6},{5,1},{6,4},{7,3},{8,10},{9,13},{10,... | collective-permute-start | bytes 786440 | tf_op jit(solution)/shard_map/ppermute | solution.py:62
  608.5 26.0 %collective-permute-start.85 = (bf16[256,512]{1,0:T(8,128)(2,1)}, bf16[256,512]{1,0:T(8,128)(2,1)S(1)}, u32[]{:S(2)}, u32[]{:S(2)}) collective-permute-start(bf16[256,512]{1,0:T(8,128)(2,1)} %get-tuple-element.752), channel_id=1, source_target_pairs={{0,8},{1,9},{2,10},{3,11},{4,12},{5,13},{6,14},{7,15},{8,0},{9,1},... | collective-permute-start | bytes 786440 | tf_op jit(solution)/shard_map/ppermute | solution.py:62
  609.1 25.6 %collective-permute-start.87 = (bf16[64,128]{1,0:T(8,128)(2,1)S(1)}, bf16[64,128]{1,0:T(8,128)(2,1)S(1)}, u32[]{:S(2)}, u32[]{:S(2)}) collective-permute-start(bf16[64,128]{1,0:T(8,128)(2,1)S(1)} %get-tuple-element.759), channel_id=1, source_target_pairs={{0,2},{1,5},{2,0},{3,7},{4,6},{5,1},{6,4},{7,3},{8,10},{9,13},{10,... | collective-permute-start | bytes 49160 | tf_op jit(solution)/shard_map/ppermute | solution.py:62
  655.5 18.8 %collective-permute-start.93 = (bf16[256,1024]{1,0:T(8,128)(2,1)S(1)}, bf16[256,1024]{1,0:T(8,128)(2,1)S(1)}, u32[]{:S(2)}, u32[]{:S(2)}) collective-permute-start(bf16[256,1024]{1,0:T(8,128)(2,1)S(1)} %slice.1021), channel_id=1, source_target_pairs={{0,2},{1,3},{2,0},{3,1},{4,6},{5,7},{6,4},{7,5},{8,10},{9,11},{10,... | collective-permute-start | bytes 1572872 | tf_op jit(solution)/shard_map/ppermute | solution.py:62
  656.7 17.6 %collective-permute-start.94 = (bf16[64,4096]{1,0:T(8,128)(2,1)S(1)}, bf16[64,4096]{1,0:T(8,128)(2,1)S(1)}, u32[]{:S(2)}, u32[]{:S(2)}) collective-permute-start(bf16[64,4096]{1,0:T(8,128)(2,1)S(1)} %get-tuple-element.786), channel_id=1, source_target_pairs={{0,8},{1,9},{2,10},{3,11},{4,12},{5,13},{6,14},{7,15},{8,0},{9,1},... | collective-permute-start | bytes 1572872 | tf_op jit(solution)/shard_map/ppermute | solution.py:62
  (182 other events, 1870.3 us)

commit v7 on v6

--- a/solution.py
+++ b/solution.py
@@ -971,7 +971,7 @@
         else:
             mix_pair = (left_mix, (branch_low, branch_got), D)
             a_sum = SumUnit(weight_terms((left_stream, (low, low_got), 3 * D), mix_pair))
-            low, low_sums = phase((low, low_sums), a_sum, settle=[i_sum, before.a] if before else [i_sum])
+            low, low_sums = phase((low, low_sums), a_sum, settle=[i_sum, *o_sums, before.a] if before else [i_sum])
             (upstream,) = product(
                 low, w_three, 256, lambda total, g: (g + total,), (f32,), (), (first_sum_grad,), transposed=True
             )

time: 697 us -> 694 us (level)
    unnamed x274 -> x282, local copies, waits for them, and re-layouts: 24.8 us -> 25 us
  transfers between devices with their start and end apart: 99 -> 99, of which waited for: 46 -> 45; matrix products, arithmetic and copies ran while one was open for 8% -> 8% of each run, Pallas kernels for 43% -> 44%
where the time goes in v7:
time: 694 us; the launch traced here: 687 us
  Pallas kernels  308 us (44%)
  waiting for transfers between devices  181 us (26%)
  starting transfers between devices  75.4 us (11%)
  other arithmetic  67 us (10%)
  local copies, waits for them, and re-layouts  52.4 us (8%)
    ppermute x99, waiting for transfers between devices, send(): return lax.ppermute(value, AXES, to)  181 us
    pallas_call x14, Pallas kernels, product(): pl.pallas_call(kernel, grid=(width // tile,), in_specs=[pl.BlockSpec((tok...  107 us
    ppermute x99, starting transfers between devices, send(): return lax.ppermute(value, AXES, to)  75.4 us
    pallas_call x4, Pallas kernels, call_attention(): pl.pallas_call(kernel, grid=(pairs_count,), in_specs=in_specs, out_specs=...  66.6 us
    pallas_call x6, Pallas kernels, place(): pl.pallas_call(kernel, in_specs=[pl.BlockSpec(memory_space=pltpu.SMEM)] +...  39.2 us
    pallas_call x4, Pallas kernels, weight_terms(): pl.pallas_call(kernel, grid=(columns // tile,), in_specs=in_specs, out_sp...  34.2 us
    convert_element_type x16, other arithmetic, local(): self.kept = self.kept.astype(bf16)  26.2 us
    unnamed x282, local copies, waits for them, and re-layouts  25 us
  transfers between devices with their start and end apart: 99, of which 45 were waited for; matrix products, arithmetic and copies ran while one was open for 8% of the time, Pallas kernels for 44%

profile of v7, /device:TPU:0, one launch (start us, length us, event | category | flops | bytes accessed | tf_op | source)
XLA Modules:
  0.0 687.3 jit_solution(17878043197187013139)
XLA Ops:
  21.3 4.2 collective-permute-done.4
  25.5 4.7 collective-permute-done
  40.9 7.2 %collective-permute-done.8 = bf16[1,160,1024]{2,1,0:T(8,128)(2,1)S(1)} collective-permute-done((bf16[1,160,1024]{2,1,0:T(8,128)(2,1)S(1)}, bf16[1,160,1024]{2,1,0:T(8,128)(2,1)S(1)}, u32[]{:S(2)}, u32[]{:S(2)}) %collective-permute-start.8) | collective-permute-done | bytes 327712 | tf_op jit(solution)/shard_map/ppermute | solution.py:62
  56.8 6.0 collective-permute-done.10
  76.5 7.6 %collective-permute-done.14 = bf16[2,160,1024]{2,1,0:T(8,128)(2,1)} collective-permute-done((bf16[2,160,1024]{2,1,0:T(8,128)(2,1)}, bf16[2,160,1024]{2,1,0:T(8,128)(2,1)}, u32[]{:S(2)}, u32[]{:S(2)}) %collective-permute-start.14) | collective-permute-done | bytes 655392 | tf_op jit(solution)/shard_map/ppermute | solution.py:62
  91.3 5.8 shard_map.305
  97.2 5.9 shard_map.306.q_ref.km_ref.vm_ref
  114.7 12.4 %shard_map.308 = (bf16[512,1024]{1,0:T(8,128)(2,1)S(1)}, f32[8,2,512]{2,1,0:T(2,128)S(1)}) custom-call(s32[1]{0:T(128)} %bitcast.s_ref, bf16[512,3072]{1,0:T(8,128)(2,1)S(1)} %shard_map.306.q_ref.km_ref.vm_ref, bf16[512,3072]{1,0:T(8,128)(2,1)S(1)} %shard_map.306.q_ref.km_ref.vm_ref, bf16[512,3072]{1,0:T(8,128)(2,1)} %collective-permute-done.18.ko_ref.vo_ref, ...), custom_call_target="tpu_custom_call" | custom-call | flops 1024 | bytes 1024 | tf_op jit(solution)/shard_map/pallas_call | solution.py:497
  131.9 8.7 %collective-permute-done.20.refs_1_ = bf16[8,160,1024]{2,1,0:T(8,128)(2,1)} collective-permute-done((bf16[8,160,1024]{2,1,0:T(8,128)(2,1)S(1)}, bf16[8,160,1024]{2,1,0:T(8,128)(2,1)}, u32[]{:S(2)}, u32[]{:S(2)}) %collective-permute-start.20) | collective-permute-done | bytes 2621472 | tf_op jit(solution)/shard_map/ppermute | solution.py:62
  147.0 7.9 %shard_map.309 = (bf16[4,2,2,2,32,4096]{5,4,3,2,1,0:T(8,128)(2,1)}, bf16[4,2,2,2,32,1024]{5,4,3,2,1,0:T(8,128)(2,1)}) custom-call(s32[4]{0:T(128)S(1)} %pad_add_fusion.coords_ref, bf16[8,160,1024]{2,1,0:T(8,128)(2,1)S(1)} %pad_maximum_fusion.refs_0_, bf16[8,160,1024]{2,1,0:T(8,128)(2,1)} %collective-permute-done.20.refs_1_, ...), custom_call_target="tpu_custom_call" | custom-call | flops 1024 | bytes 1024 | tf_op jit(solution)/shard_map/pallas_call | solution.py:97
  154.9 5.0 shard_map.310
  171.8 8.7 %collective-permute-done.33 = bf16[2,128,1024]{2,1,0:T(8,128)(2,1)S(1)} collective-permute-done((bf16[2,128,1024]{2,1,0:T(8,128)(2,1)S(1)}, bf16[2,128,1024]{2,1,0:T(8,128)(2,1)S(1)}, u32[]{:S(2)}, u32[]{:S(2)}) %collective-permute-start.33) | collective-permute-done | bytes 524320 | tf_op jit(solution)/shard_map/ppermute | solution.py:62
  181.3 11.3 %shard_map.312 = (bf16[512,4096]{1,0:T(8,128)(2,1)S(1)}, bf16[512,4096]{1,0:T(8,128)(2,1)}) custom-call(bf16[512,1024]{1,0:T(8,128)(2,1)S(1)} %copy-done.27, bf16[1024,4096]{1,0:T(8,128)(2,1)} %bitcast.289, f32[1,4096]{1,0:T(1,128)S(1)} %get-tuple-element.888.refs_0_), custom_call_target="tpu_custom_call" | custom-call | flops 1024 | bytes 1024 | tf_op jit(solution)/shard_map/pallas_call | solution.py:606
  192.7 9.3 %collective-permute-done.30.refs_1_ = bf16[8,128,1024]{2,1,0:T(8,128)(2,1)S(1)} collective-permute-done((bf16[8,128,1024]{2,1,0:T(8,128)(2,1)S(1)}, bf16[8,128,1024]{2,1,0:T(8,128)(2,1)S(1)}, u32[]{:S(2)}, u32[]{:S(2)}) %collective-permute-start.30) | collective-permute-done | bytes 2097184 | tf_op jit(solution)/shard_map/ppermute | solution.py:62
  209.0 4.8 shard_map.313
  213.8 8.5 %shard_map.314.total_ref = f32[512,1024]{1,0:T(8,128)S(1)} custom-call(bf16[512,4096]{1,0:T(8,128)(2,1)} %copy-done.14, bf16[4096,1024]{1,0:T(8,128)(2,1)} %bitcast.281, f32[1,1024]{1,0:T(1,128)S(1)} %get-tuple-element.877.refs_0_, f32[512,1024]{1,0:T(8,128)S(1)} %copy-done.32), custom_call_target="tpu_custom_call" | custom-call | flops 1024 | bytes 1024 | tf_op jit(solution)/shard_map/pallas_call | solution.py:606
  224.1 7.2 %collective-permute-done.35.refs_1_ = bf16[8,128,1024]{2,1,0:T(8,128)(2,1)} collective-permute-done((bf16[8,128,1024]{2,1,0:T(8,128)(2,1)}, bf16[8,128,1024]{2,1,0:T(8,128)(2,1)}, u32[]{:S(2)}, u32[]{:S(2)}) %collective-permute-start.35) | collective-permute-done | bytes 2097184 | tf_op jit(solution)/shard_map/ppermute | solution.py:62
  237.8 7.2 %shard_map.315 = (bf16[4,2,2,2,32,3072]{5,4,3,2,1,0:T(8,128)(2,1)}, bf16[4,2,2,2,32,1024]{5,4,3,2,1,0:T(8,128)(2,1)}) custom-call(s32[4]{0:T(128)S(1)} %pad_add_fusion.coords_ref, bf16[8,128,1024]{2,1,0:T(8,128)(2,1)} %pad_maximum_fusion.2.refs_0_, bf16[8,128,1024]{2,1,0:T(8,128)(2,1)} %collective-permute-done.35.refs_1_, ...), custom_call_target="tpu_custom_call" | custom-call | flops 1024 | bytes 1024 | tf_op jit(solution)/shard_map/pallas_call | solution.py:97
  245.0 5.9 shard_map.316.q_ref.km_ref.vm_ref
  262.1 12.4 %shard_map.318 = (bf16[512,1024]{1,0:T(8,128)(2,1)S(1)}, f32[8,2,512]{2,1,0:T(2,128)S(1)}) custom-call(s32[1]{0:T(128)} %bitcast.s_ref, bf16[512,3072]{1,0:T(8,128)(2,1)S(1)} %shard_map.316.q_ref.km_ref.vm_ref, bf16[512,3072]{1,0:T(8,128)(2,1)S(1)} %shard_map.316.q_ref.km_ref.vm_ref, bf16[512,3072]{1,0:T(8,128)(2,1)} %copy-done.58, ...), custom_call_target="tpu_custom_call" | custom-call | flops 1024 | bytes 1024 | tf_op jit(solution)/shard_map/pallas_call | solution.py:497
  274.6 6.7 collective-permute-done.44.refs_1_
  284.1 5.1 shard_map.319
  290.6 6.8 collective-permute-done.46
  305.3 8.7 %shard_map.321 = bf16[4,2,2,2,32,4096]{5,4,3,2,1,0:T(8,128)(2,1)} custom-call(s32[4]{0:T(128)S(1)} %pad_add_fusion.coords_ref, bf16[8,128,1024]{2,1,0:T(8,128)(2,1)} %pad_maximum_fusion.3.refs_0_, bf16[8,128,1024]{2,1,0:T(8,128)(2,1)} %collective-permute-done.44.refs_1_, bf16[8,128,1024]{2,1,0:T(8,128)(2,1)} %collective-permute-done.45.refs_2_, ...), custom_call_target="tpu_custom_call" | custom-call | flops 1024 | bytes 1024 | tf_op jit(solution)/shard_map/pallas_call | solution.py:97
  314.0 10.9 %shard_map.322 = (bf16[512,4096]{1,0:T(8,128)(2,1)S(1)}, bf16[512,4096]{1,0:T(8,128)(2,1)}) custom-call(bf16[512,1024]{1,0:T(8,128)(2,1)S(1)} %copy-done.29, bf16[1024,4096]{1,0:T(8,128)(2,1)} %bitcast.283, f32[1,4096]{1,0:T(1,128)S(1)} %get-tuple-element.887.refs_0_), custom_call_target="tpu_custom_call" | custom-call | flops 1024 | bytes 1024 | tf_op jit(solution)/shard_map/pallas_call | solution.py:606
  329.3 4.8 shard_map.323
  336.0 8.5 %shard_map.324.total_ref = f32[512,1024]{1,0:T(8,128)S(1)} custom-call(bf16[512,4096]{1,0:T(8,128)(2,1)} %copy-done.6, bf16[4096,1024]{1,0:T(8,128)(2,1)} %bitcast.285, f32[1,1024]{1,0:T(1,128)S(1)} %get-tuple-element.869.refs_0_, f32[512,1024]{1,0:T(8,128)S(1)} %copy-done.35), custom_call_target="tpu_custom_call" | custom-call | flops 1024 | bytes 1024 | tf_op jit(solution)/shard_map/pallas_call | solution.py:606
  348.4 9.4 %shard_map.326 = (bf16[512,4096]{1,0:T(8,128)(2,1)}, f32[1,4096]{1,0:T(1,128)S(1)}) custom-call(bf16[512,1024]{1,0:T(8,128)(2,1)S(1)} %get-tuple-element.605.rows_ref.refs_4_, bf16[4096,1024]{1,0:T(8,128)(2,1)} %bitcast.286, bf16[512,4096]{1,0:T(8,128)(2,1)} %get-tuple-element.606.refs_0_), custom_call_target="tpu_custom_call" | custom-call | flops 1024 | bytes 1024 | tf_op jit(solution)/shard_map/pallas_call | solution.py:606
  365.0 11.1 %shard_map.327 = (bf16[1024,1024]{1,0:T(8,128)(2,1)S(1)}, bf16[1024,1024]{1,0:T(8,128)(2,1)}) custom-call(s32[32]{0:T(128)S(1)} %stack.442.order_ref, bf16[512,4096]{1,0:T(8,128)(2,1)} %copy-done.6, bf16[512,4096]{1,0:T(8,128)(2,1)} %copy-done.6, bf16[512,4096]{1,0:T(8,128)(2,1)} %copy-done.61, bf16[512,4096]{1,0:T(8,128)(2,1)} %copy-done.61, ...), custom_call_target="tpu_custom_call" | custom-call | flops 1024 | bytes 1024 | tf_op jit(solution)/shard_map/pallas_call | solution.py:309
  377.9 8.5 %shard_map.328.up_ref = f32[512,1024]{1,0:T(8,128)S(1)} custom-call(bf16[512,4096]{1,0:T(8,128)(2,1)} %get-tuple-element.624.rows_ref.refs_2_, bf16[1024,4096]{1,0:T(8,128)(2,1)} %bitcast.284, f32[512,1024]{1,0:T(8,128)S(1)} %copy-done.45), custom_call_target="tpu_custom_call" | custom-call | flops 1024 | bytes 1024 | tf_op jit(solution)/shard_map/pallas_call | solution.py:606
  392.1 8.4 %shard_map.331 = (bf16[256,4096]{1,0:T(8,128)(2,1)}, bf16[256,4096]{1,0:T(8,128)(2,1)S(1)}) custom-call(bf16[512,512]{1,0:T(8,128)(2,1)} %copy-done.55, bf16[512,512]{1,0:T(8,128)(2,1)} %copy-done.112, bf16[512,4096]{1,0:T(8,128)(2,1)} %get-tuple-element.624.rows_ref.refs_2_, bf16[512,4096]{1,0:T(8,128)(2,1)} %collective-permute-done.55.refs_3_), custom_call_target="tpu_custom_call" | custom-call | flops 1024 | bytes 1024 | tf_op jit(solution)/shard_map/pallas_call | solution.py:273
  404.1 20.9 %shard_map.332 = (bf16[512,1024]{1,0:T(8,128)(2,1)S(1)}, f32[2,512,1024]{2,1,0:T(8,128)}, bf16[2,512,1024]{2,1,0:T(8,128)(2,1)S(1)}) custom-call(s32[1]{0:T(128)} %bitcast.s_ref, bf16[512,3072]{1,0:T(8,128)(2,1)} %copy-done.3, bf16[512,3072]{1,0:T(8,128)(2,1)} %copy-done.3, bf16[512,3072]{1,0:T(8,128)(2,1)} %copy-done.58, bf16[512,3072]{1,0:T(8,128)(2,1)} %copy-done.3, ...), custom_call_target="tpu_custom_call" | custom-call | flops 1024 | bytes 1024 | tf_op jit(solution)/shard_map/pallas_call | solution.py:497
  429.2 5.3 add_convert_fusion.8
  440.4 7.1 %shard_map.334.up_ref = f32[512,1024]{1,0:T(8,128)S(1)} custom-call(bf16[512,3072]{1,0:T(8,128)(2,1)} %get-tuple-element.653.rows_ref.refs_2_, bf16[1024,3072]{1,0:T(8,128)(2,1)} %bitcast.292, f32[512,1024]{1,0:T(8,128)S(1)} %get-tuple-element.645.refs_0_), custom_call_target="tpu_custom_call" | custom-call | flops 1024 | bytes 1024 | tf_op jit(solution)/shard_map/pallas_call | solution.py:606
  450.0 9.2 %shard_map.335 = (bf16[256,4096]{1,0:T(8,128)(2,1)}, bf16[256,4096]{1,0:T(8,128)(2,1)}) custom-call(bf16[512,512]{1,0:T(8,128)(2,1)} %copy-done.53, bf16[512,512]{1,0:T(8,128)(2,1)} %collective-permute-done.42.refs_1_, bf16[512,3072]{1,0:T(8,128)(2,1)} %get-tuple-element.653.rows_ref.refs_2_, bf16[512,3072]{1,0:T(8,128)(2,1)} %collective-permute-done.62.refs_3_, ...), custom_call_target="tpu_custom_call" | custom-call | flops 1024 | bytes 1024 | tf_op jit(solution)/shard_map/pallas_call | solution.py:273
  467.9 9.8 %shard_map.337 = (bf16[512,4096]{1,0:T(8,128)(2,1)}, f32[1,4096]{1,0:T(1,128)S(1)}) custom-call(bf16[512,1024]{1,0:T(8,128)(2,1)S(1)} %get-tuple-element.667.rows_ref.b1, bf16[4096,1024]{1,0:T(8,128)(2,1)} %bitcast.282, bf16[512,4096]{1,0:T(8,128)(2,1)} %get-tuple-element.668.refs_0_), custom_call_target="tpu_custom_call" | custom-call | flops 1024 | bytes 1024 | tf_op jit(solution)/shard_map/pallas_call | solution.py:606
  477.8 4.0 collective-permute-done.64
  486.8 15.1 %shard_map.338 = (bf16[2,8,128,512]{3,2,1,0:T(8,128)(2,1)S(1)}, bf16[2,8,128,512]{3,2,1,0:T(8,128)(2,1)}) custom-call(s32[32]{0:T(128)S(1)} %stack.444.order_ref, s32[16]{0:T(128)S(1)} %select_reduce_fusion.place_ref, bf16[512,4096]{1,0:T(8,128)(2,1)} %copy-done.14, bf16[512,4096]{1,0:T(8,128)(2,1)} %collective-permute-done.43.a2, ...), custom_call_target="tpu_custom_call" | custom-call | flops 1024 | bytes 1024 | tf_op jit(solution)/shard_map/pallas_call | solution.py:346
  517.2 8.5 %shard_map.339.up_ref = f32[512,1024]{1,0:T(8,128)S(1)} custom-call(bf16[512,4096]{1,0:T(8,128)(2,1)} %get-tuple-element.701.rows_ref.refs_2_, bf16[1024,4096]{1,0:T(8,128)(2,1)} %bitcast.290, f32[512,1024]{1,0:T(8,128)S(1)} %copy-done.43), custom_call_target="tpu_custom_call" | custom-call | flops 1024 | bytes 1024 | tf_op jit(solution)/shard_map/pallas_call | solution.py:606
  532.1 7.5 %shard_map.342 = (bf16[256,4096]{1,0:T(8,128)(2,1)S(1)}, bf16[256,4096]{1,0:T(8,128)(2,1)S(1)}) custom-call(bf16[512,512]{1,0:T(8,128)(2,1)} %copy-done.52, bf16[512,512]{1,0:T(8,128)(2,1)} %copy-done.102, bf16[512,4096]{1,0:T(8,128)(2,1)} %get-tuple-element.701.rows_ref.refs_2_, bf16[512,4096]{1,0:T(8,128)(2,1)} %collective-permute-done.66.refs_3_), custom_call_target="tpu_custom_call" | custom-call | flops 1024 | bytes 1024 | tf_op jit(solution)/shard_map/pallas_call | solution.py:273
  553.5 20.9 %shard_map.343 = (bf16[512,1024]{1,0:T(8,128)(2,1)S(1)}, f32[2,512,1024]{2,1,0:T(8,128)}, bf16[2,512,1024]{2,1,0:T(8,128)(2,1)S(1)}) custom-call(s32[1]{0:T(128)} %bitcast.s_ref, bf16[512,3072]{1,0:T(8,128)(2,1)} %copy-done.2, bf16[512,3072]{1,0:T(8,128)(2,1)} %copy-done.2, bf16[512,3072]{1,0:T(8,128)(2,1)} %collective-permute-done.18.ko_ref.vo_ref, ...), custom_call_target="tpu_custom_call" | custom-call | flops 1024 | bytes 1024 | tf_op jit(solution)/shard_map/pallas_call | solution.py:497
  575.7 6.0 collective-permute-done.74
  596.2 9.1 %shard_map.345 = (bf16[256,4096]{1,0:T(8,128)(2,1)}, bf16[256,4096]{1,0:T(8,128)(2,1)}) custom-call(bf16[512,512]{1,0:T(8,128)(2,1)} %copy-done.50, bf16[512,512]{1,0:T(8,128)(2,1)} %copy-done.100, bf16[512,3072]{1,0:T(8,128)(2,1)} %copy-done.19, bf16[512,3072]{1,0:T(8,128)(2,1)} %copy-done.70, bf16[512,512]{1,0:T(8,128)(2,1)} %copy-done.51, ...), custom_call_target="tpu_custom_call" | custom-call | flops 1024 | bytes 1024 | tf_op jit(solution)/shard_map/pallas_call | solution.py:273
  611.9 7.2 %shard_map.346 = f32[512,1024]{1,0:T(8,128)S(1)} custom-call(bf16[512,3072]{1,0:T(8,128)(2,1)} %copy-done.19, bf16[1024,3072]{1,0:T(8,128)(2,1)} %bitcast.288, f32[512,1024]{1,0:T(8,128)S(1)} %copy-done.41), custom_call_target="tpu_custom_call" | custom-call | flops 1024 | bytes 1024 | tf_op jit(solution)/shard_map/pallas_call | solution.py:606
  619.1 13.5 %collective-permute-done.87 = bf16[64,128]{1,0:T(8,128)(2,1)S(1)} collective-permute-done((bf16[64,128]{1,0:T(8,128)(2,1)S(1)}, bf16[64,128]{1,0:T(8,128)(2,1)S(1)}, u32[]{:S(2)}, u32[]{:S(2)}) %collective-permute-start.87) | collective-permute-done | bytes 16416 | tf_op jit(solution)/shard_map/ppermute | solution.py:62
  644.1 7.4 %collective-permute-done.92 = bf16[32,128]{1,0:T(8,128)(2,1)S(1)} collective-permute-done((bf16[32,128]{1,0:T(8,128)(2,1)S(1)}, bf16[32,128]{1,0:T(8,128)(2,1)S(1)}, u32[]{:S(2)}, u32[]{:S(2)}) %collective-permute-start.92) | collective-permute-done | bytes 8224 | tf_op jit(solution)/shard_map/ppermute | solution.py:62
  659.3 12.6 %collective-permute-done.96 = bf16[16,128]{1,0:T(8,128)(2,1)S(1)} collective-permute-done((bf16[16,128]{1,0:T(8,128)(2,1)S(1)}, bf16[16,128]{1,0:T(8,128)(2,1)S(1)}, u32[]{:S(2)}, u32[]{:S(2)}) %collective-permute-start.96) | collective-permute-done | bytes 4128 | tf_op jit(solution)/shard_map/ppermute | solution.py:62
  678.0 6.7 collective-permute-done.97
  (641 shorter events, 273.9 us)
Async XLA Ops:
  30.3 20.3 %collective-permute-start.6 = (bf16[256,1024]{1,0:T(8,128)(2,1)}, bf16[256,1024]{1,0:T(8,128)(2,1)}, u32[]{:S(2)}, u32[]{:S(2)}) collective-permute-start(bf16[256,1024]{1,0:T(8,128)(2,1)} %get-tuple-element.424), channel_id=1, source_target_pairs={{0,2},{1,3},{2,0},{3,1},{4,6},{5,7},{6,4},{7,5},{8,10},{9,11},{10,... | collective-permute-start | bytes 1572872 | tf_op jit(solution)/shard_map/ppermute | solution.py:62
  66.0 20.5 %collective-permute-start.12 = (bf16[8,96,1024]{2,1,0:T(8,128)(2,1)S(1)}, bf16[8,96,1024]{2,1,0:T(8,128)(2,1)S(1)}, u32[]{:S(2)}, u32[]{:S(2)}) collective-permute-start(bf16[8,96,1024]{2,1,0:T(8,128)(2,1)S(1)} %pad_maximum_fusion.5.refs_0_), channel_id=1, source_target_pairs={{0,2},{1,5},{2,0},{3,7},{4,6},{5,1},{6,4},{7,3},{8,10},{9,13},{10,... | collective-permute-start | bytes 4718600 | tf_op jit(solution)/shard_map/ppermute | solution.py:62
  66.6 19.9 %collective-permute-start.13 = (bf16[8,96,1024]{2,1,0:T(8,128)(2,1)S(1)}, bf16[8,96,1024]{2,1,0:T(8,128)(2,1)}, u32[]{:S(2)}, u32[]{:S(2)}) collective-permute-start(bf16[8,96,1024]{2,1,0:T(8,128)(2,1)S(1)} %pad_maximum_fusion.5.refs_0_), channel_id=1, source_target_pairs={{0,1},{1,0},{2,3},{3,2},{4,5},{5,4},{6,7},{7,6},{8,9},{9,8},{10,11... | collective-permute-start | bytes 4718600 | tf_op jit(solution)/shard_map/ppermute | solution.py:62
  66.6 17.5 %collective-permute-start.14 = (bf16[2,160,1024]{2,1,0:T(8,128)(2,1)}, bf16[2,160,1024]{2,1,0:T(8,128)(2,1)}, u32[]{:S(2)}, u32[]{:S(2)}) collective-permute-start(bf16[2,160,1024]{2,1,0:T(8,128)(2,1)} %pad_maximum_fusion.14), channel_id=1, source_target_pairs={{0,8},{1,9},{2,10},{3,11},{4,12},{5,13},{6,14},{7,15},{8,0},{9,1},... | collective-permute-start | bytes 1966088 | tf_op jit(solution)/shard_map/ppermute | solution.py:62
  87.9 17.7 %collective-permute-start.16 = (bf16[4,160,1024]{2,1,0:T(8,128)(2,1)S(1)}, bf16[4,160,1024]{2,1,0:T(8,128)(2,1)S(1)}, u32[]{:S(2)}, u32[]{:S(2)}) collective-permute-start(bf16[4,160,1024]{2,1,0:T(8,128)(2,1)S(1)} %pad_maximum_fusion.6), channel_id=1, source_target_pairs={{0,4},{1,3},{2,6},{3,1},{4,0},{5,7},{6,2},{7,5},{8,12},{9,11},{10,... | collective-permute-start | bytes 3932168 | tf_op jit(solution)/shard_map/ppermute | solution.py:62
  108.8 31.8 %collective-permute-start.20 = (bf16[8,160,1024]{2,1,0:T(8,128)(2,1)S(1)}, bf16[8,160,1024]{2,1,0:T(8,128)(2,1)}, u32[]{:S(2)}, u32[]{:S(2)}) collective-permute-start(bf16[8,160,1024]{2,1,0:T(8,128)(2,1)S(1)} %pad_maximum_fusion.refs_0_), channel_id=1, source_target_pairs={{0,2},{1,5},{2,0},{3,7},{4,6},{5,1},{6,4},{7,3},{8,10},{9,13},{10,... | collective-permute-start | bytes 7864328 | tf_op jit(solution)/shard_map/ppermute | solution.py:62
  109.4 31.2 %collective-permute-start.21 = (bf16[8,160,1024]{2,1,0:T(8,128)(2,1)S(1)}, bf16[8,160,1024]{2,1,0:T(8,128)(2,1)}, u32[]{:S(2)}, u32[]{:S(2)}) collective-permute-start(bf16[8,160,1024]{2,1,0:T(8,128)(2,1)S(1)} %pad_maximum_fusion.refs_0_), channel_id=1, source_target_pairs={{0,1},{1,0},{2,3},{3,2},{4,5},{5,4},{6,7},{7,6},{8,9},{9,8},{10,11... | collective-permute-start | bytes 7864328 | tf_op jit(solution)/shard_map/ppermute | solution.py:62
  111.9 18.0 %collective-permute-start.19 = (bf16[512,512]{1,0:T(8,128)(2,1)S(1)}, bf16[512,512]{1,0:T(8,128)(2,1)S(1)}, u32[]{:S(2)}, u32[]{:S(2)}) collective-permute-start(bf16[512,512]{1,0:T(8,128)(2,1)S(1)} %get-tuple-element.472), channel_id=1, source_target_pairs={{0,1},{1,0},{2,3},{3,2},{4,5},{5,4},{6,7},{7,6},{8,9},{9,8},{10,11... | collective-permute-start | bytes 1572872 | tf_op jit(solution)/shard_map/ppermute | solution.py:62
  112.0 20.0 %collective-permute-start.22 = (bf16[2,128,1024]{2,1,0:T(8,128)(2,1)S(1)}, bf16[2,128,1024]{2,1,0:T(8,128)(2,1)S(1)}, u32[]{:S(2)}, u32[]{:S(2)}) collective-permute-start(bf16[2,128,1024]{2,1,0:T(8,128)(2,1)S(1)} %pad_maximum_fusion.15), channel_id=1, source_target_pairs={{0,8},{1,9},{2,10},{3,11},{4,12},{5,13},{6,14},{7,15},{8,0},{9,1},... | collective-permute-start | bytes 1572872 | tf_op jit(solution)/shard_map/ppermute | solution.py:62
  141.9 20.2 %collective-permute-start.25 = (bf16[4,128,1024]{2,1,0:T(8,128)(2,1)S(1)}, bf16[4,128,1024]{2,1,0:T(8,128)(2,1)S(1)}, u32[]{:S(2)}, u32[]{:S(2)}) collective-permute-start(bf16[4,128,1024]{2,1,0:T(8,128)(2,1)S(1)} %pad_maximum_fusion.7), channel_id=1, source_target_pairs={{0,4},{1,3},{2,6},{3,1},{4,0},{5,7},{6,2},{7,5},{8,12},{9,11},{10,... | collective-permute-start | bytes 3145736 | tf_op jit(solution)/shard_map/ppermute | solution.py:62
  143.4 18.6 %collective-permute-start.26 = (bf16[2,128,1024]{2,1,0:T(8,128)(2,1)S(1)}, bf16[2,128,1024]{2,1,0:T(8,128)(2,1)S(1)}, u32[]{:S(2)}, u32[]{:S(2)}) collective-permute-start(bf16[2,128,1024]{2,1,0:T(8,128)(2,1)S(1)} %pad_maximum_fusion.16), channel_id=1, source_target_pairs={{0,8},{1,9},{2,10},{3,11},{4,12},{5,13},{6,14},{7,15},{8,0},{9,1},... | collective-permute-start | bytes 1572872 | tf_op jit(solution)/shard_map/ppermute | solution.py:62
  164.7 37.3 %collective-permute-start.30 = (bf16[8,128,1024]{2,1,0:T(8,128)(2,1)S(1)}, bf16[8,128,1024]{2,1,0:T(8,128)(2,1)S(1)}, u32[]{:S(2)}, u32[]{:S(2)}) collective-permute-start(bf16[8,128,1024]{2,1,0:T(8,128)(2,1)S(1)} %pad_maximum_fusion.1.refs_0_), channel_id=1, source_target_pairs={{0,2},{1,5},{2,0},{3,7},{4,6},{5,1},{6,4},{7,3},{8,10},{9,13},{10,... | collective-permute-start | bytes 6291464 | tf_op jit(solution)/shard_map/ppermute | solution.py:62
  166.2 35.8 %collective-permute-start.31 = (bf16[8,128,1024]{2,1,0:T(8,128)(2,1)S(1)}, bf16[8,128,1024]{2,1,0:T(8,128)(2,1)S(1)}, u32[]{:S(2)}, u32[]{:S(2)}) collective-permute-start(bf16[8,128,1024]{2,1,0:T(8,128)(2,1)S(1)} %pad_maximum_fusion.1.refs_0_), channel_id=1, source_target_pairs={{0,1},{1,0},{2,3},{3,2},{4,5},{5,4},{6,7},{7,6},{8,9},{9,8},{10,11... | collective-permute-start | bytes 6291464 | tf_op jit(solution)/shard_map/ppermute | solution.py:62
  166.2 26.5 %collective-permute-start.32 = (bf16[4,128,1024]{2,1,0:T(8,128)(2,1)}, bf16[4,128,1024]{2,1,0:T(8,128)(2,1)}, u32[]{:S(2)}, u32[]{:S(2)}) collective-permute-start(bf16[4,128,1024]{2,1,0:T(8,128)(2,1)} %pad_maximum_fusion.8), channel_id=1, source_target_pairs={{0,4},{1,3},{2,6},{3,1},{4,0},{5,7},{6,2},{7,5},{8,12},{9,11},{10,... | collective-permute-start | bytes 3145736 | tf_op jit(solution)/shard_map/ppermute | solution.py:62
  171.8 20.8 %collective-permute-start.28 = (bf16[512,512]{1,0:T(8,128)(2,1)}, bf16[512,512]{1,0:T(8,128)(2,1)S(1)}, u32[]{:S(2)}, u32[]{:S(2)}) collective-permute-start(bf16[512,512]{1,0:T(8,128)(2,1)} %get-tuple-element.508), channel_id=1, source_target_pairs={{0,1},{1,0},{2,3},{3,2},{4,5},{5,4},{6,7},{7,6},{8,9},{9,8},{10,11... | collective-permute-start | bytes 1572872 | tf_op jit(solution)/shard_map/ppermute | solution.py:62
  204.9 26.4 %collective-permute-start.35 = (bf16[8,128,1024]{2,1,0:T(8,128)(2,1)}, bf16[8,128,1024]{2,1,0:T(8,128)(2,1)}, u32[]{:S(2)}, u32[]{:S(2)}) collective-permute-start(bf16[8,128,1024]{2,1,0:T(8,128)(2,1)} %pad_maximum_fusion.2.refs_0_), channel_id=1, source_target_pairs={{0,2},{1,5},{2,0},{3,7},{4,6},{5,1},{6,4},{7,3},{8,10},{9,13},{10,... | collective-permute-start | bytes 6291464 | tf_op jit(solution)/shard_map/ppermute | solution.py:62
  206.4 24.9 %collective-permute-start.36 = (bf16[8,128,1024]{2,1,0:T(8,128)(2,1)}, bf16[8,128,1024]{2,1,0:T(8,128)(2,1)}, u32[]{:S(2)}, u32[]{:S(2)}) collective-permute-start(bf16[8,128,1024]{2,1,0:T(8,128)(2,1)} %pad_maximum_fusion.2.refs_0_), channel_id=1, source_target_pairs={{0,1},{1,0},{2,3},{3,2},{4,5},{5,4},{6,7},{7,6},{8,9},{9,8},{10,11... | collective-permute-start | bytes 6291464 | tf_op jit(solution)/shard_map/ppermute | solution.py:62
  206.6 17.4 %collective-permute-start.37 = (bf16[1,128,1024]{2,1,0:T(8,128)(2,1)}, bf16[1,128,1024]{2,1,0:T(8,128)(2,1)S(1)}, u32[]{:S(2)}, u32[]{:S(2)}) collective-permute-start(bf16[1,128,1024]{2,1,0:T(8,128)(2,1)} %bitcast.100), channel_id=1, source_target_pairs={{0,16},{1,17},{2,18},{3,19},{4,20},{5,21},{6,22},{7,23},{8,24},{9,... | collective-permute-start | bytes 786440 | tf_op jit(solution)/shard_map/ppermute | solution.py:62
  233.4 17.5 %collective-permute-start.39 = (bf16[4,128,1024]{2,1,0:T(8,128)(2,1)}, bf16[4,128,1024]{2,1,0:T(8,128)(2,1)}, u32[]{:S(2)}, u32[]{:S(2)}) collective-permute-start(bf16[4,128,1024]{2,1,0:T(8,128)(2,1)} %pad_maximum_fusion.9), channel_id=1, source_target_pairs={{0,4},{1,3},{2,6},{3,1},{4,0},{5,7},{6,2},{7,5},{8,12},{9,11},{10,... | collective-permute-start | bytes 3145736 | tf_op jit(solution)/shard_map/ppermute | solution.py:62
  234.9 46.3 %collective-permute-start.43 = (bf16[512,4096]{1,0:T(8,128)(2,1)S(1)}, bf16[512,4096]{1,0:T(8,128)(2,1)}, u32[]{:S(2)}, u32[]{:S(2)}) collective-permute-start(bf16[512,4096]{1,0:T(8,128)(2,1)S(1)} %copy-done.15), channel_id=1, source_target_pairs={{0,1},{1,0},{2,3},{3,2},{4,5},{5,4},{6,7},{7,6},{8,9},{9,8},{10,11... | collective-permute-start | bytes 12582920 | tf_op jit(solution)/shard_map/ppermute | solution.py:62
  254.9 26.4 %collective-permute-start.44 = (bf16[8,128,1024]{2,1,0:T(8,128)(2,1)}, bf16[8,128,1024]{2,1,0:T(8,128)(2,1)}, u32[]{:S(2)}, u32[]{:S(2)}) collective-permute-start(bf16[8,128,1024]{2,1,0:T(8,128)(2,1)} %pad_maximum_fusion.3.refs_0_), channel_id=1, source_target_pairs={{0,2},{1,5},{2,0},{3,7},{4,6},{5,1},{6,4},{7,3},{8,10},{9,13},{10,... | collective-permute-start | bytes 6291464 | tf_op jit(solution)/shard_map/ppermute | solution.py:62
  256.4 24.9 %collective-permute-start.45 = (bf16[8,128,1024]{2,1,0:T(8,128)(2,1)}, bf16[8,128,1024]{2,1,0:T(8,128)(2,1)}, u32[]{:S(2)}, u32[]{:S(2)}) collective-permute-start(bf16[8,128,1024]{2,1,0:T(8,128)(2,1)} %pad_maximum_fusion.3.refs_0_), channel_id=1, source_target_pairs={{0,1},{1,0},{2,3},{3,2},{4,5},{5,4},{6,7},{7,6},{8,9},{9,8},{10,11... | collective-permute-start | bytes 6291464 | tf_op jit(solution)/shard_map/ppermute | solution.py:62
  284.1 21.2 %collective-permute-start.47 = (bf16[8,128,1024]{2,1,0:T(8,128)(2,1)}, bf16[8,128,1024]{2,1,0:T(8,128)(2,1)}, u32[]{:S(2)}, u32[]{:S(2)}) collective-permute-start(bf16[8,128,1024]{2,1,0:T(8,128)(2,1)} %collective-permute-done.44.refs_1_), channel_id=1, source_target_pairs={{0,1},{1,0},{2,3},{3,2},{4,5},{5,4},{6,7},{7,6},{8,9},{9,8},{10,11... | collective-permute-start | bytes 6291464 | tf_op jit(solution)/shard_map/ppermute | solution.py:62
  298.8 26.1 %collective-permute-start.50 = (bf16[8,128,1024]{2,1,0:T(8,128)(2,1)S(1)}, bf16[8,128,1024]{2,1,0:T(8,128)(2,1)S(1)}, u32[]{:S(2)}, u32[]{:S(2)}) collective-permute-start(bf16[8,128,1024]{2,1,0:T(8,128)(2,1)S(1)} %pad_maximum_fusion.4.refs_0_), channel_id=1, source_target_pairs={{0,2},{1,5},{2,0},{3,7},{4,6},{5,1},{6,4},{7,3},{8,10},{9,13},{10,... | collective-permute-start | bytes 6291464 | tf_op jit(solution)/shard_map/ppermute | solution.py:62
  300.4 24.6 %collective-permute-start.51 = (bf16[8,128,1024]{2,1,0:T(8,128)(2,1)S(1)}, bf16[8,128,1024]{2,1,0:T(8,128)(2,1)S(1)}, u32[]{:S(2)}, u32[]{:S(2)}) collective-permute-start(bf16[8,128,1024]{2,1,0:T(8,128)(2,1)S(1)} %pad_maximum_fusion.4.refs_0_), channel_id=1, source_target_pairs={{0,1},{1,0},{2,3},{3,2},{4,5},{5,4},{6,7},{7,6},{8,9},{9,8},{10,11... | collective-permute-start | bytes 6291464 | tf_op jit(solution)/shard_map/ppermute | solution.py:62
  304.8 20.1 %collective-permute-start.48 = (bf16[512,512]{1,0:T(8,128)(2,1)S(1)}, bf16[512,512]{1,0:T(8,128)(2,1)S(1)}, u32[]{:S(2)}, u32[]{:S(2)}) collective-permute-start(bf16[512,512]{1,0:T(8,128)(2,1)S(1)} %get-tuple-element.581), channel_id=1, source_target_pairs={{0,1},{1,0},{2,3},{3,2},{4,5},{5,4},{6,7},{7,6},{8,9},{9,8},{10,11... | collective-permute-start | bytes 1572872 | tf_op jit(solution)/shard_map/ppermute | solution.py:62
  305.3 19.6 %collective-permute-start.49 = (bf16[512,512]{1,0:T(8,128)(2,1)S(1)}, bf16[512,512]{1,0:T(8,128)(2,1)S(1)}, u32[]{:S(2)}, u32[]{:S(2)}) collective-permute-start(bf16[512,512]{1,0:T(8,128)(2,1)S(1)} %get-tuple-element.583), channel_id=1, source_target_pairs={{0,1},{1,0},{2,3},{3,2},{4,5},{5,4},{6,7},{7,6},{8,9},{9,8},{10,11... | collective-permute-start | bytes 1572872 | tf_op jit(solution)/shard_map/ppermute | solution.py:62
  358.7 18.0 %collective-permute-start.55 = (bf16[512,4096]{1,0:T(8,128)(2,1)}, bf16[512,4096]{1,0:T(8,128)(2,1)}, u32[]{:S(2)}, u32[]{:S(2)}) collective-permute-start(bf16[512,4096]{1,0:T(8,128)(2,1)} %get-tuple-element.624.rows_ref.refs_2_), channel_id=1, source_target_pairs={{0,1},{1,0},{2,3},{3,2},{4,5},{5,4},{6,7},{7,6},{8,9},{9,8},{10,11... | collective-permute-start | bytes 12582920 | tf_op jit(solution)/shard_map/ppermute | solution.py:62
  376.7 26.2 %collective-permute-start.57 = (bf16[1024,1024]{1,0:T(8,128)(2,1)S(1)}, bf16[1024,1024]{1,0:T(8,128)(2,1)}, u32[]{:S(2)}, u32[]{:S(2)}) collective-permute-start(bf16[1024,1024]{1,0:T(8,128)(2,1)S(1)} %get-tuple-element.628), channel_id=1, source_target_pairs={{0,2},{1,5},{2,0},{3,7},{4,6},{5,1},{6,4},{7,3},{8,10},{9,13},{10,... | collective-permute-start | bytes 6291464 | tf_op jit(solution)/shard_map/ppermute | solution.py:62
  402.9 26.2 %collective-permute-start.58 = (bf16[256,4096]{1,0:T(8,128)(2,1)}, bf16[256,4096]{1,0:T(8,128)(2,1)S(1)}, u32[]{:S(2)}, u32[]{:S(2)}) collective-permute-start(bf16[256,4096]{1,0:T(8,128)(2,1)} %get-tuple-element.635), channel_id=1, source_target_pairs={{0,2},{1,5},{2,0},{3,7},{4,6},{5,1},{6,4},{7,3},{8,10},{9,13},{10,... | collective-permute-start | bytes 6291464 | tf_op jit(solution)/shard_map/ppermute | solution.py:62
  439.2 20.0 %collective-permute-start.61 = (bf16[512,1024]{1,0:T(8,128)(2,1)}, bf16[512,1024]{1,0:T(8,128)(2,1)}, u32[]{:S(2)}, u32[]{:S(2)}) collective-permute-start(bf16[512,1024]{1,0:T(8,128)(2,1)} %get-tuple-element.649), channel_id=1, source_target_pairs={{0,4},{1,3},{2,6},{3,1},{4,0},{5,7},{6,2},{7,5},{8,12},{9,11},{10,... | collective-permute-start | bytes 3145736 | tf_op jit(solution)/shard_map/ppermute | solution.py:62
  483.8 26.4 %collective-permute-start.66 = (bf16[512,4096]{1,0:T(8,128)(2,1)}, bf16[512,4096]{1,0:T(8,128)(2,1)}, u32[]{:S(2)}, u32[]{:S(2)}) collective-permute-start(bf16[512,4096]{1,0:T(8,128)(2,1)} %get-tuple-element.701.rows_ref.refs_2_), channel_id=1, source_target_pairs={{0,1},{1,0},{2,3},{3,2},{4,5},{5,4},{6,7},{7,6},{8,9},{9,8},{10,11... | collective-permute-start | bytes 12582920 | tf_op jit(solution)/shard_map/ppermute | solution.py:62
  483.8 26.4 %collective-permute-start.67 = (bf16[256,4096]{1,0:T(8,128)(2,1)}, bf16[256,4096]{1,0:T(8,128)(2,1)}, u32[]{:S(2)}, u32[]{:S(2)}) collective-permute-start(bf16[256,4096]{1,0:T(8,128)(2,1)} %get-tuple-element.684), channel_id=1, source_target_pairs={{0,2},{1,5},{2,0},{3,7},{4,6},{5,1},{6,4},{7,3},{8,10},{9,13},{10,... | collective-permute-start | bytes 6291464 | tf_op jit(solution)/shard_map/ppermute | solution.py:62
  485.1 20.0 %collective-permute-start.69 = (bf16[128,1024]{1,0:T(8,128)(2,1)}, bf16[128,1024]{1,0:T(8,128)(2,1)S(1)}, u32[]{:S(2)}, u32[]{:S(2)}) collective-permute-start(bf16[128,1024]{1,0:T(8,128)(2,1)} %add_convert_fusion.32), channel_id=1, source_target_pairs={{0,16},{1,17},{2,18},{3,19},{4,20},{5,21},{6,22},{7,23},{8,24},{9,... | collective-permute-start | bytes 786440 | tf_op jit(solution)/shard_map/ppermute | solution.py:62
  486.6 19.7 %collective-permute-start.68 = (bf16[64,4096]{1,0:T(8,128)(2,1)}, bf16[64,4096]{1,0:T(8,128)(2,1)S(1)}, u32[]{:S(2)}, u32[]{:S(2)}) collective-permute-start(bf16[64,4096]{1,0:T(8,128)(2,1)} %get-tuple-element.685), channel_id=1, source_target_pairs={{0,8},{1,9},{2,10},{3,11},{4,12},{5,13},{6,14},{7,15},{8,0},{9,1},... | collective-permute-start | bytes 1572872 | tf_op jit(solution)/shard_map/ppermute | solution.py:62
  513.7 30.7 %collective-permute-start.70 = (bf16[1024,512]{1,0:T(8,128)(2,1)}, bf16[1024,512]{1,0:T(8,128)(2,1)}, u32[]{:S(2)}, u32[]{:S(2)}) collective-permute-start(bf16[1024,512]{1,0:T(8,128)(2,1)} %bitcast.154), channel_id=1, source_target_pairs={{0,8},{1,9},{2,10},{3,11},{4,12},{5,13},{6,14},{7,15},{8,0},{9,1},... | collective-permute-start | bytes 3145736 | tf_op jit(solution)/shard_map/ppermute | solution.py:62
  514.1 30.4 %collective-permute-start.71 = (bf16[1024,512]{1,0:T(8,128)(2,1)}, bf16[1024,512]{1,0:T(8,128)(2,1)}, u32[]{:S(2)}, u32[]{:S(2)}) collective-permute-start(bf16[1024,512]{1,0:T(8,128)(2,1)} %bitcast.156), channel_id=1, source_target_pairs={{0,2},{1,5},{2,0},{3,7},{4,6},{5,1},{6,4},{7,3},{8,10},{9,13},{10,... | collective-permute-start | bytes 3145736 | tf_op jit(solution)/shard_map/ppermute | solution.py:62
  514.9 29.6 %collective-permute-start.72 = (bf16[128,4096]{1,0:T(8,128)(2,1)}, bf16[128,4096]{1,0:T(8,128)(2,1)S(1)}, u32[]{:S(2)}, u32[]{:S(2)}) collective-permute-start(bf16[128,4096]{1,0:T(8,128)(2,1)} %get-tuple-element.707), channel_id=1, source_target_pairs={{0,4},{1,3},{2,6},{3,1},{4,0},{5,7},{6,2},{7,5},{8,12},{9,11},{10,... | collective-permute-start | bytes 3145736 | tf_op jit(solution)/shard_map/ppermute | solution.py:62
  515.8 26.3 %collective-permute-start.73 = (bf16[32,4096]{1,0:T(8,128)(2,1)S(1)}, bf16[32,4096]{1,0:T(8,128)(2,1)S(1)}, u32[]{:S(2)}, u32[]{:S(2)}) collective-permute-start(bf16[32,4096]{1,0:T(8,128)(2,1)S(1)} %add_convert_fusion.31), channel_id=1, source_target_pairs={{0,16},{1,17},{2,18},{3,19},{4,20},{5,21},{6,22},{7,23},{8,24},{9,... | collective-permute-start | bytes 786440 | tf_op jit(solution)/shard_map/ppermute | solution.py:62
  550.1 31.6 %collective-permute-start.74 = (bf16[256,4096]{1,0:T(8,128)(2,1)S(1)}, bf16[256,4096]{1,0:T(8,128)(2,1)}, u32[]{:S(2)}, u32[]{:S(2)}) collective-permute-start(bf16[256,4096]{1,0:T(8,128)(2,1)S(1)} %get-tuple-element.719), channel_id=1, source_target_pairs={{0,2},{1,5},{2,0},{3,7},{4,6},{5,1},{6,4},{7,3},{8,10},{9,13},{10,... | collective-permute-start | bytes 6291464 | tf_op jit(solution)/shard_map/ppermute | solution.py:62
  550.8 24.8 %collective-permute-start.75 = (bf16[512,512]{1,0:T(8,128)(2,1)}, bf16[512,512]{1,0:T(8,128)(2,1)S(1)}, u32[]{:S(2)}, u32[]{:S(2)}) collective-permute-start(bf16[512,512]{1,0:T(8,128)(2,1)} %get-tuple-element.720), channel_id=1, source_target_pairs={{0,16},{1,17},{2,18},{3,19},{4,20},{5,21},{6,22},{7,23},{8,24},{9,... | collective-permute-start | bytes 1572872 | tf_op jit(solution)/shard_map/ppermute | solution.py:62
  552.0 23.6 %collective-permute-start.76 = (bf16[512,512]{1,0:T(8,128)(2,1)}, bf16[512,512]{1,0:T(8,128)(2,1)S(1)}, u32[]{:S(2)}, u32[]{:S(2)}) collective-permute-start(bf16[512,512]{1,0:T(8,128)(2,1)} %get-tuple-element.721), channel_id=1, source_target_pairs={{0,4},{1,3},{2,6},{3,1},{4,0},{5,7},{6,2},{7,5},{8,12},{9,11},{10,... | collective-permute-start | bytes 1572872 | tf_op jit(solution)/shard_map/ppermute | solution.py:62
  553.0 22.7 %collective-permute-start.77 = (bf16[64,4096]{1,0:T(8,128)(2,1)}, bf16[64,4096]{1,0:T(8,128)(2,1)S(1)}, u32[]{:S(2)}, u32[]{:S(2)}) collective-permute-start(bf16[64,4096]{1,0:T(8,128)(2,1)} %get-tuple-element.722), channel_id=1, source_target_pairs={{0,8},{1,9},{2,10},{3,11},{4,12},{5,13},{6,14},{7,15},{8,0},{9,1},... | collective-permute-start | bytes 1572872 | tf_op jit(solution)/shard_map/ppermute | solution.py:62
  553.5 35.2 %collective-permute-start.79 = (bf16[512,1024]{1,0:T(8,128)(2,1)S(1)}, bf16[512,1024]{1,0:T(8,128)(2,1)S(1)}, u32[]{:S(2)}, u32[]{:S(2)}) collective-permute-start(bf16[512,1024]{1,0:T(8,128)(2,1)S(1)} %get-tuple-element.697.rows_ref.refs_6_), channel_id=1, source_target_pairs={{0,1},{1,0},{2,3},{3,2},{4,5},{5,4},{6,7},{7,6},{8,9},{9,8},{10,11... | collective-permute-start | bytes 3145736 | tf_op jit(solution)/shard_map/ppermute | solution.py:62
  588.8 17.4 %collective-permute-start.81 = (bf16[128,4096]{1,0:T(8,128)(2,1)S(1)}, bf16[128,4096]{1,0:T(8,128)(2,1)S(1)}, u32[]{:S(2)}, u32[]{:S(2)}) collective-permute-start(bf16[128,4096]{1,0:T(8,128)(2,1)S(1)} %get-tuple-element.743), channel_id=1, source_target_pairs={{0,4},{1,3},{2,6},{3,1},{4,0},{5,7},{6,2},{7,5},{8,12},{9,11},{10,... | collective-permute-start | bytes 3145736 | tf_op jit(solution)/shard_map/ppermute | solution.py:62
  606.2 26.4 %collective-permute-start.85 = (bf16[256,4096]{1,0:T(8,128)(2,1)}, bf16[256,4096]{1,0:T(8,128)(2,1)}, u32[]{:S(2)}, u32[]{:S(2)}) collective-permute-start(bf16[256,4096]{1,0:T(8,128)(2,1)} %get-tuple-element.753), channel_id=1, source_target_pairs={{0,2},{1,5},{2,0},{3,7},{4,6},{5,1},{6,4},{7,3},{8,10},{9,13},{10,... | collective-permute-start | bytes 6291464 | tf_op jit(solution)/shard_map/ppermute | solution.py:62
  609.3 23.4 %collective-permute-start.87 = (bf16[64,128]{1,0:T(8,128)(2,1)S(1)}, bf16[64,128]{1,0:T(8,128)(2,1)S(1)}, u32[]{:S(2)}, u32[]{:S(2)}) collective-permute-start(bf16[64,128]{1,0:T(8,128)(2,1)S(1)} %get-tuple-element.763), channel_id=1, source_target_pairs={{0,2},{1,5},{2,0},{3,7},{4,6},{5,1},{6,4},{7,3},{8,10},{9,13},{10,... | collective-permute-start | bytes 49160 | tf_op jit(solution)/shard_map/ppermute | solution.py:62
  653.2 18.7 %collective-permute-start.93 = (bf16[256,1024]{1,0:T(8,128)(2,1)S(1)}, bf16[256,1024]{1,0:T(8,128)(2,1)S(1)}, u32[]{:S(2)}, u32[]{:S(2)}) collective-permute-start(bf16[256,1024]{1,0:T(8,128)(2,1)S(1)} %slice.1021), channel_id=1, source_target_pairs={{0,2},{1,3},{2,0},{3,1},{4,6},{5,7},{6,4},{7,5},{8,10},{9,11},{10,... | collective-permute-start | bytes 1572872 | tf_op jit(solution)/shard_map/ppermute | solution.py:62
  (186 other events, 1861.6 us)

commit v8 on v7

--- a/solution.py
+++ b/solution.py
@@ -941,7 +941,7 @@
                 (second_grad, inner_low, inner_got, output_got), *o_sums
             )
         (first_grad,) = product(
-            inner_low, w_inner, 256, lambda total, g: (g + total,), (f32,), (), (second_grad,), transposed=True
+            inner_low, w_inner, 512, lambda total, g: (g + total,), (f32,), (), (second_grad,), transposed=True
         )
         first_sum_grad, branch_low, first_sums = norm_backward_rows(first_sum, gain1, first_grad)
         branch_got = send(branch_low, TO_CORE)
@@ -964,7 +964,7 @@
         low_got = send(low, TO_CORE)
         if layer:
             (upstream,) = product(
-                low, w_three, 256, lambda total, g: (g + total,), (f32,), (), (first_sum_grad,), transposed=True
+                low, w_three, 512, lambda total, g: (g + total,), (f32,), (), (first_sum_grad,), transposed=True
             )
             mix_pair = (left_mix, (branch_low, branch_got), D)
             a_sum = SumUnit(weight_terms((left_stream, tie((low, low_got), upstream), 3 * D), mix_pair))
@@ -973,7 +973,7 @@
             a_sum = SumUnit(weight_terms((left_stream, (low, low_got), 3 * D), mix_pair))
             low, low_sums = phase((low, low_sums), a_sum, settle=[i_sum, *o_sums, before.a] if before else [i_sum])
             (upstream,) = product(
-                low, w_three, 256, lambda total, g: (g + total,), (f32,), (), (first_sum_grad,), transposed=True
+                low, w_three, 512, lambda total, g: (g + total,), (f32,), (), (first_sum_grad,), transposed=True
             )
         small_grads[layer] = jnp.stack(
             [

time: 694 us -> 694 us (level)
  transfers between devices with their start and end apart: 99 -> 99, of which waited for: 45 -> 47; matrix products, arithmetic and copies ran while one was open for 8% -> 8% of each run, Pallas kernels for 44% -> 43%
where the time goes in v8:
time: 694 us; the launch traced here: 687 us
  Pallas kernels  307 us (44%)
  waiting for transfers between devices  182 us (26%)
  starting transfers between devices  75.5 us (11%)
  other arithmetic  67 us (10%)
  local copies, waits for them, and re-layouts  52.4 us (8%)
    ppermute x99, waiting for transfers between devices, send(): return lax.ppermute(value, AXES, to)  182 us
    pallas_call x14, Pallas kernels, product(): pl.pallas_call(kernel, grid=(width // tile,), in_specs=[pl.BlockSpec((tok...  106 us
    ppermute x99, starting transfers between devices, send(): return lax.ppermute(value, AXES, to)  75.5 us
    pallas_call x4, Pallas kernels, call_attention(): pl.pallas_call(kernel, grid=(pairs_count,), in_specs=in_specs, out_specs=...  66.8 us
    pallas_call x6, Pallas kernels, place(): pl.pallas_call(kernel, in_specs=[pl.BlockSpec(memory_space=pltpu.SMEM)] +...  39.1 us
    pallas_call x4, Pallas kernels, weight_terms(): pl.pallas_call(kernel, grid=(columns // tile,), in_specs=in_specs, out_sp...  34.2 us
    convert_element_type x16, other arithmetic, local(): self.kept = self.kept.astype(bf16)  26.2 us
    unnamed x282, local copies, waits for them, and re-layouts  25 us
  transfers between devices with their start and end apart: 99, of which 47 were waited for; matrix products, arithmetic and copies ran while one was open for 8% of the time, Pallas kernels for 43%

profile of v8, /device:TPU:0, one launch (start us, length us, event | category | flops | bytes accessed | tf_op | source)
XLA Modules:
  0.0 687.4 jit_solution(11055204765817616007)
XLA Ops:
  21.3 4.2 collective-permute-done.4
  25.5 4.7 collective-permute-done
  40.9 7.2 %collective-permute-done.8 = bf16[1,160,1024]{2,1,0:T(8,128)(2,1)S(1)} collective-permute-done((bf16[1,160,1024]{2,1,0:T(8,128)(2,1)S(1)}, bf16[1,160,1024]{2,1,0:T(8,128)(2,1)S(1)}, u32[]{:S(2)}, u32[]{:S(2)}) %collective-permute-start.8) | collective-permute-done | bytes 327712 | tf_op jit(solution)/shard_map/ppermute | solution.py:62
  56.8 6.0 collective-permute-done.10
  76.5 7.6 %collective-permute-done.14 = bf16[2,160,1024]{2,1,0:T(8,128)(2,1)} collective-permute-done((bf16[2,160,1024]{2,1,0:T(8,128)(2,1)}, bf16[2,160,1024]{2,1,0:T(8,128)(2,1)}, u32[]{:S(2)}, u32[]{:S(2)}) %collective-permute-start.14) | collective-permute-done | bytes 655392 | tf_op jit(solution)/shard_map/ppermute | solution.py:62
  91.3 5.7 shard_map.305
  97.0 5.9 shard_map.306.q_ref.km_ref.vm_ref
  114.7 12.4 %shard_map.308 = (bf16[512,1024]{1,0:T(8,128)(2,1)S(1)}, f32[8,2,512]{2,1,0:T(2,128)S(1)}) custom-call(s32[1]{0:T(128)} %bitcast.s_ref, bf16[512,3072]{1,0:T(8,128)(2,1)S(1)} %shard_map.306.q_ref.km_ref.vm_ref, bf16[512,3072]{1,0:T(8,128)(2,1)S(1)} %shard_map.306.q_ref.km_ref.vm_ref, bf16[512,3072]{1,0:T(8,128)(2,1)} %collective-permute-done.18.ko_ref.vo_ref, ...), custom_call_target="tpu_custom_call" | custom-call | flops 1024 | bytes 1024 | tf_op jit(solution)/shard_map/pallas_call | solution.py:497
  131.9 8.7 %collective-permute-done.20.refs_1_ = bf16[8,160,1024]{2,1,0:T(8,128)(2,1)} collective-permute-done((bf16[8,160,1024]{2,1,0:T(8,128)(2,1)S(1)}, bf16[8,160,1024]{2,1,0:T(8,128)(2,1)}, u32[]{:S(2)}, u32[]{:S(2)}) %collective-permute-start.20) | collective-permute-done | bytes 2621472 | tf_op jit(solution)/shard_map/ppermute | solution.py:62
  147.0 7.9 %shard_map.309 = (bf16[4,2,2,2,32,4096]{5,4,3,2,1,0:T(8,128)(2,1)}, bf16[4,2,2,2,32,1024]{5,4,3,2,1,0:T(8,128)(2,1)}) custom-call(s32[4]{0:T(128)S(1)} %pad_add_fusion.coords_ref, bf16[8,160,1024]{2,1,0:T(8,128)(2,1)S(1)} %pad_maximum_fusion.refs_0_, bf16[8,160,1024]{2,1,0:T(8,128)(2,1)} %collective-permute-done.20.refs_1_, ...), custom_call_target="tpu_custom_call" | custom-call | flops 1024 | bytes 1024 | tf_op jit(solution)/shard_map/pallas_call | solution.py:97
  154.9 5.0 shard_map.310
  171.8 8.7 %collective-permute-done.33 = bf16[2,128,1024]{2,1,0:T(8,128)(2,1)S(1)} collective-permute-done((bf16[2,128,1024]{2,1,0:T(8,128)(2,1)S(1)}, bf16[2,128,1024]{2,1,0:T(8,128)(2,1)S(1)}, u32[]{:S(2)}, u32[]{:S(2)}) %collective-permute-start.33) | collective-permute-done | bytes 524320 | tf_op jit(solution)/shard_map/ppermute | solution.py:62
  181.3 11.0 %shard_map.312 = (bf16[512,4096]{1,0:T(8,128)(2,1)S(1)}, bf16[512,4096]{1,0:T(8,128)(2,1)}) custom-call(bf16[512,1024]{1,0:T(8,128)(2,1)S(1)} %copy-done.27, bf16[1024,4096]{1,0:T(8,128)(2,1)} %bitcast.289, f32[1,4096]{1,0:T(1,128)S(1)} %get-tuple-element.888.refs_0_), custom_call_target="tpu_custom_call" | custom-call | flops 1024 | bytes 1024 | tf_op jit(solution)/shard_map/pallas_call | solution.py:606
  192.6 9.4 %collective-permute-done.30.refs_1_ = bf16[8,128,1024]{2,1,0:T(8,128)(2,1)S(1)} collective-permute-done((bf16[8,128,1024]{2,1,0:T(8,128)(2,1)S(1)}, bf16[8,128,1024]{2,1,0:T(8,128)(2,1)S(1)}, u32[]{:S(2)}, u32[]{:S(2)}) %collective-permute-start.30) | collective-permute-done | bytes 2097184 | tf_op jit(solution)/shard_map/ppermute | solution.py:62
  209.0 4.8 shard_map.313
  213.8 8.5 %shard_map.314.total_ref = f32[512,1024]{1,0:T(8,128)S(1)} custom-call(bf16[512,4096]{1,0:T(8,128)(2,1)} %copy-done.14, bf16[4096,1024]{1,0:T(8,128)(2,1)} %bitcast.281, f32[1,1024]{1,0:T(1,128)S(1)} %get-tuple-element.877.refs_0_, f32[512,1024]{1,0:T(8,128)S(1)} %copy-done.32), custom_call_target="tpu_custom_call" | custom-call | flops 1024 | bytes 1024 | tf_op jit(solution)/shard_map/pallas_call | solution.py:606
  224.1 7.2 %collective-permute-done.35.refs_1_ = bf16[8,128,1024]{2,1,0:T(8,128)(2,1)} collective-permute-done((bf16[8,128,1024]{2,1,0:T(8,128)(2,1)}, bf16[8,128,1024]{2,1,0:T(8,128)(2,1)}, u32[]{:S(2)}, u32[]{:S(2)}) %collective-permute-start.35) | collective-permute-done | bytes 2097184 | tf_op jit(solution)/shard_map/ppermute | solution.py:62
  237.8 7.2 %shard_map.315 = (bf16[4,2,2,2,32,3072]{5,4,3,2,1,0:T(8,128)(2,1)}, bf16[4,2,2,2,32,1024]{5,4,3,2,1,0:T(8,128)(2,1)}) custom-call(s32[4]{0:T(128)S(1)} %pad_add_fusion.coords_ref, bf16[8,128,1024]{2,1,0:T(8,128)(2,1)} %pad_maximum_fusion.2.refs_0_, bf16[8,128,1024]{2,1,0:T(8,128)(2,1)} %collective-permute-done.35.refs_1_, ...), custom_call_target="tpu_custom_call" | custom-call | flops 1024 | bytes 1024 | tf_op jit(solution)/shard_map/pallas_call | solution.py:97
  245.0 5.9 shard_map.316.q_ref.km_ref.vm_ref
  262.1 12.4 %shard_map.318 = (bf16[512,1024]{1,0:T(8,128)(2,1)S(1)}, f32[8,2,512]{2,1,0:T(2,128)S(1)}) custom-call(s32[1]{0:T(128)} %bitcast.s_ref, bf16[512,3072]{1,0:T(8,128)(2,1)S(1)} %shard_map.316.q_ref.km_ref.vm_ref, bf16[512,3072]{1,0:T(8,128)(2,1)S(1)} %shard_map.316.q_ref.km_ref.vm_ref, bf16[512,3072]{1,0:T(8,128)(2,1)} %copy-done.58, ...), custom_call_target="tpu_custom_call" | custom-call | flops 1024 | bytes 1024 | tf_op jit(solution)/shard_map/pallas_call | solution.py:497
  274.6 6.7 collective-permute-done.44.refs_1_
  284.1 5.3 shard_map.319
  290.8 6.6 collective-permute-done.46
  305.3 8.7 %shard_map.321 = bf16[4,2,2,2,32,4096]{5,4,3,2,1,0:T(8,128)(2,1)} custom-call(s32[4]{0:T(128)S(1)} %pad_add_fusion.coords_ref, bf16[8,128,1024]{2,1,0:T(8,128)(2,1)} %pad_maximum_fusion.3.refs_0_, bf16[8,128,1024]{2,1,0:T(8,128)(2,1)} %collective-permute-done.44.refs_1_, bf16[8,128,1024]{2,1,0:T(8,128)(2,1)} %collective-permute-done.45.refs_2_, ...), custom_call_target="tpu_custom_call" | custom-call | flops 1024 | bytes 1024 | tf_op jit(solution)/shard_map/pallas_call | solution.py:97
  314.0 10.9 %shard_map.322 = (bf16[512,4096]{1,0:T(8,128)(2,1)S(1)}, bf16[512,4096]{1,0:T(8,128)(2,1)}) custom-call(bf16[512,1024]{1,0:T(8,128)(2,1)S(1)} %copy-done.29, bf16[1024,4096]{1,0:T(8,128)(2,1)} %bitcast.283, f32[1,4096]{1,0:T(1,128)S(1)} %get-tuple-element.887.refs_0_), custom_call_target="tpu_custom_call" | custom-call | flops 1024 | bytes 1024 | tf_op jit(solution)/shard_map/pallas_call | solution.py:606
  329.3 4.8 shard_map.323
  336.0 8.5 %shard_map.324.total_ref = f32[512,1024]{1,0:T(8,128)S(1)} custom-call(bf16[512,4096]{1,0:T(8,128)(2,1)} %copy-done.6, bf16[4096,1024]{1,0:T(8,128)(2,1)} %bitcast.285, f32[1,1024]{1,0:T(1,128)S(1)} %get-tuple-element.869.refs_0_, f32[512,1024]{1,0:T(8,128)S(1)} %copy-done.35), custom_call_target="tpu_custom_call" | custom-call | flops 1024 | bytes 1024 | tf_op jit(solution)/shard_map/pallas_call | solution.py:606
  348.4 9.4 %shard_map.326 = (bf16[512,4096]{1,0:T(8,128)(2,1)}, f32[1,4096]{1,0:T(1,128)S(1)}) custom-call(bf16[512,1024]{1,0:T(8,128)(2,1)S(1)} %get-tuple-element.605.rows_ref.refs_4_, bf16[4096,1024]{1,0:T(8,128)(2,1)} %bitcast.286, bf16[512,4096]{1,0:T(8,128)(2,1)} %get-tuple-element.606.refs_0_), custom_call_target="tpu_custom_call" | custom-call | flops 1024 | bytes 1024 | tf_op jit(solution)/shard_map/pallas_call | solution.py:606
  365.0 11.1 %shard_map.327 = (bf16[1024,1024]{1,0:T(8,128)(2,1)S(1)}, bf16[1024,1024]{1,0:T(8,128)(2,1)}) custom-call(s32[32]{0:T(128)S(1)} %stack.442.order_ref, bf16[512,4096]{1,0:T(8,128)(2,1)} %copy-done.6, bf16[512,4096]{1,0:T(8,128)(2,1)} %copy-done.6, bf16[512,4096]{1,0:T(8,128)(2,1)} %copy-done.61, bf16[512,4096]{1,0:T(8,128)(2,1)} %copy-done.61, ...), custom_call_target="tpu_custom_call" | custom-call | flops 1024 | bytes 1024 | tf_op jit(solution)/shard_map/pallas_call | solution.py:309
  377.9 8.5 %shard_map.328.up_ref = f32[512,1024]{1,0:T(8,128)S(1)} custom-call(bf16[512,4096]{1,0:T(8,128)(2,1)} %get-tuple-element.624.rows_ref.refs_2_, bf16[1024,4096]{1,0:T(8,128)(2,1)} %bitcast.284, f32[512,1024]{1,0:T(8,128)S(1)} %copy-done.45), custom_call_target="tpu_custom_call" | custom-call | flops 1024 | bytes 1024 | tf_op jit(solution)/shard_map/pallas_call | solution.py:606
  391.9 8.4 %shard_map.331 = (bf16[256,4096]{1,0:T(8,128)(2,1)}, bf16[256,4096]{1,0:T(8,128)(2,1)S(1)}) custom-call(bf16[512,512]{1,0:T(8,128)(2,1)} %copy-done.55, bf16[512,512]{1,0:T(8,128)(2,1)} %copy-done.112, bf16[512,4096]{1,0:T(8,128)(2,1)} %get-tuple-element.624.rows_ref.refs_2_, bf16[512,4096]{1,0:T(8,128)(2,1)} %collective-permute-done.55.refs_3_), custom_call_target="tpu_custom_call" | custom-call | flops 1024 | bytes 1024 | tf_op jit(solution)/shard_map/pallas_call | solution.py:273
  404.1 20.9 %shard_map.332 = (bf16[512,1024]{1,0:T(8,128)(2,1)S(1)}, f32[2,512,1024]{2,1,0:T(8,128)}, bf16[2,512,1024]{2,1,0:T(8,128)(2,1)S(1)}) custom-call(s32[1]{0:T(128)} %bitcast.s_ref, bf16[512,3072]{1,0:T(8,128)(2,1)} %copy-done.3, bf16[512,3072]{1,0:T(8,128)(2,1)} %copy-done.3, bf16[512,3072]{1,0:T(8,128)(2,1)} %copy-done.58, bf16[512,3072]{1,0:T(8,128)(2,1)} %copy-done.3, ...), custom_call_target="tpu_custom_call" | custom-call | flops 1024 | bytes 1024 | tf_op jit(solution)/shard_map/pallas_call | solution.py:497
  429.2 5.3 add_convert_fusion.8
  440.4 6.7 shard_map.334.up_ref
  449.6 9.4 %shard_map.335 = (bf16[256,4096]{1,0:T(8,128)(2,1)}, bf16[256,4096]{1,0:T(8,128)(2,1)}) custom-call(bf16[512,512]{1,0:T(8,128)(2,1)} %copy-done.53, bf16[512,512]{1,0:T(8,128)(2,1)} %collective-permute-done.42.refs_1_, bf16[512,3072]{1,0:T(8,128)(2,1)} %get-tuple-element.653.rows_ref.refs_2_, bf16[512,3072]{1,0:T(8,128)(2,1)} %collective-permute-done.62.refs_3_, ...), custom_call_target="tpu_custom_call" | custom-call | flops 1024 | bytes 1024 | tf_op jit(solution)/shard_map/pallas_call | solution.py:273
  467.7 9.4 %shard_map.337 = (bf16[512,4096]{1,0:T(8,128)(2,1)}, f32[1,4096]{1,0:T(1,128)S(1)}) custom-call(bf16[512,1024]{1,0:T(8,128)(2,1)S(1)} %get-tuple-element.667.rows_ref.b1, bf16[4096,1024]{1,0:T(8,128)(2,1)} %bitcast.282, bf16[512,4096]{1,0:T(8,128)(2,1)} %get-tuple-element.668.refs_0_), custom_call_target="tpu_custom_call" | custom-call | flops 1024 | bytes 1024 | tf_op jit(solution)/shard_map/pallas_call | solution.py:606
  477.2 4.4 collective-permute-done.64
  486.6 15.1 %shard_map.338 = (bf16[2,8,128,512]{3,2,1,0:T(8,128)(2,1)S(1)}, bf16[2,8,128,512]{3,2,1,0:T(8,128)(2,1)}) custom-call(s32[32]{0:T(128)S(1)} %stack.444.order_ref, s32[16]{0:T(128)S(1)} %select_reduce_fusion.place_ref, bf16[512,4096]{1,0:T(8,128)(2,1)} %copy-done.14, bf16[512,4096]{1,0:T(8,128)(2,1)} %collective-permute-done.43.a2, ...), custom_call_target="tpu_custom_call" | custom-call | flops 1024 | bytes 1024 | tf_op jit(solution)/shard_map/pallas_call | solution.py:346
  517.0 8.4 %shard_map.339.up_ref = f32[512,1024]{1,0:T(8,128)S(1)} custom-call(bf16[512,4096]{1,0:T(8,128)(2,1)} %get-tuple-element.701.rows_ref.refs_2_, bf16[1024,4096]{1,0:T(8,128)(2,1)} %bitcast.290, f32[512,1024]{1,0:T(8,128)S(1)} %copy-done.43), custom_call_target="tpu_custom_call" | custom-call | flops 1024 | bytes 1024 | tf_op jit(solution)/shard_map/pallas_call | solution.py:606
  531.8 7.5 %shard_map.342 = (bf16[256,4096]{1,0:T(8,128)(2,1)S(1)}, bf16[256,4096]{1,0:T(8,128)(2,1)S(1)}) custom-call(bf16[512,512]{1,0:T(8,128)(2,1)} %copy-done.52, bf16[512,512]{1,0:T(8,128)(2,1)} %copy-done.102, bf16[512,4096]{1,0:T(8,128)(2,1)} %get-tuple-element.701.rows_ref.refs_2_, bf16[512,4096]{1,0:T(8,128)(2,1)} %collective-permute-done.66.refs_3_), custom_call_target="tpu_custom_call" | custom-call | flops 1024 | bytes 1024 | tf_op jit(solution)/shard_map/pallas_call | solution.py:273
  553.3 21.1 %shard_map.343 = (bf16[512,1024]{1,0:T(8,128)(2,1)S(1)}, f32[2,512,1024]{2,1,0:T(8,128)}, bf16[2,512,1024]{2,1,0:T(8,128)(2,1)S(1)}) custom-call(s32[1]{0:T(128)} %bitcast.s_ref, bf16[512,3072]{1,0:T(8,128)(2,1)} %copy-done.2, bf16[512,3072]{1,0:T(8,128)(2,1)} %copy-done.2, bf16[512,3072]{1,0:T(8,128)(2,1)} %collective-permute-done.18.ko_ref.vo_ref, ...), custom_call_target="tpu_custom_call" | custom-call | flops 1024 | bytes 1024 | tf_op jit(solution)/shard_map/pallas_call | solution.py:497
  575.5 6.0 collective-permute-done.74
  596.0 8.9 %shard_map.345 = (bf16[256,4096]{1,0:T(8,128)(2,1)}, bf16[256,4096]{1,0:T(8,128)(2,1)}) custom-call(bf16[512,512]{1,0:T(8,128)(2,1)} %copy-done.50, bf16[512,512]{1,0:T(8,128)(2,1)} %copy-done.100, bf16[512,3072]{1,0:T(8,128)(2,1)} %copy-done.19, bf16[512,3072]{1,0:T(8,128)(2,1)} %copy-done.70, bf16[512,512]{1,0:T(8,128)(2,1)} %copy-done.51, ...), custom_call_target="tpu_custom_call" | custom-call | flops 1024 | bytes 1024 | tf_op jit(solution)/shard_map/pallas_call | solution.py:273
  611.7 7.1 %shard_map.346 = f32[512,1024]{1,0:T(8,128)S(1)} custom-call(bf16[512,3072]{1,0:T(8,128)(2,1)} %copy-done.19, bf16[1024,3072]{1,0:T(8,128)(2,1)} %bitcast.288, f32[512,1024]{1,0:T(8,128)S(1)} %copy-done.41), custom_call_target="tpu_custom_call" | custom-call | flops 1024 | bytes 1024 | tf_op jit(solution)/shard_map/pallas_call | solution.py:606
  618.8 13.6 %collective-permute-done.87 = bf16[64,128]{1,0:T(8,128)(2,1)S(1)} collective-permute-done((bf16[64,128]{1,0:T(8,128)(2,1)S(1)}, bf16[64,128]{1,0:T(8,128)(2,1)S(1)}, u32[]{:S(2)}, u32[]{:S(2)}) %collective-permute-start.87) | collective-permute-done | bytes 16416 | tf_op jit(solution)/shard_map/ppermute | solution.py:62
  643.9 7.4 %collective-permute-done.92 = bf16[32,128]{1,0:T(8,128)(2,1)S(1)} collective-permute-done((bf16[32,128]{1,0:T(8,128)(2,1)S(1)}, bf16[32,128]{1,0:T(8,128)(2,1)S(1)}, u32[]{:S(2)}, u32[]{:S(2)}) %collective-permute-start.92) | collective-permute-done | bytes 8224 | tf_op jit(solution)/shard_map/ppermute | solution.py:62
  659.2 12.6 %collective-permute-done.96 = bf16[16,128]{1,0:T(8,128)(2,1)S(1)} collective-permute-done((bf16[16,128]{1,0:T(8,128)(2,1)S(1)}, bf16[16,128]{1,0:T(8,128)(2,1)S(1)}, u32[]{:S(2)}, u32[]{:S(2)}) %collective-permute-start.96) | collective-permute-done | bytes 4128 | tf_op jit(solution)/shard_map/ppermute | solution.py:62
  677.8 6.7 collective-permute-done.97
  (641 shorter events, 274.2 us)
Async XLA Ops:
  30.3 20.3 %collective-permute-start.6 = (bf16[256,1024]{1,0:T(8,128)(2,1)}, bf16[256,1024]{1,0:T(8,128)(2,1)}, u32[]{:S(2)}, u32[]{:S(2)}) collective-permute-start(bf16[256,1024]{1,0:T(8,128)(2,1)} %get-tuple-element.424), channel_id=1, source_target_pairs={{0,2},{1,3},{2,0},{3,1},{4,6},{5,7},{6,4},{7,5},{8,10},{9,11},{10,... | collective-permute-start | bytes 1572872 | tf_op jit(solution)/shard_map/ppermute | solution.py:62
  66.0 20.5 %collective-permute-start.12 = (bf16[8,96,1024]{2,1,0:T(8,128)(2,1)S(1)}, bf16[8,96,1024]{2,1,0:T(8,128)(2,1)S(1)}, u32[]{:S(2)}, u32[]{:S(2)}) collective-permute-start(bf16[8,96,1024]{2,1,0:T(8,128)(2,1)S(1)} %pad_maximum_fusion.5.refs_0_), channel_id=1, source_target_pairs={{0,2},{1,5},{2,0},{3,7},{4,6},{5,1},{6,4},{7,3},{8,10},{9,13},{10,... | collective-permute-start | bytes 4718600 | tf_op jit(solution)/shard_map/ppermute | solution.py:62
  66.6 19.9 %collective-permute-start.13 = (bf16[8,96,1024]{2,1,0:T(8,128)(2,1)S(1)}, bf16[8,96,1024]{2,1,0:T(8,128)(2,1)}, u32[]{:S(2)}, u32[]{:S(2)}) collective-permute-start(bf16[8,96,1024]{2,1,0:T(8,128)(2,1)S(1)} %pad_maximum_fusion.5.refs_0_), channel_id=1, source_target_pairs={{0,1},{1,0},{2,3},{3,2},{4,5},{5,4},{6,7},{7,6},{8,9},{9,8},{10,11... | collective-permute-start | bytes 4718600 | tf_op jit(solution)/shard_map/ppermute | solution.py:62
  66.6 17.5 %collective-permute-start.14 = (bf16[2,160,1024]{2,1,0:T(8,128)(2,1)}, bf16[2,160,1024]{2,1,0:T(8,128)(2,1)}, u32[]{:S(2)}, u32[]{:S(2)}) collective-permute-start(bf16[2,160,1024]{2,1,0:T(8,128)(2,1)} %pad_maximum_fusion.14), channel_id=1, source_target_pairs={{0,8},{1,9},{2,10},{3,11},{4,12},{5,13},{6,14},{7,15},{8,0},{9,1},... | collective-permute-start | bytes 1966088 | tf_op jit(solution)/shard_map/ppermute | solution.py:62
  87.9 17.7 %collective-permute-start.16 = (bf16[4,160,1024]{2,1,0:T(8,128)(2,1)S(1)}, bf16[4,160,1024]{2,1,0:T(8,128)(2,1)S(1)}, u32[]{:S(2)}, u32[]{:S(2)}) collective-permute-start(bf16[4,160,1024]{2,1,0:T(8,128)(2,1)S(1)} %pad_maximum_fusion.6), channel_id=1, source_target_pairs={{0,4},{1,3},{2,6},{3,1},{4,0},{5,7},{6,2},{7,5},{8,12},{9,11},{10,... | collective-permute-start | bytes 3932168 | tf_op jit(solution)/shard_map/ppermute | solution.py:62
  108.8 31.8 %collective-permute-start.20 = (bf16[8,160,1024]{2,1,0:T(8,128)(2,1)S(1)}, bf16[8,160,1024]{2,1,0:T(8,128)(2,1)}, u32[]{:S(2)}, u32[]{:S(2)}) collective-permute-start(bf16[8,160,1024]{2,1,0:T(8,128)(2,1)S(1)} %pad_maximum_fusion.refs_0_), channel_id=1, source_target_pairs={{0,2},{1,5},{2,0},{3,7},{4,6},{5,1},{6,4},{7,3},{8,10},{9,13},{10,... | collective-permute-start | bytes 7864328 | tf_op jit(solution)/shard_map/ppermute | solution.py:62
  109.4 31.2 %collective-permute-start.21 = (bf16[8,160,1024]{2,1,0:T(8,128)(2,1)S(1)}, bf16[8,160,1024]{2,1,0:T(8,128)(2,1)}, u32[]{:S(2)}, u32[]{:S(2)}) collective-permute-start(bf16[8,160,1024]{2,1,0:T(8,128)(2,1)S(1)} %pad_maximum_fusion.refs_0_), channel_id=1, source_target_pairs={{0,1},{1,0},{2,3},{3,2},{4,5},{5,4},{6,7},{7,6},{8,9},{9,8},{10,11... | collective-permute-start | bytes 7864328 | tf_op jit(solution)/shard_map/ppermute | solution.py:62
  111.9 18.0 %collective-permute-start.19 = (bf16[512,512]{1,0:T(8,128)(2,1)S(1)}, bf16[512,512]{1,0:T(8,128)(2,1)S(1)}, u32[]{:S(2)}, u32[]{:S(2)}) collective-permute-start(bf16[512,512]{1,0:T(8,128)(2,1)S(1)} %get-tuple-element.472), channel_id=1, source_target_pairs={{0,1},{1,0},{2,3},{3,2},{4,5},{5,4},{6,7},{7,6},{8,9},{9,8},{10,11... | collective-permute-start | bytes 1572872 | tf_op jit(solution)/shard_map/ppermute | solution.py:62
  112.0 20.0 %collective-permute-start.22 = (bf16[2,128,1024]{2,1,0:T(8,128)(2,1)S(1)}, bf16[2,128,1024]{2,1,0:T(8,128)(2,1)S(1)}, u32[]{:S(2)}, u32[]{:S(2)}) collective-permute-start(bf16[2,128,1024]{2,1,0:T(8,128)(2,1)S(1)} %pad_maximum_fusion.15), channel_id=1, source_target_pairs={{0,8},{1,9},{2,10},{3,11},{4,12},{5,13},{6,14},{7,15},{8,0},{9,1},... | collective-permute-start | bytes 1572872 | tf_op jit(solution)/shard_map/ppermute | solution.py:62
  141.9 20.2 %collective-permute-start.25 = (bf16[4,128,1024]{2,1,0:T(8,128)(2,1)S(1)}, bf16[4,128,1024]{2,1,0:T(8,128)(2,1)S(1)}, u32[]{:S(2)}, u32[]{:S(2)}) collective-permute-start(bf16[4,128,1024]{2,1,0:T(8,128)(2,1)S(1)} %pad_maximum_fusion.7), channel_id=1, source_target_pairs={{0,4},{1,3},{2,6},{3,1},{4,0},{5,7},{6,2},{7,5},{8,12},{9,11},{10,... | collective-permute-start | bytes 3145736 | tf_op jit(solution)/shard_map/ppermute | solution.py:62
  143.4 18.6 %collective-permute-start.26 = (bf16[2,128,1024]{2,1,0:T(8,128)(2,1)S(1)}, bf16[2,128,1024]{2,1,0:T(8,128)(2,1)S(1)}, u32[]{:S(2)}, u32[]{:S(2)}) collective-permute-start(bf16[2,128,1024]{2,1,0:T(8,128)(2,1)S(1)} %pad_maximum_fusion.16), channel_id=1, source_target_pairs={{0,8},{1,9},{2,10},{3,11},{4,12},{5,13},{6,14},{7,15},{8,0},{9,1},... | collective-permute-start | bytes 1572872 | tf_op jit(solution)/shard_map/ppermute | solution.py:62
  164.7 37.3 %collective-permute-start.30 = (bf16[8,128,1024]{2,1,0:T(8,128)(2,1)S(1)}, bf16[8,128,1024]{2,1,0:T(8,128)(2,1)S(1)}, u32[]{:S(2)}, u32[]{:S(2)}) collective-permute-start(bf16[8,128,1024]{2,1,0:T(8,128)(2,1)S(1)} %pad_maximum_fusion.1.refs_0_), channel_id=1, source_target_pairs={{0,2},{1,5},{2,0},{3,7},{4,6},{5,1},{6,4},{7,3},{8,10},{9,13},{10,... | collective-permute-start | bytes 6291464 | tf_op jit(solution)/shard_map/ppermute | solution.py:62
  166.2 35.8 %collective-permute-start.31 = (bf16[8,128,1024]{2,1,0:T(8,128)(2,1)S(1)}, bf16[8,128,1024]{2,1,0:T(8,128)(2,1)S(1)}, u32[]{:S(2)}, u32[]{:S(2)}) collective-permute-start(bf16[8,128,1024]{2,1,0:T(8,128)(2,1)S(1)} %pad_maximum_fusion.1.refs_0_), channel_id=1, source_target_pairs={{0,1},{1,0},{2,3},{3,2},{4,5},{5,4},{6,7},{7,6},{8,9},{9,8},{10,11... | collective-permute-start | bytes 6291464 | tf_op jit(solution)/shard_map/ppermute | solution.py:62
  166.2 26.4 %collective-permute-start.32 = (bf16[4,128,1024]{2,1,0:T(8,128)(2,1)}, bf16[4,128,1024]{2,1,0:T(8,128)(2,1)}, u32[]{:S(2)}, u32[]{:S(2)}) collective-permute-start(bf16[4,128,1024]{2,1,0:T(8,128)(2,1)} %pad_maximum_fusion.8), channel_id=1, source_target_pairs={{0,4},{1,3},{2,6},{3,1},{4,0},{5,7},{6,2},{7,5},{8,12},{9,11},{10,... | collective-permute-start | bytes 3145736 | tf_op jit(solution)/shard_map/ppermute | solution.py:62
  171.8 20.5 %collective-permute-start.28 = (bf16[512,512]{1,0:T(8,128)(2,1)}, bf16[512,512]{1,0:T(8,128)(2,1)S(1)}, u32[]{:S(2)}, u32[]{:S(2)}) collective-permute-start(bf16[512,512]{1,0:T(8,128)(2,1)} %get-tuple-element.508), channel_id=1, source_target_pairs={{0,1},{1,0},{2,3},{3,2},{4,5},{5,4},{6,7},{7,6},{8,9},{9,8},{10,11... | collective-permute-start | bytes 1572872 | tf_op jit(solution)/shard_map/ppermute | solution.py:62
  204.9 26.4 %collective-permute-start.35 = (bf16[8,128,1024]{2,1,0:T(8,128)(2,1)}, bf16[8,128,1024]{2,1,0:T(8,128)(2,1)}, u32[]{:S(2)}, u32[]{:S(2)}) collective-permute-start(bf16[8,128,1024]{2,1,0:T(8,128)(2,1)} %pad_maximum_fusion.2.refs_0_), channel_id=1, source_target_pairs={{0,2},{1,5},{2,0},{3,7},{4,6},{5,1},{6,4},{7,3},{8,10},{9,13},{10,... | collective-permute-start | bytes 6291464 | tf_op jit(solution)/shard_map/ppermute | solution.py:62
  206.4 24.9 %collective-permute-start.36 = (bf16[8,128,1024]{2,1,0:T(8,128)(2,1)}, bf16[8,128,1024]{2,1,0:T(8,128)(2,1)}, u32[]{:S(2)}, u32[]{:S(2)}) collective-permute-start(bf16[8,128,1024]{2,1,0:T(8,128)(2,1)} %pad_maximum_fusion.2.refs_0_), channel_id=1, source_target_pairs={{0,1},{1,0},{2,3},{3,2},{4,5},{5,4},{6,7},{7,6},{8,9},{9,8},{10,11... | collective-permute-start | bytes 6291464 | tf_op jit(solution)/shard_map/ppermute | solution.py:62
  206.6 17.4 %collective-permute-start.37 = (bf16[1,128,1024]{2,1,0:T(8,128)(2,1)}, bf16[1,128,1024]{2,1,0:T(8,128)(2,1)S(1)}, u32[]{:S(2)}, u32[]{:S(2)}) collective-permute-start(bf16[1,128,1024]{2,1,0:T(8,128)(2,1)} %bitcast.100), channel_id=1, source_target_pairs={{0,16},{1,17},{2,18},{3,19},{4,20},{5,21},{6,22},{7,23},{8,24},{9,... | collective-permute-start | bytes 786440 | tf_op jit(solution)/shard_map/ppermute | solution.py:62
  233.4 17.5 %collective-permute-start.39 = (bf16[4,128,1024]{2,1,0:T(8,128)(2,1)}, bf16[4,128,1024]{2,1,0:T(8,128)(2,1)}, u32[]{:S(2)}, u32[]{:S(2)}) collective-permute-start(bf16[4,128,1024]{2,1,0:T(8,128)(2,1)} %pad_maximum_fusion.9), channel_id=1, source_target_pairs={{0,4},{1,3},{2,6},{3,1},{4,0},{5,7},{6,2},{7,5},{8,12},{9,11},{10,... | collective-permute-start | bytes 3145736 | tf_op jit(solution)/shard_map/ppermute | solution.py:62
  234.9 46.3 %collective-permute-start.43 = (bf16[512,4096]{1,0:T(8,128)(2,1)S(1)}, bf16[512,4096]{1,0:T(8,128)(2,1)}, u32[]{:S(2)}, u32[]{:S(2)}) collective-permute-start(bf16[512,4096]{1,0:T(8,128)(2,1)S(1)} %copy-done.15), channel_id=1, source_target_pairs={{0,1},{1,0},{2,3},{3,2},{4,5},{5,4},{6,7},{7,6},{8,9},{9,8},{10,11... | collective-permute-start | bytes 12582920 | tf_op jit(solution)/shard_map/ppermute | solution.py:62
  254.9 26.4 %collective-permute-start.44 = (bf16[8,128,1024]{2,1,0:T(8,128)(2,1)}, bf16[8,128,1024]{2,1,0:T(8,128)(2,1)}, u32[]{:S(2)}, u32[]{:S(2)}) collective-permute-start(bf16[8,128,1024]{2,1,0:T(8,128)(2,1)} %pad_maximum_fusion.3.refs_0_), channel_id=1, source_target_pairs={{0,2},{1,5},{2,0},{3,7},{4,6},{5,1},{6,4},{7,3},{8,10},{9,13},{10,... | collective-permute-start | bytes 6291464 | tf_op jit(solution)/shard_map/ppermute | solution.py:62
  256.4 24.9 %collective-permute-start.45 = (bf16[8,128,1024]{2,1,0:T(8,128)(2,1)}, bf16[8,128,1024]{2,1,0:T(8,128)(2,1)}, u32[]{:S(2)}, u32[]{:S(2)}) collective-permute-start(bf16[8,128,1024]{2,1,0:T(8,128)(2,1)} %pad_maximum_fusion.3.refs_0_), channel_id=1, source_target_pairs={{0,1},{1,0},{2,3},{3,2},{4,5},{5,4},{6,7},{7,6},{8,9},{9,8},{10,11... | collective-permute-start | bytes 6291464 | tf_op jit(solution)/shard_map/ppermute | solution.py:62
  284.1 21.2 %collective-permute-start.47 = (bf16[8,128,1024]{2,1,0:T(8,128)(2,1)}, bf16[8,128,1024]{2,1,0:T(8,128)(2,1)}, u32[]{:S(2)}, u32[]{:S(2)}) collective-permute-start(bf16[8,128,1024]{2,1,0:T(8,128)(2,1)} %collective-permute-done.44.refs_1_), channel_id=1, source_target_pairs={{0,1},{1,0},{2,3},{3,2},{4,5},{5,4},{6,7},{7,6},{8,9},{9,8},{10,11... | collective-permute-start | bytes 6291464 | tf_op jit(solution)/shard_map/ppermute | solution.py:62
  298.9 26.1 %collective-permute-start.50 = (bf16[8,128,1024]{2,1,0:T(8,128)(2,1)S(1)}, bf16[8,128,1024]{2,1,0:T(8,128)(2,1)S(1)}, u32[]{:S(2)}, u32[]{:S(2)}) collective-permute-start(bf16[8,128,1024]{2,1,0:T(8,128)(2,1)S(1)} %pad_maximum_fusion.4.refs_0_), channel_id=1, source_target_pairs={{0,2},{1,5},{2,0},{3,7},{4,6},{5,1},{6,4},{7,3},{8,10},{9,13},{10,... | collective-permute-start | bytes 6291464 | tf_op jit(solution)/shard_map/ppermute | solution.py:62
  300.4 24.6 %collective-permute-start.51 = (bf16[8,128,1024]{2,1,0:T(8,128)(2,1)S(1)}, bf16[8,128,1024]{2,1,0:T(8,128)(2,1)S(1)}, u32[]{:S(2)}, u32[]{:S(2)}) collective-permute-start(bf16[8,128,1024]{2,1,0:T(8,128)(2,1)S(1)} %pad_maximum_fusion.4.refs_0_), channel_id=1, source_target_pairs={{0,1},{1,0},{2,3},{3,2},{4,5},{5,4},{6,7},{7,6},{8,9},{9,8},{10,11... | collective-permute-start | bytes 6291464 | tf_op jit(solution)/shard_map/ppermute | solution.py:62
  304.8 20.1 %collective-permute-start.48 = (bf16[512,512]{1,0:T(8,128)(2,1)S(1)}, bf16[512,512]{1,0:T(8,128)(2,1)S(1)}, u32[]{:S(2)}, u32[]{:S(2)}) collective-permute-start(bf16[512,512]{1,0:T(8,128)(2,1)S(1)} %get-tuple-element.581), channel_id=1, source_target_pairs={{0,1},{1,0},{2,3},{3,2},{4,5},{5,4},{6,7},{7,6},{8,9},{9,8},{10,11... | collective-permute-start | bytes 1572872 | tf_op jit(solution)/shard_map/ppermute | solution.py:62
  305.3 19.6 %collective-permute-start.49 = (bf16[512,512]{1,0:T(8,128)(2,1)S(1)}, bf16[512,512]{1,0:T(8,128)(2,1)S(1)}, u32[]{:S(2)}, u32[]{:S(2)}) collective-permute-start(bf16[512,512]{1,0:T(8,128)(2,1)S(1)} %get-tuple-element.583), channel_id=1, source_target_pairs={{0,1},{1,0},{2,3},{3,2},{4,5},{5,4},{6,7},{7,6},{8,9},{9,8},{10,11... | collective-permute-start | bytes 1572872 | tf_op jit(solution)/shard_map/ppermute | solution.py:62
  358.7 18.0 %collective-permute-start.55 = (bf16[512,4096]{1,0:T(8,128)(2,1)}, bf16[512,4096]{1,0:T(8,128)(2,1)}, u32[]{:S(2)}, u32[]{:S(2)}) collective-permute-start(bf16[512,4096]{1,0:T(8,128)(2,1)} %get-tuple-element.624.rows_ref.refs_2_), channel_id=1, source_target_pairs={{0,1},{1,0},{2,3},{3,2},{4,5},{5,4},{6,7},{7,6},{8,9},{9,8},{10,11... | collective-permute-start | bytes 12582920 | tf_op jit(solution)/shard_map/ppermute | solution.py:62
  376.7 26.2 %collective-permute-start.57 = (bf16[1024,1024]{1,0:T(8,128)(2,1)S(1)}, bf16[1024,1024]{1,0:T(8,128)(2,1)}, u32[]{:S(2)}, u32[]{:S(2)}) collective-permute-start(bf16[1024,1024]{1,0:T(8,128)(2,1)S(1)} %get-tuple-element.628), channel_id=1, source_target_pairs={{0,2},{1,5},{2,0},{3,7},{4,6},{5,1},{6,4},{7,3},{8,10},{9,13},{10,... | collective-permute-start | bytes 6291464 | tf_op jit(solution)/shard_map/ppermute | solution.py:62
  402.9 26.2 %collective-permute-start.58 = (bf16[256,4096]{1,0:T(8,128)(2,1)}, bf16[256,4096]{1,0:T(8,128)(2,1)S(1)}, u32[]{:S(2)}, u32[]{:S(2)}) collective-permute-start(bf16[256,4096]{1,0:T(8,128)(2,1)} %get-tuple-element.635), channel_id=1, source_target_pairs={{0,2},{1,5},{2,0},{3,7},{4,6},{5,1},{6,4},{7,3},{8,10},{9,13},{10,... | collective-permute-start | bytes 6291464 | tf_op jit(solution)/shard_map/ppermute | solution.py:62
  439.2 19.8 %collective-permute-start.61 = (bf16[512,1024]{1,0:T(8,128)(2,1)}, bf16[512,1024]{1,0:T(8,128)(2,1)}, u32[]{:S(2)}, u32[]{:S(2)}) collective-permute-start(bf16[512,1024]{1,0:T(8,128)(2,1)} %get-tuple-element.649), channel_id=1, source_target_pairs={{0,4},{1,3},{2,6},{3,1},{4,0},{5,7},{6,2},{7,5},{8,12},{9,11},{10,... | collective-permute-start | bytes 3145736 | tf_op jit(solution)/shard_map/ppermute | solution.py:62
  483.6 26.4 %collective-permute-start.66 = (bf16[512,4096]{1,0:T(8,128)(2,1)}, bf16[512,4096]{1,0:T(8,128)(2,1)}, u32[]{:S(2)}, u32[]{:S(2)}) collective-permute-start(bf16[512,4096]{1,0:T(8,128)(2,1)} %get-tuple-element.701.rows_ref.refs_2_), channel_id=1, source_target_pairs={{0,1},{1,0},{2,3},{3,2},{4,5},{5,4},{6,7},{7,6},{8,9},{9,8},{10,11... | collective-permute-start | bytes 12582920 | tf_op jit(solution)/shard_map/ppermute | solution.py:62
  483.6 26.4 %collective-permute-start.67 = (bf16[256,4096]{1,0:T(8,128)(2,1)}, bf16[256,4096]{1,0:T(8,128)(2,1)}, u32[]{:S(2)}, u32[]{:S(2)}) collective-permute-start(bf16[256,4096]{1,0:T(8,128)(2,1)} %get-tuple-element.684), channel_id=1, source_target_pairs={{0,2},{1,5},{2,0},{3,7},{4,6},{5,1},{6,4},{7,3},{8,10},{9,13},{10,... | collective-permute-start | bytes 6291464 | tf_op jit(solution)/shard_map/ppermute | solution.py:62
  484.9 20.0 %collective-permute-start.69 = (bf16[128,1024]{1,0:T(8,128)(2,1)}, bf16[128,1024]{1,0:T(8,128)(2,1)S(1)}, u32[]{:S(2)}, u32[]{:S(2)}) collective-permute-start(bf16[128,1024]{1,0:T(8,128)(2,1)} %add_convert_fusion.32), channel_id=1, source_target_pairs={{0,16},{1,17},{2,18},{3,19},{4,20},{5,21},{6,22},{7,23},{8,24},{9,... | collective-permute-start | bytes 786440 | tf_op jit(solution)/shard_map/ppermute | solution.py:62
  486.3 19.8 %collective-permute-start.68 = (bf16[64,4096]{1,0:T(8,128)(2,1)}, bf16[64,4096]{1,0:T(8,128)(2,1)S(1)}, u32[]{:S(2)}, u32[]{:S(2)}) collective-permute-start(bf16[64,4096]{1,0:T(8,128)(2,1)} %get-tuple-element.685), channel_id=1, source_target_pairs={{0,8},{1,9},{2,10},{3,11},{4,12},{5,13},{6,14},{7,15},{8,0},{9,1},... | collective-permute-start | bytes 1572872 | tf_op jit(solution)/shard_map/ppermute | solution.py:62
  513.5 30.7 %collective-permute-start.70 = (bf16[1024,512]{1,0:T(8,128)(2,1)}, bf16[1024,512]{1,0:T(8,128)(2,1)}, u32[]{:S(2)}, u32[]{:S(2)}) collective-permute-start(bf16[1024,512]{1,0:T(8,128)(2,1)} %bitcast.154), channel_id=1, source_target_pairs={{0,8},{1,9},{2,10},{3,11},{4,12},{5,13},{6,14},{7,15},{8,0},{9,1},... | collective-permute-start | bytes 3145736 | tf_op jit(solution)/shard_map/ppermute | solution.py:62
  513.9 30.4 %collective-permute-start.71 = (bf16[1024,512]{1,0:T(8,128)(2,1)}, bf16[1024,512]{1,0:T(8,128)(2,1)}, u32[]{:S(2)}, u32[]{:S(2)}) collective-permute-start(bf16[1024,512]{1,0:T(8,128)(2,1)} %bitcast.156), channel_id=1, source_target_pairs={{0,2},{1,5},{2,0},{3,7},{4,6},{5,1},{6,4},{7,3},{8,10},{9,13},{10,... | collective-permute-start | bytes 3145736 | tf_op jit(solution)/shard_map/ppermute | solution.py:62
  514.7 29.6 %collective-permute-start.72 = (bf16[128,4096]{1,0:T(8,128)(2,1)}, bf16[128,4096]{1,0:T(8,128)(2,1)S(1)}, u32[]{:S(2)}, u32[]{:S(2)}) collective-permute-start(bf16[128,4096]{1,0:T(8,128)(2,1)} %get-tuple-element.707), channel_id=1, source_target_pairs={{0,4},{1,3},{2,6},{3,1},{4,0},{5,7},{6,2},{7,5},{8,12},{9,11},{10,... | collective-permute-start | bytes 3145736 | tf_op jit(solution)/shard_map/ppermute | solution.py:62
  515.6 26.3 %collective-permute-start.73 = (bf16[32,4096]{1,0:T(8,128)(2,1)S(1)}, bf16[32,4096]{1,0:T(8,128)(2,1)S(1)}, u32[]{:S(2)}, u32[]{:S(2)}) collective-permute-start(bf16[32,4096]{1,0:T(8,128)(2,1)S(1)} %add_convert_fusion.31), channel_id=1, source_target_pairs={{0,16},{1,17},{2,18},{3,19},{4,20},{5,21},{6,22},{7,23},{8,24},{9,... | collective-permute-start | bytes 786440 | tf_op jit(solution)/shard_map/ppermute | solution.py:62
  549.9 31.6 %collective-permute-start.74 = (bf16[256,4096]{1,0:T(8,128)(2,1)S(1)}, bf16[256,4096]{1,0:T(8,128)(2,1)}, u32[]{:S(2)}, u32[]{:S(2)}) collective-permute-start(bf16[256,4096]{1,0:T(8,128)(2,1)S(1)} %get-tuple-element.719), channel_id=1, source_target_pairs={{0,2},{1,5},{2,0},{3,7},{4,6},{5,1},{6,4},{7,3},{8,10},{9,13},{10,... | collective-permute-start | bytes 6291464 | tf_op jit(solution)/shard_map/ppermute | solution.py:62
  550.6 24.8 %collective-permute-start.75 = (bf16[512,512]{1,0:T(8,128)(2,1)}, bf16[512,512]{1,0:T(8,128)(2,1)S(1)}, u32[]{:S(2)}, u32[]{:S(2)}) collective-permute-start(bf16[512,512]{1,0:T(8,128)(2,1)} %get-tuple-element.720), channel_id=1, source_target_pairs={{0,16},{1,17},{2,18},{3,19},{4,20},{5,21},{6,22},{7,23},{8,24},{9,... | collective-permute-start | bytes 1572872 | tf_op jit(solution)/shard_map/ppermute | solution.py:62
  551.8 23.6 %collective-permute-start.76 = (bf16[512,512]{1,0:T(8,128)(2,1)}, bf16[512,512]{1,0:T(8,128)(2,1)S(1)}, u32[]{:S(2)}, u32[]{:S(2)}) collective-permute-start(bf16[512,512]{1,0:T(8,128)(2,1)} %get-tuple-element.721), channel_id=1, source_target_pairs={{0,4},{1,3},{2,6},{3,1},{4,0},{5,7},{6,2},{7,5},{8,12},{9,11},{10,... | collective-permute-start | bytes 1572872 | tf_op jit(solution)/shard_map/ppermute | solution.py:62
  552.8 22.7 %collective-permute-start.77 = (bf16[64,4096]{1,0:T(8,128)(2,1)}, bf16[64,4096]{1,0:T(8,128)(2,1)S(1)}, u32[]{:S(2)}, u32[]{:S(2)}) collective-permute-start(bf16[64,4096]{1,0:T(8,128)(2,1)} %get-tuple-element.722), channel_id=1, source_target_pairs={{0,8},{1,9},{2,10},{3,11},{4,12},{5,13},{6,14},{7,15},{8,0},{9,1},... | collective-permute-start | bytes 1572872 | tf_op jit(solution)/shard_map/ppermute | solution.py:62
  553.3 35.2 %collective-permute-start.79 = (bf16[512,1024]{1,0:T(8,128)(2,1)S(1)}, bf16[512,1024]{1,0:T(8,128)(2,1)S(1)}, u32[]{:S(2)}, u32[]{:S(2)}) collective-permute-start(bf16[512,1024]{1,0:T(8,128)(2,1)S(1)} %get-tuple-element.697.rows_ref.refs_6_), channel_id=1, source_target_pairs={{0,1},{1,0},{2,3},{3,2},{4,5},{5,4},{6,7},{7,6},{8,9},{9,8},{10,11... | collective-permute-start | bytes 3145736 | tf_op jit(solution)/shard_map/ppermute | solution.py:62
  588.6 17.4 %collective-permute-start.81 = (bf16[128,4096]{1,0:T(8,128)(2,1)S(1)}, bf16[128,4096]{1,0:T(8,128)(2,1)S(1)}, u32[]{:S(2)}, u32[]{:S(2)}) collective-permute-start(bf16[128,4096]{1,0:T(8,128)(2,1)S(1)} %get-tuple-element.743), channel_id=1, source_target_pairs={{0,4},{1,3},{2,6},{3,1},{4,0},{5,7},{6,2},{7,5},{8,12},{9,11},{10,... | collective-permute-start | bytes 3145736 | tf_op jit(solution)/shard_map/ppermute | solution.py:62
  606.0 26.4 %collective-permute-start.85 = (bf16[256,4096]{1,0:T(8,128)(2,1)}, bf16[256,4096]{1,0:T(8,128)(2,1)}, u32[]{:S(2)}, u32[]{:S(2)}) collective-permute-start(bf16[256,4096]{1,0:T(8,128)(2,1)} %get-tuple-element.753), channel_id=1, source_target_pairs={{0,2},{1,5},{2,0},{3,7},{4,6},{5,1},{6,4},{7,3},{8,10},{9,13},{10,... | collective-permute-start | bytes 6291464 | tf_op jit(solution)/shard_map/ppermute | solution.py:62
  609.1 23.4 %collective-permute-start.87 = (bf16[64,128]{1,0:T(8,128)(2,1)S(1)}, bf16[64,128]{1,0:T(8,128)(2,1)S(1)}, u32[]{:S(2)}, u32[]{:S(2)}) collective-permute-start(bf16[64,128]{1,0:T(8,128)(2,1)S(1)} %get-tuple-element.763), channel_id=1, source_target_pairs={{0,2},{1,5},{2,0},{3,7},{4,6},{5,1},{6,4},{7,3},{8,10},{9,13},{10,... | collective-permute-start | bytes 49160 | tf_op jit(solution)/shard_map/ppermute | solution.py:62
  653.0 18.7 %collective-permute-start.93 = (bf16[256,1024]{1,0:T(8,128)(2,1)S(1)}, bf16[256,1024]{1,0:T(8,128)(2,1)S(1)}, u32[]{:S(2)}, u32[]{:S(2)}) collective-permute-start(bf16[256,1024]{1,0:T(8,128)(2,1)S(1)} %slice.1021), channel_id=1, source_target_pairs={{0,2},{1,3},{2,0},{3,1},{4,6},{5,7},{6,4},{7,5},{8,10},{9,11},{10,... | collective-permute-start | bytes 1572872 | tf_op jit(solution)/shard_map/ppermute | solution.py:62
  (186 other events, 1862.3 us)
